TPU v7x, 128 devices: a whole 4x4x4 slice. The times are simulated.
128 devices in a mesh: seq: 64 (over x, z, y), head: 2 (over core).
Axes of the slice: x: 4, y: 4, z: 4, core: 2. Of those that a mesh axis runs over, the one named last changes fastest.
Arguments:
- hidden: bfloat16 [16384, 2048], P('seq', 'head'), may hold values from -16 to 16
- proj_weights: bfloat16 [2048, 3, 1024], P(None, None, 'head'), may hold values from -0.125 to 0.125
- level_mix: float32 [15, 8, 16384], P(None, 'head', 'seq'), may hold values from 0.25 to 1
- out_grad: bfloat16 [16384, 1024], P('seq', 'head'), may hold values from -1.5 to 1.5
Outputs:
- attended: bfloat16 [16384, 1024], P('seq', 'head')
- input_grad: bfloat16 [16384, 2048], P('seq', 'head')
- weight_grad: float32 [2048, 3, 1024], P('seq', None, 'head')
- level_grad: float32 [15, 8, 16384], P(None, 'head', 'seq')
All inputs are finite; a program needn't handle non-finite values.
Results may differ from a plain program's by a relative error of at most 0.0062.
Values may be sent and summed in bfloat16 or wider, within the bound.
No kernel may reach another device: no remote copies, remote signals or barrier semaphores. Data moves between devices by JAX's collectives and lax.ppermute only.
A program may use at most 128 MiB of HBM per device.

v0:
```python
import jax
import jax.numpy as jnp
from jax import lax
from jax.sharding import Mesh
from jax.sharding import PartitionSpec as P

DH = 128
SEQ = ("seq_0", "seq_1", "seq_2")


UPPER_LIMIT = lax.Precision.HIGHEST


def swapped(value, axis, bit):
    mask = 2**bit
    pairs = [(source, source ^ mask) for source in range(lax.axis_size(axis))]
    return lax.ppermute(value, axis, pairs)


def split_up(array, dim, length):
    shape = array.shape
    blocks = array.reshape(*shape[:dim], length, shape[dim] // length, *shape[dim + 1 :])
    return jnp.moveaxis(blocks, dim, 0)


def sent_and_summed(array, axis, dim):
    blocks = split_up(array, dim, lax.axis_size(axis))
    arrived = lax.all_to_all(blocks, axis, split_axis=0, concat_axis=0, tiled=True)
    return arrived.sum(axis=0)


def sum_by_axis(total, axes):
    for axis in axes:
        total = lax.psum_scatter(total, axis, scatter_dimension=0, tiled=True)
    return total


def digit_count(numbers, digits):
    counted = jnp.zeros(numbers.shape, jnp.int32)
    for place in range(digits):
        counted = counted + (numbers >= 1 << place).astype(jnp.int32)
    return counted


def level_table(count, digits):
    positions = jnp.arange(count, dtype=jnp.int32)
    levels = digit_count(jnp.bitwise_xor(positions[:, None], positions[None, :]), digits)
    return jnp.where(positions[None, :] <= positions[:, None], levels, -1)


def level_scale(count):
    order = jnp.arange(count, dtype=jnp.float32)
    return jnp.where(order < 0.5, 1.0, jnp.exp2(-0.5 * (order - 1.0)))


def inner_head(queries, key_rows, values, grads, weights, table):
    scores = jnp.dot(queries, key_rows.T, preferred_element_type=jnp.float32)
    weighting = jnp.zeros(scores.shape, jnp.float32)
    for level_no in range(weights.shape[0]):
        weighting = jnp.where(table == level_no, weights[level_no][:, None], weighting)
    mixed = (weighting * scores).astype(jnp.bfloat16)
    result = jnp.dot(mixed, values, preferred_element_type=jnp.float32)
    mix_grad = jnp.dot(grads, values.T, preferred_element_type=jnp.float32)
    value_grad = jnp.dot(mixed.T, grads, preferred_element_type=jnp.float32)
    score_grad = (weighting * mix_grad).astype(jnp.bfloat16)
    query_gradient = jnp.dot(score_grad, key_rows, preferred_element_type=jnp.float32)
    key_grad = jnp.dot(score_grad.T, queries, preferred_element_type=jnp.float32)
    product = mix_grad * scores
    level_grad = jnp.stack(
        [
            jnp.sum(jnp.where(table == level_no, product, 0.0), axis=1)
            for level_no in range(weights.shape[0])
        ]
    )
    return (result, query_gradient, key_grad, value_grad, level_grad)


def bucket_tree(local_state, bit_flags, log_seq):
    group_sum = local_state
    found = []
    for bit_no in range(log_seq):
        other = swapped(group_sum, SEQ, bit_no)
        found.append(other * bit_flags[bit_no])
        group_sum = group_sum + other
    return jnp.stack(found)


def adjoint_tree(bucket_grads, bit_flags, log_seq):
    pending = bucket_grads
    gathered = jnp.zeros(bucket_grads.shape[1:], jnp.float32)
    for bit_no in range(log_seq):
        other = swapped(pending, SEQ, bit_no)
        gathered = gathered + other[0] * (1.0 - bit_flags[bit_no])
        pending = (pending + other)[1:]
    return gathered


def on_device(hidden, proj_weights, level_mix, out_grad):
    tokens_here = hidden.shape[0]
    log_tok = tokens_here.bit_length() - 1
    seq_count = lax.axis_size(SEQ)
    log_seq = seq_count.bit_length() - 1
    device_index = lax.axis_index(SEQ)
    head_count = proj_weights.shape[2] // DH
    inner_levels = log_tok + 1
    root = DH ** (-0.5)
    features = lax.all_gather(hidden, "head", axis=1, tiled=True)
    projected = jnp.einsum(
        "td,dme->mte", features, proj_weights, preferred_element_type=jnp.float32
    )
    queries = (projected[0] * root).astype(jnp.bfloat16)
    key_rows = projected[1].astype(jnp.bfloat16)
    values = projected[2].astype(jnp.bfloat16)

    def by_head(array):
        return array.reshape(tokens_here, head_count, DH).transpose(1, 0, 2)

    def by_token(array):
        return array.transpose(1, 0, 2).reshape(tokens_here, head_count * DH)

    head_queries = by_head(queries)
    key_per_head = by_head(key_rows)
    value_per_head = by_head(values)
    head_grads = by_head(out_grad)
    bit_flags = jnp.stack(
        [(device_index // (1 << bit_no) % 2).astype(jnp.float32) for bit_no in range(log_seq)]
    )
    scale = level_scale(level_mix.shape[0])
    level_weights = level_mix * scale[:, None, None]
    inner_weights = level_weights[:inner_levels].transpose(1, 0, 2)
    outer_weights = level_weights[inner_levels:] * bit_flags[:, None, None]
    local_state = jnp.einsum(
        "scf,scr->sfr", key_per_head, value_per_head, preferred_element_type=jnp.float32
    )
    buckets = bucket_tree(local_state, bit_flags, log_seq)
    table = level_table(tokens_here, log_tok)

    def one_head(bundle):
        return inner_head(bundle[0], bundle[1], bundle[2], bundle[3], bundle[4], table)

    inner_out, inner_query, inner_key, inner_value, inner_level = lax.map(
        one_head, (head_queries, key_per_head, value_per_head, head_grads, inner_weights)
    )
    query_wide = head_queries.astype(jnp.float32)
    grads_wide = head_grads.astype(jnp.float32)
    reads = jnp.einsum("htk,jhkv->jhtv", query_wide, buckets, precision=UPPER_LIMIT)
    outer_out = jnp.sum(outer_weights[..., None] * reads, axis=0)
    attended = by_token(inner_out + outer_out).astype(jnp.bfloat16)
    outer_level = jnp.sum(grads_wide[None] * reads, axis=-1)
    weighted = outer_weights[..., None] * grads_wide[None]
    outer_query = jnp.einsum("jhtv,jhkv->htk", weighted, buckets, precision=UPPER_LIMIT)
    bucket_grads = jnp.einsum("htk,jhtv->jhkv", query_wide, weighted, precision=UPPER_LIMIT)
    flat_queries = by_token((inner_query + outer_query) * root).astype(jnp.bfloat16)
    grad_scale = (tokens_here * seq_count) ** (-0.5)
    state_gradient = adjoint_tree(bucket_grads, bit_flags, log_seq)
    outer_key = jnp.einsum(
        "cag,crg->car", value_per_head.astype(jnp.float32), state_gradient, precision=UPPER_LIMIT
    )
    outer_value = jnp.einsum(
        "may,mye->mae", key_per_head.astype(jnp.float32), state_gradient, precision=UPPER_LIMIT
    )
    flat_keys = by_token(inner_key + outer_key).astype(jnp.bfloat16)
    flat_values = by_token(inner_value + outer_value).astype(jnp.bfloat16)
    grad_stack = jnp.stack([flat_queries, flat_keys, flat_values], axis=1)
    level_grad = (
        jnp.concatenate([inner_level.transpose(1, 0, 2), outer_level], axis=0)
        * scale[:, None, None]
    )
    partial_inputs = jnp.einsum(
        "tme,dme->td", grad_stack, proj_weights, preferred_element_type=jnp.float32
    )
    input_grad = sent_and_summed(partial_inputs, "head", 1).astype(jnp.bfloat16)
    weight_grad = sum_by_axis(
        jnp.einsum("td,tme->dme", features, grad_stack, preferred_element_type=jnp.float32)
        * grad_scale,
        SEQ,
    )
    return (attended, input_grad, weight_grad, level_grad)


def solution(mesh):
    split = Mesh(
        mesh.devices.reshape(4, 4, 4, mesh.shape["head"]), ("seq_0", "seq_1", "seq_2", "head")
    )
    placed = (P(SEQ, "head"), P(None, None, "head"), P(None, "head", SEQ), P(SEQ, "head"))
    return jax.shard_map(
        on_device,
        mesh=split,
        in_specs=placed,
        out_specs=(P(SEQ, "head"), P(SEQ, "head"), P(SEQ, None, "head"), P(None, "head", SEQ)),
        check_vma=False,
    )
```

profile of v0, /device:TPU:0, one launch (start us, length us, event | category | flops | bytes accessed | tf_op | source)
XLA Modules:
  0.0 418.4 jit_solution(2239120874331085848)
XLA Ops:
  8.2 0.9 broadcast_multiply_fusion
  9.2 1.1 copy.56
  10.3 13.5 %all-gather.2.cloned.1.call-done = bf16[256,2048]{1,0:T(8,128)(2,1)} async-done(((bf16[256,1024]{1,0:T(8,128)(2,1)}), bf16[256,2048]{1,0:T(8,128)(2,1)}) %all-gather.2.cloned.1.call-update) | async-done | bytes 1048592 | tf_op jit(solution)/shard_map/all_gather | solution.py:107
  23.9 5.9 %fusion.102 = (bf16[3,256,512]{1,2,0:T(8,128)(2,1)}, f32[3,256,512]{1,2,0:T(8,128)S(1)}) fusion(bf16[2048,3,512]{2,0,1:T(8,128)(2,1)} %param.7, bf16[256,2048]{1,0:T(8,128)(2,1)} %all-gather.2.cloned.1.call-done), kind=kOutput, calls=%fused_computation.149 | convolution fusion | flops 1611005952 | bytes 9699328 | tf_op jit(solution)/shard_map/td,dme->mte/dot_general | solution.py:108
  30.0 1.7 fusion.53
  31.7 1.7 collective-permute-start.6
  33.4 35.0 %collective-permute-done.6 = f32[6,4,128,128]{2,3,0,1:T(8,128)S(1)} collective-permute-done((f32[6,4,128,128]{2,3,0,1:T(8,128)S(1)}, f32[6,4,128,128]{2,3,0,1:T(8,128)S(1)}, u32[]{:S(2)}, u32[]{:S(2)}) %collective-permute-start.6) | collective-permute-done | bytes 1572896 | tf_op jit(solution)/shard_map/ppermute | solution.py:17
  68.6 1.0 copy-done
  69.5 3.1 collective-permute-start.7
  72.6 28.5 %collective-permute-done.7 = f32[5,4,128,128]{2,3,0,1:T(8,128)S(1)} collective-permute-done((f32[5,4,128,128]{2,3,0,1:T(8,128)S(1)}, f32[5,4,128,128]{2,3,0,1:T(8,128)S(1)}, u32[]{:S(2)}, u32[]{:S(2)}) %collective-permute-start.7) | collective-permute-done | bytes 1310752 | tf_op jit(solution)/shard_map/ppermute | solution.py:17
  101.3 0.9 copy-done.1
  102.2 1.6 collective-permute-start.8
  104.3 1.6 collective-permute-start
  105.9 5.0 %collective-permute-done = f32[4,128,128]{2,1,0:T(8,128)S(1)} collective-permute-done((f32[4,128,128]{2,1,0:T(8,128)S(1)}, f32[4,128,128]{2,1,0:T(8,128)S(1)}, u32[]{:S(2)}, u32[]{:S(2)}) %collective-permute-start) | collective-permute-done | bytes 262176 | tf_op jit(solution)/shard_map/ppermute | solution.py:17
  110.9 3.1 collective-permute-start.1
  114.0 4.8 %collective-permute-done.1 = f32[4,128,128]{2,1,0:T(8,128)S(1)} collective-permute-done((f32[4,128,128]{2,1,0:T(8,128)S(1)}, f32[4,128,128]{2,1,0:T(8,128)S(1)}, u32[]{:S(2)}, u32[]{:S(2)}) %collective-permute-start.1) | collective-permute-done | bytes 262176 | tf_op jit(solution)/shard_map/ppermute | solution.py:17
  119.4 12.2 %collective-permute-done.2 = f32[4,128,128]{2,1,0:T(8,128)} collective-permute-done((f32[4,128,128]{2,1,0:T(8,128)S(1)}, f32[4,128,128]{2,1,0:T(8,128)}, u32[]{:S(2)}, u32[]{:S(2)}) %collective-permute-start.2) | collective-permute-done | bytes 262176 | tf_op jit(solution)/shard_map/ppermute | solution.py:17
  131.6 1.0 add.383
  132.6 3.3 collective-permute-start.3
  135.9 2.1 slice_add_fusion.2
  138.3 19.2 %while.20 = (s32[]{:T(128)}, f32[4,256,128]{1,2,0:T(8,128)}, f32[4,256,128]{1,2,0:T(8,128)}, f32[4,256,128]{1,2,0:T(8,128)}, f32[4,256,128]{1,2,0:T(8,128)}, /*i...) while((s32[]{:T(128)}, f32[4,256,128]{1,2,0:T(8,128)}, ...), condition=%wide.region_10.11_spmd.clone.clone, body=%wide.region_0.10_spmd.clone.clone.sunk | while | flops 116258560 | bytes 3534157 | solution.py:141
  138.5 1.0 fusion.132
  139.5 1.0 fusion.128
  141.1 1.0 fusion.131
  142.1 1.0 fusion.130
  143.4 1.0 fusion.132
  144.4 1.0 fusion.128
  145.9 1.0 fusion.131
  146.9 1.0 fusion.130
  148.2 1.0 fusion.132
  149.1 1.0 fusion.128
  150.7 1.0 fusion.131
  151.7 1.0 fusion.130
  152.9 1.0 fusion.132
  153.9 1.0 fusion.128
  155.5 1.0 fusion.131
  156.5 1.0 fusion.130
  157.5 1.0 bitcast_dynamic-update-slice_fusion.5
  158.5 1.0 add.384
  159.4 1.6 collective-permute-start.4
  161.1 1.0 bitcast_dynamic-update-slice_fusion.3
  162.1 3.8 collective-permute-done.4
  165.9 3.8 collective-permute-start.5
  169.8 1.3 slice_add_fusion.3
  171.0 1.9 collective-permute-start.10
  173.0 1.0 bitcast_dynamic-update-slice_fusion.2
  174.0 3.0 collective-permute-done.5
  176.9 6.2 %collective-permute-done.10 = f32[2,4,128,128]{2,3,0,1:T(8,128)S(1)} collective-permute-done((f32[2,4,128,128]{2,3,0,1:T(8,128)S(1)}, f32[2,4,128,128]{2,3,0,1:T(8,128)S(1)}, u32[]{:S(2)}, u32[]{:S(2)}) %collective-permute-start.10) | collective-permute-done | bytes 524320 | tf_op jit(solution)/shard_map/ppermute | solution.py:17
  183.9 3.1 collective-permute-start.11
  187.0 2.2 fusion.74
  189.3 2.8 collective-permute-done.11
  192.1 1.5 fusion.87
  193.9 1.1 fusion.79
  195.0 1.1 copy.71
  196.3 7.6 %multiply_bitcast_fusion = f32[2048,3,512]{0,2,1:T(8,128)} fusion(bf16[256,2048]{1,0:T(8,128)(2,1)} %all-gather.2.cloned.1.call-done, bf16[256,1,512]{2,0,1:T(8,128)(2,1)S(1)} %copy.72, bf16[256,1,512]{2,0,1:T(8,128)(2,1)S(1)} %copy.71, bf16[256,1,512]{2,0,1:T(8,128)(2,1)S(1)} %copy.70), kind=kOutput, calls=%fused_computation.74 | convolution fusion | flops 1614544896 | bytes 14417920 | tf_op jit(solution)/shard_map/td,tme->dme/dot_general | solution.py:174
  204.0 117.0 %reduce-scatter.3.cloned.1.call-done = f32[512,3,512]{0,2,1:T(8,128)} async-done(((f32[2048,3,512]{0,2,1:T(8,128)}), f32[512,3,512]{0,2,1:T(8,128)}) %reduce-scatter.3.cloned.1.call-update) | async-done | bytes 3145744 | tf_op jit(solution)/shard_map/reduce_scatter | solution.py:34
  322.9 2.6 fusion.48
  325.5 36.2 %reduce-scatter.5.cloned.1.call-done = f32[128,3,512]{0,2,1:T(8,128)} async-done(((f32[512,3,512]{0,2,1:T(8,128)}), f32[128,3,512]{0,2,1:T(8,128)}) %reduce-scatter.5.cloned.1.call-update) | async-done | bytes 786448 | tf_op jit(solution)/shard_map/reduce_scatter | solution.py:34
  361.7 2.5 copy.75
  365.9 4.6 %fusion.84 = f32[256,2048,1]{1,0,2:T(8,128)S(1)} fusion(bf16[2048,3,512]{2,0,1:T(8,128)(2,1)} %param.7, bf16[256,1,512]{2,0,1:T(8,128)(2,1)S(1)} %copy.72, bf16[256,1,512]{2,0,1:T(8,128)(2,1)S(1)} %copy.71, bf16[256,1,512]{2,0,1:T(8,128)(2,1)S(1)} %copy.70), kind=kOutput, calls=%fused_computation.111 | convolution fusion | flops 1611399168 | bytes 9175040 | tf_op jit(solution)/shard_map/tme,dme->td/dot_general | solution.py:169
  370.8 5.4 %all_to_all.5 = f32[2,256,1024]{2,1,0:T(8,128)S(1)} all-to-all(f32[2,256,1024]{2,1,0:T(8,128)S(1)} %bitcast.251), channel_id=1, replica_groups=mesh['seq_0'=4,'seq_1'=4,'seq_2'=4,'head'=2] {'head'}, dimensions={0} | all-to-all | bytes 4194304 | tf_op jit(solution)/shard_map/all_to_all | solution.py:28
  376.2 1.1 reduce_sum.109
  377.3 32.8 %all-reduce.3.cloned.1.call-done = f32[128,3,512]{2,1,0:T(4,128)} async-done(((f32[128,3,512]{2,1,0:T(4,128)}), f32[128,3,512]{2,1,0:T(4,128)}) %all-reduce.3.cloned.1.call-update) | async-done | bytes 786448
  410.1 1.0 constant_dynamic-slice_fusion.9
  (96 shorter events, 11.4 us)
Async XLA Ops:
  7.2 16.7 %all-gather.2.cloned.1.call-start = ((), (), s32[]{:S(2)}) async-start(), calls=%async_computation.3 | async-start | bytes 1572864 | tf_op jit(solution)/shard_map/all_gather | solution.py:107
  7.9 313.1 %reduce-scatter.3.cloned.1.call-start = ((), (), s32[]{:S(2)}) async-start(), calls=%async_computation.4 | async-start | bytes 15728640 | tf_op jit(solution)/shard_map/reduce_scatter | solution.py:34
  31.7 36.7 %collective-permute-start.6 = (f32[6,4,128,128]{2,3,0,1:T(8,128)S(1)}, f32[6,4,128,128]{2,3,0,1:T(8,128)S(1)}, u32[]{:S(2)}, u32[]{:S(2)}) collective-permute-start(f32[6,4,128,128]{2,3,0,1:T(8,128)S(1)} %fusion.53), channel_id=1, source_target_pairs={{0,2},{2,0},{4,6},{6,4},{8,10},{10,8},{12,14},{14,12},{16,18},{18,... | collective-permute-start | bytes 4718600 | tf_op jit(solution)/shard_map/ppermute | solution.py:17
  68.4 1.2 copy-start
  69.5 34.3 %copy-start.9 = (bf16[3,256,512]{1,2,0:T(8,128)(2,1)S(1)}, bf16[3,256,512]{1,2,0:T(8,128)(2,1)}, u32[]{:S(2)}) copy-start(bf16[3,256,512]{1,2,0:T(8,128)(2,1)} %get-tuple-element.285) | copy-start | bytes 2359300
  69.5 31.6 %collective-permute-start.7 = (f32[5,4,128,128]{2,3,0,1:T(8,128)S(1)}, f32[5,4,128,128]{2,3,0,1:T(8,128)S(1)}, u32[]{:S(2)}, u32[]{:S(2)}) collective-permute-start(f32[5,4,128,128]{2,3,0,1:T(8,128)S(1)} %slice_add_fusion), channel_id=1, source_target_pairs={{0,4},{2,6},{4,0},{6,2},{8,12},{10,14},{12,8},{14,10},{16,20},{18,... | collective-permute-start | bytes 3932168 | tf_op jit(solution)/shard_map/ppermute | solution.py:17
  101.2 1.1 copy-start.1
  102.2 33.7 %collective-permute-start.8 = (f32[4,4,128,128]{2,3,0,1:T(8,128)S(1)}, f32[4,4,128,128]{2,3,0,1:T(8,128)}, u32[]{:S(2)}, u32[]{:S(2)}) collective-permute-start(f32[4,4,128,128]{2,3,0,1:T(8,128)S(1)} %slice_add_fusion.1), channel_id=1, source_target_pairs={{0,8},{2,10},{4,12},{6,14},{8,0},{10,2},{12,4},{14,6},{16,24},{18,... | collective-permute-start | bytes 3145736 | tf_op jit(solution)/shard_map/ppermute | solution.py:17
  104.3 6.6 %collective-permute-start = (f32[4,128,128]{2,1,0:T(8,128)S(1)}, f32[4,128,128]{2,1,0:T(8,128)S(1)}, u32[]{:S(2)}, u32[]{:S(2)}) collective-permute-start(f32[4,128,128]{2,1,0:T(8,128)S(1)} %fusion.98), channel_id=1, source_target_pairs={{0,2},{2,0},{4,6},{6,4},{8,10},{10,8},{12,14},{14,12},{16,18},{18,... | collective-permute-start | bytes 786440 | tf_op jit(solution)/shard_map/ppermute | solution.py:17
  110.9 8.0 %copy-start.2 = (f32[4,128,128]{2,1,0:T(8,128)}, f32[4,128,128]{2,1,0:T(8,128)S(1)}, u32[]{:S(2)}) copy-start(f32[4,128,128]{2,1,0:T(8,128)S(1)} %collective-permute-done) | copy-start | bytes 786436
  110.9 8.0 %collective-permute-start.1 = (f32[4,128,128]{2,1,0:T(8,128)S(1)}, f32[4,128,128]{2,1,0:T(8,128)S(1)}, u32[]{:S(2)}, u32[]{:S(2)}) collective-permute-start(f32[4,128,128]{2,1,0:T(8,128)S(1)} %add.381), channel_id=1, source_target_pairs={{0,4},{2,6},{4,0},{6,2},{8,12},{10,14},{12,8},{14,10},{16,20},{18,... | collective-permute-start | bytes 786440 | tf_op jit(solution)/shard_map/ppermute | solution.py:17
  118.9 12.6 %collective-permute-start.2 = (f32[4,128,128]{2,1,0:T(8,128)S(1)}, f32[4,128,128]{2,1,0:T(8,128)}, u32[]{:S(2)}, u32[]{:S(2)}) collective-permute-start(f32[4,128,128]{2,1,0:T(8,128)S(1)} %add.382), channel_id=1, source_target_pairs={{0,8},{2,10},{4,12},{6,14},{8,0},{10,2},{12,4},{14,6},{16,24},{18,... | collective-permute-start | bytes 786440 | tf_op jit(solution)/shard_map/ppermute | solution.py:17
  132.6 25.9 %collective-permute-start.3 = (f32[4,128,128]{2,1,0:T(8,128)S(1)}, f32[4,128,128]{2,1,0:T(8,128)}, u32[]{:S(2)}, u32[]{:S(2)}) collective-permute-start(f32[4,128,128]{2,1,0:T(8,128)S(1)} %add.383), channel_id=1, source_target_pairs={{0,16},{2,18},{4,20},{6,22},{8,24},{10,26},{12,28},{14,30},{16,0},... | collective-permute-start | bytes 786440 | tf_op jit(solution)/shard_map/ppermute | solution.py:17
  138.0 31.7 %collective-permute-start.9 = (f32[3,4,128,128]{2,3,0,1:T(8,128)}, f32[3,4,128,128]{2,3,0,1:T(8,128)}, u32[]{:S(2)}, u32[]{:S(2)}) collective-permute-start(f32[3,4,128,128]{2,3,0,1:T(8,128)} %slice_add_fusion.2), channel_id=1, source_target_pairs={{0,16},{2,18},{4,20},{6,22},{8,24},{10,26},{12,28},{14,30},{16,0},... | collective-permute-start | bytes 2359304 | tf_op jit(solution)/shard_map/ppermute | solution.py:17
  159.4 6.5 %collective-permute-start.4 = (f32[4,128,128]{2,1,0:T(8,128)S(1)}, f32[4,128,128]{2,1,0:T(8,128)S(1)}, u32[]{:S(2)}, u32[]{:S(2)}) collective-permute-start(f32[4,128,128]{2,1,0:T(8,128)S(1)} %add.384), channel_id=1, source_target_pairs={{0,32},{2,34},{4,36},{6,38},{8,40},{10,42},{12,44},{14,46},{16,48}... | collective-permute-start | bytes 786440 | tf_op jit(solution)/shard_map/ppermute | solution.py:17
  165.9 11.0 %collective-permute-start.5 = (f32[4,128,128]{2,1,0:T(8,128)S(1)}, f32[4,128,128]{2,1,0:T(8,128)S(1)}, u32[]{:S(2)}, u32[]{:S(2)}) collective-permute-start(f32[4,128,128]{2,1,0:T(8,128)S(1)} %add.385), channel_id=1, source_target_pairs={{0,64},{2,66},{4,68},{6,70},{8,72},{10,74},{12,76},{14,78},{16,80}... | collective-permute-start | bytes 786440 | tf_op jit(solution)/shard_map/ppermute | solution.py:17
  171.0 16.0 %copy-start.8 = (f32[4,256,128]{1,2,0:T(8,128)S(1)}, f32[4,256,128]{1,2,0:T(8,128)}, u32[]{:S(2)}) copy-start(f32[4,256,128]{1,2,0:T(8,128)} %get-tuple-element.122) | copy-start | bytes 1572868
  171.0 12.1 %collective-permute-start.10 = (f32[2,4,128,128]{2,3,0,1:T(8,128)S(1)}, f32[2,4,128,128]{2,3,0,1:T(8,128)S(1)}, u32[]{:S(2)}, u32[]{:S(2)}) collective-permute-start(f32[2,4,128,128]{2,3,0,1:T(8,128)S(1)} %slice_add_fusion.3), channel_id=1, source_target_pairs={{0,32},{2,34},{4,36},{6,38},{8,40},{10,42},{12,44},{14,46},{16,48}... | collective-permute-start | bytes 1572872 | tf_op jit(solution)/shard_map/ppermute | solution.py:17
  183.1 3.9 copy-start.3
  183.9 8.2 %collective-permute-start.11 = (f32[1,4,128,128]{2,3,0,1:T(8,128)}, f32[1,4,128,128]{2,3,0,1:T(8,128)}, u32[]{:S(2)}, u32[]{:S(2)}) collective-permute-start(f32[1,4,128,128]{2,3,0,1:T(8,128)} %slice_add_fusion.4), channel_id=1, source_target_pairs={{0,64},{2,66},{4,68},{6,70},{8,72},{10,74},{12,76},{14,78},{16,80}... | collective-permute-start | bytes 786440 | tf_op jit(solution)/shard_map/ppermute | solution.py:17
  189.3 4.2 %copy-start.4 = (f32[4,256,128]{1,2,0:T(8,128)S(1)}, f32[4,256,128]{1,2,0:T(8,128)}, u32[]{:S(2)}) copy-start(f32[4,256,128]{1,2,0:T(8,128)} %get-tuple-element.124) | copy-start | bytes 1572868
  189.3 4.6 %copy-start.5 = (f32[4,256,128]{1,2,0:T(8,128)S(1)}, f32[4,256,128]{1,2,0:T(8,128)}, u32[]{:S(2)}) copy-start(f32[4,256,128]{1,2,0:T(8,128)} %get-tuple-element.123) | copy-start | bytes 1572868
  204.0 157.8 %reduce-scatter.5.cloned.1.call-start = ((), (), s32[]{:S(2)}) async-start(), calls=%async_computation.5 | async-start | bytes 3932160 | tf_op jit(solution)/shard_map/reduce_scatter | solution.py:34
  321.0 0.7 copy-start.10
  321.0 89.1 %all-reduce.3.cloned.1.call-start = ((), (), s32[]{:S(2)}) async-start(), calls=%async_computation.6 | async-start | bytes 2097152
  325.5 38.7 %copy-start.6 = (f32[4,256,128]{1,2,0:T(8,128)S(1)}, f32[4,256,128]{1,2,0:T(8,128)}, u32[]{:S(2)}) copy-start(f32[4,256,128]{1,2,0:T(8,128)} %get-tuple-element.121) | copy-start | bytes 1572868
  325.5 38.7 %copy-start.7 = (f32[4,256,128]{1,2,0:T(8,128)S(1)}, f32[4,256,128]{1,2,0:T(8,128)}, u32[]{:S(2)}) copy-start(f32[4,256,128]{1,2,0:T(8,128)} %get-tuple-element.249) | copy-start | bytes 1572868
Sparse Core Ops, SparseCore 0:
  9.6 14.1 all-gather.1
  204.1 116.8 reduce-scatter.2
  323.4 38.2 reduce-scatter.4
  364.4 45.6 all-reduce.2
where the time goes:
time: 419 us; the launch traced here: 418 us
  waiting for transfers between devices  301 us (72%)
  matrix products  43.9 us (10%)
  starting transfers between devices  25.8 us (6%)
  other arithmetic  14.9 us (4%)
  between operations  14.8 us (4%)
  local copies, waits for them, and re-layouts  11.9 us (3%)
  blocking collectives  5.42 us (1%)
    reduce_scatter x2, waiting for transfers between devices, sum_by_axis(): total = lax.psum_scatter(total, axis, scatter_dimension=0, tiled=True)  153 us
    ppermute x12, waiting for transfers between devices, swapped(): return lax.ppermute(value, axis, pairs)  101 us
    unnamed x5, waiting for transfers between devices  33.5 us
    ppermute x12, starting transfers between devices, swapped(): return lax.ppermute(value, axis, pairs)  25.7 us
    all_gather x1, waiting for transfers between devices, on_device(): features = lax.all_gather(hidden, 'head', axis=1, tiled=True)  13.5 us
  transfers between devices with their start and end apart: 16, of which 13 were waited for; matrix products, arithmetic and copies ran while one was open for 10% of the time, Pallas kernels for 0%

commit v1 on v0

v1 whole, which is shorter than its diff:
```python
import functools

import jax
import jax.numpy as jnp
from jax import lax
from jax.experimental import pallas as pl
from jax.experimental.pallas import tpu as pltpu
from jax.sharding import Mesh
from jax.sharding import PartitionSpec as P

DH = 128
SEQ = ("seq_0", "seq_1", "seq_2")
ALL = SEQ + ("head",)
BF = jnp.bfloat16
F32 = jnp.float32
X, Z, Y = 0, 1, 2


def scale_of(level):
    return 1.0 if level == 0 else 2.0 ** (-(level - 1) / 2)


def places():
    return [
        (x, z, y, h) for x in range(4) for z in range(4) for y in range(4) for h in range(2)
    ]


def index_of(place):
    x, z, y, h = place
    return ((x * 4 + z) * 4 + y) * 2 + h


def shifted(value, axes, step, which="all"):
    pairs = []
    for place in places():
        axis = axes[place[3]]
        target = list(place)
        target[axis] = (place[axis] + step) % 4
        if which == "up" and target[axis] < place[axis]:
            continue
        if which == "down" and target[axis] > place[axis]:
            continue
        pairs.append((index_of(place), index_of(target)))
    return lax.ppermute(value, ALL, pairs)


def partner(value):
    return lax.ppermute(value, "head", [(0, 1), (1, 0)])


def dot(a, b, dims):
    return lax.dot_general(a, b, (dims, ((), ())), preferred_element_type=F32)


def flag(condition):
    return jnp.where(condition, 1.0, 0.0).astype(F32)


def turned(array):
    return array.astype(F32).T


def state_kernel(pos, q, k, v, g, mix, s_out, b0, b1, b2, b3, b5, u3):
    qt = turned(q[0])
    kt = turned(k[0]).astype(BF)
    gg = g[...]
    s_out[...] = dot(kt, v[0], ((1,), (0,))).astype(BF)

    def grad(j):
        row = mix[0, 9 + j : 10 + j, :] * scale_of(9 + j)
        return dot((qt * row).astype(BF), gg, ((1,), (0,)))

    b0[...] = grad(0).astype(BF)
    b1[...] = grad(1).astype(BF)
    b2[...] = grad(2).astype(BF)
    b3[...] = grad(3).astype(BF)
    g4, g5 = grad(4), grad(5)
    b5[...] = g5.astype(BF)
    two = flag(pos[X] == 2)
    u3[...] = (g5 * two + g4 * (1.0 - two)).astype(BF)


def up_terms(p, low, high):
    one = high * flag(p == 3)
    two = high * flag(p >= 2)
    three = low * flag((p == 1) | (p == 3)) + high * flag(p == 2)
    return one, two, three


def middle_kernel(pos, s, gy1, gy2, gy3, r1, r2, r3, b2, b3, p1, p2, p3, held):
    group = s[...].astype(F32) + gy1[...] + gy2[...] + gy3[...]
    held_now = r1[...].astype(F32) + r2[...] + r3[...]
    held[...] = held_now
    terms = up_terms(pos[Z], b2[...].astype(F32), b3[...].astype(F32))
    group = group.astype(BF)
    for out, term in zip((p1, p2, p3), terms):
        out[:512] = group
        out[512:] = (held_now + term).astype(BF)


def late_kernel(pos, p1, rz1, rz2, rz3, held, b0, b1, group, q1, q2, q3, held_out):
    whole = p1[:512].astype(F32) + rz1[:512] + rz2[:512] + rz3[:512]
    group[...] = whole.astype(BF)
    held_now = held[...] + rz1[512:].astype(F32) + rz2[512:] + rz3[512:]
    held_out[...] = held_now
    terms = up_terms(pos[Y], b0[...].astype(F32), b1[...].astype(F32))
    for out, term in zip((q1, q2, q3), terms):
        out[...] = (held_now + term).astype(BF)


def inner_kernel(q, k, v, g, mix, out_t, query_t, key_out, value_out, level_out, table):
    @pl.when(pl.program_id(0) == 0)
    def _():
        s_at = lax.broadcasted_iota(jnp.int32, (256, 256), 0)
        t_at = lax.broadcasted_iota(jnp.int32, (256, 256), 1)
        apart = s_at ^ t_at
        level = jnp.zeros((256, 256), jnp.int32)
        for place in range(8):
            level = level + (apart >= (1 << place)).astype(jnp.int32)
        table[...] = jnp.where(s_at <= t_at, level, -1)

    qq, kk, vv, gg = q[0], k[0], v[0], g[...]
    kt = turned(kk).astype(BF)
    vt = turned(vv).astype(BF)
    scores = dot(kk, qq, ((1,), (1,)))
    mix_grad = dot(vv, gg, ((1,), (1,)))
    levels = table[...]
    weight = jnp.zeros((256, 256), F32)
    product = scores * mix_grad
    for level in range(9):
        here = levels == level
        weight = jnp.where(here, mix[0, level : level + 1, :] * scale_of(level), weight)
        level_out[0, level : level + 1, :] = jnp.sum(
            jnp.where(here, product, 0.0), axis=0, keepdims=True
        ) * scale_of(level)
    mixed = (weight * scores).astype(BF)
    score_grad = (weight * mix_grad).astype(BF)
    out_t[0] = dot(vt, mixed, ((1,), (0,)))
    query_t[0] = dot(kt, score_grad, ((1,), (0,)))
    key_out[...] = dot(score_grad, qq, ((1,), (0,)))
    value_out[...] = dot(mixed, gg, ((1,), (0,)))


def outer_kernel(
    pos, q, k, v, g, mix, out_t, query_t, key_in, value_in, level_in,
    gy1, gy2, gy3, rz1, rz2, rz3, gx1, gx2, gx3, held, ry1, ry2, ry3,
    attended, grads, level_out,
):
    qt = turned(q[0]).astype(BF)
    gt = turned(g[...])

    def pair(p, one, two, three):
        one, two, three = one[...].astype(F32), two[...].astype(F32), three[...].astype(F32)
        low = one * flag((p == 1) | (p == 3))
        high = one * flag(p == 2) + two * flag(p >= 2) + three * flag(p == 3)
        return low.astype(BF), high.astype(BF)

    buckets = (
        pair(pos[Y], gy1, gy2, gy3) + pair(pos[Z], rz1, rz2, rz3) + pair(pos[X], gx1, gx2, gx3)
    )
    total = out_t[0]
    query = query_t[0]
    level_out[0, :9, :] = level_in[0, :9, :]
    for j, bucket in enumerate(buckets):
        row = mix[0, 9 + j : 10 + j, :] * scale_of(9 + j)
        reads = dot(bucket, qt, ((0,), (0,)))
        total = total + reads * row
        level_out[0, 9 + j : 10 + j, :] = jnp.sum(reads * gt, axis=0, keepdims=True) * scale_of(
            9 + j
        )
        query = query + dot(bucket, (gt * row).astype(BF), ((1,), (0,)))
    attended[...] = total.T.astype(BF)
    grads[0] = (query * DH**-0.5).T.astype(BF)
    state = (held[...] + ry1[...].astype(F32) + ry2[...] + ry3[...]).astype(BF)
    grads[1] = (key_in[...] + dot(v[0], state, ((1,), (1,)))).astype(BF)
    grads[2] = (value_in[...] + dot(k[0], state, ((1,), (0,)))).astype(BF)


def part(index):
    return pl.BlockSpec((1, 256, DH), lambda h: (index, 0, h))


COLUMNS = pl.BlockSpec((256, DH), lambda h: (0, h))
STATE = pl.BlockSpec((DH, DH), lambda h: (h, 0))
MIX = pl.BlockSpec((1, 15, 256), lambda h: (h, 0, 0))
TURNED = pl.BlockSpec((1, DH, 256), lambda h: (h, 0, 0))
SCALARS = pl.BlockSpec(memory_space=pltpu.SMEM)


def shape(dims, kind):
    return jax.ShapeDtypeStruct(dims, kind)


def on_device(hidden, proj_weights, level_mix, out_grad):
    x, z, y = (lax.axis_index(name) for name in SEQ)
    core = lax.axis_index("head")
    first = core == 0
    pos = jnp.stack([x, z, y]).astype(jnp.int32)
    other = partner(hidden)
    features = jnp.concatenate(
        [jnp.where(first, hidden, other), jnp.where(first, other, hidden)], axis=1
    )
    root = jnp.array([DH**-0.5, 1.0, 1.0], F32)[:, None, None]
    projected = (
        jnp.einsum("td,dme->mte", features, proj_weights, preferred_element_type=F32) * root
    ).astype(BF)
    mix = level_mix.transpose(1, 0, 2)

    by_z = features.reshape(256, 4, 4, 128).transpose(0, 2, 1, 3).reshape(256, 2048)
    sorted_features = jnp.where(first, features, by_z)
    line = jnp.where(first, x, z)

    def columns(step):
        return lax.dynamic_slice_in_dim(sorted_features, 512 * ((line + step) % 4), 512, 1)

    hidden_blocks = [columns(0)] + [shifted(columns(n), (X, Z), n) for n in (1, 2, 3)]

    state_shape = shape((512, DH), BF)
    states, b0, b1, b2, b3, b5, u3 = pl.pallas_call(
        state_kernel,
        grid=(4,),
        in_specs=[SCALARS, part(0), part(1), part(2), COLUMNS, MIX],
        out_specs=[STATE] * 7,
        out_shape=[state_shape] * 7,
    )(pos, projected, projected, projected, out_grad, mix)

    def line_of(axis):
        return (axis, axis)

    gy = [shifted(states, line_of(Y), n) for n in (1, 2, 3)]
    rx = [shifted(a, line_of(X), n, "down") for n, a in ((1, b5), (2, b5), (3, u3))]
    out_t, query_t, key_in, value_in, level_in = pl.pallas_call(
        inner_kernel,
        grid=(4,),
        in_specs=[part(0), part(1), part(2), COLUMNS, MIX],
        out_specs=[
            TURNED,
            TURNED,
            COLUMNS,
            COLUMNS,
            pl.BlockSpec((1, 16, 256), lambda h: (h, 0, 0)),
        ],
        out_shape=[
            shape((4, DH, 256), F32),
            shape((4, DH, 256), F32),
            shape((256, 512), F32),
            shape((256, 512), F32),
            shape((4, 16, 256), F32),
        ],
        scratch_shapes=[pltpu.VMEM((256, 256), jnp.int32)],
    )(projected, projected, projected, out_grad, mix)
    whole = pl.BlockSpec(memory_space=pltpu.VMEM)
    p1, p2, p3, held = pl.pallas_call(
        middle_kernel,
        in_specs=[SCALARS] + [whole] * 9,
        out_specs=[whole] * 4,
        out_shape=[shape((1024, DH), BF)] * 3 + [shape((512, DH), F32)],
    )(pos, states, *gy, *rx, b2, b3)
    rz = [shifted(a, line_of(Z), n) for n, a in ((1, p1), (2, p2), (3, p3))]
    group, q1, q2, q3, held = pl.pallas_call(
        late_kernel,
        in_specs=[SCALARS] + [whole] * 7,
        out_specs=[whole] * 5,
        out_shape=[state_shape] * 4 + [shape((512, DH), F32)],
    )(pos, p1, *rz, held, b0, b1)
    ry = [shifted(a, line_of(Y), n) for n, a in ((1, q1), (2, q2), (3, q3))]
    gx = [shifted(group, line_of(X), n, "up") for n in (1, 2, 3)]
    attended, grads, level_grad = pl.pallas_call(
        outer_kernel,
        grid=(4,),
        in_specs=[SCALARS, part(0), part(1), part(2), COLUMNS, MIX, TURNED, TURNED]
        + [COLUMNS, COLUMNS, pl.BlockSpec((1, 16, 256), lambda h: (h, 0, 0))]
        + [STATE] * 13,
        out_specs=[COLUMNS, pl.BlockSpec((3, 256, DH), lambda h: (0, 0, h)), MIX],
        out_shape=[
            shape((256, 512), BF),
            shape((3, 256, 512), BF),
            shape((4, 15, 256), F32),
        ],
    )(
        pos, projected, projected, projected, out_grad, mix, out_t, query_t, key_in, value_in,
        level_in, *gy, *rz, *gx, held, *ry,
    )
    level_grad = level_grad.transpose(1, 0, 2)

    grad_blocks = [grads] + [shifted(grads, (X, Z), n) for n in (1, 2, 3)]

    partial_inputs = jnp.einsum("mte,dme->td", grads, proj_weights, preferred_element_type=F32)
    mine = lax.dynamic_slice_in_dim(partial_inputs, 1024 * core, 1024, 1)
    theirs = lax.dynamic_slice_in_dim(partial_inputs, 1024 * (1 - core), 1024, 1)
    input_grad = (mine + partner(theirs)).astype(BF)

    partial_weights = functools.reduce(
        jnp.add,
        [
            jnp.einsum("td,mte->mde", h, g, preferred_element_type=F32)
            for h, g in zip(hidden_blocks, grad_blocks)
        ],
    )

    def reduced(array, at, axes, rows):
        def rows_of(step):
            return lax.dynamic_slice_in_dim(array, rows * ((at + step) % 4), rows, 1)

        came = [shifted(rows_of(n).astype(BF), axes, n) for n in (1, 2, 3)]
        return rows_of(0) + came[0] + came[1] + came[2]

    partial_weights = reduced(partial_weights, jnp.where(first, z, x), (Z, X), 128)
    partial_weights = reduced(partial_weights, y, (Y, Y), 32)
    weight_grad = (partial_weights * 16384**-0.5).transpose(1, 0, 2)
    return (attended, input_grad, weight_grad, level_grad)


def solution(mesh):
    split = Mesh(mesh.devices.reshape(4, 4, 4, 2), ALL)
    return jax.shard_map(
        on_device,
        mesh=split,
        in_specs=(P(SEQ, "head"), P(None, None, "head"), P(None, "head", SEQ), P(SEQ, "head")),
        out_specs=(P(SEQ, "head"), P(SEQ, "head"), P(SEQ, None, "head"), P(None, "head", SEQ)),
        check_vma=False,
    )
```

time: 419 us -> 136 us (0.32)
  waiting for transfers between devices: 301 us -> 39.2 us
  matrix products: 43.9 us -> 13.3 us
  Pallas kernels: 0 us -> 19.1 us
  starting transfers between devices: 25.8 us -> 44.9 us
  between operations: 14.8 us -> 0.97 us
  other arithmetic: 14.9 us -> 6.47 us
  blocking collectives: 5.42 us -> 0 us
    reduce_scatter x2 -> x0, waiting for transfers between devices: 153 us -> none  [sum_by_axis(): total = lax.psum_scatter(total, axis, scatter_dimension=0, tiled=True)]
    ppermute x12 -> x29, waiting for transfers between devices: 101 us -> 39.2 us  [the longest x27 39.2 us: shifted(): return lax.ppermute(value, ALL, pairs)]
    unnamed x5 -> x0, waiting for transfers between devices: 33.5 us -> none
    dot_general x32 -> x5, matrix products: 38 us -> 7.79 us  [the longest x1 4.85 us: on_device(): jnp.einsum('mte,dme->td', grads, proj_weights, preferred_element_type=F32)]
    ppermute x12 -> x29, starting transfers between devices: 25.7 us -> 44.9 us  [the longest x27 44.8 us: shifted(): return lax.ppermute(value, ALL, pairs)]
    pallas_call x0 -> x5, Pallas kernels: none -> 19.1 us  [the longest x1 5.27 us: on_device(): pl.pallas_call(inner_kernel, grid=(4,), in_specs=[part(0), part(1), part(...]
    all_gather x1 -> x0, waiting for transfers between devices: 13.5 us -> none  [on_device(): features = lax.all_gather(hidden, 'head', axis=1, tiled=True)]
    add x11 -> x1, other arithmetic: 7.99 us -> 1.43 us  [reduced(): return rows_of(0) + came[0] + came[1] + came[2]]
  transfers between devices with their start and end apart: 16 -> 29, of which waited for: 13 -> 12; matrix products, arithmetic and copies ran while one was open for 10% -> 16% of each run, Pallas kernels for 0% -> 8%
where the time goes in v1:
time: 136 us; the launch traced here: 135 us
  starting transfers between devices  44.9 us (33%)
  waiting for transfers between devices  39.2 us (29%)
  Pallas kernels  19.1 us (14%)
  matrix products  13.3 us (10%)
  local copies, waits for them, and re-layouts  11 us (8%)
  other arithmetic  6.47 us (5%)
    ppermute x27, starting transfers between devices, shifted(): return lax.ppermute(value, ALL, pairs)  44.8 us
    ppermute x27, waiting for transfers between devices, shifted(): return lax.ppermute(value, ALL, pairs)  39.2 us
    dot_general x1, matrix products, on_device(): jnp.einsum('td,dme->mte', features, proj_weights, preferred_element_type=...  5.46 us
    pallas_call x1, Pallas kernels, on_device(): pl.pallas_call(inner_kernel, grid=(4,), in_specs=[part(0), part(1), part(...  5.27 us
    pallas_call x1, Pallas kernels, on_device(): pl.pallas_call(outer_kernel, grid=(4,), in_specs=[SCALARS, part(0), part(...  5.25 us
    dot_general x1, matrix products, on_device(): jnp.einsum('mte,dme->td', grads, proj_weights, preferred_element_type=F32)  4.85 us
    unnamed x38, local copies, waits for them, and re-layouts  4.53 us
    reshape x3, local copies, waits for them, and re-layouts, on_device(): features.reshape(256, 4, 4, 128).transpose(0, 2, 1, 3).reshape(256, 2048)  4.14 us
  transfers between devices with their start and end apart: 29, of which 12 were waited for; matrix products, arithmetic and copies ran while one was open for 16% of the time, Pallas kernels for 8%

profile of v1, /device:TPU:0, one launch (start us, length us, event | category | flops | bytes accessed | tf_op | source)
XLA Modules:
  0.0 134.9 jit_solution(5246285337062850717)
XLA Ops:
  0.6 0.1 collective-permute-start
  0.7 1.5 %copy.27 = f32[15,4,256]{2,0,1:T(8,128)} copy(f32[15,4,256]{2,1,0:T(4,128)} %param.7) | data formatting | bytes 122880 | tf_op args[2]
  2.2 0.6 pad_add_fusion.pos
  2.8 1.1 broadcast_select_fusion.2
  3.9 5.5 %fusion.q.k.v = bf16[3,256,512]{2,1,0:T(8,128)(2,1)} fusion(bf16[2048,3,512]{2,0,1:T(8,128)(2,1)} %param.6, f32[3]{0:T(128)} %constant.92.clone, bf16[256,1024]{1,0:T(8,128)(2,1)S(1)} %get-tuple-element.63, bf16[256,1024]{1,0:T(8,128)(2,1)S(1)} %get-tuple-element.62), kind=kOutput, calls=%fused_computation.3 | convolution fusion | flops 1613496320 | bytes 8126476 | tf_op jit(solution)/shard_map/td,dme->mte/dot_general | solution.py:206
  9.4 3.9 %shard_map.85 = (bf16[512,128]{1,0:T(8,128)(2,1)}, bf16[512,128]{1,0:T(8,128)(2,1)}, bf16[512,128]{1,0:T(8,128)(2,1)}, bf16[512,128]{1,0:T(8,128)(2,1)}, bf16[51...) custom-call(s32[3]{0:T(128)} %pad_add_fusion.pos, bf16[3,256,512]{2,1,0:T(8,128)(2,1)} %fusion.q.k.v, ...), custom_call_target="tpu_custom_call" | custom-call | tf_op jit(solution)/shard_map/pallas_call | solution.py:220
  13.3 1.8 %collective-permute-start.1 = (bf16[512,128]{1,0:T(8,128)(2,1)}, bf16[512,128]{1,0:T(8,128)(2,1)S(1)}, u32[]{:S(2)}, u32[]{:S(2)}) collective-permute-start(bf16[512,128]{1,0:T(8,128)(2,1)} %get-tuple-element.33.s), channel_id=1, source_target_pairs={{0,2},{1,3},{2,4},{3,5},{4,6},{5,7},{6,0},{7,1},{8,10},{9,11},{10,... | collective-permute-start | bytes 393224 | tf_op jit(solution)/shard_map/ppermute | solution.py:45
  15.0 2.9 %collective-permute-start.2 = (bf16[512,128]{1,0:T(8,128)(2,1)}, bf16[512,128]{1,0:T(8,128)(2,1)S(1)}, u32[]{:S(2)}, u32[]{:S(2)}) collective-permute-start(bf16[512,128]{1,0:T(8,128)(2,1)} %get-tuple-element.33.s), channel_id=1, source_target_pairs={{0,4},{1,5},{2,6},{3,7},{4,0},{5,1},{6,2},{7,3},{8,12},{9,13},{10,... | collective-permute-start | bytes 393224 | tf_op jit(solution)/shard_map/ppermute | solution.py:45
  17.9 1.3 collective-permute-start.3
  19.3 1.3 collective-permute-start.4
  20.6 1.3 collective-permute-start.5
  21.9 1.3 collective-permute-start.6
  23.2 1.6 %collective-permute-done.2.gy2 = bf16[512,128]{1,0:T(8,128)(2,1)S(1)} collective-permute-done((bf16[512,128]{1,0:T(8,128)(2,1)}, bf16[512,128]{1,0:T(8,128)(2,1)S(1)}, u32[]{:S(2)}, u32[]{:S(2)}) %collective-permute-start.2) | collective-permute-done | bytes 131104 | tf_op jit(solution)/shard_map/ppermute | solution.py:45
  24.8 5.6 %collective-permute-done.4.r1 = bf16[512,128]{1,0:T(8,128)(2,1)S(1)} collective-permute-done((bf16[512,128]{1,0:T(8,128)(2,1)}, bf16[512,128]{1,0:T(8,128)(2,1)S(1)}, u32[]{:S(2)}, u32[]{:S(2)}) %collective-permute-start.4) | collective-permute-done | bytes 131104 | tf_op jit(solution)/shard_map/ppermute | solution.py:45
  30.5 0.6 copy-done.13
  31.2 2.4 %shard_map.86 = (bf16[1024,128]{1,0:T(8,128)(2,1)}, bf16[1024,128]{1,0:T(8,128)(2,1)}, bf16[1024,128]{1,0:T(8,128)(2,1)}, f32[512,128]{1,0:T(8,128)}) custom-call(s32[3]{0:T(128)} %pad_add_fusion.pos, bf16[512,128]{1,0:T(8,128)(2,1)} %get-tuple-element.33.s, bf16[512,128]{1,0:T(8,128)(2,1)} %copy-done.4, bf16[512,128]{1,0:T(8,128)(2,1)} %copy-done.5, ...), custom_call_target="tpu_custom_call" | custom-call | tf_op jit(solution)/shard_map/pallas_call | solution.py:254
  33.6 1.9 %collective-permute-start.7 = (bf16[1024,128]{1,0:T(8,128)(2,1)}, bf16[1024,128]{1,0:T(8,128)(2,1)S(1)}, u32[]{:S(2)}, u32[]{:S(2)}) collective-permute-start(bf16[1024,128]{1,0:T(8,128)(2,1)} %get-tuple-element.38.p1), channel_id=1, source_target_pairs={{0,8},{1,9},{2,10},{3,11},{4,12},{5,13},{6,14},{7,15},{8,16},{9,17... | collective-permute-start | bytes 786440 | tf_op jit(solution)/shard_map/ppermute | solution.py:45
  35.5 3.6 %collective-permute-start.8 = (bf16[1024,128]{1,0:T(8,128)(2,1)}, bf16[1024,128]{1,0:T(8,128)(2,1)}, u32[]{:S(2)}, u32[]{:S(2)}) collective-permute-start(bf16[1024,128]{1,0:T(8,128)(2,1)} %get-tuple-element.39), channel_id=1, source_target_pairs={{0,16},{1,17},{2,18},{3,19},{4,20},{5,21},{6,22},{7,23},{8,24},{9,... | collective-permute-start | bytes 786440 | tf_op jit(solution)/shard_map/ppermute | solution.py:45
  39.1 1.0 collective-permute-start.9
  40.1 0.1 pad_maximum_fusion
  40.2 0.8 reshape.15
  41.0 1.5 %copy.26 = bf16[256,4,4,128]{3,1,2,0:T(4,128)(2,1)} copy(bf16[256,4,4,128]{3,2,1,0:T(4,128)(2,1)S(1)} %reshape.15) | data formatting | bytes 2097152 | tf_op jit(solution)/shard_map/reshape | solution.py:210
  42.5 1.8 %reshape.16 = bf16[256,2048]{1,0:T(8,128)(2,1)S(1)} reshape(bf16[256,4,4,128]{3,2,1,0:T(4,128)(2,1)} %bitcast.52) | data formatting | bytes 2097152 | tf_op jit(solution)/shard_map/reshape | solution.py:210
  44.4 0.4 collective-permute-done.7.rz1
  44.8 4.0 %collective-permute-done.8.rz2 = bf16[1024,128]{1,0:T(8,128)(2,1)} collective-permute-done((bf16[1024,128]{1,0:T(8,128)(2,1)}, bf16[1024,128]{1,0:T(8,128)(2,1)}, u32[]{:S(2)}, u32[]{:S(2)}) %collective-permute-start.8) | collective-permute-done | bytes 262176 | tf_op jit(solution)/shard_map/ppermute | solution.py:45
  48.8 2.3 %shard_map.87 = (bf16[512,128]{1,0:T(8,128)(2,1)}, bf16[512,128]{1,0:T(8,128)(2,1)}, bf16[512,128]{1,0:T(8,128)(2,1)}, bf16[512,128]{1,0:T(8,128)(2,1)}, f32[512,128]{1,0:T(8,128)}) custom-call(s32[3]{0:T(128)} %pad_add_fusion.pos, bf16[1024,128]{1,0:T(8,128)(2,1)} %get-tuple-element.38.p1, bf16[1024,128]{1,0:T(8,128)(2,1)} %copy-done.2, ...), custom_call_target="tpu_custom_call" | custom-call | tf_op jit(solution)/shard_map/pallas_call | solution.py:261
  51.1 6.8 %collective-permute-start.10 = (bf16[512,128]{1,0:T(8,128)(2,1)}, bf16[512,128]{1,0:T(8,128)(2,1)S(1)}, u32[]{:S(2)}, u32[]{:S(2)}) collective-permute-start(bf16[512,128]{1,0:T(8,128)(2,1)} %get-tuple-element.44), channel_id=1, source_target_pairs={{0,32},{1,33},{2,34},{3,35},{4,36},{5,37},{6,38},{7,39},{8,40},{9,... | collective-permute-start | bytes 393224 | tf_op jit(solution)/shard_map/ppermute | solution.py:45
  57.9 0.4 broadcast_select_fusion
  58.3 5.3 %shard_map.84 = (f32[4,128,256]{2,1,0:T(8,128)}, f32[4,128,256]{2,1,0:T(8,128)}, f32[256,512]{1,0:T(8,128)}, f32[256,512]{1,0:T(8,128)}, f32[4,16,256]{2,1,0:T(8,128)}) custom-call(bf16[3,256,512]{2,1,0:T(8,128)(2,1)} %fusion.q.k.v, bf16[3,256,512]{2,1,0:T(8,128)(2,1)} %fusion.q.k.v, bf16[3,256,512]{2,1,0:T(8,128)(2,1)} %fusion.q.k.v, bf16[256,512]{1,0:T(8,128)(2,1)} %g.5, ...), custom_call_target="tpu_custom_call" | custom-call | tf_op jit(solution)/shard_map/pallas_call | solution.py:233
  63.6 1.6 %collective-permute-start.11 = (bf16[512,128]{1,0:T(8,128)(2,1)}, bf16[512,128]{1,0:T(8,128)(2,1)S(1)}, u32[]{:S(2)}, u32[]{:S(2)}) collective-permute-start(bf16[512,128]{1,0:T(8,128)(2,1)} %get-tuple-element.44), channel_id=1, source_target_pairs={{0,64},{1,65},{2,66},{3,67},{4,68},{5,69},{6,70},{7,71},{8,72},{9,... | collective-permute-start | bytes 393224 | tf_op jit(solution)/shard_map/ppermute | solution.py:45
  65.2 1.3 collective-permute-start.12
  66.5 0.7 collective-permute-start.13
  67.3 1.3 collective-permute-start.14
  68.6 1.5 %collective-permute-start.15 = (bf16[512,128]{1,0:T(8,128)(2,1)S(1)}, bf16[512,128]{1,0:T(8,128)(2,1)S(1)}, u32[]{:S(2)}, u32[]{:S(2)}) collective-permute-start(bf16[512,128]{1,0:T(8,128)(2,1)S(1)} %copy-done.16), channel_id=1, source_target_pairs={{0,6},{1,7},{2,0},{3,1},{4,2},{5,3},{6,4},{7,5},{8,14},{9,15},{10,... | collective-permute-start | bytes 393224 | tf_op jit(solution)/shard_map/ppermute | solution.py:45
  70.3 2.0 %collective-permute-start.20 = (bf16[256,512]{1,0:T(8,128)(2,1)S(1)}, bf16[256,512]{1,0:T(8,128)(2,1)S(1)}, u32[]{:S(2)}, u32[]{:S(2)}) collective-permute-start(bf16[256,512]{1,0:T(8,128)(2,1)S(1)} %get-tuple-element.60), channel_id=1, source_target_pairs={{0,64},{1,17},{2,66},{3,19},{4,68},{5,21},{6,70},{7,23},{8,72},{9,... | collective-permute-start | bytes 786440 | tf_op jit(solution)/shard_map/ppermute | solution.py:45
  72.3 2.5 %collective-permute-done.13.ry1 = bf16[512,128]{1,0:T(8,128)(2,1)S(1)} collective-permute-done((bf16[512,128]{1,0:T(8,128)(2,1)}, bf16[512,128]{1,0:T(8,128)(2,1)S(1)}, u32[]{:S(2)}, u32[]{:S(2)}) %collective-permute-start.13) | collective-permute-done | bytes 131104 | tf_op jit(solution)/shard_map/ppermute | solution.py:45
  74.8 0.5 collective-permute-done.15.ry3
  75.3 0.2 copy-done.10
  75.5 0.4 copy-done.12
  75.9 5.3 %shard_map.88 = (bf16[256,512]{1,0:T(8,128)(2,1)}, bf16[3,256,512]{2,1,0:T(8,128)(2,1)}, f32[4,15,256]{2,1,0:T(8,128)}) custom-call(s32[3]{0:T(128)} %pad_add_fusion.pos, bf16[3,256,512]{2,1,0:T(8,128)(2,1)} %fusion.q.k.v, bf16[3,256,512]{2,1,0:T(8,128)(2,1)} %fusion.q.k.v, bf16[3,256,512]{2,1,0:T(8,128)(2,1)} %fusion.q.k.v, bf16[256,512]{1,0:T(8,128)(2,1)} %g.5, ...), custom_call_target="tpu_custom_call" | custom-call | tf_op jit(solution)/shard_map/pallas_call | solution.py:269
  81.2 0.8 collective-permute-start.19
  82.1 2.4 %collective-permute-start.21 = (bf16[3,256,512]{2,1,0:T(8,128)(2,1)}, bf16[3,256,512]{2,1,0:T(8,128)(2,1)S(1)}, u32[]{:S(2)}, u32[]{:S(2)}) collective-permute-start(bf16[3,256,512]{2,1,0:T(8,128)(2,1)} %get-tuple-element.50), channel_id=1, source_target_pairs={{0,96},{1,25},{2,98},{3,27},{4,100},{5,29},{6,102},{7,31},{8,104},... | collective-permute-start | bytes 2359304 | tf_op jit(solution)/shard_map/ppermute | solution.py:45
  84.5 4.9 %convolution_bitcast_fusion = f32[256,2048]{1,0:T(8,128)S(1)} fusion(bf16[3,256,512]{2,1,0:T(8,128)(2,1)} %get-tuple-element.50, bf16[2048,3,512]{2,0,1:T(8,128)(2,1)} %param.6), kind=kOutput, calls=%fused_computation.1 | convolution fusion | flops 1610612736 | bytes 9175040 | tf_op jit(solution)/shard_map/mte,dme->td/dot_general | solution.py:289
  89.4 0.6 fusion.15
  90.0 1.1 constant_dynamic-slice_fusion.3
  91.1 0.9 collective-permute-start.22
  92.1 11.0 %collective-permute-done.17 = bf16[3,256,512]{2,1,0:T(8,128)(2,1)S(1)} collective-permute-done((bf16[3,256,512]{2,1,0:T(8,128)(2,1)}, bf16[3,256,512]{2,1,0:T(8,128)(2,1)S(1)}, u32[]{:S(2)}, u32[]{:S(2)}) %collective-permute-start.17) | collective-permute-done | bytes 786464 | tf_op jit(solution)/shard_map/ppermute | solution.py:45
  103.1 0.6 fusion.13
  103.7 0.6 fusion.11
  104.3 2.4 %collective-permute-done.22 = bf16[256,512]{1,0:T(8,128)(2,1)S(1)} collective-permute-done((bf16[256,512]{1,0:T(8,128)(2,1)S(1)}, bf16[256,512]{1,0:T(8,128)(2,1)S(1)}, u32[]{:S(2)}, u32[]{:S(2)}) %collective-permute-start.22) | collective-permute-done | bytes 262176 | tf_op jit(solution)/shard_map/ppermute | solution.py:45
  106.8 1.1 add_add_fusion
  107.9 1.1 fusion.4
  108.9 2.0 %collective-permute-start.23 = (bf16[3,128,512]{2,1,0:T(8,128)(2,1)}, bf16[3,128,512]{2,1,0:T(8,128)(2,1)}, u32[]{:S(2)}, u32[]{:S(2)}) collective-permute-start(bf16[3,128,512]{2,1,0:T(8,128)(2,1)} %get-tuple-element.56), channel_id=1, source_target_pairs={{0,8},{1,33},{2,10},{3,35},{4,12},{5,37},{6,14},{7,39},{8,16},{9,4... | collective-permute-start | bytes 1179656 | tf_op jit(solution)/shard_map/ppermute | solution.py:45
  110.9 2.7 %collective-permute-start.24 = (bf16[3,128,512]{2,1,0:T(8,128)(2,1)}, bf16[3,128,512]{2,1,0:T(8,128)(2,1)}, u32[]{:S(2)}, u32[]{:S(2)}) collective-permute-start(bf16[3,128,512]{2,1,0:T(8,128)(2,1)} %get-tuple-element.58), channel_id=1, source_target_pairs={{0,16},{1,65},{2,18},{3,67},{4,20},{5,69},{6,22},{7,71},{8,24},{9,... | collective-permute-start | bytes 1179656 | tf_op jit(solution)/shard_map/ppermute | solution.py:45
  113.6 1.7 %copy.15 = f32[15,4,256]{2,1,0:T(4,128)} copy(f32[15,4,256]{2,0,1:T(8,128)} %bitcast.56) | data formatting | bytes 122880
  115.3 2.9 %collective-permute-done.23 = bf16[3,128,512]{2,1,0:T(8,128)(2,1)} collective-permute-done((bf16[3,128,512]{2,1,0:T(8,128)(2,1)}, bf16[3,128,512]{2,1,0:T(8,128)(2,1)}, u32[]{:S(2)}, u32[]{:S(2)}) %collective-permute-start.23) | collective-permute-done | bytes 393248 | tf_op jit(solution)/shard_map/ppermute | solution.py:45
  118.3 5.7 %collective-permute-done.24 = bf16[3,128,512]{2,1,0:T(8,128)(2,1)} collective-permute-done((bf16[3,128,512]{2,1,0:T(8,128)(2,1)}, bf16[3,128,512]{2,1,0:T(8,128)(2,1)}, u32[]{:S(2)}, u32[]{:S(2)}) %collective-permute-start.24) | collective-permute-done | bytes 393248 | tf_op jit(solution)/shard_map/ppermute | solution.py:45
  123.9 1.4 %fusion.3 = f32[3,128,512]{2,1,0:T(8,128)S(1)} fusion(bf16[3,128,512]{2,1,0:T(8,128)(2,1)} %collective-permute-done.25, bf16[3,128,512]{2,1,0:T(8,128)(2,1)} %collective-permute-done.24, bf16[3,128,512]{2,1,0:T(8,128)(2,1)} %collective-permute-done.23, f32[3,512,512]{1,2,0:T(8,128)S(1)} %add_add_fusion, s32[]{:T(128)S(6)} %select_n.137), kind=kLoop, calls=%fused_computation.11 | loop fusion | flops 1179648 | bytes 2752516 | tf_op jit(solution)/shard_map/add | solution.py:307
  125.4 0.5 collective-permute-start.26
  125.9 3.6 %collective-permute-start.27 = (bf16[3,32,512]{2,1,0:T(8,128)(2,1)S(1)}, bf16[3,32,512]{2,1,0:T(8,128)(2,1)S(1)}, u32[]{:S(2)}, u32[]{:S(2)}) collective-permute-start(bf16[3,32,512]{2,1,0:T(8,128)(2,1)S(1)} %get-tuple-element.66), channel_id=1, source_target_pairs={{0,4},{1,5},{2,6},{3,7},{4,0},{5,1},{6,2},{7,3},{8,12},{9,13},{10,... | collective-permute-start | bytes 294920 | tf_op jit(solution)/shard_map/ppermute | solution.py:45
  129.6 2.2 %add_convert_fusion = bf16[256,1024]{1,0:T(8,128)(2,1)} fusion(f32[256,1024]{1,0:T(8,128)} %collective-permute-done.16, f32[256,2048]{1,0:T(8,128)S(1)} %copy-done.1, s32[]{:T(128)S(6)} %select_n.122), kind=kLoop, calls=%fused_computation.7 | loop fusion | flops 524288 | bytes 2621444 | tf_op jit(solution)/shard_map/convert_element_type | solution.py:292
  131.7 1.5 %collective-permute-done.27 = bf16[3,32,512]{2,1,0:T(8,128)(2,1)S(1)} collective-permute-done((bf16[3,32,512]{2,1,0:T(8,128)(2,1)S(1)}, bf16[3,32,512]{2,1,0:T(8,128)(2,1)S(1)}, u32[]{:S(2)}, u32[]{:S(2)}) %collective-permute-start.27) | collective-permute-done | bytes 98336 | tf_op jit(solution)/shard_map/ppermute | solution.py:45
  133.2 1.0 collective-permute-done.28
  134.2 0.7 multiply_bitcast_fusion
  (57 shorter events, 0.6 us)
Async XLA Ops:
  0.6 2.2 %collective-permute-start = (bf16[256,1024]{1,0:T(8,128)(2,1)}, bf16[256,1024]{1,0:T(8,128)(2,1)S(1)}, u32[]{:S(2)}, u32[]{:S(2)}) collective-permute-start(bf16[256,1024]{1,0:T(8,128)(2,1)} %param.5), channel_id=1, source_target_pairs={{0,1},{1,0},{2,3},{3,2},{4,5},{5,4},{6,7},{7,6},{8,9},{9,8},{10,11... | collective-permute-start | bytes 1572872 | tf_op jit(solution)/shard_map/ppermute | solution.py:49
  13.3 8.6 %collective-permute-start.1 = (bf16[512,128]{1,0:T(8,128)(2,1)}, bf16[512,128]{1,0:T(8,128)(2,1)S(1)}, u32[]{:S(2)}, u32[]{:S(2)}) collective-permute-start(bf16[512,128]{1,0:T(8,128)(2,1)} %get-tuple-element.33.s), channel_id=1, source_target_pairs={{0,2},{1,3},{2,4},{3,5},{4,6},{5,7},{6,0},{7,1},{8,10},{9,11},{10,... | collective-permute-start | bytes 393224 | tf_op jit(solution)/shard_map/ppermute | solution.py:45
  15.0 9.7 %collective-permute-start.2 = (bf16[512,128]{1,0:T(8,128)(2,1)}, bf16[512,128]{1,0:T(8,128)(2,1)S(1)}, u32[]{:S(2)}, u32[]{:S(2)}) collective-permute-start(bf16[512,128]{1,0:T(8,128)(2,1)} %get-tuple-element.33.s), channel_id=1, source_target_pairs={{0,4},{1,5},{2,6},{3,7},{4,0},{5,1},{6,2},{7,3},{8,12},{9,13},{10,... | collective-permute-start | bytes 393224 | tf_op jit(solution)/shard_map/ppermute | solution.py:45
  17.9 6.8 %collective-permute-start.3 = (bf16[512,128]{1,0:T(8,128)(2,1)}, bf16[512,128]{1,0:T(8,128)(2,1)S(1)}, u32[]{:S(2)}, u32[]{:S(2)}) collective-permute-start(bf16[512,128]{1,0:T(8,128)(2,1)} %get-tuple-element.33.s), channel_id=1, source_target_pairs={{0,6},{1,7},{2,0},{3,1},{4,2},{5,3},{6,4},{7,5},{8,14},{9,15},{10,... | collective-permute-start | bytes 393224 | tf_op jit(solution)/shard_map/ppermute | solution.py:45
  19.3 11.1 %collective-permute-start.4 = (bf16[512,128]{1,0:T(8,128)(2,1)}, bf16[512,128]{1,0:T(8,128)(2,1)S(1)}, u32[]{:S(2)}, u32[]{:S(2)}) collective-permute-start(bf16[512,128]{1,0:T(8,128)(2,1)} %get-tuple-element.34), channel_id=1, source_target_pairs={{96,0},{97,1},{98,2},{99,3},{100,4},{101,5},{102,6},{103,7},{104,8... | collective-permute-start | bytes 393224 | tf_op jit(solution)/shard_map/ppermute | solution.py:45
  20.6 9.8 %collective-permute-start.5 = (bf16[512,128]{1,0:T(8,128)(2,1)}, bf16[512,128]{1,0:T(8,128)(2,1)S(1)}, u32[]{:S(2)}, u32[]{:S(2)}) collective-permute-start(bf16[512,128]{1,0:T(8,128)(2,1)} %get-tuple-element.34), channel_id=1, source_target_pairs={{64,0},{65,1},{66,2},{67,3},{68,4},{69,5},{70,6},{71,7},{72,8},{73... | collective-permute-start | bytes 393224 | tf_op jit(solution)/shard_map/ppermute | solution.py:45
  21.9 8.6 %copy-start.4 = (bf16[512,128]{1,0:T(8,128)(2,1)}, bf16[512,128]{1,0:T(8,128)(2,1)S(1)}, u32[]{:S(2)}) copy-start(bf16[512,128]{1,0:T(8,128)(2,1)S(1)} %collective-permute-done.1.gy1) | copy-start | bytes 393220
  21.9 8.5 %collective-permute-start.6 = (bf16[512,128]{1,0:T(8,128)(2,1)}, bf16[512,128]{1,0:T(8,128)(2,1)S(1)}, u32[]{:S(2)}, u32[]{:S(2)}) collective-permute-start(bf16[512,128]{1,0:T(8,128)(2,1)} %get-tuple-element.35), channel_id=1, source_target_pairs={{32,0},{33,1},{34,2},{35,3},{36,4},{37,5},{38,6},{39,7},{40,8},{41... | collective-permute-start | bytes 393224 | tf_op jit(solution)/shard_map/ppermute | solution.py:45
  24.8 5.7 %copy-start.5 = (bf16[512,128]{1,0:T(8,128)(2,1)}, bf16[512,128]{1,0:T(8,128)(2,1)S(1)}, u32[]{:S(2)}) copy-start(bf16[512,128]{1,0:T(8,128)(2,1)S(1)} %collective-permute-done.2.gy2) | copy-start | bytes 393220
  24.8 5.7 %copy-start.6 = (bf16[512,128]{1,0:T(8,128)(2,1)}, bf16[512,128]{1,0:T(8,128)(2,1)S(1)}, u32[]{:S(2)}) copy-start(bf16[512,128]{1,0:T(8,128)(2,1)S(1)} %collective-permute-done.3.gy3) | copy-start | bytes 393220
  30.4 0.7 copy-start.13
  30.4 0.7 copy-start.14
  30.4 0.8 copy-start.15
  33.6 11.1 %collective-permute-start.7 = (bf16[1024,128]{1,0:T(8,128)(2,1)}, bf16[1024,128]{1,0:T(8,128)(2,1)S(1)}, u32[]{:S(2)}, u32[]{:S(2)}) collective-permute-start(bf16[1024,128]{1,0:T(8,128)(2,1)} %get-tuple-element.38.p1), channel_id=1, source_target_pairs={{0,8},{1,9},{2,10},{3,11},{4,12},{5,13},{6,14},{7,15},{8,16},{9,17... | collective-permute-start | bytes 786440 | tf_op jit(solution)/shard_map/ppermute | solution.py:45
  35.5 13.3 %collective-permute-start.8 = (bf16[1024,128]{1,0:T(8,128)(2,1)}, bf16[1024,128]{1,0:T(8,128)(2,1)}, u32[]{:S(2)}, u32[]{:S(2)}) collective-permute-start(bf16[1024,128]{1,0:T(8,128)(2,1)} %get-tuple-element.39), channel_id=1, source_target_pairs={{0,16},{1,17},{2,18},{3,19},{4,20},{5,21},{6,22},{7,23},{8,24},{9,... | collective-permute-start | bytes 786440 | tf_op jit(solution)/shard_map/ppermute | solution.py:45
  39.1 9.7 %collective-permute-start.9 = (bf16[1024,128]{1,0:T(8,128)(2,1)}, bf16[1024,128]{1,0:T(8,128)(2,1)}, u32[]{:S(2)}, u32[]{:S(2)}) collective-permute-start(bf16[1024,128]{1,0:T(8,128)(2,1)} %get-tuple-element.40), channel_id=1, source_target_pairs={{0,24},{1,25},{2,26},{3,27},{4,28},{5,29},{6,30},{7,31},{8,0},{9,1... | collective-permute-start | bytes 786440 | tf_op jit(solution)/shard_map/ppermute | solution.py:45
  44.8 4.0 %copy-start.2 = (bf16[1024,128]{1,0:T(8,128)(2,1)}, bf16[1024,128]{1,0:T(8,128)(2,1)S(1)}, u32[]{:S(2)}) copy-start(bf16[1024,128]{1,0:T(8,128)(2,1)S(1)} %collective-permute-done.7.rz1) | copy-start | bytes 786436
  51.1 16.2 %copy-start.17 = (bf16[512,128]{1,0:T(8,128)(2,1)S(1)}, bf16[512,128]{1,0:T(8,128)(2,1)}, u32[]{:S(2)}) copy-start(bf16[512,128]{1,0:T(8,128)(2,1)} %get-tuple-element.47) | copy-start | bytes 393220
  51.1 17.5 %copy-start.16 = (bf16[512,128]{1,0:T(8,128)(2,1)S(1)}, bf16[512,128]{1,0:T(8,128)(2,1)}, u32[]{:S(2)}) copy-start(bf16[512,128]{1,0:T(8,128)(2,1)} %get-tuple-element.48) | copy-start | bytes 393220
  51.1 17.5 %collective-permute-start.10 = (bf16[512,128]{1,0:T(8,128)(2,1)}, bf16[512,128]{1,0:T(8,128)(2,1)S(1)}, u32[]{:S(2)}, u32[]{:S(2)}) collective-permute-start(bf16[512,128]{1,0:T(8,128)(2,1)} %get-tuple-element.44), channel_id=1, source_target_pairs={{0,32},{1,33},{2,34},{3,35},{4,36},{5,37},{6,38},{7,39},{8,40},{9,... | collective-permute-start | bytes 393224 | tf_op jit(solution)/shard_map/ppermute | solution.py:45
  63.6 6.6 %collective-permute-start.11 = (bf16[512,128]{1,0:T(8,128)(2,1)}, bf16[512,128]{1,0:T(8,128)(2,1)S(1)}, u32[]{:S(2)}, u32[]{:S(2)}) collective-permute-start(bf16[512,128]{1,0:T(8,128)(2,1)} %get-tuple-element.44), channel_id=1, source_target_pairs={{0,64},{1,65},{2,66},{3,67},{4,68},{5,69},{6,70},{7,71},{8,72},{9,... | collective-permute-start | bytes 393224 | tf_op jit(solution)/shard_map/ppermute | solution.py:45
  65.2 5.1 %collective-permute-start.12 = (bf16[512,128]{1,0:T(8,128)(2,1)}, bf16[512,128]{1,0:T(8,128)(2,1)S(1)}, u32[]{:S(2)}, u32[]{:S(2)}) collective-permute-start(bf16[512,128]{1,0:T(8,128)(2,1)} %get-tuple-element.44), channel_id=1, source_target_pairs={{0,96},{1,97},{2,98},{3,99},{4,100},{5,101},{6,102},{7,103},{8,104... | collective-permute-start | bytes 393224 | tf_op jit(solution)/shard_map/ppermute | solution.py:45
  66.5 8.3 %collective-permute-start.13 = (bf16[512,128]{1,0:T(8,128)(2,1)}, bf16[512,128]{1,0:T(8,128)(2,1)S(1)}, u32[]{:S(2)}, u32[]{:S(2)}) collective-permute-start(bf16[512,128]{1,0:T(8,128)(2,1)} %get-tuple-element.46), channel_id=1, source_target_pairs={{0,2},{1,3},{2,4},{3,5},{4,6},{5,7},{6,0},{7,1},{8,10},{9,11},{10,... | collective-permute-start | bytes 393224 | tf_op jit(solution)/shard_map/ppermute | solution.py:45
  67.3 7.5 %collective-permute-start.14 = (bf16[512,128]{1,0:T(8,128)(2,1)S(1)}, bf16[512,128]{1,0:T(8,128)(2,1)S(1)}, u32[]{:S(2)}, u32[]{:S(2)}) collective-permute-start(bf16[512,128]{1,0:T(8,128)(2,1)S(1)} %copy-done.17), channel_id=1, source_target_pairs={{0,4},{1,5},{2,6},{3,7},{4,0},{5,1},{6,2},{7,3},{8,12},{9,13},{10,... | collective-permute-start | bytes 393224 | tf_op jit(solution)/shard_map/ppermute | solution.py:45
  68.6 6.7 %copy-start.7 = (bf16[512,128]{1,0:T(8,128)(2,1)}, bf16[512,128]{1,0:T(8,128)(2,1)S(1)}, u32[]{:S(2)}) copy-start(bf16[512,128]{1,0:T(8,128)(2,1)S(1)} %collective-permute-done.10.gx1) | copy-start | bytes 393220
  68.6 6.7 %collective-permute-start.15 = (bf16[512,128]{1,0:T(8,128)(2,1)S(1)}, bf16[512,128]{1,0:T(8,128)(2,1)S(1)}, u32[]{:S(2)}, u32[]{:S(2)}) collective-permute-start(bf16[512,128]{1,0:T(8,128)(2,1)S(1)} %copy-done.16), channel_id=1, source_target_pairs={{0,6},{1,7},{2,0},{3,1},{4,2},{5,3},{6,4},{7,5},{8,14},{9,15},{10,... | collective-permute-start | bytes 393224 | tf_op jit(solution)/shard_map/ppermute | solution.py:45
  70.2 5.1 %copy-start.8 = (bf16[512,128]{1,0:T(8,128)(2,1)}, bf16[512,128]{1,0:T(8,128)(2,1)S(1)}, u32[]{:S(2)}) copy-start(bf16[512,128]{1,0:T(8,128)(2,1)S(1)} %collective-permute-done.11.gx2) | copy-start | bytes 393220
  70.2 20.9 %collective-permute-start.18 = (bf16[256,512]{1,0:T(8,128)(2,1)S(1)}, bf16[256,512]{1,0:T(8,128)(2,1)S(1)}, u32[]{:S(2)}, u32[]{:S(2)}) collective-permute-start(bf16[256,512]{1,0:T(8,128)(2,1)S(1)} %get-tuple-element.61), channel_id=1, source_target_pairs={{0,32},{1,9},{2,34},{3,11},{4,36},{5,13},{6,38},{7,15},{8,40},{9,1... | collective-permute-start | bytes 786440 | tf_op jit(solution)/shard_map/ppermute | solution.py:45
  70.3 5.0 %copy-start.9 = (bf16[512,128]{1,0:T(8,128)(2,1)}, bf16[512,128]{1,0:T(8,128)(2,1)S(1)}, u32[]{:S(2)}) copy-start(bf16[512,128]{1,0:T(8,128)(2,1)S(1)} %collective-permute-done.12.gx3) | copy-start | bytes 393220
  70.3 33.4 %collective-permute-start.20 = (bf16[256,512]{1,0:T(8,128)(2,1)S(1)}, bf16[256,512]{1,0:T(8,128)(2,1)S(1)}, u32[]{:S(2)}, u32[]{:S(2)}) collective-permute-start(bf16[256,512]{1,0:T(8,128)(2,1)S(1)} %get-tuple-element.60), channel_id=1, source_target_pairs={{0,64},{1,17},{2,66},{3,19},{4,68},{5,21},{6,70},{7,23},{8,72},{9,... | collective-permute-start | bytes 786440 | tf_op jit(solution)/shard_map/ppermute | solution.py:45
  74.8 0.7 copy-start.10
  74.8 0.7 copy-start.11
  75.2 0.7 copy-start.12
  81.2 8.2 %copy-start.3 = (bf16[3,256,512]{2,1,0:T(8,128)(2,1)S(1)}, bf16[3,256,512]{2,1,0:T(8,128)(2,1)}, u32[]{:S(2)}) copy-start(bf16[3,256,512]{2,1,0:T(8,128)(2,1)} %get-tuple-element.50) | copy-start | bytes 2359300
  81.2 21.9 %collective-permute-start.17 = (bf16[3,256,512]{2,1,0:T(8,128)(2,1)}, bf16[3,256,512]{2,1,0:T(8,128)(2,1)S(1)}, u32[]{:S(2)}, u32[]{:S(2)}) collective-permute-start(bf16[3,256,512]{2,1,0:T(8,128)(2,1)} %get-tuple-element.50), channel_id=1, source_target_pairs={{0,32},{1,9},{2,34},{3,11},{4,36},{5,13},{6,38},{7,15},{8,40},{9,1... | collective-permute-start | bytes 2359304 | tf_op jit(solution)/shard_map/ppermute | solution.py:45
  81.2 22.5 %collective-permute-start.19 = (bf16[3,256,512]{2,1,0:T(8,128)(2,1)}, bf16[3,256,512]{2,1,0:T(8,128)(2,1)S(1)}, u32[]{:S(2)}, u32[]{:S(2)}) collective-permute-start(bf16[3,256,512]{2,1,0:T(8,128)(2,1)} %get-tuple-element.50), channel_id=1, source_target_pairs={{0,64},{1,17},{2,66},{3,19},{4,68},{5,21},{6,70},{7,23},{8,72},{9,... | collective-permute-start | bytes 2359304 | tf_op jit(solution)/shard_map/ppermute | solution.py:45
  82.1 24.7 %collective-permute-start.21 = (bf16[3,256,512]{2,1,0:T(8,128)(2,1)}, bf16[3,256,512]{2,1,0:T(8,128)(2,1)S(1)}, u32[]{:S(2)}, u32[]{:S(2)}) collective-permute-start(bf16[3,256,512]{2,1,0:T(8,128)(2,1)} %get-tuple-element.50), channel_id=1, source_target_pairs={{0,96},{1,25},{2,98},{3,27},{4,100},{5,29},{6,102},{7,31},{8,104},... | collective-permute-start | bytes 2359304 | tf_op jit(solution)/shard_map/ppermute | solution.py:45
  89.3 1.8 %copy-start = (f32[256,2048]{1,0:T(8,128)}, f32[256,2048]{1,0:T(8,128)S(1)}, u32[]{:S(2)}) copy-start(f32[256,2048]{1,0:T(8,128)S(1)} %convolution_bitcast_fusion) | copy-start | bytes 6291460
  91.1 15.7 %collective-permute-start.22 = (bf16[256,512]{1,0:T(8,128)(2,1)S(1)}, bf16[256,512]{1,0:T(8,128)(2,1)S(1)}, u32[]{:S(2)}, u32[]{:S(2)}) collective-permute-start(bf16[256,512]{1,0:T(8,128)(2,1)S(1)} %get-tuple-element.59), channel_id=1, source_target_pairs={{0,96},{1,25},{2,98},{3,27},{4,100},{5,29},{6,102},{7,31},{8,104},... | collective-permute-start | bytes 786440 | tf_op jit(solution)/shard_map/ppermute | solution.py:45
  103.1 26.5 %collective-permute-start.16 = (f32[256,1024]{1,0:T(8,128)}, f32[256,1024]{1,0:T(8,128)}, u32[]{:S(2)}, u32[]{:S(2)}) collective-permute-start(f32[256,1024]{1,0:T(8,128)} %constant_dynamic-slice_fusion.3), channel_id=1, source_target_pairs={{0,1},{1,0},{2,3},{3,2},{4,5},{5,4},{6,7},{7,6},{8,9},{9,8},{10,11... | collective-permute-start | bytes 3145736 | tf_op jit(solution)/shard_map/ppermute | solution.py:49
  108.9 9.3 %collective-permute-start.23 = (bf16[3,128,512]{2,1,0:T(8,128)(2,1)}, bf16[3,128,512]{2,1,0:T(8,128)(2,1)}, u32[]{:S(2)}, u32[]{:S(2)}) collective-permute-start(bf16[3,128,512]{2,1,0:T(8,128)(2,1)} %get-tuple-element.56), channel_id=1, source_target_pairs={{0,8},{1,33},{2,10},{3,35},{4,12},{5,37},{6,14},{7,39},{8,16},{9,4... | collective-permute-start | bytes 1179656 | tf_op jit(solution)/shard_map/ppermute | solution.py:45
  110.9 13.0 %collective-permute-start.24 = (bf16[3,128,512]{2,1,0:T(8,128)(2,1)}, bf16[3,128,512]{2,1,0:T(8,128)(2,1)}, u32[]{:S(2)}, u32[]{:S(2)}) collective-permute-start(bf16[3,128,512]{2,1,0:T(8,128)(2,1)} %get-tuple-element.58), channel_id=1, source_target_pairs={{0,16},{1,65},{2,18},{3,67},{4,20},{5,69},{6,22},{7,71},{8,24},{9,... | collective-permute-start | bytes 1179656 | tf_op jit(solution)/shard_map/ppermute | solution.py:45
  113.6 10.3 %collective-permute-start.25 = (bf16[3,128,512]{2,1,0:T(8,128)(2,1)S(1)}, bf16[3,128,512]{2,1,0:T(8,128)(2,1)}, u32[]{:S(2)}, u32[]{:S(2)}) collective-permute-start(bf16[3,128,512]{2,1,0:T(8,128)(2,1)S(1)} %get-tuple-element.57), channel_id=1, source_target_pairs={{0,24},{1,97},{2,26},{3,99},{4,28},{5,101},{6,30},{7,103},{8,0},{9... | collective-permute-start | bytes 1179656 | tf_op jit(solution)/shard_map/ppermute | solution.py:45
  113.6 15.9 %copy-start.1 = (f32[256,2048]{1,0:T(8,128)S(1)}, f32[256,2048]{1,0:T(8,128)}, u32[]{:S(2)}) copy-start(f32[256,2048]{1,0:T(8,128)} %copy-done) | copy-start | bytes 6291460
  125.4 6.3 %collective-permute-start.26 = (bf16[3,32,512]{2,1,0:T(8,128)(2,1)S(1)}, bf16[3,32,512]{2,1,0:T(8,128)(2,1)S(1)}, u32[]{:S(2)}, u32[]{:S(2)}) collective-permute-start(bf16[3,32,512]{2,1,0:T(8,128)(2,1)S(1)} %get-tuple-element.64), channel_id=1, source_target_pairs={{0,2},{1,3},{2,4},{3,5},{4,6},{5,7},{6,0},{7,1},{8,10},{9,11},{10,... | collective-permute-start | bytes 294920 | tf_op jit(solution)/shard_map/ppermute | solution.py:45
  125.9 7.3 %collective-permute-start.27 = (bf16[3,32,512]{2,1,0:T(8,128)(2,1)S(1)}, bf16[3,32,512]{2,1,0:T(8,128)(2,1)S(1)}, u32[]{:S(2)}, u32[]{:S(2)}) collective-permute-start(bf16[3,32,512]{2,1,0:T(8,128)(2,1)S(1)} %get-tuple-element.66), channel_id=1, source_target_pairs={{0,4},{1,5},{2,6},{3,7},{4,0},{5,1},{6,2},{7,3},{8,12},{9,13},{10,... | collective-permute-start | bytes 294920 | tf_op jit(solution)/shard_map/ppermute | solution.py:45
  129.6 4.6 %collective-permute-start.28 = (bf16[3,32,512]{2,1,0:T(8,128)(2,1)S(1)}, bf16[3,32,512]{2,1,0:T(8,128)(2,1)S(1)}, u32[]{:S(2)}, u32[]{:S(2)}) collective-permute-start(bf16[3,32,512]{2,1,0:T(8,128)(2,1)S(1)} %get-tuple-element.65), channel_id=1, source_target_pairs={{0,6},{1,7},{2,0},{3,1},{4,2},{5,3},{6,4},{7,5},{8,14},{9,15},{10,... | collective-permute-start | bytes 294920 | tf_op jit(solution)/shard_map/ppermute | solution.py:45

commit v2 on v1

--- a/solution.py
+++ b/solution.py
@@ -7,6 +7,7 @@
 from jax.experimental.pallas import tpu as pltpu
 from jax.sharding import Mesh
 from jax.sharding import PartitionSpec as P
+
 
 DH = 128
 SEQ = ("seq_0", "seq_1", "seq_2")
@@ -142,9 +143,14 @@
     value_out[...] = dot(mixed, gg, ((1,), (0,)))
 
 
-def outer_kernel(
-    pos, q, k, v, g, mix, out_t, query_t, key_in, value_in, level_in,
-    gy1, gy2, gy3, rz1, rz2, rz3, gx1, gx2, gx3, held, ry1, ry2, ry3,
+def key_value_kernel(k, v, key_in, value_in, held, ry1, ry2, ry3, grads):
+    state = (held[...] + ry1[...].astype(F32) + ry2[...] + ry3[...]).astype(BF)
+    grads[0] = (key_in[...] + dot(v[0], state, ((1,), (1,)))).astype(BF)
+    grads[1] = (value_in[...] + dot(k[0], state, ((1,), (0,)))).astype(BF)
+
+
+def query_kernel(
+    pos, q, g, mix, out_t, query_t, level_in, gy1, gy2, gy3, rz1, rz2, rz3, gx1, gx2, gx3,
     attended, grads, level_out,
 ):
     qt = turned(q[0]).astype(BF)
@@ -172,9 +178,18 @@
         query = query + dot(bucket, (gt * row).astype(BF), ((1,), (0,)))
     attended[...] = total.T.astype(BF)
     grads[0] = (query * DH**-0.5).T.astype(BF)
-    state = (held[...] + ry1[...].astype(F32) + ry2[...] + ry3[...]).astype(BF)
-    grads[1] = (key_in[...] + dot(v[0], state, ((1,), (1,)))).astype(BF)
-    grads[2] = (value_in[...] + dot(k[0], state, ((1,), (0,)))).astype(BF)
+
+
+def column_kernel(pos, left, right, c0, c1, c2, c3, whole):
+    whole[:, :1024] = left[...]
+    whole[:, 1024:] = right[...]
+    first = pos[3] == 0
+    line = jnp.where(first, pos[X], pos[Z])
+    for step, out in enumerate((c0, c1, c2, c3)):
+        at = lax.rem(line + step, 4)
+        for tile in range(4):
+            column = jnp.where(first, 512 * at + 128 * tile, 512 * tile + 128 * at)
+            out[:, 128 * tile : 128 * (tile + 1)] = whole[:, pl.ds(pl.multiple_of(column, 128), 128)]
 
 
 def part(index):
@@ -192,33 +207,37 @@
     return jax.ShapeDtypeStruct(dims, kind)
 
 
-def on_device(hidden, proj_weights, level_mix, out_grad):
+def layer(hidden, proj_weights, level_mix, out_grad):
     x, z, y = (lax.axis_index(name) for name in SEQ)
     core = lax.axis_index("head")
     first = core == 0
-    pos = jnp.stack([x, z, y]).astype(jnp.int32)
+    pos = jnp.stack([x, z, y, core]).astype(jnp.int32)
     other = partner(hidden)
-    features = jnp.concatenate(
-        [jnp.where(first, hidden, other), jnp.where(first, other, hidden)], axis=1
-    )
+    left, right = jnp.where(first, hidden, other), jnp.where(first, other, hidden)
     root = jnp.array([DH**-0.5, 1.0, 1.0], F32)[:, None, None]
-    projected = (
-        jnp.einsum("td,dme->mte", features, proj_weights, preferred_element_type=F32) * root
-    ).astype(BF)
+    near = lax.dynamic_slice_in_dim(proj_weights, 1024 * core, 1024, 0)
+    far = lax.dynamic_slice_in_dim(proj_weights, 1024 * (1 - core), 1024, 0)
+    near_part = jnp.einsum("td,dme->mte", hidden, near, preferred_element_type=F32)
+    far_part = jnp.einsum("td,dme->mte", other, far, preferred_element_type=F32)
+    projected = ((near_part + far_part) * root).astype(BF)
     mix = level_mix.transpose(1, 0, 2)
 
-    by_z = features.reshape(256, 4, 4, 128).transpose(0, 2, 1, 3).reshape(256, 2048)
-    sorted_features = jnp.where(first, features, by_z)
-    line = jnp.where(first, x, z)
-
-    def columns(step):
-        return lax.dynamic_slice_in_dim(sorted_features, 512 * ((line + step) % 4), 512, 1)
-
-    hidden_blocks = [columns(0)] + [shifted(columns(n), (X, Z), n) for n in (1, 2, 3)]
+    whole = pl.BlockSpec(memory_space=pltpu.VMEM)
+    own_columns, *far_columns = pl.pallas_call(
+        column_kernel,
+        in_specs=[SCALARS, whole, whole],
+        out_specs=[whole] * 4,
+        out_shape=[shape((256, 512), BF)] * 4,
+        scratch_shapes=[pltpu.VMEM((256, 2048), BF)],
+    )(pos, left, right)
+    hidden_blocks = [own_columns]
+    for n, block in zip((1, 2, 3), far_columns):
+        hidden_blocks.append(shifted(block, (X, Z), n))
 
     state_shape = shape((512, DH), BF)
     states, b0, b1, b2, b3, b5, u3 = pl.pallas_call(
         state_kernel,
+        name="state",
         grid=(4,),
         in_specs=[SCALARS, part(0), part(1), part(2), COLUMNS, MIX],
         out_specs=[STATE] * 7,
@@ -228,10 +247,17 @@
     def line_of(axis):
         return (axis, axis)
 
-    gy = [shifted(states, line_of(Y), n) for n in (1, 2, 3)]
-    rx = [shifted(a, line_of(X), n, "down") for n, a in ((1, b5), (2, b5), (3, u3))]
-    out_t, query_t, key_in, value_in, level_in = pl.pallas_call(
+    def sent(pieces, axis, which="all"):
+        out = []
+        for n, piece in zip((1, 2, 3), pieces):
+            out.append(shifted(piece, line_of(axis), n, which))
+        return out
+
+    gy = sent([states] * 3, Y)
+    rx = sent([b5, b5, u3], X, "down")
+    inner_call = pl.pallas_call(
         inner_kernel,
+        name="inner",
         grid=(4,),
         in_specs=[part(0), part(1), part(2), COLUMNS, MIX],
         out_specs=[
@@ -249,61 +275,84 @@
             shape((4, 16, 256), F32),
         ],
         scratch_shapes=[pltpu.VMEM((256, 256), jnp.int32)],
-    )(projected, projected, projected, out_grad, mix)
-    whole = pl.BlockSpec(memory_space=pltpu.VMEM)
-    p1, p2, p3, held = pl.pallas_call(
+    )
+    out_t, query_t, key_in, value_in, level_in = inner_call(
+        projected, projected, projected, out_grad, mix
+    )
+    middle_call = pl.pallas_call(
         middle_kernel,
+        name="middle",
         in_specs=[SCALARS] + [whole] * 9,
         out_specs=[whole] * 4,
         out_shape=[shape((1024, DH), BF)] * 3 + [shape((512, DH), F32)],
-    )(pos, states, *gy, *rx, b2, b3)
-    rz = [shifted(a, line_of(Z), n) for n, a in ((1, p1), (2, p2), (3, p3))]
-    group, q1, q2, q3, held = pl.pallas_call(
+    )
+    p1, p2, p3, held = middle_call(pos, states, *gy, *rx, b2, b3)
+    rz = sent([p1, p2, p3], Z)
+    late_call = pl.pallas_call(
         late_kernel,
+        name="late",
         in_specs=[SCALARS] + [whole] * 7,
         out_specs=[whole] * 5,
         out_shape=[state_shape] * 4 + [shape((512, DH), F32)],
-    )(pos, p1, *rz, held, b0, b1)
-    ry = [shifted(a, line_of(Y), n) for n, a in ((1, q1), (2, q2), (3, q3))]
-    gx = [shifted(group, line_of(X), n, "up") for n in (1, 2, 3)]
-    attended, grads, level_grad = pl.pallas_call(
-        outer_kernel,
+    )
+    group, q1, q2, q3, held = late_call(pos, p1, *rz, held, b0, b1)
+    gx = sent([group] * 3, X, "up")
+    ry = sent([q1, q2, q3], Y)
+    grads = [None, None]
+    grads[0] = pl.pallas_call(
+        key_value_kernel,
         grid=(4,),
-        in_specs=[SCALARS, part(0), part(1), part(2), COLUMNS, MIX, TURNED, TURNED]
-        + [COLUMNS, COLUMNS, pl.BlockSpec((1, 16, 256), lambda h: (h, 0, 0))]
-        + [STATE] * 13,
-        out_specs=[COLUMNS, pl.BlockSpec((3, 256, DH), lambda h: (0, 0, h)), MIX],
+        in_specs=[part(1), part(2), COLUMNS, COLUMNS] + [STATE] * 4,
+        out_specs=pl.BlockSpec((2, 256, DH), lambda h: (0, 0, h)),
+        out_shape=shape((2, 256, 512), BF),
+    )(projected, projected, key_in, value_in, held, *ry)
+    attended, grads[1], level_grad = pl.pallas_call(
+        query_kernel,
+        grid=(4,),
+        in_specs=[SCALARS, part(0), COLUMNS, MIX, TURNED, TURNED]
+        + [pl.BlockSpec((1, 16, 256), lambda h: (h, 0, 0))]
+        + [STATE] * 9,
+        out_specs=[COLUMNS, part(0), MIX],
         out_shape=[
             shape((256, 512), BF),
-            shape((3, 256, 512), BF),
+            shape((1, 256, 512), BF),
             shape((4, 15, 256), F32),
         ],
-    )(
-        pos, projected, projected, projected, out_grad, mix, out_t, query_t, key_in, value_in,
-        level_in, *gy, *rz, *gx, held, *ry,
-    )
+    )(pos, projected, out_grad, mix, out_t, query_t, level_in, *gy, *rz, *gx)
     level_grad = level_grad.transpose(1, 0, 2)
 
-    grad_blocks = [grads] + [shifted(grads, (X, Z), n) for n in (1, 2, 3)]
-
-    partial_inputs = jnp.einsum("mte,dme->td", grads, proj_weights, preferred_element_type=F32)
+    grad_blocks = [[grads[0]], [grads[1]]]
+    for i in (0, 1):
+        for n in (1, 2, 3):
+            grad_blocks[i].append(shifted(grads[i], (X, Z), n))
+
+    all_grads = jnp.concatenate([grads[1], grads[0]], axis=0)
+    partial_inputs = jnp.einsum("mte,dme->td", all_grads, proj_weights, preferred_element_type=F32)
     mine = lax.dynamic_slice_in_dim(partial_inputs, 1024 * core, 1024, 1)
     theirs = lax.dynamic_slice_in_dim(partial_inputs, 1024 * (1 - core), 1024, 1)
-    input_grad = (mine + partner(theirs)).astype(BF)
-
-    partial_weights = functools.reduce(
-        jnp.add,
-        [
-            jnp.einsum("td,mte->mde", h, g, preferred_element_type=F32)
-            for h, g in zip(hidden_blocks, grad_blocks)
-        ],
-    )
+    came = partner(theirs)
+    input_grad = (mine + came).astype(BF)
+
+    def products(blocks):
+        return functools.reduce(
+            jnp.add,
+            [
+                jnp.einsum("td,mte->mde", h, g, preferred_element_type=F32)
+                for h, g in zip(hidden_blocks, blocks)
+            ],
+        )
+
+    key_value_products = products(grad_blocks[0])
+    query_products = products(grad_blocks[1])
+    partial_weights = jnp.concatenate([query_products, key_value_products], axis=0)
 
     def reduced(array, at, axes, rows):
         def rows_of(step):
             return lax.dynamic_slice_in_dim(array, rows * ((at + step) % 4), rows, 1)
 
-        came = [shifted(rows_of(n).astype(BF), axes, n) for n in (1, 2, 3)]
+        came = []
+        for n in (1, 2, 3):
+            came.append(shifted(rows_of(n).astype(BF), axes, n))
         return rows_of(0) + came[0] + came[1] + came[2]
 
     partial_weights = reduced(partial_weights, jnp.where(first, z, x), (Z, X), 128)
@@ -315,7 +364,7 @@
 def solution(mesh):
     split = Mesh(mesh.devices.reshape(4, 4, 4, 2), ALL)
     return jax.shard_map(
-        on_device,
+        layer,
         mesh=split,
         in_specs=(P(SEQ, "head"), P(None, None, "head"), P(None, "head", SEQ), P(SEQ, "head")),
         out_specs=(P(SEQ, "head"), P(SEQ, "head"), P(SEQ, None, "head"), P(None, "head", SEQ)),

time: 136 us -> 146 us (1.074)
  starting transfers between devices: 44.9 us -> 52.3 us
  Pallas kernels: 19.1 us -> 25 us
  local copies, waits for them, and re-layouts: 11 us -> 5.67 us
  waiting for transfers between devices: 39.2 us -> 37.2 us
  other arithmetic: 6.47 us -> 8.34 us
  matrix products: 13.3 us -> 15.1 us
    ppermute x27 -> x30, starting transfers between devices: 44.8 us -> 52.2 us  [shifted(): return lax.ppermute(value, ALL, pairs)]
    pallas_call x5 -> x7, Pallas kernels: 19.1 us -> 25 us  [the longest x1 5.26 us: layer(): inner_call(projected, projected, projected, out_grad, mix)]
    reshape x3 -> x0, local copies, waits for them, and re-layouts: 4.14 us -> none  [on_device(): features.reshape(256, 4, 4, 128).transpose(0, 2, 1, 3).reshape(256, 2048)]
    ppermute x27 -> x30, waiting for transfers between devices: 39.2 us -> 37.2 us  [shifted(): return lax.ppermute(value, ALL, pairs)]
    dot_general x6 -> x11, matrix products: 13.3 us -> 15.1 us  [the longest x1 4.84 us: layer(): jnp.einsum('mte,dme->td', all_grads, proj_weights, preferred_element_type...]
    convert_element_type x1 -> x2, other arithmetic: 2.15 us -> 3.56 us  [the longest x1 2.47 us: layer(): input_grad = (mine + came).astype(BF)]
    unnamed x38 -> x50, local copies, waits for them, and re-layouts: 4.53 us -> 4.59 us
  transfers between devices with their start and end apart: 29 -> 32, of which waited for: 12 -> 11; matrix products, arithmetic and copies ran while one was open for 16% -> 13% of each run, Pallas kernels for 8% -> 11%
where the time goes in v2:
time: 146 us; the launch traced here: 145 us
  starting transfers between devices  52.3 us (36%)
  waiting for transfers between devices  37.2 us (25%)
  Pallas kernels  25 us (17%)
  matrix products  15.1 us (10%)
  other arithmetic  8.34 us (6%)
  local copies, waits for them, and re-layouts  5.67 us (4%)
    ppermute x30, starting transfers between devices, shifted(): return lax.ppermute(value, ALL, pairs)  52.2 us
    ppermute x30, waiting for transfers between devices, shifted(): return lax.ppermute(value, ALL, pairs)  37.2 us
    pallas_call x1, Pallas kernels, layer(): inner_call(projected, projected, projected, out_grad, mix)  5.26 us
    dot_general x1, matrix products, layer(): jnp.einsum('mte,dme->td', all_grads, proj_weights, preferred_element_type...  4.84 us
    pallas_call x1, Pallas kernels, layer(): pl.pallas_call(query_kernel, grid=(4,), in_specs=[SCALARS, part(0), COLUM...  4.73 us
    unnamed x50, local copies, waits for them, and re-layouts  4.59 us
    pallas_call x1, Pallas kernels, layer(): pl.pallas_call(state_kernel, name='state', grid=(4,), in_specs=[SCALARS,...  3.87 us
    pallas_call x1, Pallas kernels, layer(): pl.pallas_call(key_value_kernel, grid=(4,), in_specs=[part(1), part(2), C...  3.82 us
  transfers between devices with their start and end apart: 32, of which 11 were waited for; matrix products, arithmetic and copies ran while one was open for 13% of the time, Pallas kernels for 11%

profile of v2, /device:TPU:0, one launch (start us, length us, event | category | flops | bytes accessed | tf_op | source)
XLA Modules:
  0.0 144.7 jit_solution(3395745283057223302)
XLA Ops:
  0.7 1.5 %copy.32 = f32[15,4,256]{2,0,1:T(8,128)} copy(f32[15,4,256]{2,1,0:T(4,128)} %param.7) | data formatting | bytes 122880 | tf_op args[2]
  2.2 0.6 pad_add_fusion.pos
  2.8 3.0 %fusion.2 = f32[3,512,256]{1,2,0:T(8,128)S(1)} fusion(bf16[2048,3,512]{2,0,1:T(8,128)(2,1)} %param.6, s32[]{:T(128)S(6)} %select_n.82, bf16[256,1024]{1,0:T(8,128)(2,1)} %param.5), kind=kOutput, calls=%fused_computation.10 | convolution fusion | flops 805306368 | bytes 5242884 | tf_op jit(solution)/shard_map/td,dme->mte/dot_general | solution.py:220
  5.9 3.8 %fusion.9.q.k.v = bf16[3,256,512]{2,1,0:T(8,128)(2,1)} fusion(f32[3,512,256]{1,2,0:T(8,128)S(1)} %fusion.2, bf16[2048,3,512]{2,0,1:T(8,128)(2,1)} %param.6, s32[]{:T(128)S(6)} %select_n.83, f32[3]{0:T(128)S(1)} %copy-done.22, bf16[256,1024]{1,0:T(8,128)(2,1)S(1)} %collective-permute-done), kind=kOutput, calls=%fused_computation.19 | convolution fusion | flops 806486016 | bytes 6029328 | tf_op jit(solution)/shard_map/td,dme->mte/dot_general | solution.py:221
  9.7 3.9 %state.1 = (bf16[512,128]{1,0:T(8,128)(2,1)}, bf16[512,128]{1,0:T(8,128)(2,1)}, bf16[512,128]{1,0:T(8,128)(2,1)}, bf16[512,128]{1,0:T(8,128)(2,1)}, bf16[512,128...) custom-call(s32[4]{0:T(128)} %pad_add_fusion.pos, bf16[3,256,512]{2,1,0:T(8,128)(2,1)} %fusion.9.q.k.v, ...), custom_call_target="tpu_custom_call" | custom-call | tf_op jit(solution)/shard_map/state/pallas_call | solution.py:238
  13.5 1.8 %collective-permute-start.1 = (bf16[512,128]{1,0:T(8,128)(2,1)}, bf16[512,128]{1,0:T(8,128)(2,1)S(1)}, u32[]{:S(2)}, u32[]{:S(2)}) collective-permute-start(bf16[512,128]{1,0:T(8,128)(2,1)} %get-tuple-element.35.s), channel_id=1, source_target_pairs={{0,2},{1,3},{2,4},{3,5},{4,6},{5,7},{6,0},{7,1},{8,10},{9,11},{10,... | collective-permute-start | bytes 393224 | tf_op jit(solution)/shard_map/ppermute | solution.py:46
  15.3 2.9 %collective-permute-start.2 = (bf16[512,128]{1,0:T(8,128)(2,1)}, bf16[512,128]{1,0:T(8,128)(2,1)S(1)}, u32[]{:S(2)}, u32[]{:S(2)}) collective-permute-start(bf16[512,128]{1,0:T(8,128)(2,1)} %get-tuple-element.35.s), channel_id=1, source_target_pairs={{0,4},{1,5},{2,6},{3,7},{4,0},{5,1},{6,2},{7,3},{8,12},{9,13},{10,... | collective-permute-start | bytes 393224 | tf_op jit(solution)/shard_map/ppermute | solution.py:46
  18.2 1.3 collective-permute-start.3
  19.5 1.3 collective-permute-start.4
  20.8 1.3 collective-permute-start.5
  22.2 1.3 collective-permute-start.6
  23.5 1.6 %collective-permute-done.2.gy2 = bf16[512,128]{1,0:T(8,128)(2,1)S(1)} collective-permute-done((bf16[512,128]{1,0:T(8,128)(2,1)}, bf16[512,128]{1,0:T(8,128)(2,1)S(1)}, u32[]{:S(2)}, u32[]{:S(2)}) %collective-permute-start.2) | collective-permute-done | bytes 131104 | tf_op jit(solution)/shard_map/ppermute | solution.py:46
  25.1 5.6 %collective-permute-done.4.r1 = bf16[512,128]{1,0:T(8,128)(2,1)S(1)} collective-permute-done((bf16[512,128]{1,0:T(8,128)(2,1)}, bf16[512,128]{1,0:T(8,128)(2,1)S(1)}, u32[]{:S(2)}, u32[]{:S(2)}) %collective-permute-start.4) | collective-permute-done | bytes 131104 | tf_op jit(solution)/shard_map/ppermute | solution.py:46
  30.8 0.6 copy-done.15
  31.4 2.5 %middle.1 = (bf16[1024,128]{1,0:T(8,128)(2,1)}, bf16[1024,128]{1,0:T(8,128)(2,1)}, bf16[1024,128]{1,0:T(8,128)(2,1)}, f32[512,128]{1,0:T(8,128)}) custom-call(s32[4]{0:T(128)} %pad_add_fusion.pos, bf16[512,128]{1,0:T(8,128)(2,1)} %get-tuple-element.35.s, bf16[512,128]{1,0:T(8,128)(2,1)} %copy-done.8, bf16[512,128]{1,0:T(8,128)(2,1)} %copy-done.9, ...), custom_call_target="tpu_custom_call" | custom-call | tf_op jit(solution)/shard_map/middle/pallas_call | solution.py:289
  33.9 1.9 %collective-permute-start.7 = (bf16[1024,128]{1,0:T(8,128)(2,1)}, bf16[1024,128]{1,0:T(8,128)(2,1)S(1)}, u32[]{:S(2)}, u32[]{:S(2)}) collective-permute-start(bf16[1024,128]{1,0:T(8,128)(2,1)} %get-tuple-element.40.p1), channel_id=1, source_target_pairs={{0,8},{1,9},{2,10},{3,11},{4,12},{5,13},{6,14},{7,15},{8,16},{9,17... | collective-permute-start | bytes 786440 | tf_op jit(solution)/shard_map/ppermute | solution.py:46
  35.8 3.6 %collective-permute-start.8 = (bf16[1024,128]{1,0:T(8,128)(2,1)}, bf16[1024,128]{1,0:T(8,128)(2,1)S(1)}, u32[]{:S(2)}, u32[]{:S(2)}) collective-permute-start(bf16[1024,128]{1,0:T(8,128)(2,1)} %get-tuple-element.41), channel_id=1, source_target_pairs={{0,16},{1,17},{2,18},{3,19},{4,20},{5,21},{6,22},{7,23},{8,24},{9,... | collective-permute-start | bytes 786440 | tf_op jit(solution)/shard_map/ppermute | solution.py:46
  39.4 1.0 collective-permute-start.9
  40.4 4.5 %collective-permute-done.7.rz1 = bf16[1024,128]{1,0:T(8,128)(2,1)S(1)} collective-permute-done((bf16[1024,128]{1,0:T(8,128)(2,1)}, bf16[1024,128]{1,0:T(8,128)(2,1)S(1)}, u32[]{:S(2)}, u32[]{:S(2)}) %collective-permute-start.7) | collective-permute-done | bytes 262176 | tf_op jit(solution)/shard_map/ppermute | solution.py:46
  44.9 4.1 %collective-permute-done.8.rz2 = bf16[1024,128]{1,0:T(8,128)(2,1)S(1)} collective-permute-done((bf16[1024,128]{1,0:T(8,128)(2,1)}, bf16[1024,128]{1,0:T(8,128)(2,1)S(1)}, u32[]{:S(2)}, u32[]{:S(2)}) %collective-permute-start.8) | collective-permute-done | bytes 262176 | tf_op jit(solution)/shard_map/ppermute | solution.py:46
  49.1 0.7 copy-done.5
  49.9 2.3 %late.1 = (bf16[512,128]{1,0:T(8,128)(2,1)}, bf16[512,128]{1,0:T(8,128)(2,1)}, bf16[512,128]{1,0:T(8,128)(2,1)}, bf16[512,128]{1,0:T(8,128)(2,1)}, f32[512,128]{1,0:T(8,128)}) custom-call(s32[4]{0:T(128)} %pad_add_fusion.pos, bf16[1024,128]{1,0:T(8,128)(2,1)} %get-tuple-element.40.p1, bf16[1024,128]{1,0:T(8,128)(2,1)} %copy-done.4, ...), custom_call_target="tpu_custom_call" | custom-call | tf_op jit(solution)/shard_map/late/pallas_call | solution.py:298
  52.2 6.7 %collective-permute-start.10 = (bf16[512,128]{1,0:T(8,128)(2,1)}, bf16[512,128]{1,0:T(8,128)(2,1)S(1)}, u32[]{:S(2)}, u32[]{:S(2)}) collective-permute-start(bf16[512,128]{1,0:T(8,128)(2,1)} %get-tuple-element.46), channel_id=1, source_target_pairs={{0,32},{1,33},{2,34},{3,35},{4,36},{5,37},{6,38},{7,39},{8,40},{9,... | collective-permute-start | bytes 393224 | tf_op jit(solution)/shard_map/ppermute | solution.py:46
  58.9 1.6 %collective-permute-start.11 = (bf16[512,128]{1,0:T(8,128)(2,1)}, bf16[512,128]{1,0:T(8,128)(2,1)S(1)}, u32[]{:S(2)}, u32[]{:S(2)}) collective-permute-start(bf16[512,128]{1,0:T(8,128)(2,1)} %get-tuple-element.46), channel_id=1, source_target_pairs={{0,64},{1,65},{2,66},{3,67},{4,68},{5,69},{6,70},{7,71},{8,72},{9,... | collective-permute-start | bytes 393224 | tf_op jit(solution)/shard_map/ppermute | solution.py:46
  60.5 1.3 collective-permute-start.12
  61.8 0.7 collective-permute-start.13
  62.6 1.3 collective-permute-start.14
  63.9 1.4 collective-permute-start.15
  65.3 1.1 broadcast_select_fusion
  66.4 5.3 %inner.1 = (f32[4,128,256]{2,1,0:T(8,128)}, f32[4,128,256]{2,1,0:T(8,128)}, f32[256,512]{1,0:T(8,128)}, f32[256,512]{1,0:T(8,128)}, f32[4,16,256]{2,1,0:T(8,128)}) custom-call(bf16[3,256,512]{2,1,0:T(8,128)(2,1)} %fusion.9.q.k.v, bf16[3,256,512]{2,1,0:T(8,128)(2,1)} %fusion.9.q.k.v, bf16[3,256,512]{2,1,0:T(8,128)(2,1)} %fusion.9.q.k.v, bf16[256,512]{1,0:T(8,128)(2,1)} %g.5, ...), custom_call_target="tpu_custom_call" | custom-call | tf_op jit(solution)/shard_map/inner/pallas_call | solution.py:279
  71.7 2.5 %shard_map.86 = (bf16[256,512]{1,0:T(8,128)(2,1)}, bf16[256,512]{1,0:T(8,128)(2,1)}, bf16[256,512]{1,0:T(8,128)(2,1)}, bf16[256,512]{1,0:T(8,128)(2,1)}) custom-call(s32[4]{0:T(128)} %pad_add_fusion.pos, bf16[256,1024]{1,0:T(8,128)(2,1)} %get-tuple-element.68.left, bf16[256,1024]{1,0:T(8,128)(2,1)} %get-tuple-element.67.right), custom_call_target="tpu_custom_call" | custom-call | tf_op jit(solution)/shard_map/pallas_call | solution.py:226
  74.3 1.9 %collective-permute-start.20 = (bf16[256,512]{1,0:T(8,128)(2,1)}, bf16[256,512]{1,0:T(8,128)(2,1)S(1)}, u32[]{:S(2)}, u32[]{:S(2)}) collective-permute-start(bf16[256,512]{1,0:T(8,128)(2,1)} %get-tuple-element.57), channel_id=1, source_target_pairs={{0,64},{1,17},{2,66},{3,19},{4,68},{5,21},{6,70},{7,23},{8,72},{9,... | collective-permute-start | bytes 786440 | tf_op jit(solution)/shard_map/ppermute | solution.py:46
  76.2 4.7 %shard_map.84 = (bf16[256,512]{1,0:T(8,128)(2,1)}, bf16[1,256,512]{2,1,0:T(8,128)(2,1)}, f32[4,15,256]{2,1,0:T(8,128)}) custom-call(s32[4]{0:T(128)} %pad_add_fusion.pos, bf16[3,256,512]{2,1,0:T(8,128)(2,1)} %fusion.9.q.k.v, bf16[256,512]{1,0:T(8,128)(2,1)} %g.5, f32[4,15,256]{2,1,0:T(8,128)} %bitcast.63, f32[4,128,256]{2,1,0:T(8,128)} %get-tuple-element.32.out_t, ...), custom_call_target="tpu_custom_call" | custom-call | tf_op jit(solution)/shard_map/pallas_call | solution.py:309
  80.9 0.9 collective-permute-start.18
  81.8 2.4 %collective-permute-start.21 = (bf16[1,256,512]{2,1,0:T(8,128)(2,1)}, bf16[1,256,512]{2,1,0:T(8,128)(2,1)S(1)}, u32[]{:S(2)}, u32[]{:S(2)}) collective-permute-start(bf16[1,256,512]{2,1,0:T(8,128)(2,1)} %get-tuple-element.48), channel_id=1, source_target_pairs={{0,96},{1,25},{2,98},{3,27},{4,100},{5,29},{6,102},{7,31},{8,104},... | collective-permute-start | bytes 786440 | tf_op jit(solution)/shard_map/ppermute | solution.py:46
  84.3 1.1 collective-permute-start.19
  85.4 3.8 %shard_map.85 = bf16[2,256,512]{2,1,0:T(8,128)(2,1)} custom-call(bf16[3,256,512]{2,1,0:T(8,128)(2,1)} %fusion.9.q.k.v, bf16[3,256,512]{2,1,0:T(8,128)(2,1)} %fusion.9.q.k.v, f32[256,512]{1,0:T(8,128)} %get-tuple-element.49.key_in, f32[256,512]{1,0:T(8,128)} %get-tuple-element.50.value_in, f32[512,128]{1,0:T(8,128)} %get-tuple-element.51.held, ...), custom_call_target="tpu_custom_call" | custom-call | tf_op jit(solution)/shard_map/pallas_call | solution.py:302
  89.3 4.8 %convolution_bitcast_fusion = f32[256,2048]{1,0:T(8,128)S(1)} fusion(bf16[2048,3,512]{2,0,1:T(8,128)(2,1)} %param.6, bf16[2,256,512]{2,1,0:T(8,128)(2,1)} %shard_map.85, bf16[1,256,512]{2,1,0:T(8,128)(2,1)S(1)} %copy-done.11), kind=kOutput, calls=%fused_computation.12 | convolution fusion | flops 1611005952 | bytes 9175040 | tf_op jit(solution)/shard_map/mte,dme->td/dot_general | solution.py:330
  94.1 0.5 fusion.35
  94.6 1.6 %collective-permute-start.17 = (bf16[1,256,512]{2,1,0:T(8,128)(2,1)S(1)}, bf16[1,256,512]{2,1,0:T(8,128)(2,1)S(1)}, u32[]{:S(2)}, u32[]{:S(2)}) collective-permute-start(bf16[1,256,512]{2,1,0:T(8,128)(2,1)S(1)} %copy-done.11), channel_id=1, source_target_pairs={{0,32},{1,9},{2,34},{3,11},{4,36},{5,13},{6,38},{7,15},{8,40},{9,1... | collective-permute-start | bytes 786440 | tf_op jit(solution)/shard_map/ppermute | solution.py:46
  96.2 1.3 collective-permute-start.24
  97.8 1.6 %collective-permute-start.23 = (bf16[2,256,512]{2,1,0:T(8,128)(2,1)S(1)}, bf16[2,256,512]{2,1,0:T(8,128)(2,1)S(1)}, u32[]{:S(2)}, u32[]{:S(2)}) collective-permute-start(bf16[2,256,512]{2,1,0:T(8,128)(2,1)S(1)} %copy-done.2), channel_id=1, source_target_pairs={{0,32},{1,9},{2,34},{3,11},{4,36},{5,13},{6,38},{7,15},{8,40},{9,1... | collective-permute-start | bytes 1572872 | tf_op jit(solution)/shard_map/ppermute | solution.py:46
  99.4 1.7 %collective-permute-start.25 = (bf16[2,256,512]{2,1,0:T(8,128)(2,1)S(1)}, bf16[2,256,512]{2,1,0:T(8,128)(2,1)S(1)}, u32[]{:S(2)}, u32[]{:S(2)}) collective-permute-start(bf16[2,256,512]{2,1,0:T(8,128)(2,1)S(1)} %copy-done.2), channel_id=1, source_target_pairs={{0,96},{1,25},{2,98},{3,27},{4,100},{5,29},{6,102},{7,31},{8,104},... | collective-permute-start | bytes 1572872 | tf_op jit(solution)/shard_map/ppermute | solution.py:46
  101.5 6.6 %collective-permute-done.17 = bf16[1,256,512]{2,1,0:T(8,128)(2,1)S(1)} collective-permute-done((bf16[1,256,512]{2,1,0:T(8,128)(2,1)S(1)}, bf16[1,256,512]{2,1,0:T(8,128)(2,1)S(1)}, u32[]{:S(2)}, u32[]{:S(2)}) %collective-permute-start.17) | collective-permute-done | bytes 262176 | tf_op jit(solution)/shard_map/ppermute | solution.py:46
  109.3 4.4 %collective-permute-done.23 = bf16[2,256,512]{2,1,0:T(8,128)(2,1)S(1)} collective-permute-done((bf16[2,256,512]{2,1,0:T(8,128)(2,1)S(1)}, bf16[2,256,512]{2,1,0:T(8,128)(2,1)S(1)}, u32[]{:S(2)}, u32[]{:S(2)}) %collective-permute-start.23) | collective-permute-done | bytes 524320 | tf_op jit(solution)/shard_map/ppermute | solution.py:46
  113.7 0.5 fusion.33
  114.2 0.6 add_bitcast_fusion
  114.8 1.1 fusion.19
  115.9 1.1 collective-permute-start.26
  117.0 2.4 %collective-permute-start.27 = (bf16[3,128,512]{2,1,0:T(8,128)(2,1)}, bf16[3,128,512]{2,1,0:T(8,128)(2,1)}, u32[]{:S(2)}, u32[]{:S(2)}) collective-permute-start(bf16[3,128,512]{2,1,0:T(8,128)(2,1)} %get-tuple-element.65), channel_id=1, source_target_pairs={{0,16},{1,65},{2,18},{3,67},{4,20},{5,69},{6,22},{7,71},{8,24},{9,... | collective-permute-start | bytes 1179656 | tf_op jit(solution)/shard_map/ppermute | solution.py:46
  119.4 1.2 collective-permute-start.28
  120.7 1.0 constant_dynamic-slice_fusion
  121.7 3.5 %collective-permute-done.26 = bf16[3,128,512]{2,1,0:T(8,128)(2,1)} collective-permute-done((bf16[3,128,512]{2,1,0:T(8,128)(2,1)}, bf16[3,128,512]{2,1,0:T(8,128)(2,1)}, u32[]{:S(2)}, u32[]{:S(2)}) %collective-permute-start.26) | collective-permute-done | bytes 393248 | tf_op jit(solution)/shard_map/ppermute | solution.py:46
  125.2 4.5 %collective-permute-done.27 = bf16[3,128,512]{2,1,0:T(8,128)(2,1)} collective-permute-done((bf16[3,128,512]{2,1,0:T(8,128)(2,1)}, bf16[3,128,512]{2,1,0:T(8,128)(2,1)}, u32[]{:S(2)}, u32[]{:S(2)}) %collective-permute-start.27) | collective-permute-done | bytes 393248 | tf_op jit(solution)/shard_map/ppermute | solution.py:46
  129.7 0.6 collective-permute-done.28
  130.3 1.5 %fusion.17 = f32[3,128,512]{2,1,0:T(8,128)S(1)} fusion(s32[]{:T(128)S(6)} %select_n.89, f32[2,512,512]{2,1,0:T(8,128)S(1)} %add_bitcast_fusion, f32[1,512,512]{2,1,0:T(8,128)S(1)} %fusion.8, bf16[3,128,512]{2,1,0:T(8,128)(2,1)} %collective-permute-done.28, bf16[3,128,512]{2,1,0:T(8,128)(2,1)} %collective-permute-done.27, ...), kind=kLoop, calls=%fused_computation.26 | loop fusion | flops 1376256 | bytes 5111812 | tf_op jit(solution)/shard_map/add | solution.py:356
  131.8 0.9 copy-done.3
  132.7 1.4 collective-permute-start.29
  134.2 1.5 %collective-permute-start.30 = (bf16[3,32,512]{2,1,0:T(8,128)(2,1)S(1)}, bf16[3,32,512]{2,1,0:T(8,128)(2,1)S(1)}, u32[]{:S(2)}, u32[]{:S(2)}) collective-permute-start(bf16[3,32,512]{2,1,0:T(8,128)(2,1)S(1)} %get-tuple-element.71), channel_id=1, source_target_pairs={{0,4},{1,5},{2,6},{3,7},{4,0},{5,1},{6,2},{7,3},{8,12},{9,13},{10,... | collective-permute-start | bytes 294920 | tf_op jit(solution)/shard_map/ppermute | solution.py:46
  135.6 2.5 %collective-permute-start.31 = (bf16[3,32,512]{2,1,0:T(8,128)(2,1)S(1)}, bf16[3,32,512]{2,1,0:T(8,128)(2,1)S(1)}, u32[]{:S(2)}, u32[]{:S(2)}) collective-permute-start(bf16[3,32,512]{2,1,0:T(8,128)(2,1)S(1)} %get-tuple-element.70), channel_id=1, source_target_pairs={{0,6},{1,7},{2,0},{3,1},{4,2},{5,3},{6,4},{7,5},{8,14},{9,15},{10,... | collective-permute-start | bytes 294920 | tf_op jit(solution)/shard_map/ppermute | solution.py:46
  138.2 0.7 copy.18
  138.8 1.5 %collective-permute-done.30 = bf16[3,32,512]{2,1,0:T(8,128)(2,1)S(1)} collective-permute-done((bf16[3,32,512]{2,1,0:T(8,128)(2,1)S(1)}, bf16[3,32,512]{2,1,0:T(8,128)(2,1)S(1)}, u32[]{:S(2)}, u32[]{:S(2)}) %collective-permute-start.30) | collective-permute-done | bytes 98336 | tf_op jit(solution)/shard_map/ppermute | solution.py:46
  140.5 1.7 %multiply_bitcast_fusion = f32[32,3,512]{2,0,1:T(8,128)} fusion(bf16[3,32,512]{2,1,0:T(8,128)(2,1)S(1)} %collective-permute-done.31, bf16[3,32,512]{2,1,0:T(8,128)(2,1)S(1)} %collective-permute-done.30, bf16[3,32,512]{2,1,0:T(8,128)(2,1)S(1)} %collective-permute-done.29, f32[3,128,512]{2,1,0:T(8,128)} %copy-done.3, s32[]{:T(128)S(6)} %select_n.97), kind=kLoop, calls=%fused_computation.53 | loop fusion | flops 344064 | bytes 688132 | tf_op jit(solution)/shard_map/transpose | solution.py:360
  142.2 2.5 %add_convert_fusion = bf16[256,1024]{1,0:T(8,128)(2,1)} fusion(f32[256,1024]{1,0:T(8,128)} %collective-permute-done.16, f32[256,2048]{1,0:T(8,128)} %copy-done, s32[]{:T(128)S(6)} %select_n.82), kind=kLoop, calls=%fused_computation.20 | loop fusion | flops 524288 | bytes 2621444 | tf_op jit(solution)/shard_map/convert_element_type | solution.py:334
  (76 shorter events, 2.6 us)
Async XLA Ops:
  0.6 5.2 %collective-permute-start = (bf16[256,1024]{1,0:T(8,128)(2,1)}, bf16[256,1024]{1,0:T(8,128)(2,1)S(1)}, u32[]{:S(2)}, u32[]{:S(2)}) collective-permute-start(bf16[256,1024]{1,0:T(8,128)(2,1)} %param.5), channel_id=1, source_target_pairs={{0,1},{1,0},{2,3},{3,2},{4,5},{5,4},{6,7},{7,6},{8,9},{9,8},{10,11... | collective-permute-start | bytes 1572872 | tf_op jit(solution)/shard_map/ppermute | solution.py:50
  2.8 3.1 %copy-start.22 = (f32[3]{0:T(128)S(1)}, f32[3]{0:T(128)}, u32[]{:S(2)}) copy-start(f32[3]{0:T(128)} %constant.76.clone) | copy-start | bytes 40
  13.5 51.8 %copy-start.1 = (bf16[256,1024]{1,0:T(8,128)(2,1)S(1)}, bf16[256,1024]{1,0:T(8,128)(2,1)}, u32[]{:S(2)}) copy-start(bf16[256,1024]{1,0:T(8,128)(2,1)} %param.5) | copy-start | bytes 1572868
  13.5 8.6 %collective-permute-start.1 = (bf16[512,128]{1,0:T(8,128)(2,1)}, bf16[512,128]{1,0:T(8,128)(2,1)S(1)}, u32[]{:S(2)}, u32[]{:S(2)}) collective-permute-start(bf16[512,128]{1,0:T(8,128)(2,1)} %get-tuple-element.35.s), channel_id=1, source_target_pairs={{0,2},{1,3},{2,4},{3,5},{4,6},{5,7},{6,0},{7,1},{8,10},{9,11},{10,... | collective-permute-start | bytes 393224 | tf_op jit(solution)/shard_map/ppermute | solution.py:46
  15.3 9.8 %collective-permute-start.2 = (bf16[512,128]{1,0:T(8,128)(2,1)}, bf16[512,128]{1,0:T(8,128)(2,1)S(1)}, u32[]{:S(2)}, u32[]{:S(2)}) collective-permute-start(bf16[512,128]{1,0:T(8,128)(2,1)} %get-tuple-element.35.s), channel_id=1, source_target_pairs={{0,4},{1,5},{2,6},{3,7},{4,0},{5,1},{6,2},{7,3},{8,12},{9,13},{10,... | collective-permute-start | bytes 393224 | tf_op jit(solution)/shard_map/ppermute | solution.py:46
  18.2 6.9 %collective-permute-start.3 = (bf16[512,128]{1,0:T(8,128)(2,1)}, bf16[512,128]{1,0:T(8,128)(2,1)S(1)}, u32[]{:S(2)}, u32[]{:S(2)}) collective-permute-start(bf16[512,128]{1,0:T(8,128)(2,1)} %get-tuple-element.35.s), channel_id=1, source_target_pairs={{0,6},{1,7},{2,0},{3,1},{4,2},{5,3},{6,4},{7,5},{8,14},{9,15},{10,... | collective-permute-start | bytes 393224 | tf_op jit(solution)/shard_map/ppermute | solution.py:46
  19.5 11.1 %collective-permute-start.4 = (bf16[512,128]{1,0:T(8,128)(2,1)}, bf16[512,128]{1,0:T(8,128)(2,1)S(1)}, u32[]{:S(2)}, u32[]{:S(2)}) collective-permute-start(bf16[512,128]{1,0:T(8,128)(2,1)} %get-tuple-element.36), channel_id=1, source_target_pairs={{96,0},{97,1},{98,2},{99,3},{100,4},{101,5},{102,6},{103,7},{104,8... | collective-permute-start | bytes 393224 | tf_op jit(solution)/shard_map/ppermute | solution.py:46
  20.8 9.9 %collective-permute-start.5 = (bf16[512,128]{1,0:T(8,128)(2,1)}, bf16[512,128]{1,0:T(8,128)(2,1)S(1)}, u32[]{:S(2)}, u32[]{:S(2)}) collective-permute-start(bf16[512,128]{1,0:T(8,128)(2,1)} %get-tuple-element.36), channel_id=1, source_target_pairs={{64,0},{65,1},{66,2},{67,3},{68,4},{69,5},{70,6},{71,7},{72,8},{73... | collective-permute-start | bytes 393224 | tf_op jit(solution)/shard_map/ppermute | solution.py:46
  22.1 8.6 %copy-start.8 = (bf16[512,128]{1,0:T(8,128)(2,1)}, bf16[512,128]{1,0:T(8,128)(2,1)S(1)}, u32[]{:S(2)}) copy-start(bf16[512,128]{1,0:T(8,128)(2,1)S(1)} %collective-permute-done.1.gy1) | copy-start | bytes 393220
  22.2 8.5 %collective-permute-start.6 = (bf16[512,128]{1,0:T(8,128)(2,1)}, bf16[512,128]{1,0:T(8,128)(2,1)S(1)}, u32[]{:S(2)}, u32[]{:S(2)}) collective-permute-start(bf16[512,128]{1,0:T(8,128)(2,1)} %get-tuple-element.37), channel_id=1, source_target_pairs={{32,0},{33,1},{34,2},{35,3},{36,4},{37,5},{38,6},{39,7},{40,8},{41... | collective-permute-start | bytes 393224 | tf_op jit(solution)/shard_map/ppermute | solution.py:46
  25.1 5.7 %copy-start.9 = (bf16[512,128]{1,0:T(8,128)(2,1)}, bf16[512,128]{1,0:T(8,128)(2,1)S(1)}, u32[]{:S(2)}) copy-start(bf16[512,128]{1,0:T(8,128)(2,1)S(1)} %collective-permute-done.2.gy2) | copy-start | bytes 393220
  25.1 5.7 %copy-start.10 = (bf16[512,128]{1,0:T(8,128)(2,1)}, bf16[512,128]{1,0:T(8,128)(2,1)S(1)}, u32[]{:S(2)}) copy-start(bf16[512,128]{1,0:T(8,128)(2,1)S(1)} %collective-permute-done.3.gy3) | copy-start | bytes 393220
  30.7 0.7 copy-start.15
  30.7 0.7 copy-start.16
  30.7 0.7 copy-start.17
  33.9 11.0 %collective-permute-start.7 = (bf16[1024,128]{1,0:T(8,128)(2,1)}, bf16[1024,128]{1,0:T(8,128)(2,1)S(1)}, u32[]{:S(2)}, u32[]{:S(2)}) collective-permute-start(bf16[1024,128]{1,0:T(8,128)(2,1)} %get-tuple-element.40.p1), channel_id=1, source_target_pairs={{0,8},{1,9},{2,10},{3,11},{4,12},{5,13},{6,14},{7,15},{8,16},{9,17... | collective-permute-start | bytes 786440 | tf_op jit(solution)/shard_map/ppermute | solution.py:46
  35.8 13.2 %collective-permute-start.8 = (bf16[1024,128]{1,0:T(8,128)(2,1)}, bf16[1024,128]{1,0:T(8,128)(2,1)S(1)}, u32[]{:S(2)}, u32[]{:S(2)}) collective-permute-start(bf16[1024,128]{1,0:T(8,128)(2,1)} %get-tuple-element.41), channel_id=1, source_target_pairs={{0,16},{1,17},{2,18},{3,19},{4,20},{5,21},{6,22},{7,23},{8,24},{9,... | collective-permute-start | bytes 786440 | tf_op jit(solution)/shard_map/ppermute | solution.py:46
  39.4 9.6 %collective-permute-start.9 = (bf16[1024,128]{1,0:T(8,128)(2,1)}, bf16[1024,128]{1,0:T(8,128)(2,1)S(1)}, u32[]{:S(2)}, u32[]{:S(2)}) collective-permute-start(bf16[1024,128]{1,0:T(8,128)(2,1)} %get-tuple-element.42), channel_id=1, source_target_pairs={{0,24},{1,25},{2,26},{3,27},{4,28},{5,29},{6,30},{7,31},{8,0},{9,1... | collective-permute-start | bytes 786440 | tf_op jit(solution)/shard_map/ppermute | solution.py:46
  44.9 4.1 %copy-start.4 = (bf16[1024,128]{1,0:T(8,128)(2,1)}, bf16[1024,128]{1,0:T(8,128)(2,1)S(1)}, u32[]{:S(2)}) copy-start(bf16[1024,128]{1,0:T(8,128)(2,1)S(1)} %collective-permute-done.7.rz1) | copy-start | bytes 786436
  49.1 0.7 copy-start.5
  49.1 0.8 copy-start.6
  52.2 11.7 %collective-permute-start.10 = (bf16[512,128]{1,0:T(8,128)(2,1)}, bf16[512,128]{1,0:T(8,128)(2,1)S(1)}, u32[]{:S(2)}, u32[]{:S(2)}) collective-permute-start(bf16[512,128]{1,0:T(8,128)(2,1)} %get-tuple-element.46), channel_id=1, source_target_pairs={{0,32},{1,33},{2,34},{3,35},{4,36},{5,37},{6,38},{7,39},{8,40},{9,... | collective-permute-start | bytes 393224 | tf_op jit(solution)/shard_map/ppermute | solution.py:46
  58.9 15.3 %collective-permute-start.11 = (bf16[512,128]{1,0:T(8,128)(2,1)}, bf16[512,128]{1,0:T(8,128)(2,1)S(1)}, u32[]{:S(2)}, u32[]{:S(2)}) collective-permute-start(bf16[512,128]{1,0:T(8,128)(2,1)} %get-tuple-element.46), channel_id=1, source_target_pairs={{0,64},{1,65},{2,66},{3,67},{4,68},{5,69},{6,70},{7,71},{8,72},{9,... | collective-permute-start | bytes 393224 | tf_op jit(solution)/shard_map/ppermute | solution.py:46
  60.5 13.8 %collective-permute-start.12 = (bf16[512,128]{1,0:T(8,128)(2,1)}, bf16[512,128]{1,0:T(8,128)(2,1)S(1)}, u32[]{:S(2)}, u32[]{:S(2)}) collective-permute-start(bf16[512,128]{1,0:T(8,128)(2,1)} %get-tuple-element.46), channel_id=1, source_target_pairs={{0,96},{1,97},{2,98},{3,99},{4,100},{5,101},{6,102},{7,103},{8,104... | collective-permute-start | bytes 393224 | tf_op jit(solution)/shard_map/ppermute | solution.py:46
  61.8 19.1 %collective-permute-start.13 = (bf16[512,128]{1,0:T(8,128)(2,1)}, bf16[512,128]{1,0:T(8,128)(2,1)S(1)}, u32[]{:S(2)}, u32[]{:S(2)}) collective-permute-start(bf16[512,128]{1,0:T(8,128)(2,1)} %get-tuple-element.52), channel_id=1, source_target_pairs={{0,2},{1,3},{2,4},{3,5},{4,6},{5,7},{6,0},{7,1},{8,10},{9,11},{10,... | collective-permute-start | bytes 393224 | tf_op jit(solution)/shard_map/ppermute | solution.py:46
  62.6 19.3 %collective-permute-start.14 = (bf16[512,128]{1,0:T(8,128)(2,1)}, bf16[512,128]{1,0:T(8,128)(2,1)S(1)}, u32[]{:S(2)}, u32[]{:S(2)}) collective-permute-start(bf16[512,128]{1,0:T(8,128)(2,1)} %get-tuple-element.53), channel_id=1, source_target_pairs={{0,4},{1,5},{2,6},{3,7},{4,0},{5,1},{6,2},{7,3},{8,12},{9,13},{10,... | collective-permute-start | bytes 393224 | tf_op jit(solution)/shard_map/ppermute | solution.py:46
  63.9 7.8 %copy-start.12 = (bf16[512,128]{1,0:T(8,128)(2,1)}, bf16[512,128]{1,0:T(8,128)(2,1)S(1)}, u32[]{:S(2)}) copy-start(bf16[512,128]{1,0:T(8,128)(2,1)S(1)} %collective-permute-done.10.gx1) | copy-start | bytes 393220
  63.9 20.4 %collective-permute-start.15 = (bf16[512,128]{1,0:T(8,128)(2,1)}, bf16[512,128]{1,0:T(8,128)(2,1)S(1)}, u32[]{:S(2)}, u32[]{:S(2)}) collective-permute-start(bf16[512,128]{1,0:T(8,128)(2,1)} %get-tuple-element.54), channel_id=1, source_target_pairs={{0,6},{1,7},{2,0},{3,1},{4,2},{5,3},{6,4},{7,5},{8,14},{9,15},{10,... | collective-permute-start | bytes 393224 | tf_op jit(solution)/shard_map/ppermute | solution.py:46
  74.2 6.7 %copy-start.23 = (bf16[256,512]{1,0:T(8,128)(2,1)S(1)}, bf16[256,512]{1,0:T(8,128)(2,1)}, u32[]{:S(2)}) copy-start(bf16[256,512]{1,0:T(8,128)(2,1)} %get-tuple-element.56) | copy-start | bytes 786436
  74.2 2.0 %copy-start.13 = (bf16[512,128]{1,0:T(8,128)(2,1)}, bf16[512,128]{1,0:T(8,128)(2,1)S(1)}, u32[]{:S(2)}) copy-start(bf16[512,128]{1,0:T(8,128)(2,1)S(1)} %collective-permute-done.11.gx2) | copy-start | bytes 393220
  74.2 20.4 %collective-permute-start.22 = (bf16[256,512]{1,0:T(8,128)(2,1)}, bf16[256,512]{1,0:T(8,128)(2,1)S(1)}, u32[]{:S(2)}, u32[]{:S(2)}) collective-permute-start(bf16[256,512]{1,0:T(8,128)(2,1)} %get-tuple-element.58), channel_id=1, source_target_pairs={{0,96},{1,25},{2,98},{3,27},{4,100},{5,29},{6,102},{7,31},{8,104},... | collective-permute-start | bytes 786440 | tf_op jit(solution)/shard_map/ppermute | solution.py:46
  74.3 1.9 %copy-start.14 = (bf16[512,128]{1,0:T(8,128)(2,1)}, bf16[512,128]{1,0:T(8,128)(2,1)S(1)}, u32[]{:S(2)}) copy-start(bf16[512,128]{1,0:T(8,128)(2,1)S(1)} %collective-permute-done.12.gx3) | copy-start | bytes 393220
  74.3 23.5 %collective-permute-start.20 = (bf16[256,512]{1,0:T(8,128)(2,1)}, bf16[256,512]{1,0:T(8,128)(2,1)S(1)}, u32[]{:S(2)}, u32[]{:S(2)}) collective-permute-start(bf16[256,512]{1,0:T(8,128)(2,1)} %get-tuple-element.57), channel_id=1, source_target_pairs={{0,64},{1,17},{2,66},{3,19},{4,68},{5,21},{6,70},{7,23},{8,72},{9,... | collective-permute-start | bytes 786440 | tf_op jit(solution)/shard_map/ppermute | solution.py:46
  80.9 8.3 %copy-start.11 = (bf16[1,256,512]{2,1,0:T(8,128)(2,1)S(1)}, bf16[1,256,512]{2,1,0:T(8,128)(2,1)}, u32[]{:S(2)}) copy-start(bf16[1,256,512]{2,1,0:T(8,128)(2,1)} %get-tuple-element.48) | copy-start | bytes 786436
  80.9 4.5 %copy-start.18 = (bf16[512,128]{1,0:T(8,128)(2,1)}, bf16[512,128]{1,0:T(8,128)(2,1)S(1)}, u32[]{:S(2)}) copy-start(bf16[512,128]{1,0:T(8,128)(2,1)S(1)} %collective-permute-done.13.ry1) | copy-start | bytes 393220
  80.9 20.5 %collective-permute-start.18 = (bf16[256,512]{1,0:T(8,128)(2,1)S(1)}, bf16[256,512]{1,0:T(8,128)(2,1)S(1)}, u32[]{:S(2)}, u32[]{:S(2)}) collective-permute-start(bf16[256,512]{1,0:T(8,128)(2,1)S(1)} %copy-done.23), channel_id=1, source_target_pairs={{0,32},{1,9},{2,34},{3,11},{4,36},{5,13},{6,38},{7,15},{8,40},{9,1... | collective-permute-start | bytes 786440 | tf_op jit(solution)/shard_map/ppermute | solution.py:46
  81.8 3.6 %copy-start.19 = (bf16[512,128]{1,0:T(8,128)(2,1)}, bf16[512,128]{1,0:T(8,128)(2,1)S(1)}, u32[]{:S(2)}) copy-start(bf16[512,128]{1,0:T(8,128)(2,1)S(1)} %collective-permute-done.14.ry2) | copy-start | bytes 393220
  81.8 14.4 %collective-permute-start.21 = (bf16[1,256,512]{2,1,0:T(8,128)(2,1)}, bf16[1,256,512]{2,1,0:T(8,128)(2,1)S(1)}, u32[]{:S(2)}, u32[]{:S(2)}) collective-permute-start(bf16[1,256,512]{2,1,0:T(8,128)(2,1)} %get-tuple-element.48), channel_id=1, source_target_pairs={{0,96},{1,25},{2,98},{3,27},{4,100},{5,29},{6,102},{7,31},{8,104},... | collective-permute-start | bytes 786440 | tf_op jit(solution)/shard_map/ppermute | solution.py:46
  84.3 1.2 copy-start.20
  84.3 15.1 %collective-permute-start.19 = (bf16[1,256,512]{2,1,0:T(8,128)(2,1)}, bf16[1,256,512]{2,1,0:T(8,128)(2,1)S(1)}, u32[]{:S(2)}, u32[]{:S(2)}) collective-permute-start(bf16[1,256,512]{2,1,0:T(8,128)(2,1)} %get-tuple-element.48), channel_id=1, source_target_pairs={{0,64},{1,17},{2,66},{3,19},{4,68},{5,21},{6,70},{7,23},{8,72},{9,... | collective-permute-start | bytes 786440 | tf_op jit(solution)/shard_map/ppermute | solution.py:46
  89.2 4.9 %copy-start.2 = (bf16[2,256,512]{2,1,0:T(8,128)(2,1)S(1)}, bf16[2,256,512]{2,1,0:T(8,128)(2,1)}, u32[]{:S(2)}) copy-start(bf16[2,256,512]{2,1,0:T(8,128)(2,1)} %shard_map.85) | copy-start | bytes 1572868
  89.2 4.9 %copy-start.7 = (bf16[256,512]{1,0:T(8,128)(2,1)S(1)}, bf16[256,512]{1,0:T(8,128)(2,1)}, u32[]{:S(2)}) copy-start(bf16[256,512]{1,0:T(8,128)(2,1)} %get-tuple-element.55) | copy-start | bytes 786436
  94.1 26.6 %copy-start = (f32[256,2048]{1,0:T(8,128)}, f32[256,2048]{1,0:T(8,128)S(1)}, u32[]{:S(2)}) copy-start(f32[256,2048]{1,0:T(8,128)S(1)} %convolution_bitcast_fusion) | copy-start | bytes 6291460
  94.6 13.4 %collective-permute-start.17 = (bf16[1,256,512]{2,1,0:T(8,128)(2,1)S(1)}, bf16[1,256,512]{2,1,0:T(8,128)(2,1)S(1)}, u32[]{:S(2)}, u32[]{:S(2)}) collective-permute-start(bf16[1,256,512]{2,1,0:T(8,128)(2,1)S(1)} %copy-done.11), channel_id=1, source_target_pairs={{0,32},{1,9},{2,34},{3,11},{4,36},{5,13},{6,38},{7,15},{8,40},{9,1... | collective-permute-start | bytes 786440 | tf_op jit(solution)/shard_map/ppermute | solution.py:46
  96.2 12.6 %collective-permute-start.24 = (bf16[2,256,512]{2,1,0:T(8,128)(2,1)S(1)}, bf16[2,256,512]{2,1,0:T(8,128)(2,1)S(1)}, u32[]{:S(2)}, u32[]{:S(2)}) collective-permute-start(bf16[2,256,512]{2,1,0:T(8,128)(2,1)S(1)} %copy-done.2), channel_id=1, source_target_pairs={{0,64},{1,17},{2,66},{3,19},{4,68},{5,21},{6,70},{7,23},{8,72},{9,... | collective-permute-start | bytes 1572872 | tf_op jit(solution)/shard_map/ppermute | solution.py:46
  97.8 15.9 %collective-permute-start.23 = (bf16[2,256,512]{2,1,0:T(8,128)(2,1)S(1)}, bf16[2,256,512]{2,1,0:T(8,128)(2,1)S(1)}, u32[]{:S(2)}, u32[]{:S(2)}) collective-permute-start(bf16[2,256,512]{2,1,0:T(8,128)(2,1)S(1)} %copy-done.2), channel_id=1, source_target_pairs={{0,32},{1,9},{2,34},{3,11},{4,36},{5,13},{6,38},{7,15},{8,40},{9,1... | collective-permute-start | bytes 1572872 | tf_op jit(solution)/shard_map/ppermute | solution.py:46
  99.4 14.8 %collective-permute-start.25 = (bf16[2,256,512]{2,1,0:T(8,128)(2,1)S(1)}, bf16[2,256,512]{2,1,0:T(8,128)(2,1)S(1)}, u32[]{:S(2)}, u32[]{:S(2)}) collective-permute-start(bf16[2,256,512]{2,1,0:T(8,128)(2,1)S(1)} %copy-done.2), channel_id=1, source_target_pairs={{0,96},{1,25},{2,98},{3,27},{4,100},{5,29},{6,102},{7,31},{8,104},... | collective-permute-start | bytes 1572872 | tf_op jit(solution)/shard_map/ppermute | solution.py:46
  115.9 9.3 %collective-permute-start.26 = (bf16[3,128,512]{2,1,0:T(8,128)(2,1)}, bf16[3,128,512]{2,1,0:T(8,128)(2,1)}, u32[]{:S(2)}, u32[]{:S(2)}) collective-permute-start(bf16[3,128,512]{2,1,0:T(8,128)(2,1)} %get-tuple-element.64), channel_id=1, source_target_pairs={{0,8},{1,33},{2,10},{3,35},{4,12},{5,37},{6,14},{7,39},{8,16},{9,4... | collective-permute-start | bytes 1179656 | tf_op jit(solution)/shard_map/ppermute | solution.py:46
  117.0 12.7 %collective-permute-start.27 = (bf16[3,128,512]{2,1,0:T(8,128)(2,1)}, bf16[3,128,512]{2,1,0:T(8,128)(2,1)}, u32[]{:S(2)}, u32[]{:S(2)}) collective-permute-start(bf16[3,128,512]{2,1,0:T(8,128)(2,1)} %get-tuple-element.65), channel_id=1, source_target_pairs={{0,16},{1,65},{2,18},{3,67},{4,20},{5,69},{6,22},{7,71},{8,24},{9,... | collective-permute-start | bytes 1179656 | tf_op jit(solution)/shard_map/ppermute | solution.py:46
  119.4 10.9 %collective-permute-start.28 = (bf16[3,128,512]{2,1,0:T(8,128)(2,1)S(1)}, bf16[3,128,512]{2,1,0:T(8,128)(2,1)}, u32[]{:S(2)}, u32[]{:S(2)}) collective-permute-start(bf16[3,128,512]{2,1,0:T(8,128)(2,1)S(1)} %get-tuple-element.66), channel_id=1, source_target_pairs={{0,24},{1,97},{2,26},{3,99},{4,28},{5,101},{6,30},{7,103},{8,0},{9... | collective-permute-start | bytes 1179656 | tf_op jit(solution)/shard_map/ppermute | solution.py:46
  121.7 20.5 %collective-permute-start.16 = (f32[256,1024]{1,0:T(8,128)}, f32[256,1024]{1,0:T(8,128)}, u32[]{:S(2)}, u32[]{:S(2)}) collective-permute-start(f32[256,1024]{1,0:T(8,128)} %constant_dynamic-slice_fusion), channel_id=1, source_target_pairs={{0,1},{1,0},{2,3},{3,2},{4,5},{5,4},{6,7},{7,6},{8,9},{9,8},{10,11... | collective-permute-start | bytes 3145736 | tf_op jit(solution)/shard_map/ppermute | solution.py:50
  130.3 7.8 %copy-start.21 = (f32[4,15,256]{2,1,0:T(8,128)S(1)}, f32[4,15,256]{2,1,0:T(8,128)}, u32[]{:S(2)}) copy-start(f32[4,15,256]{2,1,0:T(8,128)} %get-tuple-element.59) | copy-start | bytes 184324
  131.8 0.9 copy-start.3
  132.7 6.1 %collective-permute-start.29 = (bf16[3,32,512]{2,1,0:T(8,128)(2,1)S(1)}, bf16[3,32,512]{2,1,0:T(8,128)(2,1)S(1)}, u32[]{:S(2)}, u32[]{:S(2)}) collective-permute-start(bf16[3,32,512]{2,1,0:T(8,128)(2,1)S(1)} %get-tuple-element.69), channel_id=1, source_target_pairs={{0,2},{1,3},{2,4},{3,5},{4,6},{5,7},{6,0},{7,1},{8,10},{9,11},{10,... | collective-permute-start | bytes 294920 | tf_op jit(solution)/shard_map/ppermute | solution.py:46
  134.2 6.1 %collective-permute-start.30 = (bf16[3,32,512]{2,1,0:T(8,128)(2,1)S(1)}, bf16[3,32,512]{2,1,0:T(8,128)(2,1)S(1)}, u32[]{:S(2)}, u32[]{:S(2)}) collective-permute-start(bf16[3,32,512]{2,1,0:T(8,128)(2,1)S(1)} %get-tuple-element.71), channel_id=1, source_target_pairs={{0,4},{1,5},{2,6},{3,7},{4,0},{5,1},{6,2},{7,3},{8,12},{9,13},{10,... | collective-permute-start | bytes 294920 | tf_op jit(solution)/shard_map/ppermute | solution.py:46
  135.6 4.9 %collective-permute-start.31 = (bf16[3,32,512]{2,1,0:T(8,128)(2,1)S(1)}, bf16[3,32,512]{2,1,0:T(8,128)(2,1)S(1)}, u32[]{:S(2)}, u32[]{:S(2)}) collective-permute-start(bf16[3,32,512]{2,1,0:T(8,128)(2,1)S(1)} %get-tuple-element.70), channel_id=1, source_target_pairs={{0,6},{1,7},{2,0},{3,1},{4,2},{5,3},{6,4},{7,5},{8,14},{9,15},{10,... | collective-permute-start | bytes 294920 | tf_op jit(solution)/shard_map/ppermute | solution.py:46

commit v3 on v2

v3 whole, which is shorter than its diff:
```python
import functools

import jax
import jax.numpy as jnp
from jax import lax
from jax.experimental import pallas as pl
from jax.experimental.pallas import tpu as pltpu
from jax.sharding import Mesh
from jax.sharding import PartitionSpec as P


DH = 128
SEQ = ("seq_0", "seq_1", "seq_2")
ALL = SEQ + ("head",)
BF = jnp.bfloat16
F32 = jnp.float32
X, Z, Y = 0, 1, 2


def scale_of(level):
    return 1.0 if level == 0 else 2.0 ** (-(level - 1) / 2)


def places():
    return [
        (x, z, y, h) for x in range(4) for z in range(4) for y in range(4) for h in range(2)
    ]


def index_of(place):
    x, z, y, h = place
    return ((x * 4 + z) * 4 + y) * 2 + h


def shifted(value, axes, step, which="all"):
    pairs = []
    for place in places():
        axis = axes[place[3]]
        target = list(place)
        target[axis] = (place[axis] + step) % 4
        if which == "up" and target[axis] < place[axis]:
            continue
        if which == "down" and target[axis] > place[axis]:
            continue
        pairs.append((index_of(place), index_of(target)))
    return lax.ppermute(value, ALL, pairs)


def partner(value):
    return lax.ppermute(value, "head", [(0, 1), (1, 0)])


def dot(a, b, dims):
    return lax.dot_general(a, b, (dims, ((), ())), preferred_element_type=F32)


def flag(condition):
    return jnp.where(condition, 1.0, 0.0).astype(F32)


def turned(array):
    return array.astype(F32).T


def heads():
    return [(h, slice(h * DH, (h + 1) * DH)) for h in range(4)]


def state_kernel(pos, proj, grads, mix, s_out, b0, b1, b2, b3, b5, u3):
    two = flag(pos[X] == 2)
    for h, cols in heads():
        qt = turned(proj[0, :, cols])
        kt = turned(proj[1, :, cols]).astype(BF)
        gg = grads[:, cols]
        s_out[cols, :] = dot(kt, proj[2, :, cols], ((1,), (0,))).astype(BF)

        def grad(j):
            row = mix[h, 9 + j : 10 + j, :] * scale_of(9 + j)
            return dot((qt * row).astype(BF), gg, ((1,), (0,)))

        b0[cols, :] = grad(0).astype(BF)
        b1[cols, :] = grad(1).astype(BF)
        b2[cols, :] = grad(2).astype(BF)
        b3[cols, :] = grad(3).astype(BF)
        g4, g5 = grad(4), grad(5)
        b5[cols, :] = g5.astype(BF)
        u3[cols, :] = (g5 * two + g4 * (1.0 - two)).astype(BF)


def up_terms(p, low, high):
    one = high * flag(p == 3)
    two = high * flag(p >= 2)
    three = low * flag((p == 1) | (p == 3)) + high * flag(p == 2)
    return one, two, three


def middle_kernel(pos, s, gy1, gy2, gy3, r1, r2, r3, b2, b3, p1, p2, p3, held):
    group = s[...].astype(F32) + gy1[...] + gy2[...] + gy3[...]
    held_now = r1[...].astype(F32) + r2[...] + r3[...]
    held[...] = held_now
    terms = up_terms(pos[Z], b2[...].astype(F32), b3[...].astype(F32))
    group = group.astype(BF)
    for out, term in zip((p1, p2, p3), terms):
        out[:512] = group
        out[512:] = (held_now + term).astype(BF)


def late_kernel(pos, p1, rz1, rz2, rz3, held, b0, b1, group, q1, q2, q3, held_out):
    whole = p1[:512].astype(F32) + rz1[:512] + rz2[:512] + rz3[:512]
    group[...] = whole.astype(BF)
    held_now = held[...] + rz1[512:].astype(F32) + rz2[512:] + rz3[512:]
    held_out[...] = held_now
    terms = up_terms(pos[Y], b0[...].astype(F32), b1[...].astype(F32))
    for out, term in zip((q1, q2, q3), terms):
        out[...] = (held_now + term).astype(BF)


def inner_kernel(proj, grads, mix, out_t, query_t, key_out, value_out, level_out, table):
    s_at = lax.broadcasted_iota(jnp.int32, (256, 256), 0)
    t_at = lax.broadcasted_iota(jnp.int32, (256, 256), 1)
    apart = s_at ^ t_at
    level = jnp.zeros((256, 256), jnp.int32)
    for place in range(8):
        level = level + (apart >= (1 << place)).astype(jnp.int32)
    table[...] = jnp.where(s_at <= t_at, level, -1)

    def one_head(h, _):
        cols = pl.ds(pl.multiple_of(h * DH, DH), DH)
        qq, kk, vv, gg = proj[0, :, cols], proj[1, :, cols], proj[2, :, cols], grads[:, cols]
        kt = turned(kk).astype(BF)
        vt = turned(vv).astype(BF)
        scores = dot(kk, qq, ((1,), (1,)))
        mix_grad = dot(vv, gg, ((1,), (1,)))
        levels = table[...]
        weight = jnp.zeros((256, 256), F32)
        product = scores * mix_grad
        for level in range(9):
            here = levels == level
            weight = jnp.where(here, mix[h, level : level + 1, :] * scale_of(level), weight)
            level_out[h, level : level + 1, :] = jnp.sum(
                jnp.where(here, product, 0.0), axis=0, keepdims=True
            ) * scale_of(level)
        mixed = (weight * scores).astype(BF)
        score_grad = (weight * mix_grad).astype(BF)
        out_t[h] = dot(vt, mixed, ((1,), (0,)))
        query_t[h] = dot(kt, score_grad, ((1,), (0,)))
        key_out[:, cols] = dot(score_grad, qq, ((1,), (0,)))
        value_out[:, cols] = dot(mixed, gg, ((1,), (0,)))
        return 0

    lax.fori_loop(0, 4, one_head, 0)


def key_value_kernel(proj, key_in, value_in, held, ry1, ry2, ry3, grads):
    for _, cols in heads():
        state = held[cols, :] + ry1[cols, :].astype(F32) + ry2[cols, :] + ry3[cols, :]
        state = state.astype(BF)
        grads[0, :, cols] = (key_in[:, cols] + dot(proj[2, :, cols], state, ((1,), (1,)))).astype(
            BF
        )
        grads[1, :, cols] = (
            value_in[:, cols] + dot(proj[1, :, cols], state, ((1,), (0,)))
        ).astype(BF)


def query_kernel(
    pos, proj, out_grad, mix, out_t, query_t, level_in, gy1, gy2, gy3, rz1, rz2, rz3, gx1, gx2,
    gx3, attended, grads, level_out,
):
    for h, cols in heads():
        qt = turned(proj[0, :, cols]).astype(BF)
        gt = turned(out_grad[:, cols])

        def pair(p, *parts):
            one, two, three = (a[cols, :].astype(F32) for a in parts)
            low = one * flag((p == 1) | (p == 3))
            high = one * flag(p == 2) + two * flag(p >= 2) + three * flag(p == 3)
            return low.astype(BF), high.astype(BF)

        buckets = (
            pair(pos[Y], gy1, gy2, gy3) + pair(pos[Z], rz1, rz2, rz3) + pair(pos[X], gx1, gx2, gx3)
        )
        total = out_t[h]
        query = query_t[h]
        level_out[h, :9, :] = level_in[h, :9, :]
        for j, bucket in enumerate(buckets):
            row = mix[h, 9 + j : 10 + j, :] * scale_of(9 + j)
            reads = dot(bucket, qt, ((0,), (0,)))
            total = total + reads * row
            level_out[h, 9 + j : 10 + j, :] = jnp.sum(
                reads * gt, axis=0, keepdims=True
            ) * scale_of(9 + j)
            query = query + dot(bucket, (gt * row).astype(BF), ((1,), (0,)))
        attended[:, cols] = total.T.astype(BF)
        grads[0, :, cols] = (query * DH**-0.5).T.astype(BF)


def column_kernel(pos, hidden, other, c0, c1, c2, c3, whole):
    core = pos[3]
    whole[:, pl.ds(pl.multiple_of(core * 1024, 1024), 1024)] = hidden[...]
    whole[:, pl.ds(pl.multiple_of((1 - core) * 1024, 1024), 1024)] = other[...]
    line = jnp.where(core == 0, pos[X], pos[Z])
    for step, out in enumerate((c0, c1, c2, c3)):
        at = lax.rem(line + step, 4)
        for tile in range(4):
            column = jnp.where(core == 0, 512 * at + 128 * tile, 512 * tile + 128 * at)
            out[:, 128 * tile : 128 * (tile + 1)] = whole[:, pl.ds(pl.multiple_of(column, 128), 128)]


def second_kernel(pos, query, key_value, own, o1, o2, o3):
    line = jnp.where(pos[3] == 0, pos[Z], pos[X])
    for step, out in enumerate((own, o1, o2, o3)):
        rows = pl.ds(pl.multiple_of(lax.rem(line + step, 4) * 128, 128), 128)
        out[0] = query[0, rows, :].astype(out.dtype)
        out[1] = key_value[0, rows, :].astype(out.dtype)
        out[2] = key_value[1, rows, :].astype(out.dtype)


def third_kernel(pos, mine, came1, came2, came3, own, o1, o2, o3, total):
    total[...] = mine[...] + came1[...].astype(F32) + came2[...] + came3[...]
    for step, out in enumerate((own, o1, o2, o3)):
        rows = pl.ds(pl.multiple_of(lax.rem(pos[Y] + step, 4) * 32, 32), 32)
        out[...] = total[:, rows, :].astype(out.dtype)


def shape(dims, kind):
    return pltpu.VMEM(dims, kind)


def call(kernel, arrays, outs, pos=None, scratch=()):
    whole = pl.BlockSpec(memory_space=pltpu.VMEM)
    scalars = [] if pos is None else [pl.BlockSpec(memory_space=pltpu.SMEM)]
    run = pl.pallas_call(
        kernel,
        in_specs=scalars + [whole] * len(arrays),
        out_specs=[whole] * len(outs),
        out_shape=outs,
        scratch_shapes=scratch,
        compiler_params=pltpu.CompilerParams(vmem_limit_bytes=8 << 20),
    )
    held = [pltpu.with_memory_space_constraint(a, pltpu.VMEM) for a in arrays]
    return run(*([] if pos is None else [pos]), *held)


def layer(hidden, proj_weights, level_mix, out_grad):
    x, z, y = (lax.axis_index(name) for name in SEQ)
    core = lax.axis_index("head")
    pos = jnp.stack([x, z, y, core]).astype(jnp.int32)
    other = partner(hidden)
    root = jnp.array([DH**-0.5, 1.0, 1.0], F32)[:, None, None]
    near = lax.dynamic_slice_in_dim(proj_weights, 1024 * core, 1024, 0)
    far = lax.dynamic_slice_in_dim(proj_weights, 1024 * (1 - core), 1024, 0)
    near_part = jnp.einsum("td,dme->mte", hidden, near, preferred_element_type=F32)
    far_part = jnp.einsum("td,dme->mte", other, far, preferred_element_type=F32)
    projected = ((near_part + far_part) * root).astype(BF)
    mix = level_mix.transpose(1, 0, 2)

    own_columns, *far_columns = call(
        column_kernel,
        [hidden, other],
        [shape((256, 512), BF)] * 4,
        pos,
        [pltpu.VMEM((256, 2048), BF)],
    )
    hidden_blocks = [own_columns]
    for n, block in zip((1, 2, 3), far_columns):
        hidden_blocks.append(shifted(block, (X, Z), n))

    state_shape = shape((512, DH), BF)
    states, b0, b1, b2, b3, b5, u3 = call(
        state_kernel, [projected, out_grad, mix], [state_shape] * 7, pos
    )

    def line_of(axis):
        return (axis, axis)

    def sent(pieces, axis, which="all"):
        out = []
        for n, piece in zip((1, 2, 3), pieces):
            out.append(shifted(piece, line_of(axis), n, which))
        return out

    gy = sent([states] * 3, Y)
    rx = sent([b5, b5, u3], X, "down")
    out_t, query_t, key_in, value_in, level_in = call(
        inner_kernel,
        [projected, out_grad, mix],
        [shape((4, DH, 256), F32)] * 2
        + [shape((256, 512), F32)] * 2
        + [shape((4, 16, 256), F32)],
        scratch=[pltpu.VMEM((256, 256), jnp.int32)],
    )
    p1, p2, p3, held = call(
        middle_kernel,
        [states, *gy, *rx, b2, b3],
        [shape((1024, DH), BF)] * 3 + [shape((512, DH), F32)],
        pos,
    )
    rz = sent([p1, p2, p3], Z)
    group, q1, q2, q3, held = call(
        late_kernel, [p1, *rz, held, b0, b1], [state_shape] * 4 + [shape((512, DH), F32)], pos
    )
    gx = sent([group] * 3, X, "up")
    ry = sent([q1, q2, q3], Y)
    grads = [None, None]
    (grads[0],) = call(
        key_value_kernel, [projected, key_in, value_in, held, *ry], [shape((2, 256, 512), BF)]
    )
    attended, grads[1], level_grad = call(
        query_kernel,
        [projected, out_grad, mix, out_t, query_t, level_in, *gy, *rz, *gx],
        [shape((256, 512), BF), shape((1, 256, 512), BF), shape((4, 15, 256), F32)],
        pos,
    )
    level_grad = level_grad.transpose(1, 0, 2)

    grad_blocks = [[grads[0]], [grads[1]]]
    for i in (0, 1):
        for n in (1, 2, 3):
            grad_blocks[i].append(shifted(grads[i], (X, Z), n))

    all_grads = jnp.concatenate([grads[1], grads[0]], axis=0)
    theirs = jnp.einsum("mte,dme->td", all_grads, far, preferred_element_type=F32)
    mine = lax.optimization_barrier(
        jnp.einsum("mte,dme->td", all_grads, near, preferred_element_type=F32)
    )
    came = partner(theirs)
    input_grad = (mine + came).astype(BF)

    def products(blocks):
        return functools.reduce(
            jnp.add,
            [
                jnp.einsum("td,mte->mde", h, g, preferred_element_type=F32)
                for h, g in zip(hidden_blocks, blocks)
            ],
        )

    key_value_products = products(grad_blocks[0])
    query_products = products(grad_blocks[1])

    def exchanged(pieces, axes):
        came = []
        for n, piece in zip((1, 2, 3), pieces):
            came.append(shifted(piece, axes, n))
        return came

    own, *pieces = call(
        second_kernel,
        [query_products, key_value_products],
        [shape((3, 128, 512), F32)] + [shape((3, 128, 512), BF)] * 3,
        pos,
    )
    own, *pieces = call(
        third_kernel,
        [own, *exchanged(pieces, (Z, X))],
        [shape((3, 32, 512), F32)] + [shape((3, 32, 512), BF)] * 3,
        pos,
        [pltpu.VMEM((3, 128, 512), F32)],
    )
    came = exchanged(pieces, (Y, Y))
    partial_weights = own + came[0] + came[1] + came[2]
    weight_grad = (partial_weights * 16384**-0.5).transpose(1, 0, 2)
    return (attended, input_grad, weight_grad, level_grad)


def solution(mesh):
    split = Mesh(mesh.devices.reshape(4, 4, 4, 2), ALL)
    return jax.shard_map(
        layer,
        mesh=split,
        in_specs=(P(SEQ, "head"), P(None, None, "head"), P(None, "head", SEQ), P(SEQ, "head")),
        out_specs=(P(SEQ, "head"), P(SEQ, "head"), P(SEQ, None, "head"), P(None, "head", SEQ)),
        check_vma=False,
    )
```

time: 146 us -> 123 us (0.84)
  Pallas kernels: 25 us -> 10.9 us
  other arithmetic: 8.34 us -> 1.74 us
  waiting for transfers between devices: 37.2 us -> 43.7 us
  matrix products: 15.1 us -> 11.5 us
  local copies, waits for them, and re-layouts: 5.67 us -> 2.24 us
  starting transfers between devices: 52.3 us -> 50.8 us
    pallas_call x7 -> x9, Pallas kernels: 25 us -> 10.9 us  [call(): return run(*([] if pos is None else [pos]), *held)]
    ppermute x30, waiting for transfers between devices: 37.2 us -> 43.7 us  [shifted(): return lax.ppermute(value, ALL, pairs)]
    dot_general x1 -> x2, matrix products: 4.84 us -> 2.02 us  [the longest x1 1.01 us: layer(): jnp.einsum('mte,dme->td', all_grads, far, preferred_element_type=F32)]
    unnamed x50 -> x13, local copies, waits for them, and re-layouts: 4.59 us -> 2.24 us
    convert_element_type x1, other arithmetic: 2.47 us -> 0.93 us  [layer(): input_grad = (mine + came).astype(BF)]
    ppermute x30, starting transfers between devices: 52.2 us -> 50.7 us  [shifted(): return lax.ppermute(value, ALL, pairs)]
    add x1 -> x0, other arithmetic: 1.46 us -> none  [reduced(): return rows_of(0) + came[0] + came[1] + came[2]]
  transfers between devices with their start and end apart: 32 -> 32, of which waited for: 11 -> 18; matrix products, arithmetic and copies ran while one was open for 13% -> 9% of each run, Pallas kernels for 11% -> 7%
where the time goes in v3:
time: 123 us; the launch traced here: 122 us
  starting transfers between devices  50.8 us (41%)
  waiting for transfers between devices  43.7 us (36%)
  matrix products  11.5 us (9%)
  Pallas kernels  10.9 us (9%)
  local copies, waits for them, and re-layouts  2.24 us (2%)
  other arithmetic  1.74 us (1%)
    ppermute x30, starting transfers between devices, shifted(): return lax.ppermute(value, ALL, pairs)  50.7 us
    ppermute x30, waiting for transfers between devices, shifted(): return lax.ppermute(value, ALL, pairs)  43.7 us
    pallas_call x9, Pallas kernels, call(): return run(*([] if pos is None else [pos]), *held)  10.9 us
    dot_general x8, matrix products, products(): jnp.einsum('td,mte->mde', h, g, preferred_element_type=F32)  3.4 us
    dot_general x1, matrix products, layer(): far_part = jnp.einsum('td,dme->mte', other, far, preferred_element_type=F32)  3.07 us
    dot_general x1, matrix products, layer(): jnp.einsum('td,dme->mte', hidden, near, preferred_element_type=F32)  3.04 us
  transfers between devices with their start and end apart: 32, of which 18 were waited for; matrix products, arithmetic and copies ran while one was open for 9% of the time, Pallas kernels for 7%

profile of v3, /device:TPU:0, one launch (start us, length us, event | category | flops | bytes accessed | tf_op | source)
XLA Modules:
  0.0 122.0 jit_solution(10519123394478366468)
XLA Ops:
  0.7 0.8 copy.48
  1.7 3.0 %fusion.4 = f32[3,512,256]{1,2,0:T(8,128)S(1)} fusion(bf16[2048,3,512]{2,0,1:T(8,128)(2,1)} %param.6, s32[]{:T(128)S(6)} %select_n.6, bf16[256,1024]{1,0:T(8,128)(2,1)} %hidden.1), kind=kOutput, calls=%fused_computation.4 | convolution fusion | flops 805306368 | bytes 5242884 | tf_op jit(solution)/shard_map/td,dme->mte/dot_general | solution.py:253
  4.8 3.1 %fusion.19.proj = bf16[3,256,512]{2,1,0:T(8,128)(2,1)S(1)} fusion(f32[3,512,256]{1,2,0:T(8,128)S(1)} %fusion.4, bf16[2048,3,512]{2,0,1:T(8,128)(2,1)} %param.6, s32[]{:T(128)S(6)} %select_n.7, f32[3]{0:T(128)S(1)} %copy-done.2, bf16[256,1024]{1,0:T(8,128)(2,1)S(1)} %collective-permute-done.other), kind=kOutput, calls=%fused_computation.16 | convolution fusion | flops 806486016 | bytes 6029328 | tf_op jit(solution)/shard_map/td,dme->mte/dot_general | solution.py:254
  7.9 1.3 %shard_map.85 = (bf16[512,128]{1,0:T(8,128)(2,1)S(1)}, bf16[512,128]{1,0:T(8,128)(2,1)S(1)}, bf16[512,128]{1,0:T(8,128)(2,1)S(1)}, bf16[512,128]{1,0:T(8,128)(2,...) custom-call(s32[4]{0:T(128)S(1)} %pad_add_fusion.pos, ...), custom_call_target="tpu_custom_call" | custom-call | tf_op jit(solution)/shard_map/pallas_call | solution.py:242
  9.1 1.4 %collective-permute-start.6 = (bf16[512,128]{1,0:T(8,128)(2,1)S(1)}, bf16[512,128]{1,0:T(8,128)(2,1)S(1)}, u32[]{:S(2)}, u32[]{:S(2)}) collective-permute-start(bf16[512,128]{1,0:T(8,128)(2,1)S(1)} %get-tuple-element.45), channel_id=1, source_target_pairs={{32,0},{33,1},{34,2},{35,3},{36,4},{37,5},{38,6},{39,7},{40,8},{41... | collective-permute-start | bytes 393224 | tf_op jit(solution)/shard_map/ppermute | solution.py:46
  10.6 1.3 %collective-permute-start.5 = (bf16[512,128]{1,0:T(8,128)(2,1)S(1)}, bf16[512,128]{1,0:T(8,128)(2,1)S(1)}, u32[]{:S(2)}, u32[]{:S(2)}) collective-permute-start(bf16[512,128]{1,0:T(8,128)(2,1)S(1)} %get-tuple-element.44), channel_id=1, source_target_pairs={{64,0},{65,1},{66,2},{67,3},{68,4},{69,5},{70,6},{71,7},{72,8},{73... | collective-permute-start | bytes 393224 | tf_op jit(solution)/shard_map/ppermute | solution.py:46
  11.9 1.3 %collective-permute-start.4 = (bf16[512,128]{1,0:T(8,128)(2,1)S(1)}, bf16[512,128]{1,0:T(8,128)(2,1)S(1)}, u32[]{:S(2)}, u32[]{:S(2)}) collective-permute-start(bf16[512,128]{1,0:T(8,128)(2,1)S(1)} %get-tuple-element.44), channel_id=1, source_target_pairs={{96,0},{97,1},{98,2},{99,3},{100,4},{101,5},{102,6},{103,7},{104,8... | collective-permute-start | bytes 393224 | tf_op jit(solution)/shard_map/ppermute | solution.py:46
  13.2 3.2 %collective-permute-start.3 = (bf16[512,128]{1,0:T(8,128)(2,1)S(1)}, bf16[512,128]{1,0:T(8,128)(2,1)S(1)}, u32[]{:S(2)}, u32[]{:S(2)}) collective-permute-start(bf16[512,128]{1,0:T(8,128)(2,1)S(1)} %get-tuple-element.43.s), channel_id=1, source_target_pairs={{0,6},{1,7},{2,0},{3,1},{4,2},{5,3},{6,4},{7,5},{8,14},{9,15},{10,... | collective-permute-start | bytes 393224 | tf_op jit(solution)/shard_map/ppermute | solution.py:46
  16.4 0.6 collective-permute-start.2
  17.0 1.7 %collective-permute-start.1 = (bf16[512,128]{1,0:T(8,128)(2,1)S(1)}, bf16[512,128]{1,0:T(8,128)(2,1)S(1)}, u32[]{:S(2)}, u32[]{:S(2)}) collective-permute-start(bf16[512,128]{1,0:T(8,128)(2,1)S(1)} %get-tuple-element.43.s), channel_id=1, source_target_pairs={{0,2},{1,3},{2,4},{3,5},{4,6},{5,7},{6,0},{7,1},{8,10},{9,11},{10,... | collective-permute-start | bytes 393224 | tf_op jit(solution)/shard_map/ppermute | solution.py:46
  18.7 1.3 %collective-permute-done.5.r2 = bf16[512,128]{1,0:T(8,128)(2,1)S(1)} collective-permute-done((bf16[512,128]{1,0:T(8,128)(2,1)S(1)}, bf16[512,128]{1,0:T(8,128)(2,1)S(1)}, u32[]{:S(2)}, u32[]{:S(2)}) %collective-permute-start.5) | collective-permute-done | bytes 131104 | tf_op jit(solution)/shard_map/ppermute | solution.py:46
  20.0 2.8 %collective-permute-done.4.r1 = bf16[512,128]{1,0:T(8,128)(2,1)S(1)} collective-permute-done((bf16[512,128]{1,0:T(8,128)(2,1)S(1)}, bf16[512,128]{1,0:T(8,128)(2,1)S(1)}, u32[]{:S(2)}, u32[]{:S(2)}) %collective-permute-start.4) | collective-permute-done | bytes 131104 | tf_op jit(solution)/shard_map/ppermute | solution.py:46
  22.8 1.5 %collective-permute-done.2.gy2 = bf16[512,128]{1,0:T(8,128)(2,1)S(1)} collective-permute-done((bf16[512,128]{1,0:T(8,128)(2,1)S(1)}, bf16[512,128]{1,0:T(8,128)(2,1)S(1)}, u32[]{:S(2)}, u32[]{:S(2)}) %collective-permute-start.2) | collective-permute-done | bytes 131104 | tf_op jit(solution)/shard_map/ppermute | solution.py:46
  24.3 2.0 %collective-permute-done.1.gy1 = bf16[512,128]{1,0:T(8,128)(2,1)S(1)} collective-permute-done((bf16[512,128]{1,0:T(8,128)(2,1)S(1)}, bf16[512,128]{1,0:T(8,128)(2,1)S(1)}, u32[]{:S(2)}, u32[]{:S(2)}) %collective-permute-start.1) | collective-permute-done | bytes 131104 | tf_op jit(solution)/shard_map/ppermute | solution.py:46
  26.3 0.8 shard_map.86
  27.0 3.9 %collective-permute-start.8 = (bf16[1024,128]{1,0:T(8,128)(2,1)S(1)}, bf16[1024,128]{1,0:T(8,128)(2,1)S(1)}, u32[]{:S(2)}, u32[]{:S(2)}) collective-permute-start(bf16[1024,128]{1,0:T(8,128)(2,1)S(1)} %get-tuple-element.49), channel_id=1, source_target_pairs={{0,16},{1,17},{2,18},{3,19},{4,20},{5,21},{6,22},{7,23},{8,24},{9,... | collective-permute-start | bytes 786440 | tf_op jit(solution)/shard_map/ppermute | solution.py:46
  31.0 0.7 collective-permute-start.9
  31.7 1.3 %collective-permute-start.7 = (bf16[1024,128]{1,0:T(8,128)(2,1)S(1)}, bf16[1024,128]{1,0:T(8,128)(2,1)S(1)}, u32[]{:S(2)}, u32[]{:S(2)}) collective-permute-start(bf16[1024,128]{1,0:T(8,128)(2,1)S(1)} %get-tuple-element.48.p1), channel_id=1, source_target_pairs={{0,8},{1,9},{2,10},{3,11},{4,12},{5,13},{6,14},{7,15},{8,16},{9,17... | collective-permute-start | bytes 786440 | tf_op jit(solution)/shard_map/ppermute | solution.py:46
  33.0 5.2 %collective-permute-done.8.rz2 = bf16[1024,128]{1,0:T(8,128)(2,1)S(1)} collective-permute-done((bf16[1024,128]{1,0:T(8,128)(2,1)S(1)}, bf16[1024,128]{1,0:T(8,128)(2,1)S(1)}, u32[]{:S(2)}, u32[]{:S(2)}) %collective-permute-start.8) | collective-permute-done | bytes 262176 | tf_op jit(solution)/shard_map/ppermute | solution.py:46
  38.2 5.7 %collective-permute-done.9.rz3 = bf16[1024,128]{1,0:T(8,128)(2,1)S(1)} collective-permute-done((bf16[1024,128]{1,0:T(8,128)(2,1)S(1)}, bf16[1024,128]{1,0:T(8,128)(2,1)S(1)}, u32[]{:S(2)}, u32[]{:S(2)}) %collective-permute-start.9) | collective-permute-done | bytes 262176 | tf_op jit(solution)/shard_map/ppermute | solution.py:46
  43.9 0.8 shard_map.87
  44.6 7.3 %collective-permute-start.12 = (bf16[512,128]{1,0:T(8,128)(2,1)S(1)}, bf16[512,128]{1,0:T(8,128)(2,1)S(1)}, u32[]{:S(2)}, u32[]{:S(2)}) collective-permute-start(bf16[512,128]{1,0:T(8,128)(2,1)S(1)} %get-tuple-element.54), channel_id=1, source_target_pairs={{0,96},{1,97},{2,98},{3,99},{4,100},{5,101},{6,102},{7,103},{8,104... | collective-permute-start | bytes 393224 | tf_op jit(solution)/shard_map/ppermute | solution.py:46
  51.9 1.3 %collective-permute-start.11 = (bf16[512,128]{1,0:T(8,128)(2,1)S(1)}, bf16[512,128]{1,0:T(8,128)(2,1)S(1)}, u32[]{:S(2)}, u32[]{:S(2)}) collective-permute-start(bf16[512,128]{1,0:T(8,128)(2,1)S(1)} %get-tuple-element.54), channel_id=1, source_target_pairs={{0,64},{1,65},{2,66},{3,67},{4,68},{5,69},{6,70},{7,71},{8,72},{9,... | collective-permute-start | bytes 393224 | tf_op jit(solution)/shard_map/ppermute | solution.py:46
  53.3 2.8 %collective-permute-start.10 = (bf16[512,128]{1,0:T(8,128)(2,1)S(1)}, bf16[512,128]{1,0:T(8,128)(2,1)S(1)}, u32[]{:S(2)}, u32[]{:S(2)}) collective-permute-start(bf16[512,128]{1,0:T(8,128)(2,1)S(1)} %get-tuple-element.54), channel_id=1, source_target_pairs={{0,32},{1,33},{2,34},{3,35},{4,36},{5,37},{6,38},{7,39},{8,40},{9,... | collective-permute-start | bytes 393224 | tf_op jit(solution)/shard_map/ppermute | solution.py:46
  56.1 0.9 collective-permute-start.14
  57.1 2.2 %collective-permute-start.15 = (bf16[512,128]{1,0:T(8,128)(2,1)S(1)}, bf16[512,128]{1,0:T(8,128)(2,1)S(1)}, u32[]{:S(2)}, u32[]{:S(2)}) collective-permute-start(bf16[512,128]{1,0:T(8,128)(2,1)S(1)} %get-tuple-element.62), channel_id=1, source_target_pairs={{0,6},{1,7},{2,0},{3,1},{4,2},{5,3},{6,4},{7,5},{8,14},{9,15},{10,... | collective-permute-start | bytes 393224 | tf_op jit(solution)/shard_map/ppermute | solution.py:46
  59.3 3.3 %shard_map.84 = (f32[4,128,256]{2,1,0:T(8,128)S(1)}, f32[4,128,256]{2,1,0:T(8,128)S(1)}, f32[256,512]{1,0:T(8,128)S(1)}, f32[256,512]{1,0:T(8,128)S(1)}, f32[4,16,256]{2,1,0:T(8,128)S(1)}) custom-call(bf16[3,256,512]{2,1,0:T(8,128)(2,1)S(1)} %fusion.19.proj, bf16[256,512]{1,0:T(8,128)(2,1)S(1)} %copy-done, f32[4,15,256]{2,1,0:T(8,128)S(1)} %bitcast.63), custom_call_target="tpu_custom_call" | custom-call | tf_op jit(solution)/shard_map/pallas_call | solution.py:242
  62.6 0.9 shard_map.90
  63.7 2.9 %collective-permute-start.20 = (bf16[256,512]{1,0:T(8,128)(2,1)S(1)}, bf16[256,512]{1,0:T(8,128)(2,1)S(1)}, u32[]{:S(2)}, u32[]{:S(2)}) collective-permute-start(bf16[256,512]{1,0:T(8,128)(2,1)S(1)} %get-tuple-element.65), channel_id=1, source_target_pairs={{0,64},{1,17},{2,66},{3,19},{4,68},{5,21},{6,70},{7,23},{8,72},{9,... | collective-permute-start | bytes 786440 | tf_op jit(solution)/shard_map/ppermute | solution.py:46
  66.5 2.0 %shard_map.88 = (bf16[256,512]{1,0:T(8,128)(2,1)S(1)}, bf16[1,256,512]{2,1,0:T(8,128)(2,1)S(1)}, f32[4,15,256]{2,1,0:T(8,128)S(1)}) custom-call(s32[4]{0:T(128)S(1)} %pad_add_fusion.pos, bf16[3,256,512]{2,1,0:T(8,128)(2,1)S(1)} %fusion.19.proj, bf16[256,512]{1,0:T(8,128)(2,1)S(1)} %copy-done, f32[4,15,256]{2,1,0:T(8,128)S(1)} %bitcast.64, ...), custom_call_target="tpu_custom_call" | custom-call | tf_op jit(solution)/shard_map/pallas_call | solution.py:242
  68.6 0.4 collective-permute-start.22
  69.0 1.0 collective-permute-start.21
  69.9 1.1 collective-permute-start.17
  71.3 1.0 fusion.13
  72.4 0.5 fusion.32
  72.8 1.2 collective-permute-done.18
  74.0 1.8 %collective-permute-start.19 = (bf16[1,256,512]{2,1,0:T(8,128)(2,1)S(1)}, bf16[1,256,512]{2,1,0:T(8,128)(2,1)S(1)}, u32[]{:S(2)}, u32[]{:S(2)}) collective-permute-start(bf16[1,256,512]{2,1,0:T(8,128)(2,1)S(1)} %get-tuple-element.56), channel_id=1, source_target_pairs={{0,64},{1,17},{2,66},{3,19},{4,68},{5,21},{6,70},{7,23},{8,72},{9,... | collective-permute-start | bytes 786440 | tf_op jit(solution)/shard_map/ppermute | solution.py:46
  75.9 1.7 %collective-permute-done.17 = bf16[1,256,512]{2,1,0:T(8,128)(2,1)S(1)} collective-permute-done((bf16[1,256,512]{2,1,0:T(8,128)(2,1)S(1)}, bf16[1,256,512]{2,1,0:T(8,128)(2,1)S(1)}, u32[]{:S(2)}, u32[]{:S(2)}) %collective-permute-start.17) | collective-permute-done | bytes 262176 | tf_op jit(solution)/shard_map/ppermute | solution.py:46
  77.5 1.3 %collective-permute-start.25 = (bf16[2,256,512]{2,1,0:T(8,128)(2,1)S(1)}, bf16[2,256,512]{2,1,0:T(8,128)(2,1)S(1)}, u32[]{:S(2)}, u32[]{:S(2)}) collective-permute-start(bf16[2,256,512]{2,1,0:T(8,128)(2,1)S(1)} %shard_map.89), channel_id=1, source_target_pairs={{0,96},{1,25},{2,98},{3,27},{4,100},{5,29},{6,102},{7,31},{8,104},... | collective-permute-start | bytes 1572872 | tf_op jit(solution)/shard_map/ppermute | solution.py:46
  79.2 0.7 collective-permute-start.24
  79.9 2.0 %collective-permute-done.19 = bf16[1,256,512]{2,1,0:T(8,128)(2,1)S(1)} collective-permute-done((bf16[1,256,512]{2,1,0:T(8,128)(2,1)S(1)}, bf16[1,256,512]{2,1,0:T(8,128)(2,1)S(1)}, u32[]{:S(2)}, u32[]{:S(2)}) %collective-permute-start.19) | collective-permute-done | bytes 262176 | tf_op jit(solution)/shard_map/ppermute | solution.py:46
  81.9 0.7 collective-permute-start.23
  83.4 0.3 fusion.18.query
  83.7 6.3 %collective-permute-done.24 = bf16[2,256,512]{2,1,0:T(8,128)(2,1)S(1)} collective-permute-done((bf16[2,256,512]{2,1,0:T(8,128)(2,1)S(1)}, bf16[2,256,512]{2,1,0:T(8,128)(2,1)S(1)}, u32[]{:S(2)}, u32[]{:S(2)}) %collective-permute-start.24) | collective-permute-done | bytes 524320 | tf_op jit(solution)/shard_map/ppermute | solution.py:46
  90.1 0.5 fusion.28
  90.5 5.0 %collective-permute-done.23 = bf16[2,256,512]{2,1,0:T(8,128)(2,1)S(1)} collective-permute-done((bf16[2,256,512]{2,1,0:T(8,128)(2,1)S(1)}, bf16[2,256,512]{2,1,0:T(8,128)(2,1)S(1)}, u32[]{:S(2)}, u32[]{:S(2)}) %collective-permute-start.23) | collective-permute-done | bytes 524320 | tf_op jit(solution)/shard_map/ppermute | solution.py:46
  95.6 0.5 fusion.30
  96.1 0.6 add_bitcast_fusion.key_value
  96.7 0.7 shard_map.91
  97.4 1.1 collective-permute-start.26
  98.5 3.1 %collective-permute-start.27 = (bf16[3,128,512]{2,1,0:T(8,128)(2,1)S(1)}, bf16[3,128,512]{2,1,0:T(8,128)(2,1)S(1)}, u32[]{:S(2)}, u32[]{:S(2)}) collective-permute-start(bf16[3,128,512]{2,1,0:T(8,128)(2,1)S(1)} %get-tuple-element.69), channel_id=1, source_target_pairs={{0,16},{1,65},{2,18},{3,67},{4,20},{5,69},{6,22},{7,71},{8,24},{9,... | collective-permute-start | bytes 1179656 | tf_op jit(solution)/shard_map/ppermute | solution.py:46
  101.6 1.0 collective-permute-start.28
  102.6 0.7 copy.49
  103.3 0.7 copy.28
  104.0 2.5 %collective-permute-done.26.came1 = bf16[3,128,512]{2,1,0:T(8,128)(2,1)S(1)} collective-permute-done((bf16[3,128,512]{2,1,0:T(8,128)(2,1)S(1)}, bf16[3,128,512]{2,1,0:T(8,128)(2,1)S(1)}, u32[]{:S(2)}, u32[]{:S(2)}) %collective-permute-start.26) | collective-permute-done | bytes 393248 | tf_op jit(solution)/shard_map/ppermute | solution.py:46
  106.5 5.0 %collective-permute-done.27.came2 = bf16[3,128,512]{2,1,0:T(8,128)(2,1)S(1)} collective-permute-done((bf16[3,128,512]{2,1,0:T(8,128)(2,1)S(1)}, bf16[3,128,512]{2,1,0:T(8,128)(2,1)S(1)}, u32[]{:S(2)}, u32[]{:S(2)}) %collective-permute-start.27) | collective-permute-done | bytes 393248 | tf_op jit(solution)/shard_map/ppermute | solution.py:46
  111.6 0.9 shard_map.92
  112.5 1.4 %collective-permute-start.29 = (bf16[3,32,512]{2,1,0:T(8,128)(2,1)S(1)}, bf16[3,32,512]{2,1,0:T(8,128)(2,1)S(1)}, u32[]{:S(2)}, u32[]{:S(2)}) collective-permute-start(bf16[3,32,512]{2,1,0:T(8,128)(2,1)S(1)} %get-tuple-element.72), channel_id=1, source_target_pairs={{0,2},{1,3},{2,4},{3,5},{4,6},{5,7},{6,0},{7,1},{8,10},{9,11},{10,... | collective-permute-start | bytes 294920 | tf_op jit(solution)/shard_map/ppermute | solution.py:46
  113.9 1.7 %collective-permute-start.30 = (bf16[3,32,512]{2,1,0:T(8,128)(2,1)S(1)}, bf16[3,32,512]{2,1,0:T(8,128)(2,1)S(1)}, u32[]{:S(2)}, u32[]{:S(2)}) collective-permute-start(bf16[3,32,512]{2,1,0:T(8,128)(2,1)S(1)} %get-tuple-element.73), channel_id=1, source_target_pairs={{0,4},{1,5},{2,6},{3,7},{4,0},{5,1},{6,2},{7,3},{8,12},{9,13},{10,... | collective-permute-start | bytes 294920 | tf_op jit(solution)/shard_map/ppermute | solution.py:46
  115.6 2.5 %collective-permute-start.31 = (bf16[3,32,512]{2,1,0:T(8,128)(2,1)S(1)}, bf16[3,32,512]{2,1,0:T(8,128)(2,1)S(1)}, u32[]{:S(2)}, u32[]{:S(2)}) collective-permute-start(bf16[3,32,512]{2,1,0:T(8,128)(2,1)S(1)} %get-tuple-element.74), channel_id=1, source_target_pairs={{0,6},{1,7},{2,0},{3,1},{4,2},{5,3},{6,4},{7,5},{8,14},{9,15},{10,... | collective-permute-start | bytes 294920 | tf_op jit(solution)/shard_map/ppermute | solution.py:46
  118.1 1.0 fusion.10
  119.1 0.9 collective-permute-done.30
  120.3 0.7 multiply_bitcast_fusion
  121.1 0.9 add_convert_fusion
  (38 shorter events, 2.3 us)
Async XLA Ops:
  0.6 4.1 %collective-permute-start = (bf16[256,1024]{1,0:T(8,128)(2,1)}, bf16[256,1024]{1,0:T(8,128)(2,1)S(1)}, u32[]{:S(2)}, u32[]{:S(2)}) collective-permute-start(bf16[256,1024]{1,0:T(8,128)(2,1)} %hidden.1), channel_id=1, source_target_pairs={{0,1},{1,0},{2,3},{3,2},{4,5},{5,4},{6,7},{7,6},{8,9},{9,8},{10,11... | collective-permute-start | bytes 1572872 | tf_op jit(solution)/shard_map/ppermute | solution.py:50
  1.7 3.1 %copy-start.2 = (f32[3]{0:T(128)S(1)}, f32[3]{0:T(128)}, u32[]{:S(2)}) copy-start(f32[3]{0:T(128)} %constant.27.clone) | copy-start | bytes 40
  4.7 3.1 %copy-start = (bf16[256,512]{1,0:T(8,128)(2,1)S(1)}, bf16[256,512]{1,0:T(8,128)(2,1)}, u32[]{:S(2)}) copy-start(bf16[256,512]{1,0:T(8,128)(2,1)} %out_grad.1) | copy-start | bytes 786436
  4.7 66.6 %slice-start = ((s8[6291456]{0:T(1024)(128)(4,1)}), s8[4194304]{0:T(1024)(128)(4,1)S(1)}, s32[]{:S(2)}) async-start(s8[6291456]{0:T(1024)(128)(4,1)} %bitcast.66), calls=%async_computation | async-start | bytes 8388608
  9.1 53.5 %copy-start.1 = (bf16[256,1024]{1,0:T(8,128)(2,1)S(1)}, bf16[256,1024]{1,0:T(8,128)(2,1)}, u32[]{:S(2)}) copy-start(bf16[256,1024]{1,0:T(8,128)(2,1)} %hidden.1) | copy-start | bytes 1572868
  9.1 7.9 %collective-permute-start.6 = (bf16[512,128]{1,0:T(8,128)(2,1)S(1)}, bf16[512,128]{1,0:T(8,128)(2,1)S(1)}, u32[]{:S(2)}, u32[]{:S(2)}) collective-permute-start(bf16[512,128]{1,0:T(8,128)(2,1)S(1)} %get-tuple-element.45), channel_id=1, source_target_pairs={{32,0},{33,1},{34,2},{35,3},{36,4},{37,5},{38,6},{39,7},{40,8},{41... | collective-permute-start | bytes 393224 | tf_op jit(solution)/shard_map/ppermute | solution.py:46
  10.6 9.4 %collective-permute-start.5 = (bf16[512,128]{1,0:T(8,128)(2,1)S(1)}, bf16[512,128]{1,0:T(8,128)(2,1)S(1)}, u32[]{:S(2)}, u32[]{:S(2)}) collective-permute-start(bf16[512,128]{1,0:T(8,128)(2,1)S(1)} %get-tuple-element.44), channel_id=1, source_target_pairs={{64,0},{65,1},{66,2},{67,3},{68,4},{69,5},{70,6},{71,7},{72,8},{73... | collective-permute-start | bytes 393224 | tf_op jit(solution)/shard_map/ppermute | solution.py:46
  11.9 10.9 %collective-permute-start.4 = (bf16[512,128]{1,0:T(8,128)(2,1)S(1)}, bf16[512,128]{1,0:T(8,128)(2,1)S(1)}, u32[]{:S(2)}, u32[]{:S(2)}) collective-permute-start(bf16[512,128]{1,0:T(8,128)(2,1)S(1)} %get-tuple-element.44), channel_id=1, source_target_pairs={{96,0},{97,1},{98,2},{99,3},{100,4},{101,5},{102,6},{103,7},{104,8... | collective-permute-start | bytes 393224 | tf_op jit(solution)/shard_map/ppermute | solution.py:46
  13.2 9.6 %collective-permute-start.3 = (bf16[512,128]{1,0:T(8,128)(2,1)S(1)}, bf16[512,128]{1,0:T(8,128)(2,1)S(1)}, u32[]{:S(2)}, u32[]{:S(2)}) collective-permute-start(bf16[512,128]{1,0:T(8,128)(2,1)S(1)} %get-tuple-element.43.s), channel_id=1, source_target_pairs={{0,6},{1,7},{2,0},{3,1},{4,2},{5,3},{6,4},{7,5},{8,14},{9,15},{10,... | collective-permute-start | bytes 393224 | tf_op jit(solution)/shard_map/ppermute | solution.py:46
  16.4 7.9 %collective-permute-start.2 = (bf16[512,128]{1,0:T(8,128)(2,1)S(1)}, bf16[512,128]{1,0:T(8,128)(2,1)S(1)}, u32[]{:S(2)}, u32[]{:S(2)}) collective-permute-start(bf16[512,128]{1,0:T(8,128)(2,1)S(1)} %get-tuple-element.43.s), channel_id=1, source_target_pairs={{0,4},{1,5},{2,6},{3,7},{4,0},{5,1},{6,2},{7,3},{8,12},{9,13},{10,... | collective-permute-start | bytes 393224 | tf_op jit(solution)/shard_map/ppermute | solution.py:46
  17.0 9.2 %collective-permute-start.1 = (bf16[512,128]{1,0:T(8,128)(2,1)S(1)}, bf16[512,128]{1,0:T(8,128)(2,1)S(1)}, u32[]{:S(2)}, u32[]{:S(2)}) collective-permute-start(bf16[512,128]{1,0:T(8,128)(2,1)S(1)} %get-tuple-element.43.s), channel_id=1, source_target_pairs={{0,2},{1,3},{2,4},{3,5},{4,6},{5,7},{6,0},{7,1},{8,10},{9,11},{10,... | collective-permute-start | bytes 393224 | tf_op jit(solution)/shard_map/ppermute | solution.py:46
  27.0 11.1 %collective-permute-start.8 = (bf16[1024,128]{1,0:T(8,128)(2,1)S(1)}, bf16[1024,128]{1,0:T(8,128)(2,1)S(1)}, u32[]{:S(2)}, u32[]{:S(2)}) collective-permute-start(bf16[1024,128]{1,0:T(8,128)(2,1)S(1)} %get-tuple-element.49), channel_id=1, source_target_pairs={{0,16},{1,17},{2,18},{3,19},{4,20},{5,21},{6,22},{7,23},{8,24},{9,... | collective-permute-start | bytes 786440 | tf_op jit(solution)/shard_map/ppermute | solution.py:46
  31.0 12.9 %collective-permute-start.9 = (bf16[1024,128]{1,0:T(8,128)(2,1)S(1)}, bf16[1024,128]{1,0:T(8,128)(2,1)S(1)}, u32[]{:S(2)}, u32[]{:S(2)}) collective-permute-start(bf16[1024,128]{1,0:T(8,128)(2,1)S(1)} %get-tuple-element.50), channel_id=1, source_target_pairs={{0,24},{1,25},{2,26},{3,27},{4,28},{5,29},{6,30},{7,31},{8,0},{9,1... | collective-permute-start | bytes 786440 | tf_op jit(solution)/shard_map/ppermute | solution.py:46
  31.7 12.2 %collective-permute-start.7 = (bf16[1024,128]{1,0:T(8,128)(2,1)S(1)}, bf16[1024,128]{1,0:T(8,128)(2,1)S(1)}, u32[]{:S(2)}, u32[]{:S(2)}) collective-permute-start(bf16[1024,128]{1,0:T(8,128)(2,1)S(1)} %get-tuple-element.48.p1), channel_id=1, source_target_pairs={{0,8},{1,9},{2,10},{3,11},{4,12},{5,13},{6,14},{7,15},{8,16},{9,17... | collective-permute-start | bytes 786440 | tf_op jit(solution)/shard_map/ppermute | solution.py:46
  43.9 27.4 %slice-start.1 = ((s8[6291456]{0:T(1024)(128)(4,1)}), s8[2097152]{0:T(1024)(128)(4,1)S(1)}, s32[]{:S(2)}) async-start(s8[6291456]{0:T(1024)(128)(4,1)} %bitcast.66), calls=%async_computation.1 | async-start | bytes 4194304
  44.6 12.5 %collective-permute-start.12 = (bf16[512,128]{1,0:T(8,128)(2,1)S(1)}, bf16[512,128]{1,0:T(8,128)(2,1)S(1)}, u32[]{:S(2)}, u32[]{:S(2)}) collective-permute-start(bf16[512,128]{1,0:T(8,128)(2,1)S(1)} %get-tuple-element.54), channel_id=1, source_target_pairs={{0,96},{1,97},{2,98},{3,99},{4,100},{5,101},{6,102},{7,103},{8,104... | collective-permute-start | bytes 393224 | tf_op jit(solution)/shard_map/ppermute | solution.py:46
  51.9 11.6 %collective-permute-start.11 = (bf16[512,128]{1,0:T(8,128)(2,1)S(1)}, bf16[512,128]{1,0:T(8,128)(2,1)S(1)}, u32[]{:S(2)}, u32[]{:S(2)}) collective-permute-start(bf16[512,128]{1,0:T(8,128)(2,1)S(1)} %get-tuple-element.54), channel_id=1, source_target_pairs={{0,64},{1,65},{2,66},{3,67},{4,68},{5,69},{6,70},{7,71},{8,72},{9,... | collective-permute-start | bytes 393224 | tf_op jit(solution)/shard_map/ppermute | solution.py:46
  53.3 10.4 %collective-permute-start.10 = (bf16[512,128]{1,0:T(8,128)(2,1)S(1)}, bf16[512,128]{1,0:T(8,128)(2,1)S(1)}, u32[]{:S(2)}, u32[]{:S(2)}) collective-permute-start(bf16[512,128]{1,0:T(8,128)(2,1)S(1)} %get-tuple-element.54), channel_id=1, source_target_pairs={{0,32},{1,33},{2,34},{3,35},{4,36},{5,37},{6,38},{7,39},{8,40},{9,... | collective-permute-start | bytes 393224 | tf_op jit(solution)/shard_map/ppermute | solution.py:46
  56.0 12.5 %collective-permute-start.13 = (bf16[512,128]{1,0:T(8,128)(2,1)S(1)}, bf16[512,128]{1,0:T(8,128)(2,1)S(1)}, u32[]{:S(2)}, u32[]{:S(2)}) collective-permute-start(bf16[512,128]{1,0:T(8,128)(2,1)S(1)} %get-tuple-element.60), channel_id=1, source_target_pairs={{0,2},{1,3},{2,4},{3,5},{4,6},{5,7},{6,0},{7,1},{8,10},{9,11},{10,... | collective-permute-start | bytes 393224 | tf_op jit(solution)/shard_map/ppermute | solution.py:46
  56.1 12.9 %collective-permute-start.14 = (bf16[512,128]{1,0:T(8,128)(2,1)S(1)}, bf16[512,128]{1,0:T(8,128)(2,1)S(1)}, u32[]{:S(2)}, u32[]{:S(2)}) collective-permute-start(bf16[512,128]{1,0:T(8,128)(2,1)S(1)} %get-tuple-element.61), channel_id=1, source_target_pairs={{0,4},{1,5},{2,6},{3,7},{4,0},{5,1},{6,2},{7,3},{8,12},{9,13},{10,... | collective-permute-start | bytes 393224 | tf_op jit(solution)/shard_map/ppermute | solution.py:46
  57.1 12.8 %collective-permute-start.15 = (bf16[512,128]{1,0:T(8,128)(2,1)S(1)}, bf16[512,128]{1,0:T(8,128)(2,1)S(1)}, u32[]{:S(2)}, u32[]{:S(2)}) collective-permute-start(bf16[512,128]{1,0:T(8,128)(2,1)S(1)} %get-tuple-element.62), channel_id=1, source_target_pairs={{0,6},{1,7},{2,0},{3,1},{4,2},{5,3},{6,4},{7,5},{8,14},{9,15},{10,... | collective-permute-start | bytes 393224 | tf_op jit(solution)/shard_map/ppermute | solution.py:46
  63.6 10.5 %collective-permute-start.18 = (bf16[256,512]{1,0:T(8,128)(2,1)S(1)}, bf16[256,512]{1,0:T(8,128)(2,1)S(1)}, u32[]{:S(2)}, u32[]{:S(2)}) collective-permute-start(bf16[256,512]{1,0:T(8,128)(2,1)S(1)} %get-tuple-element.64), channel_id=1, source_target_pairs={{0,32},{1,9},{2,34},{3,11},{4,36},{5,13},{6,38},{7,15},{8,40},{9,1... | collective-permute-start | bytes 786440 | tf_op jit(solution)/shard_map/ppermute | solution.py:46
  63.7 15.5 %collective-permute-start.20 = (bf16[256,512]{1,0:T(8,128)(2,1)S(1)}, bf16[256,512]{1,0:T(8,128)(2,1)S(1)}, u32[]{:S(2)}, u32[]{:S(2)}) collective-permute-start(bf16[256,512]{1,0:T(8,128)(2,1)S(1)} %get-tuple-element.65), channel_id=1, source_target_pairs={{0,64},{1,17},{2,66},{3,19},{4,68},{5,21},{6,70},{7,23},{8,72},{9,... | collective-permute-start | bytes 786440 | tf_op jit(solution)/shard_map/ppermute | solution.py:46
  68.6 14.4 %collective-permute-start.22 = (bf16[256,512]{1,0:T(8,128)(2,1)S(1)}, bf16[256,512]{1,0:T(8,128)(2,1)S(1)}, u32[]{:S(2)}, u32[]{:S(2)}) collective-permute-start(bf16[256,512]{1,0:T(8,128)(2,1)S(1)} %get-tuple-element.66), channel_id=1, source_target_pairs={{0,96},{1,25},{2,98},{3,27},{4,100},{5,29},{6,102},{7,31},{8,104},... | collective-permute-start | bytes 786440 | tf_op jit(solution)/shard_map/ppermute | solution.py:46
  69.0 14.1 %collective-permute-start.21 = (bf16[1,256,512]{2,1,0:T(8,128)(2,1)S(1)}, bf16[1,256,512]{2,1,0:T(8,128)(2,1)S(1)}, u32[]{:S(2)}, u32[]{:S(2)}) collective-permute-start(bf16[1,256,512]{2,1,0:T(8,128)(2,1)S(1)} %get-tuple-element.56), channel_id=1, source_target_pairs={{0,96},{1,25},{2,98},{3,27},{4,100},{5,29},{6,102},{7,31},{8,104},... | collective-permute-start | bytes 786440 | tf_op jit(solution)/shard_map/ppermute | solution.py:46
  69.9 7.6 %collective-permute-start.17 = (bf16[1,256,512]{2,1,0:T(8,128)(2,1)S(1)}, bf16[1,256,512]{2,1,0:T(8,128)(2,1)S(1)}, u32[]{:S(2)}, u32[]{:S(2)}) collective-permute-start(bf16[1,256,512]{2,1,0:T(8,128)(2,1)S(1)} %get-tuple-element.56), channel_id=1, source_target_pairs={{0,32},{1,9},{2,34},{3,11},{4,36},{5,13},{6,38},{7,15},{8,40},{9,1... | collective-permute-start | bytes 786440 | tf_op jit(solution)/shard_map/ppermute | solution.py:46
  74.0 7.9 %collective-permute-start.19 = (bf16[1,256,512]{2,1,0:T(8,128)(2,1)S(1)}, bf16[1,256,512]{2,1,0:T(8,128)(2,1)S(1)}, u32[]{:S(2)}, u32[]{:S(2)}) collective-permute-start(bf16[1,256,512]{2,1,0:T(8,128)(2,1)S(1)} %get-tuple-element.56), channel_id=1, source_target_pairs={{0,64},{1,17},{2,66},{3,19},{4,68},{5,21},{6,70},{7,23},{8,72},{9,... | collective-permute-start | bytes 786440 | tf_op jit(solution)/shard_map/ppermute | solution.py:46
  77.5 18.5 %collective-permute-start.25 = (bf16[2,256,512]{2,1,0:T(8,128)(2,1)S(1)}, bf16[2,256,512]{2,1,0:T(8,128)(2,1)S(1)}, u32[]{:S(2)}, u32[]{:S(2)}) collective-permute-start(bf16[2,256,512]{2,1,0:T(8,128)(2,1)S(1)} %shard_map.89), channel_id=1, source_target_pairs={{0,96},{1,25},{2,98},{3,27},{4,100},{5,29},{6,102},{7,31},{8,104},... | collective-permute-start | bytes 1572872 | tf_op jit(solution)/shard_map/ppermute | solution.py:46
  79.2 10.9 %collective-permute-start.24 = (bf16[2,256,512]{2,1,0:T(8,128)(2,1)S(1)}, bf16[2,256,512]{2,1,0:T(8,128)(2,1)S(1)}, u32[]{:S(2)}, u32[]{:S(2)}) collective-permute-start(bf16[2,256,512]{2,1,0:T(8,128)(2,1)S(1)} %shard_map.89), channel_id=1, source_target_pairs={{0,64},{1,17},{2,66},{3,19},{4,68},{5,21},{6,70},{7,23},{8,72},{9,... | collective-permute-start | bytes 1572872 | tf_op jit(solution)/shard_map/ppermute | solution.py:46
  81.9 13.7 %collective-permute-start.23 = (bf16[2,256,512]{2,1,0:T(8,128)(2,1)S(1)}, bf16[2,256,512]{2,1,0:T(8,128)(2,1)S(1)}, u32[]{:S(2)}, u32[]{:S(2)}) collective-permute-start(bf16[2,256,512]{2,1,0:T(8,128)(2,1)S(1)} %shard_map.89), channel_id=1, source_target_pairs={{0,32},{1,9},{2,34},{3,11},{4,36},{5,13},{6,38},{7,15},{8,40},{9,1... | collective-permute-start | bytes 1572872 | tf_op jit(solution)/shard_map/ppermute | solution.py:46
  82.9 38.1 %collective-permute-start.16 = (f32[256,1024]{1,0:T(8,128)S(1)}, f32[256,1024]{1,0:T(8,128)S(1)}, u32[]{:S(2)}, u32[]{:S(2)}) collective-permute-start(f32[256,1024]{1,0:T(8,128)S(1)} %fusion.13), channel_id=1, source_target_pairs={{0,1},{1,0},{2,3},{3,2},{4,5},{5,4},{6,7},{7,6},{8,9},{9,8},{10,11... | collective-permute-start | bytes 3145736 | tf_op jit(solution)/shard_map/ppermute | solution.py:50
  97.4 9.1 %collective-permute-start.26 = (bf16[3,128,512]{2,1,0:T(8,128)(2,1)S(1)}, bf16[3,128,512]{2,1,0:T(8,128)(2,1)S(1)}, u32[]{:S(2)}, u32[]{:S(2)}) collective-permute-start(bf16[3,128,512]{2,1,0:T(8,128)(2,1)S(1)} %get-tuple-element.68), channel_id=1, source_target_pairs={{0,8},{1,33},{2,10},{3,35},{4,12},{5,37},{6,14},{7,39},{8,16},{9,4... | collective-permute-start | bytes 1179656 | tf_op jit(solution)/shard_map/ppermute | solution.py:46
  98.5 13.0 %collective-permute-start.27 = (bf16[3,128,512]{2,1,0:T(8,128)(2,1)S(1)}, bf16[3,128,512]{2,1,0:T(8,128)(2,1)S(1)}, u32[]{:S(2)}, u32[]{:S(2)}) collective-permute-start(bf16[3,128,512]{2,1,0:T(8,128)(2,1)S(1)} %get-tuple-element.69), channel_id=1, source_target_pairs={{0,16},{1,65},{2,18},{3,67},{4,20},{5,69},{6,22},{7,71},{8,24},{9,... | collective-permute-start | bytes 1179656 | tf_op jit(solution)/shard_map/ppermute | solution.py:46
  101.6 10.0 %collective-permute-start.28 = (bf16[3,128,512]{2,1,0:T(8,128)(2,1)S(1)}, bf16[3,128,512]{2,1,0:T(8,128)(2,1)S(1)}, u32[]{:S(2)}, u32[]{:S(2)}) collective-permute-start(bf16[3,128,512]{2,1,0:T(8,128)(2,1)S(1)} %get-tuple-element.70), channel_id=1, source_target_pairs={{0,24},{1,97},{2,26},{3,99},{4,28},{5,101},{6,30},{7,103},{8,0},{9... | collective-permute-start | bytes 1179656 | tf_op jit(solution)/shard_map/ppermute | solution.py:46
  112.5 6.6 %collective-permute-start.29 = (bf16[3,32,512]{2,1,0:T(8,128)(2,1)S(1)}, bf16[3,32,512]{2,1,0:T(8,128)(2,1)S(1)}, u32[]{:S(2)}, u32[]{:S(2)}) collective-permute-start(bf16[3,32,512]{2,1,0:T(8,128)(2,1)S(1)} %get-tuple-element.72), channel_id=1, source_target_pairs={{0,2},{1,3},{2,4},{3,5},{4,6},{5,7},{6,0},{7,1},{8,10},{9,11},{10,... | collective-permute-start | bytes 294920 | tf_op jit(solution)/shard_map/ppermute | solution.py:46
  113.9 6.1 %collective-permute-start.30 = (bf16[3,32,512]{2,1,0:T(8,128)(2,1)S(1)}, bf16[3,32,512]{2,1,0:T(8,128)(2,1)S(1)}, u32[]{:S(2)}, u32[]{:S(2)}) collective-permute-start(bf16[3,32,512]{2,1,0:T(8,128)(2,1)S(1)} %get-tuple-element.73), channel_id=1, source_target_pairs={{0,4},{1,5},{2,6},{3,7},{4,0},{5,1},{6,2},{7,3},{8,12},{9,13},{10,... | collective-permute-start | bytes 294920 | tf_op jit(solution)/shard_map/ppermute | solution.py:46
  115.6 4.8 %collective-permute-start.31 = (bf16[3,32,512]{2,1,0:T(8,128)(2,1)S(1)}, bf16[3,32,512]{2,1,0:T(8,128)(2,1)S(1)}, u32[]{:S(2)}, u32[]{:S(2)}) collective-permute-start(bf16[3,32,512]{2,1,0:T(8,128)(2,1)S(1)} %get-tuple-element.74), channel_id=1, source_target_pairs={{0,6},{1,7},{2,0},{3,1},{4,2},{5,3},{6,4},{7,5},{8,14},{9,15},{10,... | collective-permute-start | bytes 294920 | tf_op jit(solution)/shard_map/ppermute | solution.py:46

commit v4 on v3

--- a/solution.py
+++ b/solution.py
@@ -94,21 +94,20 @@
     return one, two, three
 
 
-def middle_kernel(pos, s, gy1, gy2, gy3, r1, r2, r3, b2, b3, p1, p2, p3, held):
-    group = s[...].astype(F32) + gy1[...] + gy2[...] + gy3[...]
+def gather_kernel(mine, a1, a2, a3, group):
+    group[...] = (mine[...].astype(F32) + a1[...] + a2[...] + a3[...]).astype(BF)
+
+
+def upper_kernel(pos, r1, r2, r3, b2, b3, p1, p2, p3, held):
     held_now = r1[...].astype(F32) + r2[...] + r3[...]
     held[...] = held_now
     terms = up_terms(pos[Z], b2[...].astype(F32), b3[...].astype(F32))
-    group = group.astype(BF)
     for out, term in zip((p1, p2, p3), terms):
-        out[:512] = group
-        out[512:] = (held_now + term).astype(BF)
-
-
-def late_kernel(pos, p1, rz1, rz2, rz3, held, b0, b1, group, q1, q2, q3, held_out):
-    whole = p1[:512].astype(F32) + rz1[:512] + rz2[:512] + rz3[:512]
-    group[...] = whole.astype(BF)
-    held_now = held[...] + rz1[512:].astype(F32) + rz2[512:] + rz3[512:]
+        out[...] = (held_now + term).astype(BF)
+
+
+def lower_kernel(pos, r1, r2, r3, held, b0, b1, q1, q2, q3, held_out):
+    held_now = held[...] + r1[...].astype(F32) + r2[...] + r3[...]
     held_out[...] = held_now
     terms = up_terms(pos[Y], b0[...].astype(F32), b1[...].astype(F32))
     for out, term in zip((q1, q2, q3), terms):
@@ -197,29 +196,45 @@
 
 def column_kernel(pos, hidden, other, c0, c1, c2, c3, whole):
     core = pos[3]
-    whole[:, pl.ds(pl.multiple_of(core * 1024, 1024), 1024)] = hidden[...]
-    whole[:, pl.ds(pl.multiple_of((1 - core) * 1024, 1024), 1024)] = other[...]
-    line = jnp.where(core == 0, pos[X], pos[Z])
-    for step, out in enumerate((c0, c1, c2, c3)):
-        at = lax.rem(line + step, 4)
-        for tile in range(4):
-            column = jnp.where(core == 0, 512 * at + 128 * tile, 512 * tile + 128 * at)
-            out[:, 128 * tile : 128 * (tile + 1)] = whole[:, pl.ds(pl.multiple_of(column, 128), 128)]
-
-
-def second_kernel(pos, query, key_value, own, o1, o2, o3):
+    outs = (c0, c1, c2, c3)
+
+    @pl.when(core == 0)
+    def _():
+        whole[:, :1024] = hidden[...]
+        whole[:, 1024:] = other[...]
+        for step, out in enumerate(outs):
+            column = lax.rem(pos[X] + step, 4) * 512
+            out[...] = whole[:, pl.ds(pl.multiple_of(column, 512), 512)]
+
+    @pl.when(core == 1)
+    def _():
+        source = lax.broadcasted_iota(jnp.int32, (512, 128), 0)
+        target = lax.broadcasted_iota(jnp.int32, (512, 128), 1)
+        start = (target // 32) * 128 + target % 32
+        for step, out in enumerate(outs):
+            run = lax.rem(pos[Y] + step, 4) * 32
+            pick = jnp.where(source == start + run, 1.0, 0.0).astype(BF)
+            for tile in range(4):
+                half = other if tile < 2 else hidden
+                piece = half[:, 512 * (tile % 2) : 512 * (tile % 2) + 512]
+                out[:, 128 * tile : 128 * tile + 128] = dot(piece, pick, ((1,), (0,))).astype(BF)
+
+
+def second_kernel(pos, product, own, o1, o2, o3):
     line = jnp.where(pos[3] == 0, pos[Z], pos[X])
     for step, out in enumerate((own, o1, o2, o3)):
         rows = pl.ds(pl.multiple_of(lax.rem(line + step, 4) * 128, 128), 128)
-        out[0] = query[0, rows, :].astype(out.dtype)
-        out[1] = key_value[0, rows, :].astype(out.dtype)
-        out[2] = key_value[1, rows, :].astype(out.dtype)
-
-
-def third_kernel(pos, mine, came1, came2, came3, own, o1, o2, o3, total):
-    total[...] = mine[...] + came1[...].astype(F32) + came2[...] + came3[...]
+        out[...] = product[:, rows, :].astype(out.dtype)
+
+
+def third_kernel(
+    pos, mine0, mine1, a1, a2, a3, b1, b2, b3, own, o1, o2, o3, total
+):
+    total[0:1] = mine0[...] + a1[...].astype(F32) + a2[...] + a3[...]
+    total[1:3] = mine1[...] + b1[...].astype(F32) + b2[...] + b3[...]
+    line = jnp.where(pos[3] == 0, pos[Y], pos[Z])
     for step, out in enumerate((own, o1, o2, o3)):
-        rows = pl.ds(pl.multiple_of(lax.rem(pos[Y] + step, 4) * 32, 32), 32)
+        rows = pl.ds(pl.multiple_of(lax.rem(line + step, 4) * 32, 32), 32)
         out[...] = total[:, rows, :].astype(out.dtype)
 
 
@@ -264,7 +279,7 @@
     )
     hidden_blocks = [own_columns]
     for n, block in zip((1, 2, 3), far_columns):
-        hidden_blocks.append(shifted(block, (X, Z), n))
+        hidden_blocks.append(shifted(block, (X, Y), n))
 
     state_shape = shape((512, DH), BF)
     states, b0, b1, b2, b3, b5, u3 = call(
@@ -291,17 +306,17 @@
         scratch=[pltpu.VMEM((256, 256), jnp.int32)],
     )
     p1, p2, p3, held = call(
-        middle_kernel,
-        [states, *gy, *rx, b2, b3],
-        [shape((1024, DH), BF)] * 3 + [shape((512, DH), F32)],
-        pos,
-    )
-    rz = sent([p1, p2, p3], Z)
-    group, q1, q2, q3, held = call(
-        late_kernel, [p1, *rz, held, b0, b1], [state_shape] * 4 + [shape((512, DH), F32)], pos
-    )
+        upper_kernel, [*rx, b2, b3], [state_shape] * 3 + [shape((512, DH), F32)], pos
+    )
+    uz = sent([p1, p2, p3], Z)
+    (group,) = call(gather_kernel, [states, *gy], [state_shape])
+    rz = sent([group] * 3, Z)
+    q1, q2, q3, held = call(
+        lower_kernel, [*uz, held, b0, b1], [state_shape] * 3 + [shape((512, DH), F32)], pos
+    )
+    ry = sent([q1, q2, q3], Y)
+    (group,) = call(gather_kernel, [group, *rz], [state_shape])
     gx = sent([group] * 3, X, "up")
-    ry = sent([q1, q2, q3], Y)
     grads = [None, None]
     (grads[0],) = call(
         key_value_kernel, [projected, key_in, value_in, held, *ry], [shape((2, 256, 512), BF)]
@@ -317,7 +332,7 @@
     grad_blocks = [[grads[0]], [grads[1]]]
     for i in (0, 1):
         for n in (1, 2, 3):
-            grad_blocks[i].append(shifted(grads[i], (X, Z), n))
+            grad_blocks[i].append(shifted(grads[i], (X, Y), n))
 
     all_grads = jnp.concatenate([grads[1], grads[0]], axis=0)
     theirs = jnp.einsum("mte,dme->td", all_grads, far, preferred_element_type=F32)
@@ -345,20 +360,26 @@
             came.append(shifted(piece, axes, n))
         return came
 
-    own, *pieces = call(
-        second_kernel,
-        [query_products, key_value_products],
-        [shape((3, 128, 512), F32)] + [shape((3, 128, 512), BF)] * 3,
-        pos,
-    )
+    def second(product):
+        size = product.shape[0]
+        own, *pieces = call(
+            second_kernel,
+            [product],
+            [shape((size, 128, 512), F32)] + [shape((size, 128, 512), BF)] * 3,
+            pos,
+        )
+        return own, exchanged(pieces, (Z, X))
+
+    own1, came1 = second(key_value_products)
+    own0, came0 = second(query_products)
     own, *pieces = call(
         third_kernel,
-        [own, *exchanged(pieces, (Z, X))],
+        [own0, own1, *came0, *came1],
         [shape((3, 32, 512), F32)] + [shape((3, 32, 512), BF)] * 3,
         pos,
         [pltpu.VMEM((3, 128, 512), F32)],
     )
-    came = exchanged(pieces, (Y, Y))
+    came = exchanged(pieces, (Y, Z))
     partial_weights = own + came[0] + came[1] + came[2]
     weight_grad = (partial_weights * 16384**-0.5).transpose(1, 0, 2)
     return (attended, input_grad, weight_grad, level_grad)

time: 123 us -> 121 us (0.984)
  waiting for transfers between devices: 43.7 us -> 37.3 us
  starting transfers between devices: 50.8 us -> 55.4 us
    ppermute x30 -> x36, waiting for transfers between devices: 43.7 us -> 37.3 us  [shifted(): return lax.ppermute(value, ALL, pairs)]
    ppermute x30 -> x36, starting transfers between devices: 50.7 us -> 55.3 us  [shifted(): return lax.ppermute(value, ALL, pairs)]
    pallas_call x9 -> x12, Pallas kernels: 10.9 us -> 11.1 us  [call(): return run(*([] if pos is None else [pos]), *held)]
  transfers between devices with their start and end apart: 32 -> 38, of which waited for: 18 -> 11; matrix products, arithmetic and copies ran while one was open for 9% -> 10% of each run, Pallas kernels for 7% -> 8%
where the time goes in v4:
time: 121 us; the launch traced here: 120 us
  starting transfers between devices  55.4 us (46%)
  waiting for transfers between devices  37.3 us (31%)
  matrix products  11.5 us (10%)
  Pallas kernels  11.1 us (9%)
  local copies, waits for them, and re-layouts  2.24 us (2%)
  other arithmetic  1.73 us (1%)
    ppermute x36, starting transfers between devices, shifted(): return lax.ppermute(value, ALL, pairs)  55.3 us
    ppermute x36, waiting for transfers between devices, shifted(): return lax.ppermute(value, ALL, pairs)  37.3 us
    pallas_call x12, Pallas kernels, call(): return run(*([] if pos is None else [pos]), *held)  11.1 us
    dot_general x8, matrix products, products(): jnp.einsum('td,mte->mde', h, g, preferred_element_type=F32)  3.42 us
    dot_general x1, matrix products, layer(): far_part = jnp.einsum('td,dme->mte', other, far, preferred_element_type=F32)  3.05 us
    dot_general x1, matrix products, layer(): jnp.einsum('td,dme->mte', hidden, near, preferred_element_type=F32)  3.04 us
  transfers between devices with their start and end apart: 38, of which 11 were waited for; matrix products, arithmetic and copies ran while one was open for 10% of the time, Pallas kernels for 8%

profile of v4, /device:TPU:0, one launch (start us, length us, event | category | flops | bytes accessed | tf_op | source)
XLA Modules:
  0.0 120.4 jit_solution(12915985526997818856)
XLA Ops:
  0.7 0.8 copy.48
  1.7 3.0 %fusion.4 = f32[3,512,256]{1,2,0:T(8,128)S(1)} fusion(bf16[2048,3,512]{2,0,1:T(8,128)(2,1)} %param.6, s32[]{:T(128)S(6)} %select_n.6, bf16[256,1024]{1,0:T(8,128)(2,1)} %hidden.1), kind=kOutput, calls=%fused_computation.4 | convolution fusion | flops 805306368 | bytes 5242884 | tf_op jit(solution)/shard_map/td,dme->mte/dot_general | solution.py:268
  4.8 3.0 %fusion.19.proj = bf16[3,256,512]{2,1,0:T(8,128)(2,1)S(1)} fusion(f32[3,512,256]{1,2,0:T(8,128)S(1)} %fusion.4, bf16[2048,3,512]{2,0,1:T(8,128)(2,1)} %param.6, s32[]{:T(128)S(6)} %select_n.7, f32[3]{0:T(128)S(1)} %copy-done.2, bf16[256,1024]{1,0:T(8,128)(2,1)S(1)} %collective-permute-done.other), kind=kOutput, calls=%fused_computation.16 | convolution fusion | flops 806486016 | bytes 6029328 | tf_op jit(solution)/shard_map/td,dme->mte/dot_general | solution.py:269
  7.8 1.2 %shard_map.85 = (bf16[512,128]{1,0:T(8,128)(2,1)S(1)}, bf16[512,128]{1,0:T(8,128)(2,1)S(1)}, bf16[512,128]{1,0:T(8,128)(2,1)S(1)}, bf16[512,128]{1,0:T(8,128)(2,...) custom-call(s32[4]{0:T(128)S(1)} %pad_add_fusion.pos, ...), custom_call_target="tpu_custom_call" | custom-call | tf_op jit(solution)/shard_map/pallas_call | solution.py:257
  9.1 3.2 %collective-permute-start.3 = (bf16[512,128]{1,0:T(8,128)(2,1)S(1)}, bf16[512,128]{1,0:T(8,128)(2,1)S(1)}, u32[]{:S(2)}, u32[]{:S(2)}) collective-permute-start(bf16[512,128]{1,0:T(8,128)(2,1)S(1)} %get-tuple-element.46.mine), channel_id=1, source_target_pairs={{0,6},{1,7},{2,0},{3,1},{4,2},{5,3},{6,4},{7,5},{8,14},{9,15},{10,... | collective-permute-start | bytes 393224 | tf_op jit(solution)/shard_map/ppermute | solution.py:46
  12.3 0.6 collective-permute-start.2
  12.9 1.0 collective-permute-start.1
  13.9 1.3 %collective-permute-start.12 = (bf16[512,128]{1,0:T(8,128)(2,1)S(1)}, bf16[512,128]{1,0:T(8,128)(2,1)S(1)}, u32[]{:S(2)}, u32[]{:S(2)}) collective-permute-start(bf16[512,128]{1,0:T(8,128)(2,1)S(1)} %get-tuple-element.52), channel_id=1, source_target_pairs={{32,0},{33,1},{34,2},{35,3},{36,4},{37,5},{38,6},{39,7},{40,8},{41... | collective-permute-start | bytes 393224 | tf_op jit(solution)/shard_map/ppermute | solution.py:46
  15.2 1.3 %collective-permute-start.11 = (bf16[512,128]{1,0:T(8,128)(2,1)S(1)}, bf16[512,128]{1,0:T(8,128)(2,1)S(1)}, u32[]{:S(2)}, u32[]{:S(2)}) collective-permute-start(bf16[512,128]{1,0:T(8,128)(2,1)S(1)} %get-tuple-element.51), channel_id=1, source_target_pairs={{64,0},{65,1},{66,2},{67,3},{68,4},{69,5},{70,6},{71,7},{72,8},{73... | collective-permute-start | bytes 393224 | tf_op jit(solution)/shard_map/ppermute | solution.py:46
  16.5 2.0 %collective-permute-done.3.a3.gy3 = bf16[512,128]{1,0:T(8,128)(2,1)S(1)} collective-permute-done((bf16[512,128]{1,0:T(8,128)(2,1)S(1)}, bf16[512,128]{1,0:T(8,128)(2,1)S(1)}, u32[]{:S(2)}, u32[]{:S(2)}) %collective-permute-start.3) | collective-permute-done | bytes 131104 | tf_op jit(solution)/shard_map/ppermute | solution.py:46
  18.5 1.3 %collective-permute-start.10 = (bf16[512,128]{1,0:T(8,128)(2,1)S(1)}, bf16[512,128]{1,0:T(8,128)(2,1)S(1)}, u32[]{:S(2)}, u32[]{:S(2)}) collective-permute-start(bf16[512,128]{1,0:T(8,128)(2,1)S(1)} %get-tuple-element.51), channel_id=1, source_target_pairs={{96,0},{97,1},{98,2},{99,3},{100,4},{101,5},{102,6},{103,7},{104,8... | collective-permute-start | bytes 393224 | tf_op jit(solution)/shard_map/ppermute | solution.py:46
  19.8 0.4 collective-permute-done.2.a2.gy2
  20.2 2.0 %collective-permute-done.1.a1.gy1 = bf16[512,128]{1,0:T(8,128)(2,1)S(1)} collective-permute-done((bf16[512,128]{1,0:T(8,128)(2,1)S(1)}, bf16[512,128]{1,0:T(8,128)(2,1)S(1)}, u32[]{:S(2)}, u32[]{:S(2)}) %collective-permute-start.1) | collective-permute-done | bytes 131104 | tf_op jit(solution)/shard_map/ppermute | solution.py:46
  22.3 4.1 %collective-permute-start.6 = (bf16[512,128]{1,0:T(8,128)(2,1)S(1)}, bf16[512,128]{1,0:T(8,128)(2,1)S(1)}, u32[]{:S(2)}, u32[]{:S(2)}) collective-permute-start(bf16[512,128]{1,0:T(8,128)(2,1)S(1)} %shard_map.86.mine), channel_id=1, source_target_pairs={{0,24},{1,25},{2,26},{3,27},{4,28},{5,29},{6,30},{7,31},{8,0},{9,1... | collective-permute-start | bytes 393224 | tf_op jit(solution)/shard_map/ppermute | solution.py:46
  26.4 1.3 %collective-permute-start.4 = (bf16[512,128]{1,0:T(8,128)(2,1)S(1)}, bf16[512,128]{1,0:T(8,128)(2,1)S(1)}, u32[]{:S(2)}, u32[]{:S(2)}) collective-permute-start(bf16[512,128]{1,0:T(8,128)(2,1)S(1)} %shard_map.86.mine), channel_id=1, source_target_pairs={{0,8},{1,9},{2,10},{3,11},{4,12},{5,13},{6,14},{7,15},{8,16},{9,17... | collective-permute-start | bytes 393224 | tf_op jit(solution)/shard_map/ppermute | solution.py:46
  27.7 0.7 shard_map.89
  28.4 2.3 %collective-permute-start.13 = (bf16[512,128]{1,0:T(8,128)(2,1)S(1)}, bf16[512,128]{1,0:T(8,128)(2,1)S(1)}, u32[]{:S(2)}, u32[]{:S(2)}) collective-permute-start(bf16[512,128]{1,0:T(8,128)(2,1)S(1)} %get-tuple-element.55), channel_id=1, source_target_pairs={{0,8},{1,9},{2,10},{3,11},{4,12},{5,13},{6,14},{7,15},{8,16},{9,17... | collective-permute-start | bytes 393224 | tf_op jit(solution)/shard_map/ppermute | solution.py:46
  30.6 2.3 %collective-permute-start.14 = (bf16[512,128]{1,0:T(8,128)(2,1)S(1)}, bf16[512,128]{1,0:T(8,128)(2,1)S(1)}, u32[]{:S(2)}, u32[]{:S(2)}) collective-permute-start(bf16[512,128]{1,0:T(8,128)(2,1)S(1)} %get-tuple-element.56), channel_id=1, source_target_pairs={{0,16},{1,17},{2,18},{3,19},{4,20},{5,21},{6,22},{7,23},{8,24},{9,... | collective-permute-start | bytes 393224 | tf_op jit(solution)/shard_map/ppermute | solution.py:46
  32.9 2.1 %collective-permute-done.6.a3.rz3 = bf16[512,128]{1,0:T(8,128)(2,1)S(1)} collective-permute-done((bf16[512,128]{1,0:T(8,128)(2,1)S(1)}, bf16[512,128]{1,0:T(8,128)(2,1)S(1)}, u32[]{:S(2)}, u32[]{:S(2)}) %collective-permute-start.6) | collective-permute-done | bytes 131104 | tf_op jit(solution)/shard_map/ppermute | solution.py:46
  35.0 3.7 %collective-permute-start.15 = (bf16[512,128]{1,0:T(8,128)(2,1)S(1)}, bf16[512,128]{1,0:T(8,128)(2,1)S(1)}, u32[]{:S(2)}, u32[]{:S(2)}) collective-permute-start(bf16[512,128]{1,0:T(8,128)(2,1)S(1)} %get-tuple-element.57), channel_id=1, source_target_pairs={{0,24},{1,25},{2,26},{3,27},{4,28},{5,29},{6,30},{7,31},{8,0},{9,1... | collective-permute-start | bytes 393224 | tf_op jit(solution)/shard_map/ppermute | solution.py:46
  38.7 4.7 %collective-permute-start.9 = (bf16[512,128]{1,0:T(8,128)(2,1)S(1)}, bf16[512,128]{1,0:T(8,128)(2,1)S(1)}, u32[]{:S(2)}, u32[]{:S(2)}) collective-permute-start(bf16[512,128]{1,0:T(8,128)(2,1)S(1)} %shard_map.87), channel_id=1, source_target_pairs={{0,96},{1,97},{2,98},{3,99},{4,100},{5,101},{6,102},{7,103},{8,104... | collective-permute-start | bytes 393224 | tf_op jit(solution)/shard_map/ppermute | solution.py:46
  43.4 1.3 %collective-permute-start.8 = (bf16[512,128]{1,0:T(8,128)(2,1)S(1)}, bf16[512,128]{1,0:T(8,128)(2,1)S(1)}, u32[]{:S(2)}, u32[]{:S(2)}) collective-permute-start(bf16[512,128]{1,0:T(8,128)(2,1)S(1)} %shard_map.87), channel_id=1, source_target_pairs={{0,64},{1,65},{2,66},{3,67},{4,68},{5,69},{6,70},{7,71},{8,72},{9,... | collective-permute-start | bytes 393224 | tf_op jit(solution)/shard_map/ppermute | solution.py:46
  44.7 2.8 %collective-permute-start.7 = (bf16[512,128]{1,0:T(8,128)(2,1)S(1)}, bf16[512,128]{1,0:T(8,128)(2,1)S(1)}, u32[]{:S(2)}, u32[]{:S(2)}) collective-permute-start(bf16[512,128]{1,0:T(8,128)(2,1)S(1)} %shard_map.87), channel_id=1, source_target_pairs={{0,32},{1,33},{2,34},{3,35},{4,36},{5,37},{6,38},{7,39},{8,40},{9,... | collective-permute-start | bytes 393224 | tf_op jit(solution)/shard_map/ppermute | solution.py:46
  47.5 0.7 shard_map.90
  48.3 1.8 %collective-permute-start.17 = (bf16[512,128]{1,0:T(8,128)(2,1)S(1)}, bf16[512,128]{1,0:T(8,128)(2,1)S(1)}, u32[]{:S(2)}, u32[]{:S(2)}) collective-permute-start(bf16[512,128]{1,0:T(8,128)(2,1)S(1)} %get-tuple-element.63), channel_id=1, source_target_pairs={{0,4},{1,5},{2,6},{3,7},{4,0},{5,1},{6,2},{7,3},{8,12},{9,13},{10,... | collective-permute-start | bytes 393224 | tf_op jit(solution)/shard_map/ppermute | solution.py:46
  50.1 1.5 %collective-permute-start.18 = (bf16[512,128]{1,0:T(8,128)(2,1)S(1)}, bf16[512,128]{1,0:T(8,128)(2,1)S(1)}, u32[]{:S(2)}, u32[]{:S(2)}) collective-permute-start(bf16[512,128]{1,0:T(8,128)(2,1)S(1)} %get-tuple-element.64), channel_id=1, source_target_pairs={{0,6},{1,7},{2,0},{3,1},{4,2},{5,3},{6,4},{7,5},{8,14},{9,15},{10,... | collective-permute-start | bytes 393224 | tf_op jit(solution)/shard_map/ppermute | solution.py:46
  51.6 3.3 %shard_map.84 = (f32[4,128,256]{2,1,0:T(8,128)S(1)}, f32[4,128,256]{2,1,0:T(8,128)S(1)}, f32[256,512]{1,0:T(8,128)S(1)}, f32[256,512]{1,0:T(8,128)S(1)}, f32[4,16,256]{2,1,0:T(8,128)S(1)}) custom-call(bf16[3,256,512]{2,1,0:T(8,128)(2,1)S(1)} %fusion.19.proj, bf16[256,512]{1,0:T(8,128)(2,1)S(1)} %copy-done, f32[4,15,256]{2,1,0:T(8,128)S(1)} %bitcast.63), custom_call_target="tpu_custom_call" | custom-call | tf_op jit(solution)/shard_map/pallas_call | solution.py:257
  54.8 0.7 shard_map.92
  55.6 2.5 %collective-permute-start.23 = (bf16[256,512]{1,0:T(8,128)(2,1)S(1)}, bf16[256,512]{1,0:T(8,128)(2,1)S(1)}, u32[]{:S(2)}, u32[]{:S(2)}) collective-permute-start(bf16[256,512]{1,0:T(8,128)(2,1)S(1)} %get-tuple-element.67), channel_id=1, source_target_pairs={{0,64},{1,5},{2,66},{3,7},{4,68},{5,1},{6,70},{7,3},{8,72},{9,13},... | collective-permute-start | bytes 786440 | tf_op jit(solution)/shard_map/ppermute | solution.py:46
  58.1 1.9 %shard_map.88 = (bf16[256,512]{1,0:T(8,128)(2,1)S(1)}, bf16[1,256,512]{2,1,0:T(8,128)(2,1)S(1)}, f32[4,15,256]{2,1,0:T(8,128)S(1)}) custom-call(s32[4]{0:T(128)S(1)} %pad_add_fusion.pos, bf16[3,256,512]{2,1,0:T(8,128)(2,1)S(1)} %fusion.19.proj, bf16[256,512]{1,0:T(8,128)(2,1)S(1)} %copy-done, f32[4,15,256]{2,1,0:T(8,128)S(1)} %bitcast.64, ...), custom_call_target="tpu_custom_call" | custom-call | tf_op jit(solution)/shard_map/pallas_call | solution.py:257
  60.1 1.0 collective-permute-start.25
  61.1 1.0 collective-permute-start.24
  62.0 1.1 collective-permute-start.20
  63.4 1.0 fusion.13
  64.5 0.5 fusion.32
  64.9 1.1 collective-permute-done.21
  66.0 1.9 %collective-permute-start.22 = (bf16[1,256,512]{2,1,0:T(8,128)(2,1)S(1)}, bf16[1,256,512]{2,1,0:T(8,128)(2,1)S(1)}, u32[]{:S(2)}, u32[]{:S(2)}) collective-permute-start(bf16[1,256,512]{2,1,0:T(8,128)(2,1)S(1)} %get-tuple-element.48), channel_id=1, source_target_pairs={{0,64},{1,5},{2,66},{3,7},{4,68},{5,1},{6,70},{7,3},{8,72},{9,13},... | collective-permute-start | bytes 786440 | tf_op jit(solution)/shard_map/ppermute | solution.py:46
  67.9 1.7 %collective-permute-done.20 = bf16[1,256,512]{2,1,0:T(8,128)(2,1)S(1)} collective-permute-done((bf16[1,256,512]{2,1,0:T(8,128)(2,1)S(1)}, bf16[1,256,512]{2,1,0:T(8,128)(2,1)S(1)}, u32[]{:S(2)}, u32[]{:S(2)}) %collective-permute-start.20) | collective-permute-done | bytes 262176 | tf_op jit(solution)/shard_map/ppermute | solution.py:46
  69.6 1.3 %collective-permute-start.28 = (bf16[2,256,512]{2,1,0:T(8,128)(2,1)S(1)}, bf16[2,256,512]{2,1,0:T(8,128)(2,1)S(1)}, u32[]{:S(2)}, u32[]{:S(2)}) collective-permute-start(bf16[2,256,512]{2,1,0:T(8,128)(2,1)S(1)} %shard_map.91), channel_id=1, source_target_pairs={{0,96},{1,7},{2,98},{3,1},{4,100},{5,3},{6,102},{7,5},{8,104},{9,1... | collective-permute-start | bytes 1572872 | tf_op jit(solution)/shard_map/ppermute | solution.py:46
  71.3 0.7 collective-permute-start.27
  72.0 1.9 %collective-permute-done.22 = bf16[1,256,512]{2,1,0:T(8,128)(2,1)S(1)} collective-permute-done((bf16[1,256,512]{2,1,0:T(8,128)(2,1)S(1)}, bf16[1,256,512]{2,1,0:T(8,128)(2,1)S(1)}, u32[]{:S(2)}, u32[]{:S(2)}) %collective-permute-start.22) | collective-permute-done | bytes 262176 | tf_op jit(solution)/shard_map/ppermute | solution.py:46
  73.9 0.4 collective-permute-start.26
  74.3 0.3 fusion.36
  75.4 0.6 shard_map.93
  76.1 6.6 %collective-permute-done.27 = bf16[2,256,512]{2,1,0:T(8,128)(2,1)S(1)} collective-permute-done((bf16[2,256,512]{2,1,0:T(8,128)(2,1)S(1)}, bf16[2,256,512]{2,1,0:T(8,128)(2,1)S(1)}, u32[]{:S(2)}, u32[]{:S(2)}) %collective-permute-start.27) | collective-permute-done | bytes 524320 | tf_op jit(solution)/shard_map/ppermute | solution.py:46
  82.7 0.5 fusion.28
  83.2 9.1 %collective-permute-done.26 = bf16[2,256,512]{2,1,0:T(8,128)(2,1)S(1)} collective-permute-done((bf16[2,256,512]{2,1,0:T(8,128)(2,1)S(1)}, bf16[2,256,512]{2,1,0:T(8,128)(2,1)S(1)}, u32[]{:S(2)}, u32[]{:S(2)}) %collective-permute-start.26) | collective-permute-done | bytes 524320 | tf_op jit(solution)/shard_map/ppermute | solution.py:46
  92.3 0.5 fusion.30
  92.8 0.6 add_bitcast_fusion.product
  93.4 0.7 shard_map.94
  94.2 1.2 collective-permute-start.33
  95.4 2.0 %collective-permute-start.34 = (bf16[2,128,512]{2,1,0:T(8,128)(2,1)S(1)}, bf16[2,128,512]{2,1,0:T(8,128)(2,1)S(1)}, u32[]{:S(2)}, u32[]{:S(2)}) collective-permute-start(bf16[2,128,512]{2,1,0:T(8,128)(2,1)S(1)} %get-tuple-element.76), channel_id=1, source_target_pairs={{0,24},{1,97},{2,26},{3,99},{4,28},{5,101},{6,30},{7,103},{8,0},{9... | collective-permute-start | bytes 786440 | tf_op jit(solution)/shard_map/ppermute | solution.py:46
  97.4 0.9 collective-permute-start.31
  98.4 0.7 copy.49
  99.1 0.7 copy.28
  99.7 9.2 %collective-permute-done.31.a3 = bf16[1,128,512]{2,1,0:T(8,128)(2,1)S(1)} collective-permute-done((bf16[1,128,512]{2,1,0:T(8,128)(2,1)S(1)}, bf16[1,128,512]{2,1,0:T(8,128)(2,1)S(1)}, u32[]{:S(2)}, u32[]{:S(2)}) %collective-permute-start.31) | collective-permute-done | bytes 131104 | tf_op jit(solution)/shard_map/ppermute | solution.py:46
  109.0 0.8 shard_map.95
  109.8 1.0 collective-permute-start.35
  110.9 3.2 %collective-permute-start.36 = (bf16[3,32,512]{2,1,0:T(8,128)(2,1)S(1)}, bf16[3,32,512]{2,1,0:T(8,128)(2,1)S(1)}, u32[]{:S(2)}, u32[]{:S(2)}) collective-permute-start(bf16[3,32,512]{2,1,0:T(8,128)(2,1)S(1)} %get-tuple-element.79), channel_id=1, source_target_pairs={{0,4},{1,17},{2,6},{3,19},{4,0},{5,21},{6,2},{7,23},{8,12},{9,25},... | collective-permute-start | bytes 294920 | tf_op jit(solution)/shard_map/ppermute | solution.py:46
  114.0 2.5 %collective-permute-start.37 = (bf16[3,32,512]{2,1,0:T(8,128)(2,1)S(1)}, bf16[3,32,512]{2,1,0:T(8,128)(2,1)S(1)}, u32[]{:S(2)}, u32[]{:S(2)}) collective-permute-start(bf16[3,32,512]{2,1,0:T(8,128)(2,1)S(1)} %get-tuple-element.80), channel_id=1, source_target_pairs={{0,6},{1,25},{2,0},{3,27},{4,2},{5,29},{6,4},{7,31},{8,14},{9,1},{... | collective-permute-start | bytes 294920 | tf_op jit(solution)/shard_map/ppermute | solution.py:46
  116.6 1.0 fusion.10
  117.6 1.2 collective-permute-done.37
  118.8 0.7 multiply_bitcast_fusion
  119.5 0.9 add_convert_fusion
  (53 shorter events, 2.1 us)
Async XLA Ops:
  0.6 4.1 %collective-permute-start = (bf16[256,1024]{1,0:T(8,128)(2,1)}, bf16[256,1024]{1,0:T(8,128)(2,1)S(1)}, u32[]{:S(2)}, u32[]{:S(2)}) collective-permute-start(bf16[256,1024]{1,0:T(8,128)(2,1)} %hidden.1), channel_id=1, source_target_pairs={{0,1},{1,0},{2,3},{3,2},{4,5},{5,4},{6,7},{7,6},{8,9},{9,8},{10,11... | collective-permute-start | bytes 1572872 | tf_op jit(solution)/shard_map/ppermute | solution.py:50
  1.7 3.1 %copy-start.2 = (f32[3]{0:T(128)S(1)}, f32[3]{0:T(128)}, u32[]{:S(2)}) copy-start(f32[3]{0:T(128)} %constant.27.clone) | copy-start | bytes 40
  4.7 3.1 %copy-start = (bf16[256,512]{1,0:T(8,128)(2,1)S(1)}, bf16[256,512]{1,0:T(8,128)(2,1)}, u32[]{:S(2)}) copy-start(bf16[256,512]{1,0:T(8,128)(2,1)} %out_grad.1) | copy-start | bytes 786436
  4.7 58.7 %slice-start = ((s8[6291456]{0:T(1024)(128)(4,1)}), s8[4194304]{0:T(1024)(128)(4,1)S(1)}, s32[]{:S(2)}) async-start(s8[6291456]{0:T(1024)(128)(4,1)} %bitcast.66), calls=%async_computation | async-start | bytes 8388608
  9.1 45.7 %copy-start.1 = (bf16[256,1024]{1,0:T(8,128)(2,1)S(1)}, bf16[256,1024]{1,0:T(8,128)(2,1)}, u32[]{:S(2)}) copy-start(bf16[256,1024]{1,0:T(8,128)(2,1)} %hidden.1) | copy-start | bytes 1572868
  9.1 9.4 %collective-permute-start.3 = (bf16[512,128]{1,0:T(8,128)(2,1)S(1)}, bf16[512,128]{1,0:T(8,128)(2,1)S(1)}, u32[]{:S(2)}, u32[]{:S(2)}) collective-permute-start(bf16[512,128]{1,0:T(8,128)(2,1)S(1)} %get-tuple-element.46.mine), channel_id=1, source_target_pairs={{0,6},{1,7},{2,0},{3,1},{4,2},{5,3},{6,4},{7,5},{8,14},{9,15},{10,... | collective-permute-start | bytes 393224 | tf_op jit(solution)/shard_map/ppermute | solution.py:46
  12.3 7.9 %collective-permute-start.2 = (bf16[512,128]{1,0:T(8,128)(2,1)S(1)}, bf16[512,128]{1,0:T(8,128)(2,1)S(1)}, u32[]{:S(2)}, u32[]{:S(2)}) collective-permute-start(bf16[512,128]{1,0:T(8,128)(2,1)S(1)} %get-tuple-element.46.mine), channel_id=1, source_target_pairs={{0,4},{1,5},{2,6},{3,7},{4,0},{5,1},{6,2},{7,3},{8,12},{9,13},{10,... | collective-permute-start | bytes 393224 | tf_op jit(solution)/shard_map/ppermute | solution.py:46
  12.9 9.3 %collective-permute-start.1 = (bf16[512,128]{1,0:T(8,128)(2,1)S(1)}, bf16[512,128]{1,0:T(8,128)(2,1)S(1)}, u32[]{:S(2)}, u32[]{:S(2)}) collective-permute-start(bf16[512,128]{1,0:T(8,128)(2,1)S(1)} %get-tuple-element.46.mine), channel_id=1, source_target_pairs={{0,2},{1,3},{2,4},{3,5},{4,6},{5,7},{6,0},{7,1},{8,10},{9,11},{10,... | collective-permute-start | bytes 393224 | tf_op jit(solution)/shard_map/ppermute | solution.py:46
  13.9 12.5 %collective-permute-start.12 = (bf16[512,128]{1,0:T(8,128)(2,1)S(1)}, bf16[512,128]{1,0:T(8,128)(2,1)S(1)}, u32[]{:S(2)}, u32[]{:S(2)}) collective-permute-start(bf16[512,128]{1,0:T(8,128)(2,1)S(1)} %get-tuple-element.52), channel_id=1, source_target_pairs={{32,0},{33,1},{34,2},{35,3},{36,4},{37,5},{38,6},{39,7},{40,8},{41... | collective-permute-start | bytes 393224 | tf_op jit(solution)/shard_map/ppermute | solution.py:46
  15.2 12.5 %collective-permute-start.11 = (bf16[512,128]{1,0:T(8,128)(2,1)S(1)}, bf16[512,128]{1,0:T(8,128)(2,1)S(1)}, u32[]{:S(2)}, u32[]{:S(2)}) collective-permute-start(bf16[512,128]{1,0:T(8,128)(2,1)S(1)} %get-tuple-element.51), channel_id=1, source_target_pairs={{64,0},{65,1},{66,2},{67,3},{68,4},{69,5},{70,6},{71,7},{72,8},{73... | collective-permute-start | bytes 393224 | tf_op jit(solution)/shard_map/ppermute | solution.py:46
  18.5 9.2 %collective-permute-start.10 = (bf16[512,128]{1,0:T(8,128)(2,1)S(1)}, bf16[512,128]{1,0:T(8,128)(2,1)S(1)}, u32[]{:S(2)}, u32[]{:S(2)}) collective-permute-start(bf16[512,128]{1,0:T(8,128)(2,1)S(1)} %get-tuple-element.51), channel_id=1, source_target_pairs={{96,0},{97,1},{98,2},{99,3},{100,4},{101,5},{102,6},{103,7},{104,8... | collective-permute-start | bytes 393224 | tf_op jit(solution)/shard_map/ppermute | solution.py:46
  22.3 12.7 %collective-permute-start.6 = (bf16[512,128]{1,0:T(8,128)(2,1)S(1)}, bf16[512,128]{1,0:T(8,128)(2,1)S(1)}, u32[]{:S(2)}, u32[]{:S(2)}) collective-permute-start(bf16[512,128]{1,0:T(8,128)(2,1)S(1)} %shard_map.86.mine), channel_id=1, source_target_pairs={{0,24},{1,25},{2,26},{3,27},{4,28},{5,29},{6,30},{7,31},{8,0},{9,1... | collective-permute-start | bytes 393224 | tf_op jit(solution)/shard_map/ppermute | solution.py:46
  26.4 12.2 %collective-permute-start.5 = (bf16[512,128]{1,0:T(8,128)(2,1)S(1)}, bf16[512,128]{1,0:T(8,128)(2,1)S(1)}, u32[]{:S(2)}, u32[]{:S(2)}) collective-permute-start(bf16[512,128]{1,0:T(8,128)(2,1)S(1)} %shard_map.86.mine), channel_id=1, source_target_pairs={{0,16},{1,17},{2,18},{3,19},{4,20},{5,21},{6,22},{7,23},{8,24},{9,... | collective-permute-start | bytes 393224 | tf_op jit(solution)/shard_map/ppermute | solution.py:46
  26.4 12.2 %collective-permute-start.4 = (bf16[512,128]{1,0:T(8,128)(2,1)S(1)}, bf16[512,128]{1,0:T(8,128)(2,1)S(1)}, u32[]{:S(2)}, u32[]{:S(2)}) collective-permute-start(bf16[512,128]{1,0:T(8,128)(2,1)S(1)} %shard_map.86.mine), channel_id=1, source_target_pairs={{0,8},{1,9},{2,10},{3,11},{4,12},{5,13},{6,14},{7,15},{8,16},{9,17... | collective-permute-start | bytes 393224 | tf_op jit(solution)/shard_map/ppermute | solution.py:46
  28.4 16.3 %collective-permute-start.13 = (bf16[512,128]{1,0:T(8,128)(2,1)S(1)}, bf16[512,128]{1,0:T(8,128)(2,1)S(1)}, u32[]{:S(2)}, u32[]{:S(2)}) collective-permute-start(bf16[512,128]{1,0:T(8,128)(2,1)S(1)} %get-tuple-element.55), channel_id=1, source_target_pairs={{0,8},{1,9},{2,10},{3,11},{4,12},{5,13},{6,14},{7,15},{8,16},{9,17... | collective-permute-start | bytes 393224 | tf_op jit(solution)/shard_map/ppermute | solution.py:46
  30.6 16.8 %collective-permute-start.14 = (bf16[512,128]{1,0:T(8,128)(2,1)S(1)}, bf16[512,128]{1,0:T(8,128)(2,1)S(1)}, u32[]{:S(2)}, u32[]{:S(2)}) collective-permute-start(bf16[512,128]{1,0:T(8,128)(2,1)S(1)} %get-tuple-element.56), channel_id=1, source_target_pairs={{0,16},{1,17},{2,18},{3,19},{4,20},{5,21},{6,22},{7,23},{8,24},{9,... | collective-permute-start | bytes 393224 | tf_op jit(solution)/shard_map/ppermute | solution.py:46
  35.0 12.5 %collective-permute-start.15 = (bf16[512,128]{1,0:T(8,128)(2,1)S(1)}, bf16[512,128]{1,0:T(8,128)(2,1)S(1)}, u32[]{:S(2)}, u32[]{:S(2)}) collective-permute-start(bf16[512,128]{1,0:T(8,128)(2,1)S(1)} %get-tuple-element.57), channel_id=1, source_target_pairs={{0,24},{1,25},{2,26},{3,27},{4,28},{5,29},{6,30},{7,31},{8,0},{9,1... | collective-permute-start | bytes 393224 | tf_op jit(solution)/shard_map/ppermute | solution.py:46
  38.7 11.4 %collective-permute-start.9 = (bf16[512,128]{1,0:T(8,128)(2,1)S(1)}, bf16[512,128]{1,0:T(8,128)(2,1)S(1)}, u32[]{:S(2)}, u32[]{:S(2)}) collective-permute-start(bf16[512,128]{1,0:T(8,128)(2,1)S(1)} %shard_map.87), channel_id=1, source_target_pairs={{0,96},{1,97},{2,98},{3,99},{4,100},{5,101},{6,102},{7,103},{8,104... | collective-permute-start | bytes 393224 | tf_op jit(solution)/shard_map/ppermute | solution.py:46
  43.4 12.1 %collective-permute-start.8 = (bf16[512,128]{1,0:T(8,128)(2,1)S(1)}, bf16[512,128]{1,0:T(8,128)(2,1)S(1)}, u32[]{:S(2)}, u32[]{:S(2)}) collective-permute-start(bf16[512,128]{1,0:T(8,128)(2,1)S(1)} %shard_map.87), channel_id=1, source_target_pairs={{0,64},{1,65},{2,66},{3,67},{4,68},{5,69},{6,70},{7,71},{8,72},{9,... | collective-permute-start | bytes 393224 | tf_op jit(solution)/shard_map/ppermute | solution.py:46
  44.7 10.9 %collective-permute-start.7 = (bf16[512,128]{1,0:T(8,128)(2,1)S(1)}, bf16[512,128]{1,0:T(8,128)(2,1)S(1)}, u32[]{:S(2)}, u32[]{:S(2)}) collective-permute-start(bf16[512,128]{1,0:T(8,128)(2,1)S(1)} %shard_map.87), channel_id=1, source_target_pairs={{0,32},{1,33},{2,34},{3,35},{4,36},{5,37},{6,38},{7,39},{8,40},{9,... | collective-permute-start | bytes 393224 | tf_op jit(solution)/shard_map/ppermute | solution.py:46
  47.5 15.9 %slice-start.1 = ((s8[6291456]{0:T(1024)(128)(4,1)}), s8[2097152]{0:T(1024)(128)(4,1)S(1)}, s32[]{:S(2)}) async-start(s8[6291456]{0:T(1024)(128)(4,1)} %bitcast.66), calls=%async_computation.1 | async-start | bytes 4194304
  48.2 11.8 %collective-permute-start.16 = (bf16[512,128]{1,0:T(8,128)(2,1)S(1)}, bf16[512,128]{1,0:T(8,128)(2,1)S(1)}, u32[]{:S(2)}, u32[]{:S(2)}) collective-permute-start(bf16[512,128]{1,0:T(8,128)(2,1)S(1)} %get-tuple-element.62), channel_id=1, source_target_pairs={{0,2},{1,3},{2,4},{3,5},{4,6},{5,7},{6,0},{7,1},{8,10},{9,11},{10,... | collective-permute-start | bytes 393224 | tf_op jit(solution)/shard_map/ppermute | solution.py:46
  48.3 12.8 %collective-permute-start.17 = (bf16[512,128]{1,0:T(8,128)(2,1)S(1)}, bf16[512,128]{1,0:T(8,128)(2,1)S(1)}, u32[]{:S(2)}, u32[]{:S(2)}) collective-permute-start(bf16[512,128]{1,0:T(8,128)(2,1)S(1)} %get-tuple-element.63), channel_id=1, source_target_pairs={{0,4},{1,5},{2,6},{3,7},{4,0},{5,1},{6,2},{7,3},{8,12},{9,13},{10,... | collective-permute-start | bytes 393224 | tf_op jit(solution)/shard_map/ppermute | solution.py:46
  50.1 11.9 %collective-permute-start.18 = (bf16[512,128]{1,0:T(8,128)(2,1)S(1)}, bf16[512,128]{1,0:T(8,128)(2,1)S(1)}, u32[]{:S(2)}, u32[]{:S(2)}) collective-permute-start(bf16[512,128]{1,0:T(8,128)(2,1)S(1)} %get-tuple-element.64), channel_id=1, source_target_pairs={{0,6},{1,7},{2,0},{3,1},{4,2},{5,3},{6,4},{7,5},{8,14},{9,15},{10,... | collective-permute-start | bytes 393224 | tf_op jit(solution)/shard_map/ppermute | solution.py:46
  55.5 10.5 %collective-permute-start.21 = (bf16[256,512]{1,0:T(8,128)(2,1)S(1)}, bf16[256,512]{1,0:T(8,128)(2,1)S(1)}, u32[]{:S(2)}, u32[]{:S(2)}) collective-permute-start(bf16[256,512]{1,0:T(8,128)(2,1)S(1)} %get-tuple-element.66), channel_id=1, source_target_pairs={{0,32},{1,3},{2,34},{3,5},{4,36},{5,7},{6,38},{7,1},{8,40},{9,11},... | collective-permute-start | bytes 786440 | tf_op jit(solution)/shard_map/ppermute | solution.py:46
  55.6 15.6 %collective-permute-start.23 = (bf16[256,512]{1,0:T(8,128)(2,1)S(1)}, bf16[256,512]{1,0:T(8,128)(2,1)S(1)}, u32[]{:S(2)}, u32[]{:S(2)}) collective-permute-start(bf16[256,512]{1,0:T(8,128)(2,1)S(1)} %get-tuple-element.67), channel_id=1, source_target_pairs={{0,64},{1,5},{2,66},{3,7},{4,68},{5,1},{6,70},{7,3},{8,72},{9,13},... | collective-permute-start | bytes 786440 | tf_op jit(solution)/shard_map/ppermute | solution.py:46
  60.1 14.6 %collective-permute-start.25 = (bf16[256,512]{1,0:T(8,128)(2,1)S(1)}, bf16[256,512]{1,0:T(8,128)(2,1)S(1)}, u32[]{:S(2)}, u32[]{:S(2)}) collective-permute-start(bf16[256,512]{1,0:T(8,128)(2,1)S(1)} %get-tuple-element.68), channel_id=1, source_target_pairs={{0,96},{1,7},{2,98},{3,1},{4,100},{5,3},{6,102},{7,5},{8,104},{9,1... | collective-permute-start | bytes 786440 | tf_op jit(solution)/shard_map/ppermute | solution.py:46
  61.1 13.7 %collective-permute-start.24 = (bf16[1,256,512]{2,1,0:T(8,128)(2,1)S(1)}, bf16[1,256,512]{2,1,0:T(8,128)(2,1)S(1)}, u32[]{:S(2)}, u32[]{:S(2)}) collective-permute-start(bf16[1,256,512]{2,1,0:T(8,128)(2,1)S(1)} %get-tuple-element.48), channel_id=1, source_target_pairs={{0,96},{1,7},{2,98},{3,1},{4,100},{5,3},{6,102},{7,5},{8,104},{9,1... | collective-permute-start | bytes 786440 | tf_op jit(solution)/shard_map/ppermute | solution.py:46
  62.0 7.6 %collective-permute-start.20 = (bf16[1,256,512]{2,1,0:T(8,128)(2,1)S(1)}, bf16[1,256,512]{2,1,0:T(8,128)(2,1)S(1)}, u32[]{:S(2)}, u32[]{:S(2)}) collective-permute-start(bf16[1,256,512]{2,1,0:T(8,128)(2,1)S(1)} %get-tuple-element.48), channel_id=1, source_target_pairs={{0,32},{1,3},{2,34},{3,5},{4,36},{5,7},{6,38},{7,1},{8,40},{9,11},... | collective-permute-start | bytes 786440 | tf_op jit(solution)/shard_map/ppermute | solution.py:46
  66.0 7.9 %collective-permute-start.22 = (bf16[1,256,512]{2,1,0:T(8,128)(2,1)S(1)}, bf16[1,256,512]{2,1,0:T(8,128)(2,1)S(1)}, u32[]{:S(2)}, u32[]{:S(2)}) collective-permute-start(bf16[1,256,512]{2,1,0:T(8,128)(2,1)S(1)} %get-tuple-element.48), channel_id=1, source_target_pairs={{0,64},{1,5},{2,66},{3,7},{4,68},{5,1},{6,70},{7,3},{8,72},{9,13},... | collective-permute-start | bytes 786440 | tf_op jit(solution)/shard_map/ppermute | solution.py:46
  69.6 23.2 %collective-permute-start.28 = (bf16[2,256,512]{2,1,0:T(8,128)(2,1)S(1)}, bf16[2,256,512]{2,1,0:T(8,128)(2,1)S(1)}, u32[]{:S(2)}, u32[]{:S(2)}) collective-permute-start(bf16[2,256,512]{2,1,0:T(8,128)(2,1)S(1)} %shard_map.91), channel_id=1, source_target_pairs={{0,96},{1,7},{2,98},{3,1},{4,100},{5,3},{6,102},{7,5},{8,104},{9,1... | collective-permute-start | bytes 1572872 | tf_op jit(solution)/shard_map/ppermute | solution.py:46
  71.3 11.4 %collective-permute-start.27 = (bf16[2,256,512]{2,1,0:T(8,128)(2,1)S(1)}, bf16[2,256,512]{2,1,0:T(8,128)(2,1)S(1)}, u32[]{:S(2)}, u32[]{:S(2)}) collective-permute-start(bf16[2,256,512]{2,1,0:T(8,128)(2,1)S(1)} %shard_map.91), channel_id=1, source_target_pairs={{0,64},{1,5},{2,66},{3,7},{4,68},{5,1},{6,70},{7,3},{8,72},{9,13},... | collective-permute-start | bytes 1572872 | tf_op jit(solution)/shard_map/ppermute | solution.py:46
  73.9 18.4 %collective-permute-start.26 = (bf16[2,256,512]{2,1,0:T(8,128)(2,1)S(1)}, bf16[2,256,512]{2,1,0:T(8,128)(2,1)S(1)}, u32[]{:S(2)}, u32[]{:S(2)}) collective-permute-start(bf16[2,256,512]{2,1,0:T(8,128)(2,1)S(1)} %shard_map.91), channel_id=1, source_target_pairs={{0,32},{1,3},{2,34},{3,5},{4,36},{5,7},{6,38},{7,1},{8,40},{9,11},... | collective-permute-start | bytes 1572872 | tf_op jit(solution)/shard_map/ppermute | solution.py:46
  74.6 44.9 %collective-permute-start.19 = (f32[256,1024]{1,0:T(8,128)S(1)}, f32[256,1024]{1,0:T(8,128)S(1)}, u32[]{:S(2)}, u32[]{:S(2)}) collective-permute-start(f32[256,1024]{1,0:T(8,128)S(1)} %fusion.13), channel_id=1, source_target_pairs={{0,1},{1,0},{2,3},{3,2},{4,5},{5,4},{6,7},{7,6},{8,9},{9,8},{10,11... | collective-permute-start | bytes 3145736 | tf_op jit(solution)/shard_map/ppermute | solution.py:50
  76.0 19.3 %collective-permute-start.29 = (bf16[1,128,512]{2,1,0:T(8,128)(2,1)S(1)}, bf16[1,128,512]{2,1,0:T(8,128)(2,1)S(1)}, u32[]{:S(2)}, u32[]{:S(2)}) collective-permute-start(bf16[1,128,512]{2,1,0:T(8,128)(2,1)S(1)} %get-tuple-element.71), channel_id=1, source_target_pairs={{0,8},{1,33},{2,10},{3,35},{4,12},{5,37},{6,14},{7,39},{8,16},{9,4... | collective-permute-start | bytes 393224 | tf_op jit(solution)/shard_map/ppermute | solution.py:46
  82.7 14.7 %collective-permute-start.30 = (bf16[1,128,512]{2,1,0:T(8,128)(2,1)S(1)}, bf16[1,128,512]{2,1,0:T(8,128)(2,1)S(1)}, u32[]{:S(2)}, u32[]{:S(2)}) collective-permute-start(bf16[1,128,512]{2,1,0:T(8,128)(2,1)S(1)} %get-tuple-element.72), channel_id=1, source_target_pairs={{0,16},{1,65},{2,18},{3,67},{4,20},{5,69},{6,22},{7,71},{8,24},{9,... | collective-permute-start | bytes 393224 | tf_op jit(solution)/shard_map/ppermute | solution.py:46
  94.1 14.9 %collective-permute-start.32 = (bf16[2,128,512]{2,1,0:T(8,128)(2,1)S(1)}, bf16[2,128,512]{2,1,0:T(8,128)(2,1)S(1)}, u32[]{:S(2)}, u32[]{:S(2)}) collective-permute-start(bf16[2,128,512]{2,1,0:T(8,128)(2,1)S(1)} %get-tuple-element.74), channel_id=1, source_target_pairs={{0,8},{1,33},{2,10},{3,35},{4,12},{5,37},{6,14},{7,39},{8,16},{9,4... | collective-permute-start | bytes 786440 | tf_op jit(solution)/shard_map/ppermute | solution.py:46
  94.2 14.8 %collective-permute-start.33 = (bf16[2,128,512]{2,1,0:T(8,128)(2,1)S(1)}, bf16[2,128,512]{2,1,0:T(8,128)(2,1)S(1)}, u32[]{:S(2)}, u32[]{:S(2)}) collective-permute-start(bf16[2,128,512]{2,1,0:T(8,128)(2,1)S(1)} %get-tuple-element.75), channel_id=1, source_target_pairs={{0,16},{1,65},{2,18},{3,67},{4,20},{5,69},{6,22},{7,71},{8,24},{9,... | collective-permute-start | bytes 786440 | tf_op jit(solution)/shard_map/ppermute | solution.py:46
  95.4 13.6 %collective-permute-start.34 = (bf16[2,128,512]{2,1,0:T(8,128)(2,1)S(1)}, bf16[2,128,512]{2,1,0:T(8,128)(2,1)S(1)}, u32[]{:S(2)}, u32[]{:S(2)}) collective-permute-start(bf16[2,128,512]{2,1,0:T(8,128)(2,1)S(1)} %get-tuple-element.76), channel_id=1, source_target_pairs={{0,24},{1,97},{2,26},{3,99},{4,28},{5,101},{6,30},{7,103},{8,0},{9... | collective-permute-start | bytes 786440 | tf_op jit(solution)/shard_map/ppermute | solution.py:46
  97.4 11.6 %collective-permute-start.31 = (bf16[1,128,512]{2,1,0:T(8,128)(2,1)S(1)}, bf16[1,128,512]{2,1,0:T(8,128)(2,1)S(1)}, u32[]{:S(2)}, u32[]{:S(2)}) collective-permute-start(bf16[1,128,512]{2,1,0:T(8,128)(2,1)S(1)} %get-tuple-element.73), channel_id=1, source_target_pairs={{0,24},{1,97},{2,26},{3,99},{4,28},{5,101},{6,30},{7,103},{8,0},{9... | collective-permute-start | bytes 393224 | tf_op jit(solution)/shard_map/ppermute | solution.py:46
  109.8 7.8 %collective-permute-start.35 = (bf16[3,32,512]{2,1,0:T(8,128)(2,1)S(1)}, bf16[3,32,512]{2,1,0:T(8,128)(2,1)S(1)}, u32[]{:S(2)}, u32[]{:S(2)}) collective-permute-start(bf16[3,32,512]{2,1,0:T(8,128)(2,1)S(1)} %get-tuple-element.78), channel_id=1, source_target_pairs={{0,2},{1,9},{2,4},{3,11},{4,6},{5,13},{6,0},{7,15},{8,10},{9,17},{... | collective-permute-start | bytes 294920 | tf_op jit(solution)/shard_map/ppermute | solution.py:46
  110.9 6.7 %collective-permute-start.36 = (bf16[3,32,512]{2,1,0:T(8,128)(2,1)S(1)}, bf16[3,32,512]{2,1,0:T(8,128)(2,1)S(1)}, u32[]{:S(2)}, u32[]{:S(2)}) collective-permute-start(bf16[3,32,512]{2,1,0:T(8,128)(2,1)S(1)} %get-tuple-element.79), channel_id=1, source_target_pairs={{0,4},{1,17},{2,6},{3,19},{4,0},{5,21},{6,2},{7,23},{8,12},{9,25},... | collective-permute-start | bytes 294920 | tf_op jit(solution)/shard_map/ppermute | solution.py:46
  114.0 4.8 %collective-permute-start.37 = (bf16[3,32,512]{2,1,0:T(8,128)(2,1)S(1)}, bf16[3,32,512]{2,1,0:T(8,128)(2,1)S(1)}, u32[]{:S(2)}, u32[]{:S(2)}) collective-permute-start(bf16[3,32,512]{2,1,0:T(8,128)(2,1)S(1)} %get-tuple-element.80), channel_id=1, source_target_pairs={{0,6},{1,25},{2,0},{3,27},{4,2},{5,29},{6,4},{7,31},{8,14},{9,1},{... | collective-permute-start | bytes 294920 | tf_op jit(solution)/shard_map/ppermute | solution.py:46

commit v5 on v4

--- a/solution.py
+++ b/solution.py
@@ -75,7 +75,7 @@
         s_out[cols, :] = dot(kt, proj[2, :, cols], ((1,), (0,))).astype(BF)
 
         def grad(j):
-            row = mix[h, 9 + j : 10 + j, :] * scale_of(9 + j)
+            row = mix[9 + j, h : h + 1, :] * scale_of(9 + j)
             return dot((qt * row).astype(BF), gg, ((1,), (0,)))
 
         b0[cols, :] = grad(0).astype(BF)
@@ -114,40 +114,54 @@
         out[...] = (held_now + term).astype(BF)
 
 
-def inner_kernel(proj, grads, mix, out_t, query_t, key_out, value_out, level_out, table):
-    s_at = lax.broadcasted_iota(jnp.int32, (256, 256), 0)
-    t_at = lax.broadcasted_iota(jnp.int32, (256, 256), 1)
+def inner_kernel(
+    proj, grads, mix, out_t, query_t, key_out, value_out, level_out, table, mixed, score_grad
+):
+    half = DH
+    s_at = lax.broadcasted_iota(jnp.int32, (half, half), 0)
+    t_at = lax.broadcasted_iota(jnp.int32, (half, half), 1)
     apart = s_at ^ t_at
-    level = jnp.zeros((256, 256), jnp.int32)
-    for place in range(8):
+    level = jnp.zeros((half, half), jnp.int32)
+    for place in range(7):
         level = level + (apart >= (1 << place)).astype(jnp.int32)
     table[...] = jnp.where(s_at <= t_at, level, -1)
-
-    def one_head(h, _):
-        cols = pl.ds(pl.multiple_of(h * DH, DH), DH)
+    mixed[half:, :half] = jnp.zeros((half, half), BF)
+    score_grad[half:, :half] = jnp.zeros((half, half), BF)
+
+    for h, cols in heads():
         qq, kk, vv, gg = proj[0, :, cols], proj[1, :, cols], proj[2, :, cols], grads[:, cols]
         kt = turned(kk).astype(BF)
         vt = turned(vv).astype(BF)
         scores = dot(kk, qq, ((1,), (1,)))
         mix_grad = dot(vv, gg, ((1,), (1,)))
+
+        def row(level, at, h=h):
+            return mix[level, h : h + 1, at : at + half] * scale_of(level)
+
         levels = table[...]
-        weight = jnp.zeros((256, 256), F32)
-        product = scores * mix_grad
-        for level in range(9):
-            here = levels == level
-            weight = jnp.where(here, mix[h, level : level + 1, :] * scale_of(level), weight)
-            level_out[h, level : level + 1, :] = jnp.sum(
-                jnp.where(here, product, 0.0), axis=0, keepdims=True
-            ) * scale_of(level)
-        mixed = (weight * scores).astype(BF)
-        score_grad = (weight * mix_grad).astype(BF)
-        out_t[h] = dot(vt, mixed, ((1,), (0,)))
-        query_t[h] = dot(kt, score_grad, ((1,), (0,)))
-        key_out[:, cols] = dot(score_grad, qq, ((1,), (0,)))
-        value_out[:, cols] = dot(mixed, gg, ((1,), (0,)))
-        return 0
-
-    lax.fori_loop(0, 4, one_head, 0)
+        for at in (0, half):
+            score, grad = scores[at : at + half, at : at + half], mix_grad[at : at + half, at : at + half]
+            product = score * grad
+            weight = jnp.zeros((half, half), F32)
+            for level in range(8):
+                here = levels == level
+                weight = jnp.where(here, row(level, at), weight)
+                level_out[level, h : h + 1, at : at + half] = jnp.sum(
+                    jnp.where(here, product, 0.0), axis=0, keepdims=True
+                ) * scale_of(level)
+            mixed[at : at + half, at : at + half] = (weight * score).astype(BF)
+            score_grad[at : at + half, at : at + half] = (weight * grad).astype(BF)
+        score, grad = scores[:half, half:], mix_grad[:half, half:]
+        weight = row(8, half)
+        level_out[8, h : h + 1, :half] = jnp.zeros((1, half), F32)
+        level_out[8, h : h + 1, half:] = jnp.sum(score * grad, axis=0, keepdims=True) * scale_of(8)
+        mixed[:half, half:] = (weight * score).astype(BF)
+        score_grad[:half, half:] = (weight * grad).astype(BF)
+
+        out_t[h] = dot(vt, mixed[...], ((1,), (0,)))
+        query_t[h] = dot(kt, score_grad[...], ((1,), (0,)))
+        key_out[:, cols] = dot(score_grad[...], qq, ((1,), (0,)))
+        value_out[:, cols] = dot(mixed[...], gg, ((1,), (0,)))
 
 
 def key_value_kernel(proj, key_in, value_in, held, ry1, ry2, ry3, grads):
@@ -162,36 +176,41 @@
         ).astype(BF)
 
 
-def query_kernel(
-    pos, proj, out_grad, mix, out_t, query_t, level_in, gy1, gy2, gy3, rz1, rz2, rz3, gx1, gx2,
-    gx3, attended, grads, level_out,
-):
+def pair_of(p, *parts):
+    one, two, three = (a.astype(F32) for a in parts)
+    low = one * flag((p == 1) | (p == 3))
+    high = one * flag(p == 2) + two * flag(p >= 2) + three * flag(p == 3)
+    return low.astype(BF), high.astype(BF)
+
+
+def query_kernel(pos, out_grad, mix, query_t, *refs):
+    parts, (grads, buckets) = refs[:9], refs[9:]
+    for h, cols in heads():
+        gt = turned(out_grad[:, cols])
+        query = query_t[h]
+        for line in range(3):
+            three = (a[cols, :] for a in parts[3 * line : 3 * line + 3])
+            for j, bucket in enumerate(pair_of(pos[(Y, Z, X)[line]], *three), 2 * line):
+                buckets[j, cols, :] = bucket
+                row = mix[9 + j, h : h + 1, :] * scale_of(9 + j)
+                query = query + dot(bucket, (gt * row).astype(BF), ((1,), (0,)))
+        grads[0, :, cols] = (query * DH**-0.5).T.astype(BF)
+
+
+def read_kernel(proj, out_grad, mix, out_t, level_in, buckets, attended, level_out):
+    level_out[:9] = level_in[...]
     for h, cols in heads():
         qt = turned(proj[0, :, cols]).astype(BF)
         gt = turned(out_grad[:, cols])
-
-        def pair(p, *parts):
-            one, two, three = (a[cols, :].astype(F32) for a in parts)
-            low = one * flag((p == 1) | (p == 3))
-            high = one * flag(p == 2) + two * flag(p >= 2) + three * flag(p == 3)
-            return low.astype(BF), high.astype(BF)
-
-        buckets = (
-            pair(pos[Y], gy1, gy2, gy3) + pair(pos[Z], rz1, rz2, rz3) + pair(pos[X], gx1, gx2, gx3)
-        )
         total = out_t[h]
-        query = query_t[h]
-        level_out[h, :9, :] = level_in[h, :9, :]
-        for j, bucket in enumerate(buckets):
-            row = mix[h, 9 + j : 10 + j, :] * scale_of(9 + j)
-            reads = dot(bucket, qt, ((0,), (0,)))
+        for j in range(6):
+            row = mix[9 + j, h : h + 1, :] * scale_of(9 + j)
+            reads = dot(buckets[j, cols, :], qt, ((0,), (0,)))
             total = total + reads * row
-            level_out[h, 9 + j : 10 + j, :] = jnp.sum(
+            level_out[9 + j, h : h + 1, :] = jnp.sum(
                 reads * gt, axis=0, keepdims=True
             ) * scale_of(9 + j)
-            query = query + dot(bucket, (gt * row).astype(BF), ((1,), (0,)))
         attended[:, cols] = total.T.astype(BF)
-        grads[0, :, cols] = (query * DH**-0.5).T.astype(BF)
 
 
 def column_kernel(pos, hidden, other, c0, c1, c2, c3, whole):
@@ -268,7 +287,7 @@
     near_part = jnp.einsum("td,dme->mte", hidden, near, preferred_element_type=F32)
     far_part = jnp.einsum("td,dme->mte", other, far, preferred_element_type=F32)
     projected = ((near_part + far_part) * root).astype(BF)
-    mix = level_mix.transpose(1, 0, 2)
+    mix = level_mix
 
     own_columns, *far_columns = call(
         column_kernel,
@@ -302,8 +321,8 @@
         [projected, out_grad, mix],
         [shape((4, DH, 256), F32)] * 2
         + [shape((256, 512), F32)] * 2
-        + [shape((4, 16, 256), F32)],
-        scratch=[pltpu.VMEM((256, 256), jnp.int32)],
+        + [shape((9, 4, 256), F32)],
+        scratch=[pltpu.VMEM((DH, DH), jnp.int32)] + [pltpu.VMEM((256, 256), BF)] * 2,
     )
     p1, p2, p3, held = call(
         upper_kernel, [*rx, b2, b3], [state_shape] * 3 + [shape((512, DH), F32)], pos
@@ -321,13 +340,17 @@
     (grads[0],) = call(
         key_value_kernel, [projected, key_in, value_in, held, *ry], [shape((2, 256, 512), BF)]
     )
-    attended, grads[1], level_grad = call(
+    grads[1], buckets = call(
         query_kernel,
-        [projected, out_grad, mix, out_t, query_t, level_in, *gy, *rz, *gx],
-        [shape((256, 512), BF), shape((1, 256, 512), BF), shape((4, 15, 256), F32)],
+        [out_grad, mix, query_t, *gy, *rz, *gx],
+        [shape((1, 256, 512), BF), shape((6, 512, DH), BF)],
         pos,
     )
-    level_grad = level_grad.transpose(1, 0, 2)
+    attended, level_grad = call(
+        read_kernel,
+        [projected, out_grad, mix, out_t, level_in, buckets],
+        [shape((256, 512), BF), shape((15, 4, 256), F32)],
+    )
 
     grad_blocks = [[grads[0]], [grads[1]]]
     for i in (0, 1):

time: 121 us -> 118 us (0.975)
  starting transfers between devices: 55.4 us -> 54.1 us
    ppermute x36, starting transfers between devices: 55.3 us -> 53.9 us  [shifted(): return lax.ppermute(value, ALL, pairs)]
    pallas_call x12 -> x13, Pallas kernels: 11.1 us -> 10.2 us  [call(): return run(*([] if pos is None else [pos]), *held)]
  transfers between devices with their start and end apart: 38 -> 38, of which waited for: 11 -> 11; matrix products, arithmetic and copies ran while one was open for 10% -> 9% of each run, Pallas kernels for 8% -> 8%
where the time goes in v5:
time: 118 us; the launch traced here: 117 us
  starting transfers between devices  54.1 us (46%)
  waiting for transfers between devices  37.3 us (32%)
  matrix products  11.5 us (10%)
  Pallas kernels  10.2 us (9%)
  other arithmetic  1.76 us (1%)
  local copies, waits for them, and re-layouts  1.36 us (1%)
    ppermute x36, starting transfers between devices, shifted(): return lax.ppermute(value, ALL, pairs)  53.9 us
    ppermute x36, waiting for transfers between devices, shifted(): return lax.ppermute(value, ALL, pairs)  37.3 us
    pallas_call x13, Pallas kernels, call(): return run(*([] if pos is None else [pos]), *held)  10.2 us
    dot_general x8, matrix products, products(): jnp.einsum('td,mte->mde', h, g, preferred_element_type=F32)  3.43 us
    dot_general x1, matrix products, layer(): jnp.einsum('td,dme->mte', hidden, near, preferred_element_type=F32)  3.04 us
    dot_general x1, matrix products, layer(): far_part = jnp.einsum('td,dme->mte', other, far, preferred_element_type=F32)  3.03 us
  transfers between devices with their start and end apart: 38, of which 11 were waited for; matrix products, arithmetic and copies ran while one was open for 9% of the time, Pallas kernels for 8%

profile of v5, /device:TPU:0, one launch (start us, length us, event | category | flops | bytes accessed | tf_op | source)
XLA Modules:
  0.0 117.4 jit_solution(17067157058928832107)
XLA Ops:
  0.8 3.0 %fusion.4 = f32[3,512,256]{1,2,0:T(8,128)S(1)} fusion(bf16[2048,3,512]{2,0,1:T(8,128)(2,1)} %param.6, s32[]{:T(128)S(6)} %select_n.6, bf16[256,1024]{1,0:T(8,128)(2,1)} %hidden.1), kind=kOutput, calls=%fused_computation.4 | convolution fusion | flops 805306368 | bytes 5242884 | tf_op jit(solution)/shard_map/td,dme->mte/dot_general | solution.py:287
  3.9 3.0 %fusion.19.proj = bf16[3,256,512]{2,1,0:T(8,128)(2,1)S(1)} fusion(f32[3,512,256]{1,2,0:T(8,128)S(1)} %fusion.4, bf16[2048,3,512]{2,0,1:T(8,128)(2,1)} %param.6, s32[]{:T(128)S(6)} %select_n.7, f32[3]{0:T(128)S(1)} %copy-done.3, bf16[256,1024]{1,0:T(8,128)(2,1)S(1)} %collective-permute-done.other), kind=kOutput, calls=%fused_computation.16 | convolution fusion | flops 806486016 | bytes 6029328 | tf_op jit(solution)/shard_map/td,dme->mte/dot_general | solution.py:288
  7.0 1.3 %shard_map.85 = (bf16[512,128]{1,0:T(8,128)(2,1)S(1)}, bf16[512,128]{1,0:T(8,128)(2,1)S(1)}, bf16[512,128]{1,0:T(8,128)(2,1)S(1)}, bf16[512,128]{1,0:T(8,128)(2,...) custom-call(s32[4]{0:T(128)S(1)} %pad_add_fusion.pos, ...), custom_call_target="tpu_custom_call" | custom-call | tf_op jit(solution)/shard_map/pallas_call | solution.py:276
  8.3 3.2 %collective-permute-start.3 = (bf16[512,128]{1,0:T(8,128)(2,1)S(1)}, bf16[512,128]{1,0:T(8,128)(2,1)S(1)}, u32[]{:S(2)}, u32[]{:S(2)}) collective-permute-start(bf16[512,128]{1,0:T(8,128)(2,1)S(1)} %get-tuple-element.47.mine), channel_id=1, source_target_pairs={{0,6},{1,7},{2,0},{3,1},{4,2},{5,3},{6,4},{7,5},{8,14},{9,15},{10,... | collective-permute-start | bytes 393224 | tf_op jit(solution)/shard_map/ppermute | solution.py:46
  11.4 0.6 collective-permute-start.2
  12.1 1.0 collective-permute-start.1
  13.0 1.3 %collective-permute-start.12 = (bf16[512,128]{1,0:T(8,128)(2,1)S(1)}, bf16[512,128]{1,0:T(8,128)(2,1)S(1)}, u32[]{:S(2)}, u32[]{:S(2)}) collective-permute-start(bf16[512,128]{1,0:T(8,128)(2,1)S(1)} %get-tuple-element.54), channel_id=1, source_target_pairs={{32,0},{33,1},{34,2},{35,3},{36,4},{37,5},{38,6},{39,7},{40,8},{41... | collective-permute-start | bytes 393224 | tf_op jit(solution)/shard_map/ppermute | solution.py:46
  14.3 1.3 %collective-permute-start.11 = (bf16[512,128]{1,0:T(8,128)(2,1)S(1)}, bf16[512,128]{1,0:T(8,128)(2,1)S(1)}, u32[]{:S(2)}, u32[]{:S(2)}) collective-permute-start(bf16[512,128]{1,0:T(8,128)(2,1)S(1)} %get-tuple-element.53), channel_id=1, source_target_pairs={{64,0},{65,1},{66,2},{67,3},{68,4},{69,5},{70,6},{71,7},{72,8},{73... | collective-permute-start | bytes 393224 | tf_op jit(solution)/shard_map/ppermute | solution.py:46
  15.6 2.0 %collective-permute-done.3.a3.refs_2_ = bf16[512,128]{1,0:T(8,128)(2,1)S(1)} collective-permute-done((bf16[512,128]{1,0:T(8,128)(2,1)S(1)}, bf16[512,128]{1,0:T(8,128)(2,1)S(1)}, u32[]{:S(2)}, u32[]{:S(2)}) %collective-permute-start.3) | collective-permute-done | bytes 131104 | tf_op jit(solution)/shard_map/ppermute | solution.py:46
  17.7 1.3 %collective-permute-start.10 = (bf16[512,128]{1,0:T(8,128)(2,1)S(1)}, bf16[512,128]{1,0:T(8,128)(2,1)S(1)}, u32[]{:S(2)}, u32[]{:S(2)}) collective-permute-start(bf16[512,128]{1,0:T(8,128)(2,1)S(1)} %get-tuple-element.53), channel_id=1, source_target_pairs={{96,0},{97,1},{98,2},{99,3},{100,4},{101,5},{102,6},{103,7},{104,8... | collective-permute-start | bytes 393224 | tf_op jit(solution)/shard_map/ppermute | solution.py:46
  18.9 0.4 collective-permute-done.2.a2.refs_1_
  19.4 2.0 %collective-permute-done.1.a1.refs_0_ = bf16[512,128]{1,0:T(8,128)(2,1)S(1)} collective-permute-done((bf16[512,128]{1,0:T(8,128)(2,1)S(1)}, bf16[512,128]{1,0:T(8,128)(2,1)S(1)}, u32[]{:S(2)}, u32[]{:S(2)}) %collective-permute-start.1) | collective-permute-done | bytes 131104 | tf_op jit(solution)/shard_map/ppermute | solution.py:46
  21.4 4.1 %collective-permute-start.6 = (bf16[512,128]{1,0:T(8,128)(2,1)S(1)}, bf16[512,128]{1,0:T(8,128)(2,1)S(1)}, u32[]{:S(2)}, u32[]{:S(2)}) collective-permute-start(bf16[512,128]{1,0:T(8,128)(2,1)S(1)} %shard_map.86.mine), channel_id=1, source_target_pairs={{0,24},{1,25},{2,26},{3,27},{4,28},{5,29},{6,30},{7,31},{8,0},{9,1... | collective-permute-start | bytes 393224 | tf_op jit(solution)/shard_map/ppermute | solution.py:46
  25.6 1.3 %collective-permute-start.4 = (bf16[512,128]{1,0:T(8,128)(2,1)S(1)}, bf16[512,128]{1,0:T(8,128)(2,1)S(1)}, u32[]{:S(2)}, u32[]{:S(2)}) collective-permute-start(bf16[512,128]{1,0:T(8,128)(2,1)S(1)} %shard_map.86.mine), channel_id=1, source_target_pairs={{0,8},{1,9},{2,10},{3,11},{4,12},{5,13},{6,14},{7,15},{8,16},{9,17... | collective-permute-start | bytes 393224 | tf_op jit(solution)/shard_map/ppermute | solution.py:46
  26.8 0.7 shard_map.90
  27.5 2.3 %collective-permute-start.13 = (bf16[512,128]{1,0:T(8,128)(2,1)S(1)}, bf16[512,128]{1,0:T(8,128)(2,1)S(1)}, u32[]{:S(2)}, u32[]{:S(2)}) collective-permute-start(bf16[512,128]{1,0:T(8,128)(2,1)S(1)} %get-tuple-element.57), channel_id=1, source_target_pairs={{0,8},{1,9},{2,10},{3,11},{4,12},{5,13},{6,14},{7,15},{8,16},{9,17... | collective-permute-start | bytes 393224 | tf_op jit(solution)/shard_map/ppermute | solution.py:46
  29.8 2.3 %collective-permute-start.14 = (bf16[512,128]{1,0:T(8,128)(2,1)S(1)}, bf16[512,128]{1,0:T(8,128)(2,1)S(1)}, u32[]{:S(2)}, u32[]{:S(2)}) collective-permute-start(bf16[512,128]{1,0:T(8,128)(2,1)S(1)} %get-tuple-element.58), channel_id=1, source_target_pairs={{0,16},{1,17},{2,18},{3,19},{4,20},{5,21},{6,22},{7,23},{8,24},{9,... | collective-permute-start | bytes 393224 | tf_op jit(solution)/shard_map/ppermute | solution.py:46
  32.1 2.1 %collective-permute-done.6.a3.refs_5_ = bf16[512,128]{1,0:T(8,128)(2,1)S(1)} collective-permute-done((bf16[512,128]{1,0:T(8,128)(2,1)S(1)}, bf16[512,128]{1,0:T(8,128)(2,1)S(1)}, u32[]{:S(2)}, u32[]{:S(2)}) %collective-permute-start.6) | collective-permute-done | bytes 131104 | tf_op jit(solution)/shard_map/ppermute | solution.py:46
  34.1 3.7 %collective-permute-start.15 = (bf16[512,128]{1,0:T(8,128)(2,1)S(1)}, bf16[512,128]{1,0:T(8,128)(2,1)S(1)}, u32[]{:S(2)}, u32[]{:S(2)}) collective-permute-start(bf16[512,128]{1,0:T(8,128)(2,1)S(1)} %get-tuple-element.59), channel_id=1, source_target_pairs={{0,24},{1,25},{2,26},{3,27},{4,28},{5,29},{6,30},{7,31},{8,0},{9,1... | collective-permute-start | bytes 393224 | tf_op jit(solution)/shard_map/ppermute | solution.py:46
  37.9 4.7 %collective-permute-start.9 = (bf16[512,128]{1,0:T(8,128)(2,1)S(1)}, bf16[512,128]{1,0:T(8,128)(2,1)S(1)}, u32[]{:S(2)}, u32[]{:S(2)}) collective-permute-start(bf16[512,128]{1,0:T(8,128)(2,1)S(1)} %shard_map.87), channel_id=1, source_target_pairs={{0,96},{1,97},{2,98},{3,99},{4,100},{5,101},{6,102},{7,103},{8,104... | collective-permute-start | bytes 393224 | tf_op jit(solution)/shard_map/ppermute | solution.py:46
  42.6 1.3 %collective-permute-start.8 = (bf16[512,128]{1,0:T(8,128)(2,1)S(1)}, bf16[512,128]{1,0:T(8,128)(2,1)S(1)}, u32[]{:S(2)}, u32[]{:S(2)}) collective-permute-start(bf16[512,128]{1,0:T(8,128)(2,1)S(1)} %shard_map.87), channel_id=1, source_target_pairs={{0,64},{1,65},{2,66},{3,67},{4,68},{5,69},{6,70},{7,71},{8,72},{9,... | collective-permute-start | bytes 393224 | tf_op jit(solution)/shard_map/ppermute | solution.py:46
  43.9 2.8 %collective-permute-start.7 = (bf16[512,128]{1,0:T(8,128)(2,1)S(1)}, bf16[512,128]{1,0:T(8,128)(2,1)S(1)}, u32[]{:S(2)}, u32[]{:S(2)}) collective-permute-start(bf16[512,128]{1,0:T(8,128)(2,1)S(1)} %shard_map.87), channel_id=1, source_target_pairs={{0,32},{1,33},{2,34},{3,35},{4,36},{5,37},{6,38},{7,39},{8,40},{9,... | collective-permute-start | bytes 393224 | tf_op jit(solution)/shard_map/ppermute | solution.py:46
  46.7 0.7 shard_map.91
  47.5 1.8 %collective-permute-start.17 = (bf16[512,128]{1,0:T(8,128)(2,1)S(1)}, bf16[512,128]{1,0:T(8,128)(2,1)S(1)}, u32[]{:S(2)}, u32[]{:S(2)}) collective-permute-start(bf16[512,128]{1,0:T(8,128)(2,1)S(1)} %get-tuple-element.65), channel_id=1, source_target_pairs={{0,4},{1,5},{2,6},{3,7},{4,0},{5,1},{6,2},{7,3},{8,12},{9,13},{10,... | collective-permute-start | bytes 393224 | tf_op jit(solution)/shard_map/ppermute | solution.py:46
  49.2 1.5 %collective-permute-start.18 = (bf16[512,128]{1,0:T(8,128)(2,1)S(1)}, bf16[512,128]{1,0:T(8,128)(2,1)S(1)}, u32[]{:S(2)}, u32[]{:S(2)}) collective-permute-start(bf16[512,128]{1,0:T(8,128)(2,1)S(1)} %get-tuple-element.66), channel_id=1, source_target_pairs={{0,6},{1,7},{2,0},{3,1},{4,2},{5,3},{6,4},{7,5},{8,14},{9,15},{10,... | collective-permute-start | bytes 393224 | tf_op jit(solution)/shard_map/ppermute | solution.py:46
  50.7 1.9 %shard_map.84 = (f32[4,128,256]{2,1,0:T(8,128)S(1)}, f32[4,128,256]{2,1,0:T(8,128)S(1)}, f32[256,512]{1,0:T(8,128)S(1)}, f32[256,512]{1,0:T(8,128)S(1)}, f32[9,4,256]{2,1,0:T(4,128)S(1)}) custom-call(bf16[3,256,512]{2,1,0:T(8,128)(2,1)S(1)} %fusion.19.proj, bf16[256,512]{1,0:T(8,128)(2,1)S(1)} %copy-done, f32[15,4,256]{2,1,0:T(4,128)S(1)} %copy-done.2), custom_call_target="tpu_custom_call" | custom-call | tf_op jit(solution)/shard_map/pallas_call | solution.py:276
  52.7 0.7 shard_map.93
  53.5 2.5 %collective-permute-start.23 = (bf16[256,512]{1,0:T(8,128)(2,1)S(1)}, bf16[256,512]{1,0:T(8,128)(2,1)S(1)}, u32[]{:S(2)}, u32[]{:S(2)}) collective-permute-start(bf16[256,512]{1,0:T(8,128)(2,1)S(1)} %get-tuple-element.69), channel_id=1, source_target_pairs={{0,64},{1,5},{2,66},{3,7},{4,68},{5,1},{6,70},{7,3},{8,72},{9,13},... | collective-permute-start | bytes 786440 | tf_op jit(solution)/shard_map/ppermute | solution.py:46
  55.9 1.4 %shard_map.88 = (bf16[1,256,512]{2,1,0:T(8,128)(2,1)S(1)}, bf16[6,512,128]{2,1,0:T(8,128)(2,1)S(1)}) custom-call(s32[4]{0:T(128)S(1)} %pad_add_fusion.pos, bf16[256,512]{1,0:T(8,128)(2,1)S(1)} %copy-done, f32[15,4,256]{2,1,0:T(4,128)S(1)} %copy-done.2, f32[4,128,256]{2,1,0:T(8,128)S(1)} %get-tuple-element.46.query_t, ...), custom_call_target="tpu_custom_call" | custom-call | tf_op jit(solution)/shard_map/pallas_call | solution.py:276
  57.3 1.0 collective-permute-start.25
  58.3 1.0 collective-permute-start.24
  59.3 1.1 collective-permute-start.20
  60.7 1.0 fusion.13
  61.7 0.5 fusion.32
  62.2 1.6 %collective-permute-done.21 = bf16[256,512]{1,0:T(8,128)(2,1)S(1)} collective-permute-done((bf16[256,512]{1,0:T(8,128)(2,1)S(1)}, bf16[256,512]{1,0:T(8,128)(2,1)S(1)}, u32[]{:S(2)}, u32[]{:S(2)}) %collective-permute-start.21) | collective-permute-done | bytes 262176 | tf_op jit(solution)/shard_map/ppermute | solution.py:46
  63.8 1.4 %collective-permute-start.22 = (bf16[1,256,512]{2,1,0:T(8,128)(2,1)S(1)}, bf16[1,256,512]{2,1,0:T(8,128)(2,1)S(1)}, u32[]{:S(2)}, u32[]{:S(2)}) collective-permute-start(bf16[1,256,512]{2,1,0:T(8,128)(2,1)S(1)} %get-tuple-element.50), channel_id=1, source_target_pairs={{0,64},{1,5},{2,66},{3,7},{4,68},{5,1},{6,70},{7,3},{8,72},{9,13},... | collective-permute-start | bytes 786440 | tf_op jit(solution)/shard_map/ppermute | solution.py:46
  65.2 1.7 %collective-permute-done.20 = bf16[1,256,512]{2,1,0:T(8,128)(2,1)S(1)} collective-permute-done((bf16[1,256,512]{2,1,0:T(8,128)(2,1)S(1)}, bf16[1,256,512]{2,1,0:T(8,128)(2,1)S(1)}, u32[]{:S(2)}, u32[]{:S(2)}) %collective-permute-start.20) | collective-permute-done | bytes 262176 | tf_op jit(solution)/shard_map/ppermute | solution.py:46
  66.9 1.3 %collective-permute-start.28 = (bf16[2,256,512]{2,1,0:T(8,128)(2,1)S(1)}, bf16[2,256,512]{2,1,0:T(8,128)(2,1)S(1)}, u32[]{:S(2)}, u32[]{:S(2)}) collective-permute-start(bf16[2,256,512]{2,1,0:T(8,128)(2,1)S(1)} %shard_map.92), channel_id=1, source_target_pairs={{0,96},{1,7},{2,98},{3,1},{4,100},{5,3},{6,102},{7,5},{8,104},{9,1... | collective-permute-start | bytes 1572872 | tf_op jit(solution)/shard_map/ppermute | solution.py:46
  68.5 0.7 collective-permute-start.27
  69.2 2.5 %collective-permute-done.22 = bf16[1,256,512]{2,1,0:T(8,128)(2,1)S(1)} collective-permute-done((bf16[1,256,512]{2,1,0:T(8,128)(2,1)S(1)}, bf16[1,256,512]{2,1,0:T(8,128)(2,1)S(1)}, u32[]{:S(2)}, u32[]{:S(2)}) %collective-permute-start.22) | collective-permute-done | bytes 262176 | tf_op jit(solution)/shard_map/ppermute | solution.py:46
  71.7 0.3 fusion.36
  72.5 0.4 fusion.18.product
  72.9 0.6 shard_map.94
  73.6 5.8 %collective-permute-done.27 = bf16[2,256,512]{2,1,0:T(8,128)(2,1)S(1)} collective-permute-done((bf16[2,256,512]{2,1,0:T(8,128)(2,1)S(1)}, bf16[2,256,512]{2,1,0:T(8,128)(2,1)S(1)}, u32[]{:S(2)}, u32[]{:S(2)}) %collective-permute-start.27) | collective-permute-done | bytes 524320 | tf_op jit(solution)/shard_map/ppermute | solution.py:46
  79.4 0.5 fusion.28
  79.9 9.7 %collective-permute-done.26 = bf16[2,256,512]{2,1,0:T(8,128)(2,1)S(1)} collective-permute-done((bf16[2,256,512]{2,1,0:T(8,128)(2,1)S(1)}, bf16[2,256,512]{2,1,0:T(8,128)(2,1)S(1)}, u32[]{:S(2)}, u32[]{:S(2)}) %collective-permute-start.26) | collective-permute-done | bytes 524320 | tf_op jit(solution)/shard_map/ppermute | solution.py:46
  89.6 0.5 fusion.30
  90.0 0.6 add_bitcast_fusion.product
  90.7 0.7 shard_map.95
  91.4 1.3 %collective-permute-start.33 = (bf16[2,128,512]{2,1,0:T(8,128)(2,1)S(1)}, bf16[2,128,512]{2,1,0:T(8,128)(2,1)S(1)}, u32[]{:S(2)}, u32[]{:S(2)}) collective-permute-start(bf16[2,128,512]{2,1,0:T(8,128)(2,1)S(1)} %get-tuple-element.77), channel_id=1, source_target_pairs={{0,16},{1,65},{2,18},{3,67},{4,20},{5,69},{6,22},{7,71},{8,24},{9,... | collective-permute-start | bytes 786440 | tf_op jit(solution)/shard_map/ppermute | solution.py:46
  92.8 1.9 %collective-permute-start.34 = (bf16[2,128,512]{2,1,0:T(8,128)(2,1)S(1)}, bf16[2,128,512]{2,1,0:T(8,128)(2,1)S(1)}, u32[]{:S(2)}, u32[]{:S(2)}) collective-permute-start(bf16[2,128,512]{2,1,0:T(8,128)(2,1)S(1)} %get-tuple-element.78), channel_id=1, source_target_pairs={{0,24},{1,97},{2,26},{3,99},{4,28},{5,101},{6,30},{7,103},{8,0},{9... | collective-permute-start | bytes 786440 | tf_op jit(solution)/shard_map/ppermute | solution.py:46
  94.7 0.9 collective-permute-start.31
  95.6 1.0 shard_map.89
  96.6 0.7 copy.45
  97.3 0.6 copy.46
  98.0 8.3 %collective-permute-done.31.a3 = bf16[1,128,512]{2,1,0:T(8,128)(2,1)S(1)} collective-permute-done((bf16[1,128,512]{2,1,0:T(8,128)(2,1)S(1)}, bf16[1,128,512]{2,1,0:T(8,128)(2,1)S(1)}, u32[]{:S(2)}, u32[]{:S(2)}) %collective-permute-start.31) | collective-permute-done | bytes 131104 | tf_op jit(solution)/shard_map/ppermute | solution.py:46
  106.3 0.8 shard_map.96
  107.1 0.7 collective-permute-start.35
  107.8 3.1 %collective-permute-start.36 = (bf16[3,32,512]{2,1,0:T(8,128)(2,1)S(1)}, bf16[3,32,512]{2,1,0:T(8,128)(2,1)S(1)}, u32[]{:S(2)}, u32[]{:S(2)}) collective-permute-start(bf16[3,32,512]{2,1,0:T(8,128)(2,1)S(1)} %get-tuple-element.81), channel_id=1, source_target_pairs={{0,4},{1,17},{2,6},{3,19},{4,0},{5,21},{6,2},{7,23},{8,12},{9,25},... | collective-permute-start | bytes 294920 | tf_op jit(solution)/shard_map/ppermute | solution.py:46
  110.9 2.5 %collective-permute-start.37 = (bf16[3,32,512]{2,1,0:T(8,128)(2,1)S(1)}, bf16[3,32,512]{2,1,0:T(8,128)(2,1)S(1)}, u32[]{:S(2)}, u32[]{:S(2)}) collective-permute-start(bf16[3,32,512]{2,1,0:T(8,128)(2,1)S(1)} %get-tuple-element.82), channel_id=1, source_target_pairs={{0,6},{1,25},{2,0},{3,27},{4,2},{5,29},{6,4},{7,31},{8,14},{9,1},{... | collective-permute-start | bytes 294920 | tf_op jit(solution)/shard_map/ppermute | solution.py:46
  113.5 1.0 fusion.10
  114.5 1.2 %collective-permute-done.37 = bf16[3,32,512]{2,1,0:T(8,128)(2,1)S(1)} collective-permute-done((bf16[3,32,512]{2,1,0:T(8,128)(2,1)S(1)}, bf16[3,32,512]{2,1,0:T(8,128)(2,1)S(1)}, u32[]{:S(2)}, u32[]{:S(2)}) %collective-permute-start.37) | collective-permute-done | bytes 98336 | tf_op jit(solution)/shard_map/ppermute | solution.py:46
  115.7 0.7 multiply_bitcast_fusion
  116.4 0.9 add_convert_fusion
  (55 shorter events, 1.8 us)
Async XLA Ops:
  0.6 3.3 %collective-permute-start = (bf16[256,1024]{1,0:T(8,128)(2,1)}, bf16[256,1024]{1,0:T(8,128)(2,1)S(1)}, u32[]{:S(2)}, u32[]{:S(2)}) collective-permute-start(bf16[256,1024]{1,0:T(8,128)(2,1)} %hidden.1), channel_id=1, source_target_pairs={{0,1},{1,0},{2,3},{3,2},{4,5},{5,4},{6,7},{7,6},{8,9},{9,8},{10,11... | collective-permute-start | bytes 1572872 | tf_op jit(solution)/shard_map/ppermute | solution.py:50
  0.8 3.1 %copy-start.3 = (f32[3]{0:T(128)S(1)}, f32[3]{0:T(128)}, u32[]{:S(2)}) copy-start(f32[3]{0:T(128)} %constant.27.clone) | copy-start | bytes 40
  3.9 3.1 %copy-start = (bf16[256,512]{1,0:T(8,128)(2,1)S(1)}, bf16[256,512]{1,0:T(8,128)(2,1)}, u32[]{:S(2)}) copy-start(bf16[256,512]{1,0:T(8,128)(2,1)} %out_grad.3) | copy-start | bytes 786436
  3.9 3.1 %copy-start.2 = (f32[15,4,256]{2,1,0:T(4,128)S(1)}, f32[15,4,256]{2,1,0:T(4,128)}, u32[]{:S(2)}) copy-start(f32[15,4,256]{2,1,0:T(4,128)} %mix.7) | copy-start | bytes 184324
  3.9 56.8 %slice-start = ((s8[6291456]{0:T(1024)(128)(4,1)}), s8[4194304]{0:T(1024)(128)(4,1)S(1)}, s32[]{:S(2)}) async-start(s8[6291456]{0:T(1024)(128)(4,1)} %bitcast.58), calls=%async_computation | async-start | bytes 8388608
  8.2 44.4 %copy-start.1 = (bf16[256,1024]{1,0:T(8,128)(2,1)S(1)}, bf16[256,1024]{1,0:T(8,128)(2,1)}, u32[]{:S(2)}) copy-start(bf16[256,1024]{1,0:T(8,128)(2,1)} %hidden.1) | copy-start | bytes 1572868
  8.3 9.4 %collective-permute-start.3 = (bf16[512,128]{1,0:T(8,128)(2,1)S(1)}, bf16[512,128]{1,0:T(8,128)(2,1)S(1)}, u32[]{:S(2)}, u32[]{:S(2)}) collective-permute-start(bf16[512,128]{1,0:T(8,128)(2,1)S(1)} %get-tuple-element.47.mine), channel_id=1, source_target_pairs={{0,6},{1,7},{2,0},{3,1},{4,2},{5,3},{6,4},{7,5},{8,14},{9,15},{10,... | collective-permute-start | bytes 393224 | tf_op jit(solution)/shard_map/ppermute | solution.py:46
  11.4 7.9 %collective-permute-start.2 = (bf16[512,128]{1,0:T(8,128)(2,1)S(1)}, bf16[512,128]{1,0:T(8,128)(2,1)S(1)}, u32[]{:S(2)}, u32[]{:S(2)}) collective-permute-start(bf16[512,128]{1,0:T(8,128)(2,1)S(1)} %get-tuple-element.47.mine), channel_id=1, source_target_pairs={{0,4},{1,5},{2,6},{3,7},{4,0},{5,1},{6,2},{7,3},{8,12},{9,13},{10,... | collective-permute-start | bytes 393224 | tf_op jit(solution)/shard_map/ppermute | solution.py:46
  12.1 9.3 %collective-permute-start.1 = (bf16[512,128]{1,0:T(8,128)(2,1)S(1)}, bf16[512,128]{1,0:T(8,128)(2,1)S(1)}, u32[]{:S(2)}, u32[]{:S(2)}) collective-permute-start(bf16[512,128]{1,0:T(8,128)(2,1)S(1)} %get-tuple-element.47.mine), channel_id=1, source_target_pairs={{0,2},{1,3},{2,4},{3,5},{4,6},{5,7},{6,0},{7,1},{8,10},{9,11},{10,... | collective-permute-start | bytes 393224 | tf_op jit(solution)/shard_map/ppermute | solution.py:46
  13.0 12.5 %collective-permute-start.12 = (bf16[512,128]{1,0:T(8,128)(2,1)S(1)}, bf16[512,128]{1,0:T(8,128)(2,1)S(1)}, u32[]{:S(2)}, u32[]{:S(2)}) collective-permute-start(bf16[512,128]{1,0:T(8,128)(2,1)S(1)} %get-tuple-element.54), channel_id=1, source_target_pairs={{32,0},{33,1},{34,2},{35,3},{36,4},{37,5},{38,6},{39,7},{40,8},{41... | collective-permute-start | bytes 393224 | tf_op jit(solution)/shard_map/ppermute | solution.py:46
  14.3 12.5 %collective-permute-start.11 = (bf16[512,128]{1,0:T(8,128)(2,1)S(1)}, bf16[512,128]{1,0:T(8,128)(2,1)S(1)}, u32[]{:S(2)}, u32[]{:S(2)}) collective-permute-start(bf16[512,128]{1,0:T(8,128)(2,1)S(1)} %get-tuple-element.53), channel_id=1, source_target_pairs={{64,0},{65,1},{66,2},{67,3},{68,4},{69,5},{70,6},{71,7},{72,8},{73... | collective-permute-start | bytes 393224 | tf_op jit(solution)/shard_map/ppermute | solution.py:46
  17.7 9.2 %collective-permute-start.10 = (bf16[512,128]{1,0:T(8,128)(2,1)S(1)}, bf16[512,128]{1,0:T(8,128)(2,1)S(1)}, u32[]{:S(2)}, u32[]{:S(2)}) collective-permute-start(bf16[512,128]{1,0:T(8,128)(2,1)S(1)} %get-tuple-element.53), channel_id=1, source_target_pairs={{96,0},{97,1},{98,2},{99,3},{100,4},{101,5},{102,6},{103,7},{104,8... | collective-permute-start | bytes 393224 | tf_op jit(solution)/shard_map/ppermute | solution.py:46
  21.4 12.7 %collective-permute-start.6 = (bf16[512,128]{1,0:T(8,128)(2,1)S(1)}, bf16[512,128]{1,0:T(8,128)(2,1)S(1)}, u32[]{:S(2)}, u32[]{:S(2)}) collective-permute-start(bf16[512,128]{1,0:T(8,128)(2,1)S(1)} %shard_map.86.mine), channel_id=1, source_target_pairs={{0,24},{1,25},{2,26},{3,27},{4,28},{5,29},{6,30},{7,31},{8,0},{9,1... | collective-permute-start | bytes 393224 | tf_op jit(solution)/shard_map/ppermute | solution.py:46
  25.5 12.3 %collective-permute-start.5 = (bf16[512,128]{1,0:T(8,128)(2,1)S(1)}, bf16[512,128]{1,0:T(8,128)(2,1)S(1)}, u32[]{:S(2)}, u32[]{:S(2)}) collective-permute-start(bf16[512,128]{1,0:T(8,128)(2,1)S(1)} %shard_map.86.mine), channel_id=1, source_target_pairs={{0,16},{1,17},{2,18},{3,19},{4,20},{5,21},{6,22},{7,23},{8,24},{9,... | collective-permute-start | bytes 393224 | tf_op jit(solution)/shard_map/ppermute | solution.py:46
  25.6 12.2 %collective-permute-start.4 = (bf16[512,128]{1,0:T(8,128)(2,1)S(1)}, bf16[512,128]{1,0:T(8,128)(2,1)S(1)}, u32[]{:S(2)}, u32[]{:S(2)}) collective-permute-start(bf16[512,128]{1,0:T(8,128)(2,1)S(1)} %shard_map.86.mine), channel_id=1, source_target_pairs={{0,8},{1,9},{2,10},{3,11},{4,12},{5,13},{6,14},{7,15},{8,16},{9,17... | collective-permute-start | bytes 393224 | tf_op jit(solution)/shard_map/ppermute | solution.py:46
  27.5 16.3 %collective-permute-start.13 = (bf16[512,128]{1,0:T(8,128)(2,1)S(1)}, bf16[512,128]{1,0:T(8,128)(2,1)S(1)}, u32[]{:S(2)}, u32[]{:S(2)}) collective-permute-start(bf16[512,128]{1,0:T(8,128)(2,1)S(1)} %get-tuple-element.57), channel_id=1, source_target_pairs={{0,8},{1,9},{2,10},{3,11},{4,12},{5,13},{6,14},{7,15},{8,16},{9,17... | collective-permute-start | bytes 393224 | tf_op jit(solution)/shard_map/ppermute | solution.py:46
  29.8 16.8 %collective-permute-start.14 = (bf16[512,128]{1,0:T(8,128)(2,1)S(1)}, bf16[512,128]{1,0:T(8,128)(2,1)S(1)}, u32[]{:S(2)}, u32[]{:S(2)}) collective-permute-start(bf16[512,128]{1,0:T(8,128)(2,1)S(1)} %get-tuple-element.58), channel_id=1, source_target_pairs={{0,16},{1,17},{2,18},{3,19},{4,20},{5,21},{6,22},{7,23},{8,24},{9,... | collective-permute-start | bytes 393224 | tf_op jit(solution)/shard_map/ppermute | solution.py:46
  34.1 26.5 %slice-start.1 = ((s8[6291456]{0:T(1024)(128)(4,1)}), s8[2097152]{0:T(1024)(128)(4,1)S(1)}, s32[]{:S(2)}) async-start(s8[6291456]{0:T(1024)(128)(4,1)} %bitcast.58), calls=%async_computation.1 | async-start | bytes 4194304
  34.1 12.5 %collective-permute-start.15 = (bf16[512,128]{1,0:T(8,128)(2,1)S(1)}, bf16[512,128]{1,0:T(8,128)(2,1)S(1)}, u32[]{:S(2)}, u32[]{:S(2)}) collective-permute-start(bf16[512,128]{1,0:T(8,128)(2,1)S(1)} %get-tuple-element.59), channel_id=1, source_target_pairs={{0,24},{1,25},{2,26},{3,27},{4,28},{5,29},{6,30},{7,31},{8,0},{9,1... | collective-permute-start | bytes 393224 | tf_op jit(solution)/shard_map/ppermute | solution.py:46
  37.9 11.4 %collective-permute-start.9 = (bf16[512,128]{1,0:T(8,128)(2,1)S(1)}, bf16[512,128]{1,0:T(8,128)(2,1)S(1)}, u32[]{:S(2)}, u32[]{:S(2)}) collective-permute-start(bf16[512,128]{1,0:T(8,128)(2,1)S(1)} %shard_map.87), channel_id=1, source_target_pairs={{0,96},{1,97},{2,98},{3,99},{4,100},{5,101},{6,102},{7,103},{8,104... | collective-permute-start | bytes 393224 | tf_op jit(solution)/shard_map/ppermute | solution.py:46
  42.6 10.8 %collective-permute-start.8 = (bf16[512,128]{1,0:T(8,128)(2,1)S(1)}, bf16[512,128]{1,0:T(8,128)(2,1)S(1)}, u32[]{:S(2)}, u32[]{:S(2)}) collective-permute-start(bf16[512,128]{1,0:T(8,128)(2,1)S(1)} %shard_map.87), channel_id=1, source_target_pairs={{0,64},{1,65},{2,66},{3,67},{4,68},{5,69},{6,70},{7,71},{8,72},{9,... | collective-permute-start | bytes 393224 | tf_op jit(solution)/shard_map/ppermute | solution.py:46
  43.9 9.6 %collective-permute-start.7 = (bf16[512,128]{1,0:T(8,128)(2,1)S(1)}, bf16[512,128]{1,0:T(8,128)(2,1)S(1)}, u32[]{:S(2)}, u32[]{:S(2)}) collective-permute-start(bf16[512,128]{1,0:T(8,128)(2,1)S(1)} %shard_map.87), channel_id=1, source_target_pairs={{0,32},{1,33},{2,34},{3,35},{4,36},{5,37},{6,38},{7,39},{8,40},{9,... | collective-permute-start | bytes 393224 | tf_op jit(solution)/shard_map/ppermute | solution.py:46
  47.4 9.9 %collective-permute-start.16 = (bf16[512,128]{1,0:T(8,128)(2,1)S(1)}, bf16[512,128]{1,0:T(8,128)(2,1)S(1)}, u32[]{:S(2)}, u32[]{:S(2)}) collective-permute-start(bf16[512,128]{1,0:T(8,128)(2,1)S(1)} %get-tuple-element.64), channel_id=1, source_target_pairs={{0,2},{1,3},{2,4},{3,5},{4,6},{5,7},{6,0},{7,1},{8,10},{9,11},{10,... | collective-permute-start | bytes 393224 | tf_op jit(solution)/shard_map/ppermute | solution.py:46
  47.5 10.9 %collective-permute-start.17 = (bf16[512,128]{1,0:T(8,128)(2,1)S(1)}, bf16[512,128]{1,0:T(8,128)(2,1)S(1)}, u32[]{:S(2)}, u32[]{:S(2)}) collective-permute-start(bf16[512,128]{1,0:T(8,128)(2,1)S(1)} %get-tuple-element.65), channel_id=1, source_target_pairs={{0,4},{1,5},{2,6},{3,7},{4,0},{5,1},{6,2},{7,3},{8,12},{9,13},{10,... | collective-permute-start | bytes 393224 | tf_op jit(solution)/shard_map/ppermute | solution.py:46
  49.2 10.1 %collective-permute-start.18 = (bf16[512,128]{1,0:T(8,128)(2,1)S(1)}, bf16[512,128]{1,0:T(8,128)(2,1)S(1)}, u32[]{:S(2)}, u32[]{:S(2)}) collective-permute-start(bf16[512,128]{1,0:T(8,128)(2,1)S(1)} %get-tuple-element.66), channel_id=1, source_target_pairs={{0,6},{1,7},{2,0},{3,1},{4,2},{5,3},{6,4},{7,5},{8,14},{9,15},{10,... | collective-permute-start | bytes 393224 | tf_op jit(solution)/shard_map/ppermute | solution.py:46
  53.4 10.5 %collective-permute-start.21 = (bf16[256,512]{1,0:T(8,128)(2,1)S(1)}, bf16[256,512]{1,0:T(8,128)(2,1)S(1)}, u32[]{:S(2)}, u32[]{:S(2)}) collective-permute-start(bf16[256,512]{1,0:T(8,128)(2,1)S(1)} %get-tuple-element.68), channel_id=1, source_target_pairs={{0,32},{1,3},{2,34},{3,5},{4,36},{5,7},{6,38},{7,1},{8,40},{9,11},... | collective-permute-start | bytes 786440 | tf_op jit(solution)/shard_map/ppermute | solution.py:46
  53.5 15.1 %collective-permute-start.23 = (bf16[256,512]{1,0:T(8,128)(2,1)S(1)}, bf16[256,512]{1,0:T(8,128)(2,1)S(1)}, u32[]{:S(2)}, u32[]{:S(2)}) collective-permute-start(bf16[256,512]{1,0:T(8,128)(2,1)S(1)} %get-tuple-element.69), channel_id=1, source_target_pairs={{0,64},{1,5},{2,66},{3,7},{4,68},{5,1},{6,70},{7,3},{8,72},{9,13},... | collective-permute-start | bytes 786440 | tf_op jit(solution)/shard_map/ppermute | solution.py:46
  57.3 14.7 %collective-permute-start.25 = (bf16[256,512]{1,0:T(8,128)(2,1)S(1)}, bf16[256,512]{1,0:T(8,128)(2,1)S(1)}, u32[]{:S(2)}, u32[]{:S(2)}) collective-permute-start(bf16[256,512]{1,0:T(8,128)(2,1)S(1)} %get-tuple-element.70), channel_id=1, source_target_pairs={{0,96},{1,7},{2,98},{3,1},{4,100},{5,3},{6,102},{7,5},{8,104},{9,1... | collective-permute-start | bytes 786440 | tf_op jit(solution)/shard_map/ppermute | solution.py:46
  58.3 13.8 %collective-permute-start.24 = (bf16[1,256,512]{2,1,0:T(8,128)(2,1)S(1)}, bf16[1,256,512]{2,1,0:T(8,128)(2,1)S(1)}, u32[]{:S(2)}, u32[]{:S(2)}) collective-permute-start(bf16[1,256,512]{2,1,0:T(8,128)(2,1)S(1)} %get-tuple-element.50), channel_id=1, source_target_pairs={{0,96},{1,7},{2,98},{3,1},{4,100},{5,3},{6,102},{7,5},{8,104},{9,1... | collective-permute-start | bytes 786440 | tf_op jit(solution)/shard_map/ppermute | solution.py:46
  59.3 7.6 %collective-permute-start.20 = (bf16[1,256,512]{2,1,0:T(8,128)(2,1)S(1)}, bf16[1,256,512]{2,1,0:T(8,128)(2,1)S(1)}, u32[]{:S(2)}, u32[]{:S(2)}) collective-permute-start(bf16[1,256,512]{2,1,0:T(8,128)(2,1)S(1)} %get-tuple-element.50), channel_id=1, source_target_pairs={{0,32},{1,3},{2,34},{3,5},{4,36},{5,7},{6,38},{7,1},{8,40},{9,11},... | collective-permute-start | bytes 786440 | tf_op jit(solution)/shard_map/ppermute | solution.py:46
  63.8 7.9 %collective-permute-start.22 = (bf16[1,256,512]{2,1,0:T(8,128)(2,1)S(1)}, bf16[1,256,512]{2,1,0:T(8,128)(2,1)S(1)}, u32[]{:S(2)}, u32[]{:S(2)}) collective-permute-start(bf16[1,256,512]{2,1,0:T(8,128)(2,1)S(1)} %get-tuple-element.50), channel_id=1, source_target_pairs={{0,64},{1,5},{2,66},{3,7},{4,68},{5,1},{6,70},{7,3},{8,72},{9,13},... | collective-permute-start | bytes 786440 | tf_op jit(solution)/shard_map/ppermute | solution.py:46
  66.9 23.2 %collective-permute-start.28 = (bf16[2,256,512]{2,1,0:T(8,128)(2,1)S(1)}, bf16[2,256,512]{2,1,0:T(8,128)(2,1)S(1)}, u32[]{:S(2)}, u32[]{:S(2)}) collective-permute-start(bf16[2,256,512]{2,1,0:T(8,128)(2,1)S(1)} %shard_map.92), channel_id=1, source_target_pairs={{0,96},{1,7},{2,98},{3,1},{4,100},{5,3},{6,102},{7,5},{8,104},{9,1... | collective-permute-start | bytes 1572872 | tf_op jit(solution)/shard_map/ppermute | solution.py:46
  68.5 10.9 %collective-permute-start.27 = (bf16[2,256,512]{2,1,0:T(8,128)(2,1)S(1)}, bf16[2,256,512]{2,1,0:T(8,128)(2,1)S(1)}, u32[]{:S(2)}, u32[]{:S(2)}) collective-permute-start(bf16[2,256,512]{2,1,0:T(8,128)(2,1)S(1)} %shard_map.92), channel_id=1, source_target_pairs={{0,64},{1,5},{2,66},{3,7},{4,68},{5,1},{6,70},{7,3},{8,72},{9,13},... | collective-permute-start | bytes 1572872 | tf_op jit(solution)/shard_map/ppermute | solution.py:46
  71.7 17.8 %collective-permute-start.26 = (bf16[2,256,512]{2,1,0:T(8,128)(2,1)S(1)}, bf16[2,256,512]{2,1,0:T(8,128)(2,1)S(1)}, u32[]{:S(2)}, u32[]{:S(2)}) collective-permute-start(bf16[2,256,512]{2,1,0:T(8,128)(2,1)S(1)} %shard_map.92), channel_id=1, source_target_pairs={{0,32},{1,3},{2,34},{3,5},{4,36},{5,7},{6,38},{7,1},{8,40},{9,11},... | collective-permute-start | bytes 1572872 | tf_op jit(solution)/shard_map/ppermute | solution.py:46
  72.1 44.3 %collective-permute-start.19 = (f32[256,1024]{1,0:T(8,128)S(1)}, f32[256,1024]{1,0:T(8,128)S(1)}, u32[]{:S(2)}, u32[]{:S(2)}) collective-permute-start(f32[256,1024]{1,0:T(8,128)S(1)} %fusion.13), channel_id=1, source_target_pairs={{0,1},{1,0},{2,3},{3,2},{4,5},{5,4},{6,7},{7,6},{8,9},{9,8},{10,11... | collective-permute-start | bytes 3145736 | tf_op jit(solution)/shard_map/ppermute | solution.py:50
  73.5 19.3 %collective-permute-start.29 = (bf16[1,128,512]{2,1,0:T(8,128)(2,1)S(1)}, bf16[1,128,512]{2,1,0:T(8,128)(2,1)S(1)}, u32[]{:S(2)}, u32[]{:S(2)}) collective-permute-start(bf16[1,128,512]{2,1,0:T(8,128)(2,1)S(1)} %get-tuple-element.73), channel_id=1, source_target_pairs={{0,8},{1,33},{2,10},{3,35},{4,12},{5,37},{6,14},{7,39},{8,16},{9,4... | collective-permute-start | bytes 393224 | tf_op jit(solution)/shard_map/ppermute | solution.py:46
  79.4 15.3 %collective-permute-start.30 = (bf16[1,128,512]{2,1,0:T(8,128)(2,1)S(1)}, bf16[1,128,512]{2,1,0:T(8,128)(2,1)S(1)}, u32[]{:S(2)}, u32[]{:S(2)}) collective-permute-start(bf16[1,128,512]{2,1,0:T(8,128)(2,1)S(1)} %get-tuple-element.74), channel_id=1, source_target_pairs={{0,16},{1,65},{2,18},{3,67},{4,20},{5,69},{6,22},{7,71},{8,24},{9,... | collective-permute-start | bytes 393224 | tf_op jit(solution)/shard_map/ppermute | solution.py:46
  91.4 14.9 %collective-permute-start.32 = (bf16[2,128,512]{2,1,0:T(8,128)(2,1)S(1)}, bf16[2,128,512]{2,1,0:T(8,128)(2,1)S(1)}, u32[]{:S(2)}, u32[]{:S(2)}) collective-permute-start(bf16[2,128,512]{2,1,0:T(8,128)(2,1)S(1)} %get-tuple-element.76), channel_id=1, source_target_pairs={{0,8},{1,33},{2,10},{3,35},{4,12},{5,37},{6,14},{7,39},{8,16},{9,4... | collective-permute-start | bytes 786440 | tf_op jit(solution)/shard_map/ppermute | solution.py:46
  91.4 14.8 %collective-permute-start.33 = (bf16[2,128,512]{2,1,0:T(8,128)(2,1)S(1)}, bf16[2,128,512]{2,1,0:T(8,128)(2,1)S(1)}, u32[]{:S(2)}, u32[]{:S(2)}) collective-permute-start(bf16[2,128,512]{2,1,0:T(8,128)(2,1)S(1)} %get-tuple-element.77), channel_id=1, source_target_pairs={{0,16},{1,65},{2,18},{3,67},{4,20},{5,69},{6,22},{7,71},{8,24},{9,... | collective-permute-start | bytes 786440 | tf_op jit(solution)/shard_map/ppermute | solution.py:46
  92.8 13.5 %collective-permute-start.34 = (bf16[2,128,512]{2,1,0:T(8,128)(2,1)S(1)}, bf16[2,128,512]{2,1,0:T(8,128)(2,1)S(1)}, u32[]{:S(2)}, u32[]{:S(2)}) collective-permute-start(bf16[2,128,512]{2,1,0:T(8,128)(2,1)S(1)} %get-tuple-element.78), channel_id=1, source_target_pairs={{0,24},{1,97},{2,26},{3,99},{4,28},{5,101},{6,30},{7,103},{8,0},{9... | collective-permute-start | bytes 786440 | tf_op jit(solution)/shard_map/ppermute | solution.py:46
  94.7 11.6 %collective-permute-start.31 = (bf16[1,128,512]{2,1,0:T(8,128)(2,1)S(1)}, bf16[1,128,512]{2,1,0:T(8,128)(2,1)S(1)}, u32[]{:S(2)}, u32[]{:S(2)}) collective-permute-start(bf16[1,128,512]{2,1,0:T(8,128)(2,1)S(1)} %get-tuple-element.75), channel_id=1, source_target_pairs={{0,24},{1,97},{2,26},{3,99},{4,28},{5,101},{6,30},{7,103},{8,0},{9... | collective-permute-start | bytes 393224 | tf_op jit(solution)/shard_map/ppermute | solution.py:46
  107.1 7.4 %collective-permute-start.35 = (bf16[3,32,512]{2,1,0:T(8,128)(2,1)S(1)}, bf16[3,32,512]{2,1,0:T(8,128)(2,1)S(1)}, u32[]{:S(2)}, u32[]{:S(2)}) collective-permute-start(bf16[3,32,512]{2,1,0:T(8,128)(2,1)S(1)} %get-tuple-element.80), channel_id=1, source_target_pairs={{0,2},{1,9},{2,4},{3,11},{4,6},{5,13},{6,0},{7,15},{8,10},{9,17},{... | collective-permute-start | bytes 294920 | tf_op jit(solution)/shard_map/ppermute | solution.py:46
  107.8 6.7 %collective-permute-start.36 = (bf16[3,32,512]{2,1,0:T(8,128)(2,1)S(1)}, bf16[3,32,512]{2,1,0:T(8,128)(2,1)S(1)}, u32[]{:S(2)}, u32[]{:S(2)}) collective-permute-start(bf16[3,32,512]{2,1,0:T(8,128)(2,1)S(1)} %get-tuple-element.81), channel_id=1, source_target_pairs={{0,4},{1,17},{2,6},{3,19},{4,0},{5,21},{6,2},{7,23},{8,12},{9,25},... | collective-permute-start | bytes 294920 | tf_op jit(solution)/shard_map/ppermute | solution.py:46
  110.9 4.8 %collective-permute-start.37 = (bf16[3,32,512]{2,1,0:T(8,128)(2,1)S(1)}, bf16[3,32,512]{2,1,0:T(8,128)(2,1)S(1)}, u32[]{:S(2)}, u32[]{:S(2)}) collective-permute-start(bf16[3,32,512]{2,1,0:T(8,128)(2,1)S(1)} %get-tuple-element.82), channel_id=1, source_target_pairs={{0,6},{1,25},{2,0},{3,27},{4,2},{5,29},{6,4},{7,31},{8,14},{9,1},{... | collective-permute-start | bytes 294920 | tf_op jit(solution)/shard_map/ppermute | solution.py:46

commit v6 on v5

--- a/solution.py
+++ b/solution.py
@@ -246,6 +246,19 @@
         out[...] = product[:, rows, :].astype(out.dtype)
 
 
+def turn_kernel(h0, h1, h2, h3, turned_out):
+    for n, block in enumerate((h0, h1, h2, h3)):
+        turned_out[:, 256 * n : 256 * n + 256] = turned(block[...]).astype(BF)
+
+
+def query_second_kernel(pos, columns, g0, g1, g2, g3, own, o1, o2, o3, product):
+    total = jnp.zeros((512, 512), F32)
+    for n, block in enumerate((g0, g1, g2, g3)):
+        total = total + dot(columns[:, 256 * n : 256 * n + 256], block[0], ((1,), (0,)))
+    product[0] = total
+    second_kernel(pos, product, own, o1, o2, o3)
+
+
 def third_kernel(
     pos, mine0, mine1, a1, a2, a3, b1, b2, b3, own, o1, o2, o3, total
 ):
@@ -349,7 +362,10 @@
     attended, level_grad = call(
         read_kernel,
         [projected, out_grad, mix, out_t, level_in, buckets],
-        [shape((256, 512), BF), shape((15, 4, 256), F32)],
+        [
+            jax.ShapeDtypeStruct((256, 512), BF),
+            jax.ShapeDtypeStruct((15, 4, 256), F32),
+        ],
     )
 
     grad_blocks = [[grads[0]], [grads[1]]]
@@ -375,7 +391,7 @@
         )
 
     key_value_products = products(grad_blocks[0])
-    query_products = products(grad_blocks[1])
+    (columns_turned,) = call(turn_kernel, hidden_blocks, [shape((512, 1024), BF)])
 
     def exchanged(pieces, axes):
         came = []
@@ -394,7 +410,14 @@
         return own, exchanged(pieces, (Z, X))
 
     own1, came1 = second(key_value_products)
-    own0, came0 = second(query_products)
+    own0, *pieces = call(
+        query_second_kernel,
+        [columns_turned, *grad_blocks[1]],
+        [shape((1, 128, 512), F32)] + [shape((1, 128, 512), BF)] * 3,
+        pos,
+        [pltpu.VMEM((1, 512, 512), F32)],
+    )
+    came0 = exchanged(pieces, (Z, X))
     own, *pieces = call(
         third_kernel,
         [own0, own1, *came0, *came1],

time: 118 us -> 115 us (0.975); the launches traced: 117 us -> 113 us
  waiting for transfers between devices: 37.3 us -> 21.5 us
  starting transfers between devices: 54.1 us -> 66.7 us
  Pallas kernels: 10.2 us -> 12 us
  local copies, waits for them, and re-layouts: 1.36 us -> 0.03 us
  matrix products: 11.5 us -> 10.2 us
    ppermute x36, waiting for transfers between devices: 37.3 us -> 21.5 us  [shifted(): return lax.ppermute(value, ALL, pairs)]
    ppermute x36, starting transfers between devices: 53.9 us -> 66.6 us  [shifted(): return lax.ppermute(value, ALL, pairs)]
    pallas_call x13 -> x14, Pallas kernels: 10.2 us -> 12 us  [call(): return run(*([] if pos is None else [pos]), *held)]
    dot_general x8 -> x4, matrix products: 3.43 us -> 2.07 us  [products(): jnp.einsum('td,mte->mde', h, g, preferred_element_type=F32)]
    unnamed x14 -> x12, local copies, waits for them, and re-layouts: 1.36 us -> 0.03 us
  transfers between devices with their start and end apart: 38 -> 38, of which waited for: 11 -> 11; matrix products, arithmetic and copies ran while one was open for 9% -> 7% of each run, Pallas kernels for 8% -> 9%
where the time goes in v6:
time: 115 us; the launch traced here: 113 us
  starting transfers between devices  66.7 us (58%)
  waiting for transfers between devices  21.5 us (19%)
  Pallas kernels  12 us (10%)
  matrix products  10.2 us (9%)
  other arithmetic  1.74 us (2%)
    ppermute x36, starting transfers between devices, shifted(): return lax.ppermute(value, ALL, pairs)  66.6 us
    ppermute x36, waiting for transfers between devices, shifted(): return lax.ppermute(value, ALL, pairs)  21.5 us
    pallas_call x14, Pallas kernels, call(): return run(*([] if pos is None else [pos]), *held)  12 us
    dot_general x1, matrix products, layer(): jnp.einsum('td,dme->mte', hidden, near, preferred_element_type=F32)  3.04 us
    dot_general x1, matrix products, layer(): far_part = jnp.einsum('td,dme->mte', other, far, preferred_element_type=F32)  3.03 us
  transfers between devices with their start and end apart: 38, of which 11 were waited for; matrix products, arithmetic and copies ran while one was open for 7% of the time, Pallas kernels for 9%

profile of v6, /device:TPU:0, one launch (start us, length us, event | category | flops | bytes accessed | tf_op | source)
XLA Modules:
  0.0 113.1 jit_solution(6791691772046784213)
XLA Ops:
  0.8 3.0 %fusion.4 = f32[3,512,256]{1,2,0:T(8,128)S(1)} fusion(bf16[2048,3,512]{2,0,1:T(8,128)(2,1)} %param.6, s32[]{:T(128)S(6)} %select_n.6, bf16[256,1024]{1,0:T(8,128)(2,1)} %hidden.1), kind=kOutput, calls=%fused_computation.4 | convolution fusion | flops 805306368 | bytes 5242884 | tf_op jit(solution)/shard_map/td,dme->mte/dot_general | solution.py:300
  3.9 3.0 %fusion.16.proj = bf16[3,256,512]{2,1,0:T(8,128)(2,1)S(1)} fusion(f32[3,512,256]{1,2,0:T(8,128)S(1)} %fusion.4, bf16[2048,3,512]{2,0,1:T(8,128)(2,1)} %param.6, s32[]{:T(128)S(6)} %select_n.7, f32[3]{0:T(128)S(1)} %copy-done.3, bf16[256,1024]{1,0:T(8,128)(2,1)S(1)} %collective-permute-done.other), kind=kOutput, calls=%fused_computation.12 | convolution fusion | flops 806486016 | bytes 6029328 | tf_op jit(solution)/shard_map/td,dme->mte/dot_general | solution.py:301
  7.0 1.3 %shard_map.85 = (bf16[512,128]{1,0:T(8,128)(2,1)S(1)}, bf16[512,128]{1,0:T(8,128)(2,1)S(1)}, bf16[512,128]{1,0:T(8,128)(2,1)S(1)}, bf16[512,128]{1,0:T(8,128)(2,...) custom-call(s32[4]{0:T(128)S(1)} %pad_add_fusion.pos, ...), custom_call_target="tpu_custom_call" | custom-call | tf_op jit(solution)/shard_map/pallas_call | solution.py:289
  8.3 1.3 %collective-permute-start.12 = (bf16[512,128]{1,0:T(8,128)(2,1)S(1)}, bf16[512,128]{1,0:T(8,128)(2,1)S(1)}, u32[]{:S(2)}, u32[]{:S(2)}) collective-permute-start(bf16[512,128]{1,0:T(8,128)(2,1)S(1)} %get-tuple-element.54), channel_id=1, source_target_pairs={{32,0},{33,1},{34,2},{35,3},{36,4},{37,5},{38,6},{39,7},{40,8},{41... | collective-permute-start | bytes 393224 | tf_op jit(solution)/shard_map/ppermute | solution.py:46
  9.6 1.3 %collective-permute-start.11 = (bf16[512,128]{1,0:T(8,128)(2,1)S(1)}, bf16[512,128]{1,0:T(8,128)(2,1)S(1)}, u32[]{:S(2)}, u32[]{:S(2)}) collective-permute-start(bf16[512,128]{1,0:T(8,128)(2,1)S(1)} %get-tuple-element.53), channel_id=1, source_target_pairs={{64,0},{65,1},{66,2},{67,3},{68,4},{69,5},{70,6},{71,7},{72,8},{73... | collective-permute-start | bytes 393224 | tf_op jit(solution)/shard_map/ppermute | solution.py:46
  10.9 1.3 %collective-permute-start.10 = (bf16[512,128]{1,0:T(8,128)(2,1)S(1)}, bf16[512,128]{1,0:T(8,128)(2,1)S(1)}, u32[]{:S(2)}, u32[]{:S(2)}) collective-permute-start(bf16[512,128]{1,0:T(8,128)(2,1)S(1)} %get-tuple-element.53), channel_id=1, source_target_pairs={{96,0},{97,1},{98,2},{99,3},{100,4},{101,5},{102,6},{103,7},{104,8... | collective-permute-start | bytes 393224 | tf_op jit(solution)/shard_map/ppermute | solution.py:46
  12.2 3.2 %collective-permute-start.3 = (bf16[512,128]{1,0:T(8,128)(2,1)S(1)}, bf16[512,128]{1,0:T(8,128)(2,1)S(1)}, u32[]{:S(2)}, u32[]{:S(2)}) collective-permute-start(bf16[512,128]{1,0:T(8,128)(2,1)S(1)} %get-tuple-element.47.mine), channel_id=1, source_target_pairs={{0,6},{1,7},{2,0},{3,1},{4,2},{5,3},{6,4},{7,5},{8,14},{9,15},{10,... | collective-permute-start | bytes 393224 | tf_op jit(solution)/shard_map/ppermute | solution.py:46
  15.3 0.6 collective-permute-start.2
  16.0 0.7 shard_map.93
  16.7 1.0 collective-permute-start.1
  17.7 1.3 %collective-permute-done.11.r2 = bf16[512,128]{1,0:T(8,128)(2,1)S(1)} collective-permute-done((bf16[512,128]{1,0:T(8,128)(2,1)S(1)}, bf16[512,128]{1,0:T(8,128)(2,1)S(1)}, u32[]{:S(2)}, u32[]{:S(2)}) %collective-permute-start.11) | collective-permute-done | bytes 131104 | tf_op jit(solution)/shard_map/ppermute | solution.py:46
  19.0 2.4 %collective-permute-start.20 = (bf16[256,512]{1,0:T(8,128)(2,1)S(1)}, bf16[256,512]{1,0:T(8,128)(2,1)S(1)}, u32[]{:S(2)}, u32[]{:S(2)}) collective-permute-start(bf16[256,512]{1,0:T(8,128)(2,1)S(1)} %get-tuple-element.68), channel_id=1, source_target_pairs={{0,32},{1,3},{2,34},{3,5},{4,36},{5,7},{6,38},{7,1},{8,40},{9,11},... | collective-permute-start | bytes 786440 | tf_op jit(solution)/shard_map/ppermute | solution.py:46
  21.4 0.4 collective-permute-done.10.r1
  21.8 0.7 shard_map.90
  22.5 2.0 %collective-permute-start.13 = (bf16[512,128]{1,0:T(8,128)(2,1)S(1)}, bf16[512,128]{1,0:T(8,128)(2,1)S(1)}, u32[]{:S(2)}, u32[]{:S(2)}) collective-permute-start(bf16[512,128]{1,0:T(8,128)(2,1)S(1)} %get-tuple-element.57), channel_id=1, source_target_pairs={{0,8},{1,9},{2,10},{3,11},{4,12},{5,13},{6,14},{7,15},{8,16},{9,17... | collective-permute-start | bytes 393224 | tf_op jit(solution)/shard_map/ppermute | solution.py:46
  24.5 3.6 %collective-permute-start.14 = (bf16[512,128]{1,0:T(8,128)(2,1)S(1)}, bf16[512,128]{1,0:T(8,128)(2,1)S(1)}, u32[]{:S(2)}, u32[]{:S(2)}) collective-permute-start(bf16[512,128]{1,0:T(8,128)(2,1)S(1)} %get-tuple-element.58), channel_id=1, source_target_pairs={{0,16},{1,17},{2,18},{3,19},{4,20},{5,21},{6,22},{7,23},{8,24},{9,... | collective-permute-start | bytes 393224 | tf_op jit(solution)/shard_map/ppermute | solution.py:46
  28.1 1.0 collective-permute-start.15
  29.1 0.3 collective-permute-start.6
  29.4 0.6 collective-permute-done.13.r1
  30.0 2.8 %collective-permute-start.5 = (bf16[512,128]{1,0:T(8,128)(2,1)S(1)}, bf16[512,128]{1,0:T(8,128)(2,1)S(1)}, u32[]{:S(2)}, u32[]{:S(2)}) collective-permute-start(bf16[512,128]{1,0:T(8,128)(2,1)S(1)} %shard_map.86.mine), channel_id=1, source_target_pairs={{0,16},{1,17},{2,18},{3,19},{4,20},{5,21},{6,22},{7,23},{8,24},{9,... | collective-permute-start | bytes 393224 | tf_op jit(solution)/shard_map/ppermute | solution.py:46
  32.8 1.1 collective-permute-done.14.r2
  33.9 0.4 collective-permute-start.4
  34.4 3.6 %collective-permute-start.21 = (bf16[256,512]{1,0:T(8,128)(2,1)S(1)}, bf16[256,512]{1,0:T(8,128)(2,1)S(1)}, u32[]{:S(2)}, u32[]{:S(2)}) collective-permute-start(bf16[256,512]{1,0:T(8,128)(2,1)S(1)} %get-tuple-element.69), channel_id=1, source_target_pairs={{0,64},{1,5},{2,66},{3,7},{4,68},{5,1},{6,70},{7,3},{8,72},{9,13},... | collective-permute-start | bytes 786440 | tf_op jit(solution)/shard_map/ppermute | solution.py:46
  38.1 0.7 shard_map.91
  38.8 0.6 collective-permute-start.22
  39.4 1.2 %collective-permute-start.16 = (bf16[512,128]{1,0:T(8,128)(2,1)S(1)}, bf16[512,128]{1,0:T(8,128)(2,1)S(1)}, u32[]{:S(2)}, u32[]{:S(2)}) collective-permute-start(bf16[512,128]{1,0:T(8,128)(2,1)S(1)} %get-tuple-element.64), channel_id=1, source_target_pairs={{0,2},{1,3},{2,4},{3,5},{4,6},{5,7},{6,0},{7,1},{8,10},{9,11},{10,... | collective-permute-start | bytes 393224 | tf_op jit(solution)/shard_map/ppermute | solution.py:46
  40.6 4.3 %collective-permute-start.17 = (bf16[512,128]{1,0:T(8,128)(2,1)S(1)}, bf16[512,128]{1,0:T(8,128)(2,1)S(1)}, u32[]{:S(2)}, u32[]{:S(2)}) collective-permute-start(bf16[512,128]{1,0:T(8,128)(2,1)S(1)} %get-tuple-element.65), channel_id=1, source_target_pairs={{0,4},{1,5},{2,6},{3,7},{4,0},{5,1},{6,2},{7,3},{8,12},{9,13},{10,... | collective-permute-start | bytes 393224 | tf_op jit(solution)/shard_map/ppermute | solution.py:46
  45.0 1.4 %collective-permute-done.16.ry1 = bf16[512,128]{1,0:T(8,128)(2,1)S(1)} collective-permute-done((bf16[512,128]{1,0:T(8,128)(2,1)S(1)}, bf16[512,128]{1,0:T(8,128)(2,1)S(1)}, u32[]{:S(2)}, u32[]{:S(2)}) %collective-permute-start.16) | collective-permute-done | bytes 131104 | tf_op jit(solution)/shard_map/ppermute | solution.py:46
  46.4 4.7 %collective-permute-start.9 = (bf16[512,128]{1,0:T(8,128)(2,1)S(1)}, bf16[512,128]{1,0:T(8,128)(2,1)S(1)}, u32[]{:S(2)}, u32[]{:S(2)}) collective-permute-start(bf16[512,128]{1,0:T(8,128)(2,1)S(1)} %shard_map.87), channel_id=1, source_target_pairs={{0,96},{1,97},{2,98},{3,99},{4,100},{5,101},{6,102},{7,103},{8,104... | collective-permute-start | bytes 393224 | tf_op jit(solution)/shard_map/ppermute | solution.py:46
  51.1 3.0 %collective-permute-start.8 = (bf16[512,128]{1,0:T(8,128)(2,1)S(1)}, bf16[512,128]{1,0:T(8,128)(2,1)S(1)}, u32[]{:S(2)}, u32[]{:S(2)}) collective-permute-start(bf16[512,128]{1,0:T(8,128)(2,1)S(1)} %shard_map.87), channel_id=1, source_target_pairs={{0,64},{1,65},{2,66},{3,67},{4,68},{5,69},{6,70},{7,71},{8,72},{9,... | collective-permute-start | bytes 393224 | tf_op jit(solution)/shard_map/ppermute | solution.py:46
  54.1 1.6 %collective-permute-start.7 = (bf16[512,128]{1,0:T(8,128)(2,1)S(1)}, bf16[512,128]{1,0:T(8,128)(2,1)S(1)}, u32[]{:S(2)}, u32[]{:S(2)}) collective-permute-start(bf16[512,128]{1,0:T(8,128)(2,1)S(1)} %shard_map.87), channel_id=1, source_target_pairs={{0,32},{1,33},{2,34},{3,35},{4,36},{5,37},{6,38},{7,39},{8,40},{9,... | collective-permute-start | bytes 393224 | tf_op jit(solution)/shard_map/ppermute | solution.py:46
  55.7 1.9 %shard_map.84 = (f32[4,128,256]{2,1,0:T(8,128)S(1)}, f32[4,128,256]{2,1,0:T(8,128)S(1)}, f32[256,512]{1,0:T(8,128)S(1)}, f32[256,512]{1,0:T(8,128)S(1)}, f32[9,4,256]{2,1,0:T(4,128)S(1)}) custom-call(bf16[3,256,512]{2,1,0:T(8,128)(2,1)S(1)} %fusion.16.proj, bf16[256,512]{1,0:T(8,128)(2,1)S(1)} %copy-done, f32[15,4,256]{2,1,0:T(4,128)S(1)} %copy-done.2), custom_call_target="tpu_custom_call" | custom-call | tf_op jit(solution)/shard_map/pallas_call | solution.py:289
  57.6 0.3 shard_map.92
  58.2 0.4 shard_map.94.columns
  58.6 1.4 %shard_map.88 = (bf16[1,256,512]{2,1,0:T(8,128)(2,1)S(1)}, bf16[6,512,128]{2,1,0:T(8,128)(2,1)S(1)}) custom-call(s32[4]{0:T(128)S(1)} %pad_add_fusion.pos, bf16[256,512]{1,0:T(8,128)(2,1)S(1)} %copy-done, f32[15,4,256]{2,1,0:T(4,128)S(1)} %copy-done.2, f32[4,128,256]{2,1,0:T(8,128)S(1)} %get-tuple-element.46.query_t, ...), custom_call_target="tpu_custom_call" | custom-call | tf_op jit(solution)/shard_map/pallas_call | solution.py:289
  60.0 3.3 %collective-permute-start.25 = (bf16[1,256,512]{2,1,0:T(8,128)(2,1)S(1)}, bf16[1,256,512]{2,1,0:T(8,128)(2,1)S(1)}, u32[]{:S(2)}, u32[]{:S(2)}) collective-permute-start(bf16[1,256,512]{2,1,0:T(8,128)(2,1)S(1)} %get-tuple-element.50.g0), channel_id=1, source_target_pairs={{0,96},{1,7},{2,98},{3,1},{4,100},{5,3},{6,102},{7,5},{8,104},{9,1... | collective-permute-start | bytes 786440 | tf_op jit(solution)/shard_map/ppermute | solution.py:46
  63.3 0.8 collective-permute-start.24
  64.1 0.7 collective-permute-start.23
  64.8 2.0 %collective-permute-start.27 = (bf16[2,256,512]{2,1,0:T(8,128)(2,1)S(1)}, bf16[2,256,512]{2,1,0:T(8,128)(2,1)S(1)}, u32[]{:S(2)}, u32[]{:S(2)}) collective-permute-start(bf16[2,256,512]{2,1,0:T(8,128)(2,1)S(1)} %shard_map.92), channel_id=1, source_target_pairs={{0,64},{1,5},{2,66},{3,7},{4,68},{5,1},{6,70},{7,3},{8,72},{9,13},... | collective-permute-start | bytes 1572872 | tf_op jit(solution)/shard_map/ppermute | solution.py:46
  66.8 1.0 fusion.13
  67.8 0.5 fusion.29
  68.3 7.3 %collective-permute-done.25.g3 = bf16[1,256,512]{2,1,0:T(8,128)(2,1)S(1)} collective-permute-done((bf16[1,256,512]{2,1,0:T(8,128)(2,1)S(1)}, bf16[1,256,512]{2,1,0:T(8,128)(2,1)S(1)}, u32[]{:S(2)}, u32[]{:S(2)}) %collective-permute-start.25) | collective-permute-done | bytes 262176 | tf_op jit(solution)/shard_map/ppermute | solution.py:46
  75.6 3.7 %collective-permute-start.28 = (bf16[2,256,512]{2,1,0:T(8,128)(2,1)S(1)}, bf16[2,256,512]{2,1,0:T(8,128)(2,1)S(1)}, u32[]{:S(2)}, u32[]{:S(2)}) collective-permute-start(bf16[2,256,512]{2,1,0:T(8,128)(2,1)S(1)} %shard_map.92), channel_id=1, source_target_pairs={{0,96},{1,7},{2,98},{3,1},{4,100},{5,3},{6,102},{7,5},{8,104},{9,1... | collective-permute-start | bytes 1572872 | tf_op jit(solution)/shard_map/ppermute | solution.py:46
  79.3 0.5 collective-permute-done.23.g1
  79.8 1.3 %shard_map.95 = (f32[1,128,512]{2,1,0:T(8,128)S(1)}, bf16[1,128,512]{2,1,0:T(8,128)(2,1)S(1)}, bf16[1,128,512]{2,1,0:T(8,128)(2,1)S(1)}, bf16[1,128,512]{2,1,0:T(8,128)(2,1)S(1)}) custom-call(s32[4]{0:T(128)S(1)} %pad_add_fusion.pos, bf16[512,1024]{1,0:T(8,128)(2,1)S(1)} %shard_map.94.columns, bf16[1,256,512]{2,1,0:T(8,128)(2,1)S(1)} %get-tuple-element.50.g0, ...), custom_call_target="tpu_custom_call" | custom-call | tf_op jit(solution)/shard_map/pallas_call | solution.py:289
  81.2 2.0 %collective-permute-start.29 = (bf16[1,128,512]{2,1,0:T(8,128)(2,1)S(1)}, bf16[1,128,512]{2,1,0:T(8,128)(2,1)S(1)}, u32[]{:S(2)}, u32[]{:S(2)}) collective-permute-start(bf16[1,128,512]{2,1,0:T(8,128)(2,1)S(1)} %get-tuple-element.73), channel_id=1, source_target_pairs={{0,8},{1,33},{2,10},{3,35},{4,12},{5,37},{6,14},{7,39},{8,16},{9,4... | collective-permute-start | bytes 393224 | tf_op jit(solution)/shard_map/ppermute | solution.py:46
  83.1 3.3 %collective-permute-start.30 = (bf16[1,128,512]{2,1,0:T(8,128)(2,1)S(1)}, bf16[1,128,512]{2,1,0:T(8,128)(2,1)S(1)}, u32[]{:S(2)}, u32[]{:S(2)}) collective-permute-start(bf16[1,128,512]{2,1,0:T(8,128)(2,1)S(1)} %get-tuple-element.74), channel_id=1, source_target_pairs={{0,16},{1,65},{2,18},{3,67},{4,20},{5,69},{6,22},{7,71},{8,24},{9,... | collective-permute-start | bytes 393224 | tf_op jit(solution)/shard_map/ppermute | solution.py:46
  86.5 0.5 fusion.27
  87.0 0.5 fusion.25
  87.5 0.6 add_bitcast_fusion.product
  88.1 0.7 shard_map.96
  88.8 1.9 %collective-permute-start.32 = (bf16[2,128,512]{2,1,0:T(8,128)(2,1)S(1)}, bf16[2,128,512]{2,1,0:T(8,128)(2,1)S(1)}, u32[]{:S(2)}, u32[]{:S(2)}) collective-permute-start(bf16[2,128,512]{2,1,0:T(8,128)(2,1)S(1)} %get-tuple-element.76), channel_id=1, source_target_pairs={{0,8},{1,33},{2,10},{3,35},{4,12},{5,37},{6,14},{7,39},{8,16},{9,4... | collective-permute-start | bytes 786440 | tf_op jit(solution)/shard_map/ppermute | solution.py:46
  90.7 3.3 %collective-permute-start.33 = (bf16[2,128,512]{2,1,0:T(8,128)(2,1)S(1)}, bf16[2,128,512]{2,1,0:T(8,128)(2,1)S(1)}, u32[]{:S(2)}, u32[]{:S(2)}) collective-permute-start(bf16[2,128,512]{2,1,0:T(8,128)(2,1)S(1)} %get-tuple-element.77), channel_id=1, source_target_pairs={{0,16},{1,65},{2,18},{3,67},{4,20},{5,69},{6,22},{7,71},{8,24},{9,... | collective-permute-start | bytes 786440 | tf_op jit(solution)/shard_map/ppermute | solution.py:46
  94.1 0.7 collective-permute-start.31
  94.8 7.3 %collective-permute-done.31.a3 = bf16[1,128,512]{2,1,0:T(8,128)(2,1)S(1)} collective-permute-done((bf16[1,128,512]{2,1,0:T(8,128)(2,1)S(1)}, bf16[1,128,512]{2,1,0:T(8,128)(2,1)S(1)}, u32[]{:S(2)}, u32[]{:S(2)}) %collective-permute-start.31) | collective-permute-done | bytes 131104 | tf_op jit(solution)/shard_map/ppermute | solution.py:46
  102.1 0.8 shard_map.97
  103.1 3.8 %collective-permute-start.36 = (bf16[3,32,512]{2,1,0:T(8,128)(2,1)S(1)}, bf16[3,32,512]{2,1,0:T(8,128)(2,1)S(1)}, u32[]{:S(2)}, u32[]{:S(2)}) collective-permute-start(bf16[3,32,512]{2,1,0:T(8,128)(2,1)S(1)} %get-tuple-element.81), channel_id=1, source_target_pairs={{0,4},{1,17},{2,6},{3,19},{4,0},{5,21},{6,2},{7,23},{8,12},{9,25},... | collective-permute-start | bytes 294920 | tf_op jit(solution)/shard_map/ppermute | solution.py:46
  106.9 0.5 collective-permute-start.37
  107.3 1.0 fusion.10
  108.3 1.7 %shard_map.89 = (bf16[256,512]{1,0:T(8,128)(2,1)}, f32[15,4,256]{2,1,0:T(4,128)}) custom-call(bf16[3,256,512]{2,1,0:T(8,128)(2,1)S(1)} %fusion.16.proj, bf16[256,512]{1,0:T(8,128)(2,1)S(1)} %copy-done, f32[15,4,256]{2,1,0:T(4,128)S(1)} %copy-done.2, f32[4,128,256]{2,1,0:T(8,128)S(1)} %get-tuple-element.44.out_t, ...), custom_call_target="tpu_custom_call" | custom-call | tf_op jit(solution)/shard_map/pallas_call | solution.py:289
  110.0 0.5 collective-permute-done.36
  110.5 1.0 collective-permute-done.37
  111.5 0.7 multiply_bitcast_fusion
  112.2 0.9 add_convert_fusion
  (50 shorter events, 0.9 us)
Async XLA Ops:
  0.6 3.3 %collective-permute-start = (bf16[256,1024]{1,0:T(8,128)(2,1)}, bf16[256,1024]{1,0:T(8,128)(2,1)S(1)}, u32[]{:S(2)}, u32[]{:S(2)}) collective-permute-start(bf16[256,1024]{1,0:T(8,128)(2,1)} %hidden.1), channel_id=1, source_target_pairs={{0,1},{1,0},{2,3},{3,2},{4,5},{5,4},{6,7},{7,6},{8,9},{9,8},{10,11... | collective-permute-start | bytes 1572872 | tf_op jit(solution)/shard_map/ppermute | solution.py:50
  0.8 3.1 %copy-start.3 = (f32[3]{0:T(128)S(1)}, f32[3]{0:T(128)}, u32[]{:S(2)}) copy-start(f32[3]{0:T(128)} %constant.27.clone) | copy-start | bytes 40
  3.9 3.1 %copy-start = (bf16[256,512]{1,0:T(8,128)(2,1)S(1)}, bf16[256,512]{1,0:T(8,128)(2,1)}, u32[]{:S(2)}) copy-start(bf16[256,512]{1,0:T(8,128)(2,1)} %out_grad.3) | copy-start | bytes 786436
  3.9 3.1 %copy-start.2 = (f32[15,4,256]{2,1,0:T(4,128)S(1)}, f32[15,4,256]{2,1,0:T(4,128)}, u32[]{:S(2)}) copy-start(f32[15,4,256]{2,1,0:T(4,128)} %mix.7) | copy-start | bytes 184324
  3.9 12.1 %copy-start.1 = (bf16[256,1024]{1,0:T(8,128)(2,1)S(1)}, bf16[256,1024]{1,0:T(8,128)(2,1)}, u32[]{:S(2)}) copy-start(bf16[256,1024]{1,0:T(8,128)(2,1)} %hidden.1) | copy-start | bytes 1572868
  3.9 62.9 %slice-start = ((s8[6291456]{0:T(1024)(128)(4,1)}), s8[4194304]{0:T(1024)(128)(4,1)S(1)}, s32[]{:S(2)}) async-start(s8[6291456]{0:T(1024)(128)(4,1)} %bitcast.38), calls=%async_computation | async-start | bytes 8388608
  8.3 8.4 %collective-permute-start.12 = (bf16[512,128]{1,0:T(8,128)(2,1)S(1)}, bf16[512,128]{1,0:T(8,128)(2,1)S(1)}, u32[]{:S(2)}, u32[]{:S(2)}) collective-permute-start(bf16[512,128]{1,0:T(8,128)(2,1)S(1)} %get-tuple-element.54), channel_id=1, source_target_pairs={{32,0},{33,1},{34,2},{35,3},{36,4},{37,5},{38,6},{39,7},{40,8},{41... | collective-permute-start | bytes 393224 | tf_op jit(solution)/shard_map/ppermute | solution.py:46
  9.6 9.4 %collective-permute-start.11 = (bf16[512,128]{1,0:T(8,128)(2,1)S(1)}, bf16[512,128]{1,0:T(8,128)(2,1)S(1)}, u32[]{:S(2)}, u32[]{:S(2)}) collective-permute-start(bf16[512,128]{1,0:T(8,128)(2,1)S(1)} %get-tuple-element.53), channel_id=1, source_target_pairs={{64,0},{65,1},{66,2},{67,3},{68,4},{69,5},{70,6},{71,7},{72,8},{73... | collective-permute-start | bytes 393224 | tf_op jit(solution)/shard_map/ppermute | solution.py:46
  10.9 10.9 %collective-permute-start.10 = (bf16[512,128]{1,0:T(8,128)(2,1)S(1)}, bf16[512,128]{1,0:T(8,128)(2,1)S(1)}, u32[]{:S(2)}, u32[]{:S(2)}) collective-permute-start(bf16[512,128]{1,0:T(8,128)(2,1)S(1)} %get-tuple-element.53), channel_id=1, source_target_pairs={{96,0},{97,1},{98,2},{99,3},{100,4},{101,5},{102,6},{103,7},{104,8... | collective-permute-start | bytes 393224 | tf_op jit(solution)/shard_map/ppermute | solution.py:46
  12.2 12.3 %collective-permute-start.3 = (bf16[512,128]{1,0:T(8,128)(2,1)S(1)}, bf16[512,128]{1,0:T(8,128)(2,1)S(1)}, u32[]{:S(2)}, u32[]{:S(2)}) collective-permute-start(bf16[512,128]{1,0:T(8,128)(2,1)S(1)} %get-tuple-element.47.mine), channel_id=1, source_target_pairs={{0,6},{1,7},{2,0},{3,1},{4,2},{5,3},{6,4},{7,5},{8,14},{9,15},{10,... | collective-permute-start | bytes 393224 | tf_op jit(solution)/shard_map/ppermute | solution.py:46
  15.3 12.7 %collective-permute-start.2 = (bf16[512,128]{1,0:T(8,128)(2,1)S(1)}, bf16[512,128]{1,0:T(8,128)(2,1)S(1)}, u32[]{:S(2)}, u32[]{:S(2)}) collective-permute-start(bf16[512,128]{1,0:T(8,128)(2,1)S(1)} %get-tuple-element.47.mine), channel_id=1, source_target_pairs={{0,4},{1,5},{2,6},{3,7},{4,0},{5,1},{6,2},{7,3},{8,12},{9,13},{10,... | collective-permute-start | bytes 393224 | tf_op jit(solution)/shard_map/ppermute | solution.py:46
  16.7 12.4 %collective-permute-start.1 = (bf16[512,128]{1,0:T(8,128)(2,1)S(1)}, bf16[512,128]{1,0:T(8,128)(2,1)S(1)}, u32[]{:S(2)}, u32[]{:S(2)}) collective-permute-start(bf16[512,128]{1,0:T(8,128)(2,1)S(1)} %get-tuple-element.47.mine), channel_id=1, source_target_pairs={{0,2},{1,3},{2,4},{3,5},{4,6},{5,7},{6,0},{7,1},{8,10},{9,11},{10,... | collective-permute-start | bytes 393224 | tf_op jit(solution)/shard_map/ppermute | solution.py:46
  19.0 19.8 %collective-permute-start.20 = (bf16[256,512]{1,0:T(8,128)(2,1)S(1)}, bf16[256,512]{1,0:T(8,128)(2,1)S(1)}, u32[]{:S(2)}, u32[]{:S(2)}) collective-permute-start(bf16[256,512]{1,0:T(8,128)(2,1)S(1)} %get-tuple-element.68), channel_id=1, source_target_pairs={{0,32},{1,3},{2,34},{3,5},{4,36},{5,7},{6,38},{7,1},{8,40},{9,11},... | collective-permute-start | bytes 786440 | tf_op jit(solution)/shard_map/ppermute | solution.py:46
  22.5 7.6 %collective-permute-start.13 = (bf16[512,128]{1,0:T(8,128)(2,1)S(1)}, bf16[512,128]{1,0:T(8,128)(2,1)S(1)}, u32[]{:S(2)}, u32[]{:S(2)}) collective-permute-start(bf16[512,128]{1,0:T(8,128)(2,1)S(1)} %get-tuple-element.57), channel_id=1, source_target_pairs={{0,8},{1,9},{2,10},{3,11},{4,12},{5,13},{6,14},{7,15},{8,16},{9,17... | collective-permute-start | bytes 393224 | tf_op jit(solution)/shard_map/ppermute | solution.py:46
  24.5 9.4 %collective-permute-start.14 = (bf16[512,128]{1,0:T(8,128)(2,1)S(1)}, bf16[512,128]{1,0:T(8,128)(2,1)S(1)}, u32[]{:S(2)}, u32[]{:S(2)}) collective-permute-start(bf16[512,128]{1,0:T(8,128)(2,1)S(1)} %get-tuple-element.58), channel_id=1, source_target_pairs={{0,16},{1,17},{2,18},{3,19},{4,20},{5,21},{6,22},{7,23},{8,24},{9,... | collective-permute-start | bytes 393224 | tf_op jit(solution)/shard_map/ppermute | solution.py:46
  28.1 6.4 %collective-permute-start.15 = (bf16[512,128]{1,0:T(8,128)(2,1)S(1)}, bf16[512,128]{1,0:T(8,128)(2,1)S(1)}, u32[]{:S(2)}, u32[]{:S(2)}) collective-permute-start(bf16[512,128]{1,0:T(8,128)(2,1)S(1)} %get-tuple-element.59), channel_id=1, source_target_pairs={{0,24},{1,25},{2,26},{3,27},{4,28},{5,29},{6,30},{7,31},{8,0},{9,1... | collective-permute-start | bytes 393224 | tf_op jit(solution)/shard_map/ppermute | solution.py:46
  29.1 10.2 %collective-permute-start.6 = (bf16[512,128]{1,0:T(8,128)(2,1)S(1)}, bf16[512,128]{1,0:T(8,128)(2,1)S(1)}, u32[]{:S(2)}, u32[]{:S(2)}) collective-permute-start(bf16[512,128]{1,0:T(8,128)(2,1)S(1)} %shard_map.86.mine), channel_id=1, source_target_pairs={{0,24},{1,25},{2,26},{3,27},{4,28},{5,29},{6,30},{7,31},{8,0},{9,1... | collective-permute-start | bytes 393224 | tf_op jit(solution)/shard_map/ppermute | solution.py:46
  30.0 10.6 %collective-permute-start.5 = (bf16[512,128]{1,0:T(8,128)(2,1)S(1)}, bf16[512,128]{1,0:T(8,128)(2,1)S(1)}, u32[]{:S(2)}, u32[]{:S(2)}) collective-permute-start(bf16[512,128]{1,0:T(8,128)(2,1)S(1)} %shard_map.86.mine), channel_id=1, source_target_pairs={{0,16},{1,17},{2,18},{3,19},{4,20},{5,21},{6,22},{7,23},{8,24},{9,... | collective-permute-start | bytes 393224 | tf_op jit(solution)/shard_map/ppermute | solution.py:46
  33.9 11.1 %collective-permute-start.4 = (bf16[512,128]{1,0:T(8,128)(2,1)S(1)}, bf16[512,128]{1,0:T(8,128)(2,1)S(1)}, u32[]{:S(2)}, u32[]{:S(2)}) collective-permute-start(bf16[512,128]{1,0:T(8,128)(2,1)S(1)} %shard_map.86.mine), channel_id=1, source_target_pairs={{0,8},{1,9},{2,10},{3,11},{4,12},{5,13},{6,14},{7,15},{8,16},{9,17... | collective-permute-start | bytes 393224 | tf_op jit(solution)/shard_map/ppermute | solution.py:46
  34.4 23.5 %collective-permute-start.21 = (bf16[256,512]{1,0:T(8,128)(2,1)S(1)}, bf16[256,512]{1,0:T(8,128)(2,1)S(1)}, u32[]{:S(2)}, u32[]{:S(2)}) collective-permute-start(bf16[256,512]{1,0:T(8,128)(2,1)S(1)} %get-tuple-element.69), channel_id=1, source_target_pairs={{0,64},{1,5},{2,66},{3,7},{4,68},{5,1},{6,70},{7,3},{8,72},{9,13},... | collective-permute-start | bytes 786440 | tf_op jit(solution)/shard_map/ppermute | solution.py:46
  38.1 28.8 %slice-start.1 = ((s8[6291456]{0:T(1024)(128)(4,1)}), s8[2097152]{0:T(1024)(128)(4,1)S(1)}, s32[]{:S(2)}) async-start(s8[6291456]{0:T(1024)(128)(4,1)} %bitcast.38), calls=%async_computation.1 | async-start | bytes 4194304
  38.8 19.5 %collective-permute-start.22 = (bf16[256,512]{1,0:T(8,128)(2,1)S(1)}, bf16[256,512]{1,0:T(8,128)(2,1)S(1)}, u32[]{:S(2)}, u32[]{:S(2)}) collective-permute-start(bf16[256,512]{1,0:T(8,128)(2,1)S(1)} %get-tuple-element.70), channel_id=1, source_target_pairs={{0,96},{1,7},{2,98},{3,1},{4,100},{5,3},{6,102},{7,5},{8,104},{9,1... | collective-permute-start | bytes 786440 | tf_op jit(solution)/shard_map/ppermute | solution.py:46
  39.4 7.1 %collective-permute-start.16 = (bf16[512,128]{1,0:T(8,128)(2,1)S(1)}, bf16[512,128]{1,0:T(8,128)(2,1)S(1)}, u32[]{:S(2)}, u32[]{:S(2)}) collective-permute-start(bf16[512,128]{1,0:T(8,128)(2,1)S(1)} %get-tuple-element.64), channel_id=1, source_target_pairs={{0,2},{1,3},{2,4},{3,5},{4,6},{5,7},{6,0},{7,1},{8,10},{9,11},{10,... | collective-permute-start | bytes 393224 | tf_op jit(solution)/shard_map/ppermute | solution.py:46
  40.6 10.5 %collective-permute-start.17 = (bf16[512,128]{1,0:T(8,128)(2,1)S(1)}, bf16[512,128]{1,0:T(8,128)(2,1)S(1)}, u32[]{:S(2)}, u32[]{:S(2)}) collective-permute-start(bf16[512,128]{1,0:T(8,128)(2,1)S(1)} %get-tuple-element.65), channel_id=1, source_target_pairs={{0,4},{1,5},{2,6},{3,7},{4,0},{5,1},{6,2},{7,3},{8,12},{9,13},{10,... | collective-permute-start | bytes 393224 | tf_op jit(solution)/shard_map/ppermute | solution.py:46
  44.9 9.2 %collective-permute-start.18 = (bf16[512,128]{1,0:T(8,128)(2,1)S(1)}, bf16[512,128]{1,0:T(8,128)(2,1)S(1)}, u32[]{:S(2)}, u32[]{:S(2)}) collective-permute-start(bf16[512,128]{1,0:T(8,128)(2,1)S(1)} %get-tuple-element.66), channel_id=1, source_target_pairs={{0,6},{1,7},{2,0},{3,1},{4,2},{5,3},{6,4},{7,5},{8,14},{9,15},{10,... | collective-permute-start | bytes 393224 | tf_op jit(solution)/shard_map/ppermute | solution.py:46
  46.4 12.2 %collective-permute-start.9 = (bf16[512,128]{1,0:T(8,128)(2,1)S(1)}, bf16[512,128]{1,0:T(8,128)(2,1)S(1)}, u32[]{:S(2)}, u32[]{:S(2)}) collective-permute-start(bf16[512,128]{1,0:T(8,128)(2,1)S(1)} %shard_map.87), channel_id=1, source_target_pairs={{0,96},{1,97},{2,98},{3,99},{4,100},{5,101},{6,102},{7,103},{8,104... | collective-permute-start | bytes 393224 | tf_op jit(solution)/shard_map/ppermute | solution.py:46
  51.1 7.5 %collective-permute-start.8 = (bf16[512,128]{1,0:T(8,128)(2,1)S(1)}, bf16[512,128]{1,0:T(8,128)(2,1)S(1)}, u32[]{:S(2)}, u32[]{:S(2)}) collective-permute-start(bf16[512,128]{1,0:T(8,128)(2,1)S(1)} %shard_map.87), channel_id=1, source_target_pairs={{0,64},{1,65},{2,66},{3,67},{4,68},{5,69},{6,70},{7,71},{8,72},{9,... | collective-permute-start | bytes 393224 | tf_op jit(solution)/shard_map/ppermute | solution.py:46
  54.1 4.5 %collective-permute-start.7 = (bf16[512,128]{1,0:T(8,128)(2,1)S(1)}, bf16[512,128]{1,0:T(8,128)(2,1)S(1)}, u32[]{:S(2)}, u32[]{:S(2)}) collective-permute-start(bf16[512,128]{1,0:T(8,128)(2,1)S(1)} %shard_map.87), channel_id=1, source_target_pairs={{0,32},{1,33},{2,34},{3,35},{4,36},{5,37},{6,38},{7,39},{8,40},{9,... | collective-permute-start | bytes 393224 | tf_op jit(solution)/shard_map/ppermute | solution.py:46
  58.0 25.2 %collective-permute-start.26 = (bf16[2,256,512]{2,1,0:T(8,128)(2,1)S(1)}, bf16[2,256,512]{2,1,0:T(8,128)(2,1)S(1)}, u32[]{:S(2)}, u32[]{:S(2)}) collective-permute-start(bf16[2,256,512]{2,1,0:T(8,128)(2,1)S(1)} %shard_map.92), channel_id=1, source_target_pairs={{0,32},{1,3},{2,34},{3,5},{4,36},{5,7},{6,38},{7,1},{8,40},{9,11},... | collective-permute-start | bytes 1572872 | tf_op jit(solution)/shard_map/ppermute | solution.py:46
  60.0 15.6 %collective-permute-start.25 = (bf16[1,256,512]{2,1,0:T(8,128)(2,1)S(1)}, bf16[1,256,512]{2,1,0:T(8,128)(2,1)S(1)}, u32[]{:S(2)}, u32[]{:S(2)}) collective-permute-start(bf16[1,256,512]{2,1,0:T(8,128)(2,1)S(1)} %get-tuple-element.50.g0), channel_id=1, source_target_pairs={{0,96},{1,7},{2,98},{3,1},{4,100},{5,3},{6,102},{7,5},{8,104},{9,1... | collective-permute-start | bytes 786440 | tf_op jit(solution)/shard_map/ppermute | solution.py:46
  63.3 16.0 %collective-permute-start.24 = (bf16[1,256,512]{2,1,0:T(8,128)(2,1)S(1)}, bf16[1,256,512]{2,1,0:T(8,128)(2,1)S(1)}, u32[]{:S(2)}, u32[]{:S(2)}) collective-permute-start(bf16[1,256,512]{2,1,0:T(8,128)(2,1)S(1)} %get-tuple-element.50.g0), channel_id=1, source_target_pairs={{0,64},{1,5},{2,66},{3,7},{4,68},{5,1},{6,70},{7,3},{8,72},{9,13},... | collective-permute-start | bytes 786440 | tf_op jit(solution)/shard_map/ppermute | solution.py:46
  64.1 15.7 %collective-permute-start.23 = (bf16[1,256,512]{2,1,0:T(8,128)(2,1)S(1)}, bf16[1,256,512]{2,1,0:T(8,128)(2,1)S(1)}, u32[]{:S(2)}, u32[]{:S(2)}) collective-permute-start(bf16[1,256,512]{2,1,0:T(8,128)(2,1)S(1)} %get-tuple-element.50.g0), channel_id=1, source_target_pairs={{0,32},{1,3},{2,34},{3,5},{4,36},{5,7},{6,38},{7,1},{8,40},{9,11},... | collective-permute-start | bytes 786440 | tf_op jit(solution)/shard_map/ppermute | solution.py:46
  64.8 22.2 %collective-permute-start.27 = (bf16[2,256,512]{2,1,0:T(8,128)(2,1)S(1)}, bf16[2,256,512]{2,1,0:T(8,128)(2,1)S(1)}, u32[]{:S(2)}, u32[]{:S(2)}) collective-permute-start(bf16[2,256,512]{2,1,0:T(8,128)(2,1)S(1)} %shard_map.92), channel_id=1, source_target_pairs={{0,64},{1,5},{2,66},{3,7},{4,68},{5,1},{6,70},{7,3},{8,72},{9,13},... | collective-permute-start | bytes 1572872 | tf_op jit(solution)/shard_map/ppermute | solution.py:46
  75.6 11.9 %collective-permute-start.28 = (bf16[2,256,512]{2,1,0:T(8,128)(2,1)S(1)}, bf16[2,256,512]{2,1,0:T(8,128)(2,1)S(1)}, u32[]{:S(2)}, u32[]{:S(2)}) collective-permute-start(bf16[2,256,512]{2,1,0:T(8,128)(2,1)S(1)} %shard_map.92), channel_id=1, source_target_pairs={{0,96},{1,7},{2,98},{3,1},{4,100},{5,3},{6,102},{7,5},{8,104},{9,1... | collective-permute-start | bytes 1572872 | tf_op jit(solution)/shard_map/ppermute | solution.py:46
  79.3 32.9 %collective-permute-start.19 = (f32[256,1024]{1,0:T(8,128)S(1)}, f32[256,1024]{1,0:T(8,128)S(1)}, u32[]{:S(2)}, u32[]{:S(2)}) collective-permute-start(f32[256,1024]{1,0:T(8,128)S(1)} %fusion.13), channel_id=1, source_target_pairs={{0,1},{1,0},{2,3},{3,2},{4,5},{5,4},{6,7},{7,6},{8,9},{9,8},{10,11... | collective-permute-start | bytes 3145736 | tf_op jit(solution)/shard_map/ppermute | solution.py:50
  81.2 12.9 %collective-permute-start.29 = (bf16[1,128,512]{2,1,0:T(8,128)(2,1)S(1)}, bf16[1,128,512]{2,1,0:T(8,128)(2,1)S(1)}, u32[]{:S(2)}, u32[]{:S(2)}) collective-permute-start(bf16[1,128,512]{2,1,0:T(8,128)(2,1)S(1)} %get-tuple-element.73), channel_id=1, source_target_pairs={{0,8},{1,33},{2,10},{3,35},{4,12},{5,37},{6,14},{7,39},{8,16},{9,4... | collective-permute-start | bytes 393224 | tf_op jit(solution)/shard_map/ppermute | solution.py:46
  83.1 10.9 %collective-permute-start.30 = (bf16[1,128,512]{2,1,0:T(8,128)(2,1)S(1)}, bf16[1,128,512]{2,1,0:T(8,128)(2,1)S(1)}, u32[]{:S(2)}, u32[]{:S(2)}) collective-permute-start(bf16[1,128,512]{2,1,0:T(8,128)(2,1)S(1)} %get-tuple-element.74), channel_id=1, source_target_pairs={{0,16},{1,65},{2,18},{3,67},{4,20},{5,69},{6,22},{7,71},{8,24},{9,... | collective-permute-start | bytes 393224 | tf_op jit(solution)/shard_map/ppermute | solution.py:46
  88.8 13.3 %collective-permute-start.32 = (bf16[2,128,512]{2,1,0:T(8,128)(2,1)S(1)}, bf16[2,128,512]{2,1,0:T(8,128)(2,1)S(1)}, u32[]{:S(2)}, u32[]{:S(2)}) collective-permute-start(bf16[2,128,512]{2,1,0:T(8,128)(2,1)S(1)} %get-tuple-element.76), channel_id=1, source_target_pairs={{0,8},{1,33},{2,10},{3,35},{4,12},{5,37},{6,14},{7,39},{8,16},{9,4... | collective-permute-start | bytes 786440 | tf_op jit(solution)/shard_map/ppermute | solution.py:46
  90.7 11.4 %collective-permute-start.33 = (bf16[2,128,512]{2,1,0:T(8,128)(2,1)S(1)}, bf16[2,128,512]{2,1,0:T(8,128)(2,1)S(1)}, u32[]{:S(2)}, u32[]{:S(2)}) collective-permute-start(bf16[2,128,512]{2,1,0:T(8,128)(2,1)S(1)} %get-tuple-element.77), channel_id=1, source_target_pairs={{0,16},{1,65},{2,18},{3,67},{4,20},{5,69},{6,22},{7,71},{8,24},{9,... | collective-permute-start | bytes 786440 | tf_op jit(solution)/shard_map/ppermute | solution.py:46
  94.0 8.1 %collective-permute-start.34 = (bf16[2,128,512]{2,1,0:T(8,128)(2,1)S(1)}, bf16[2,128,512]{2,1,0:T(8,128)(2,1)S(1)}, u32[]{:S(2)}, u32[]{:S(2)}) collective-permute-start(bf16[2,128,512]{2,1,0:T(8,128)(2,1)S(1)} %get-tuple-element.78), channel_id=1, source_target_pairs={{0,24},{1,97},{2,26},{3,99},{4,28},{5,101},{6,30},{7,103},{8,0},{9... | collective-permute-start | bytes 786440 | tf_op jit(solution)/shard_map/ppermute | solution.py:46
  94.1 8.1 %collective-permute-start.31 = (bf16[1,128,512]{2,1,0:T(8,128)(2,1)S(1)}, bf16[1,128,512]{2,1,0:T(8,128)(2,1)S(1)}, u32[]{:S(2)}, u32[]{:S(2)}) collective-permute-start(bf16[1,128,512]{2,1,0:T(8,128)(2,1)S(1)} %get-tuple-element.75), channel_id=1, source_target_pairs={{0,24},{1,97},{2,26},{3,99},{4,28},{5,101},{6,30},{7,103},{8,0},{9... | collective-permute-start | bytes 393224 | tf_op jit(solution)/shard_map/ppermute | solution.py:46
  103.0 7.1 %collective-permute-start.35 = (bf16[3,32,512]{2,1,0:T(8,128)(2,1)S(1)}, bf16[3,32,512]{2,1,0:T(8,128)(2,1)S(1)}, u32[]{:S(2)}, u32[]{:S(2)}) collective-permute-start(bf16[3,32,512]{2,1,0:T(8,128)(2,1)S(1)} %get-tuple-element.80), channel_id=1, source_target_pairs={{0,2},{1,9},{2,4},{3,11},{4,6},{5,13},{6,0},{7,15},{8,10},{9,17},{... | collective-permute-start | bytes 294920 | tf_op jit(solution)/shard_map/ppermute | solution.py:46
  103.1 7.5 %collective-permute-start.36 = (bf16[3,32,512]{2,1,0:T(8,128)(2,1)S(1)}, bf16[3,32,512]{2,1,0:T(8,128)(2,1)S(1)}, u32[]{:S(2)}, u32[]{:S(2)}) collective-permute-start(bf16[3,32,512]{2,1,0:T(8,128)(2,1)S(1)} %get-tuple-element.81), channel_id=1, source_target_pairs={{0,4},{1,17},{2,6},{3,19},{4,0},{5,21},{6,2},{7,23},{8,12},{9,25},... | collective-permute-start | bytes 294920 | tf_op jit(solution)/shard_map/ppermute | solution.py:46
  106.9 4.6 %collective-permute-start.37 = (bf16[3,32,512]{2,1,0:T(8,128)(2,1)S(1)}, bf16[3,32,512]{2,1,0:T(8,128)(2,1)S(1)}, u32[]{:S(2)}, u32[]{:S(2)}) collective-permute-start(bf16[3,32,512]{2,1,0:T(8,128)(2,1)S(1)} %get-tuple-element.82), channel_id=1, source_target_pairs={{0,6},{1,25},{2,0},{3,27},{4,2},{5,29},{6,4},{7,31},{8,14},{9,1},{... | collective-permute-start | bytes 294920 | tf_op jit(solution)/shard_map/ppermute | solution.py:46

commit v7 on v5

--- a/solution.py
+++ b/solution.py
@@ -1,5 +1,3 @@
-import functools
-
 import jax
 import jax.numpy as jnp
 from jax import lax
@@ -246,6 +244,18 @@
         out[...] = product[:, rows, :].astype(out.dtype)
 
 
+def turn_kernel(h0, h1, h2, h3, turned_out):
+    for n, block in enumerate((h0, h1, h2, h3)):
+        turned_out[:, 256 * n : 256 * n + 256] = turned(block[...]).astype(BF)
+
+
+def product_kernel(pos, columns, g0, g1, g2, g3, own, o1, o2, o3, product):
+    for m in range(product.shape[0]):
+        rows = jnp.concatenate([block[m] for block in (g0, g1, g2, g3)], axis=0)
+        product[m] = dot(columns[...], rows, ((1,), (0,)))
+    second_kernel(pos, product, own, o1, o2, o3)
+
+
 def third_kernel(
     pos, mine0, mine1, a1, a2, a3, b1, b2, b3, own, o1, o2, o3, total
 ):
@@ -270,7 +280,7 @@
         out_specs=[whole] * len(outs),
         out_shape=outs,
         scratch_shapes=scratch,
-        compiler_params=pltpu.CompilerParams(vmem_limit_bytes=8 << 20),
+        compiler_params=pltpu.CompilerParams(vmem_limit_bytes=12 << 20),
     )
     held = [pltpu.with_memory_space_constraint(a, pltpu.VMEM) for a in arrays]
     return run(*([] if pos is None else [pos]), *held)
@@ -349,7 +359,10 @@
     attended, level_grad = call(
         read_kernel,
         [projected, out_grad, mix, out_t, level_in, buckets],
-        [shape((256, 512), BF), shape((15, 4, 256), F32)],
+        [
+            jax.ShapeDtypeStruct((256, 512), BF),
+            jax.ShapeDtypeStruct((15, 4, 256), F32),
+        ],
     )
 
     grad_blocks = [[grads[0]], [grads[1]]]
@@ -365,17 +378,7 @@
     came = partner(theirs)
     input_grad = (mine + came).astype(BF)
 
-    def products(blocks):
-        return functools.reduce(
-            jnp.add,
-            [
-                jnp.einsum("td,mte->mde", h, g, preferred_element_type=F32)
-                for h, g in zip(hidden_blocks, blocks)
-            ],
-        )
-
-    key_value_products = products(grad_blocks[0])
-    query_products = products(grad_blocks[1])
+    (columns_turned,) = call(turn_kernel, hidden_blocks, [shape((512, 1024), BF)])
 
     def exchanged(pieces, axes):
         came = []
@@ -383,18 +386,19 @@
             came.append(shifted(piece, axes, n))
         return came
 
-    def second(product):
-        size = product.shape[0]
+    def second(blocks):
+        size = blocks[0].shape[0]
         own, *pieces = call(
-            second_kernel,
-            [product],
+            product_kernel,
+            [columns_turned, *blocks],
             [shape((size, 128, 512), F32)] + [shape((size, 128, 512), BF)] * 3,
             pos,
+            [pltpu.VMEM((size, 512, 512), F32)],
         )
         return own, exchanged(pieces, (Z, X))
 
-    own1, came1 = second(key_value_products)
-    own0, came0 = second(query_products)
+    own1, came1 = second(grad_blocks[0])
+    own0, came0 = second(grad_blocks[1])
     own, *pieces = call(
         third_kernel,
         [own0, own1, *came0, *came1],

time: 118 us -> 116 us (0.983)
  starting transfers between devices: 54.1 us -> 59.3 us
  waiting for transfers between devices: 37.3 us -> 32.7 us
  matrix products: 11.5 us -> 8.08 us
  Pallas kernels: 10.2 us -> 13.2 us
  local copies, waits for them, and re-layouts: 1.36 us -> 0.04 us
    ppermute x2, starting transfers between devices: 0.17 us -> 5.23 us  [partner(): return lax.ppermute(value, 'head', [(0, 1), (1, 0)])]
    ppermute x36, waiting for transfers between devices: 37.3 us -> 32.7 us  [shifted(): return lax.ppermute(value, ALL, pairs)]
    dot_general x8 -> x0, matrix products: 3.43 us -> none  [products(): jnp.einsum('td,mte->mde', h, g, preferred_element_type=F32)]
    pallas_call x13 -> x14, Pallas kernels: 10.2 us -> 13.2 us  [call(): return run(*([] if pos is None else [pos]), *held)]
    unnamed x14 -> x12, local copies, waits for them, and re-layouts: 1.36 us -> 0.04 us
  transfers between devices with their start and end apart: 38 -> 38, of which waited for: 11 -> 14; matrix products, arithmetic and copies ran while one was open for 9% -> 5% of each run, Pallas kernels for 8% -> 10%
where the time goes in v7:
time: 116 us
  starting transfers between devices  59.3 us (51%)
  waiting for transfers between devices  32.7 us (28%)
  Pallas kernels  13.2 us (11%)
  matrix products  8.08 us (7%)
  other arithmetic  1.73 us (1%)
    ppermute x36, starting transfers between devices, shifted(): return lax.ppermute(value, ALL, pairs)  54.1 us
    ppermute x36, waiting for transfers between devices, shifted(): return lax.ppermute(value, ALL, pairs)  32.7 us
    pallas_call x14, Pallas kernels, call(): return run(*([] if pos is None else [pos]), *held)  13.2 us
    ppermute x2, starting transfers between devices, partner(): return lax.ppermute(value, 'head', [(0, 1), (1, 0)])  5.23 us
    dot_general x1, matrix products, layer(): jnp.einsum('td,dme->mte', hidden, near, preferred_element_type=F32)  3.03 us
    dot_general x1, matrix products, layer(): far_part = jnp.einsum('td,dme->mte', other, far, preferred_element_type=F32)  3.03 us
  transfers between devices with their start and end apart: 38, of which 14 were waited for; matrix products, arithmetic and copies ran while one was open for 5% of the time, Pallas kernels for 10%

profile of v7, /device:TPU:0, one launch (start us, length us, event | category | flops | bytes accessed | tf_op | source)
XLA Modules:
  0.0 116.0 jit_solution(17004885672087763549)
XLA Ops:
  0.8 3.0 %fusion.4 = f32[3,512,256]{1,2,0:T(8,128)S(1)} fusion(bf16[2048,3,512]{2,0,1:T(8,128)(2,1)} %param.6, s32[]{:T(128)S(6)} %select_n.6, bf16[256,1024]{1,0:T(8,128)(2,1)} %hidden.1), kind=kOutput, calls=%fused_computation.4 | convolution fusion | flops 805306368 | bytes 5242884 | tf_op jit(solution)/shard_map/td,dme->mte/dot_general | solution.py:297
  3.9 3.0 %fusion.16.proj = bf16[3,256,512]{2,1,0:T(8,128)(2,1)S(1)} fusion(f32[3,512,256]{1,2,0:T(8,128)S(1)} %fusion.4, bf16[2048,3,512]{2,0,1:T(8,128)(2,1)} %param.6, s32[]{:T(128)S(6)} %select_n.7, f32[3]{0:T(128)S(1)} %copy-done.3, bf16[256,1024]{1,0:T(8,128)(2,1)S(1)} %collective-permute-done.other), kind=kOutput, calls=%fused_computation.11 | convolution fusion | flops 806486016 | bytes 6029328 | tf_op jit(solution)/shard_map/td,dme->mte/dot_general | solution.py:298
  7.0 1.3 %shard_map.85 = (bf16[512,128]{1,0:T(8,128)(2,1)S(1)}, bf16[512,128]{1,0:T(8,128)(2,1)S(1)}, bf16[512,128]{1,0:T(8,128)(2,1)S(1)}, bf16[512,128]{1,0:T(8,128)(2,...) custom-call(s32[4]{0:T(128)S(1)} %pad_add_fusion.pos, ...), custom_call_target="tpu_custom_call" | custom-call | tf_op jit(solution)/shard_map/pallas_call | solution.py:286
  8.3 1.3 %collective-permute-start.12 = (bf16[512,128]{1,0:T(8,128)(2,1)S(1)}, bf16[512,128]{1,0:T(8,128)(2,1)S(1)}, u32[]{:S(2)}, u32[]{:S(2)}) collective-permute-start(bf16[512,128]{1,0:T(8,128)(2,1)S(1)} %get-tuple-element.54), channel_id=1, source_target_pairs={{32,0},{33,1},{34,2},{35,3},{36,4},{37,5},{38,6},{39,7},{40,8},{41... | collective-permute-start | bytes 393224 | tf_op jit(solution)/shard_map/ppermute | solution.py:44
  9.6 1.3 %collective-permute-start.11 = (bf16[512,128]{1,0:T(8,128)(2,1)S(1)}, bf16[512,128]{1,0:T(8,128)(2,1)S(1)}, u32[]{:S(2)}, u32[]{:S(2)}) collective-permute-start(bf16[512,128]{1,0:T(8,128)(2,1)S(1)} %get-tuple-element.53), channel_id=1, source_target_pairs={{64,0},{65,1},{66,2},{67,3},{68,4},{69,5},{70,6},{71,7},{72,8},{73... | collective-permute-start | bytes 393224 | tf_op jit(solution)/shard_map/ppermute | solution.py:44
  10.9 1.3 %collective-permute-start.10 = (bf16[512,128]{1,0:T(8,128)(2,1)S(1)}, bf16[512,128]{1,0:T(8,128)(2,1)S(1)}, u32[]{:S(2)}, u32[]{:S(2)}) collective-permute-start(bf16[512,128]{1,0:T(8,128)(2,1)S(1)} %get-tuple-element.53), channel_id=1, source_target_pairs={{96,0},{97,1},{98,2},{99,3},{100,4},{101,5},{102,6},{103,7},{104,8... | collective-permute-start | bytes 393224 | tf_op jit(solution)/shard_map/ppermute | solution.py:44
  12.2 3.2 %collective-permute-start.3 = (bf16[512,128]{1,0:T(8,128)(2,1)S(1)}, bf16[512,128]{1,0:T(8,128)(2,1)S(1)}, u32[]{:S(2)}, u32[]{:S(2)}) collective-permute-start(bf16[512,128]{1,0:T(8,128)(2,1)S(1)} %get-tuple-element.47.mine), channel_id=1, source_target_pairs={{0,6},{1,7},{2,0},{3,1},{4,2},{5,3},{6,4},{7,5},{8,14},{9,15},{10,... | collective-permute-start | bytes 393224 | tf_op jit(solution)/shard_map/ppermute | solution.py:44
  15.3 0.6 collective-permute-start.2
  16.0 1.7 %collective-permute-start.1 = (bf16[512,128]{1,0:T(8,128)(2,1)S(1)}, bf16[512,128]{1,0:T(8,128)(2,1)S(1)}, u32[]{:S(2)}, u32[]{:S(2)}) collective-permute-start(bf16[512,128]{1,0:T(8,128)(2,1)S(1)} %get-tuple-element.47.mine), channel_id=1, source_target_pairs={{0,2},{1,3},{2,4},{3,5},{4,6},{5,7},{6,0},{7,1},{8,10},{9,11},{10,... | collective-permute-start | bytes 393224 | tf_op jit(solution)/shard_map/ppermute | solution.py:44
  17.7 1.3 %collective-permute-done.11.r2 = bf16[512,128]{1,0:T(8,128)(2,1)S(1)} collective-permute-done((bf16[512,128]{1,0:T(8,128)(2,1)S(1)}, bf16[512,128]{1,0:T(8,128)(2,1)S(1)}, u32[]{:S(2)}, u32[]{:S(2)}) %collective-permute-start.11) | collective-permute-done | bytes 131104 | tf_op jit(solution)/shard_map/ppermute | solution.py:44
  19.0 2.8 %collective-permute-done.10.r1 = bf16[512,128]{1,0:T(8,128)(2,1)S(1)} collective-permute-done((bf16[512,128]{1,0:T(8,128)(2,1)S(1)}, bf16[512,128]{1,0:T(8,128)(2,1)S(1)}, u32[]{:S(2)}, u32[]{:S(2)}) %collective-permute-start.10) | collective-permute-done | bytes 131104 | tf_op jit(solution)/shard_map/ppermute | solution.py:44
  21.8 0.7 shard_map.90
  22.5 2.0 %collective-permute-start.13 = (bf16[512,128]{1,0:T(8,128)(2,1)S(1)}, bf16[512,128]{1,0:T(8,128)(2,1)S(1)}, u32[]{:S(2)}, u32[]{:S(2)}) collective-permute-start(bf16[512,128]{1,0:T(8,128)(2,1)S(1)} %get-tuple-element.57), channel_id=1, source_target_pairs={{0,8},{1,9},{2,10},{3,11},{4,12},{5,13},{6,14},{7,15},{8,16},{9,17... | collective-permute-start | bytes 393224 | tf_op jit(solution)/shard_map/ppermute | solution.py:44
  24.5 3.6 %collective-permute-start.14 = (bf16[512,128]{1,0:T(8,128)(2,1)S(1)}, bf16[512,128]{1,0:T(8,128)(2,1)S(1)}, u32[]{:S(2)}, u32[]{:S(2)}) collective-permute-start(bf16[512,128]{1,0:T(8,128)(2,1)S(1)} %get-tuple-element.58), channel_id=1, source_target_pairs={{0,16},{1,17},{2,18},{3,19},{4,20},{5,21},{6,22},{7,23},{8,24},{9,... | collective-permute-start | bytes 393224 | tf_op jit(solution)/shard_map/ppermute | solution.py:44
  28.1 1.0 collective-permute-start.15
  29.1 0.3 collective-permute-start.6
  29.4 2.9 %collective-permute-start.5 = (bf16[512,128]{1,0:T(8,128)(2,1)S(1)}, bf16[512,128]{1,0:T(8,128)(2,1)S(1)}, u32[]{:S(2)}, u32[]{:S(2)}) collective-permute-start(bf16[512,128]{1,0:T(8,128)(2,1)S(1)} %shard_map.86.mine), channel_id=1, source_target_pairs={{0,16},{1,17},{2,18},{3,19},{4,20},{5,21},{6,22},{7,23},{8,24},{9,... | collective-permute-start | bytes 393224 | tf_op jit(solution)/shard_map/ppermute | solution.py:44
  32.3 1.6 %collective-permute-done.14.r2 = bf16[512,128]{1,0:T(8,128)(2,1)S(1)} collective-permute-done((bf16[512,128]{1,0:T(8,128)(2,1)S(1)}, bf16[512,128]{1,0:T(8,128)(2,1)S(1)}, u32[]{:S(2)}, u32[]{:S(2)}) %collective-permute-start.14) | collective-permute-done | bytes 131104 | tf_op jit(solution)/shard_map/ppermute | solution.py:44
  33.9 0.5 collective-permute-done.15.r3
  34.4 0.7 shard_map.91
  35.1 2.4 %collective-permute-start.16 = (bf16[512,128]{1,0:T(8,128)(2,1)S(1)}, bf16[512,128]{1,0:T(8,128)(2,1)S(1)}, u32[]{:S(2)}, u32[]{:S(2)}) collective-permute-start(bf16[512,128]{1,0:T(8,128)(2,1)S(1)} %get-tuple-element.64), channel_id=1, source_target_pairs={{0,2},{1,3},{2,4},{3,5},{4,6},{5,7},{6,0},{7,1},{8,10},{9,11},{10,... | collective-permute-start | bytes 393224 | tf_op jit(solution)/shard_map/ppermute | solution.py:44
  37.6 1.7 %collective-permute-done.4.a1.refs_3_ = bf16[512,128]{1,0:T(8,128)(2,1)S(1)} collective-permute-done((bf16[512,128]{1,0:T(8,128)(2,1)S(1)}, bf16[512,128]{1,0:T(8,128)(2,1)S(1)}, u32[]{:S(2)}, u32[]{:S(2)}) %collective-permute-start.4) | collective-permute-done | bytes 131104 | tf_op jit(solution)/shard_map/ppermute | solution.py:44
  39.3 6.7 %collective-permute-start.9 = (bf16[512,128]{1,0:T(8,128)(2,1)S(1)}, bf16[512,128]{1,0:T(8,128)(2,1)S(1)}, u32[]{:S(2)}, u32[]{:S(2)}) collective-permute-start(bf16[512,128]{1,0:T(8,128)(2,1)S(1)} %shard_map.87), channel_id=1, source_target_pairs={{0,96},{1,97},{2,98},{3,99},{4,100},{5,101},{6,102},{7,103},{8,104... | collective-permute-start | bytes 393224 | tf_op jit(solution)/shard_map/ppermute | solution.py:44
  46.0 1.3 %collective-permute-start.8 = (bf16[512,128]{1,0:T(8,128)(2,1)S(1)}, bf16[512,128]{1,0:T(8,128)(2,1)S(1)}, u32[]{:S(2)}, u32[]{:S(2)}) collective-permute-start(bf16[512,128]{1,0:T(8,128)(2,1)S(1)} %shard_map.87), channel_id=1, source_target_pairs={{0,64},{1,65},{2,66},{3,67},{4,68},{5,69},{6,70},{7,71},{8,72},{9,... | collective-permute-start | bytes 393224 | tf_op jit(solution)/shard_map/ppermute | solution.py:44
  47.3 2.8 %collective-permute-start.7 = (bf16[512,128]{1,0:T(8,128)(2,1)S(1)}, bf16[512,128]{1,0:T(8,128)(2,1)S(1)}, u32[]{:S(2)}, u32[]{:S(2)}) collective-permute-start(bf16[512,128]{1,0:T(8,128)(2,1)S(1)} %shard_map.87), channel_id=1, source_target_pairs={{0,32},{1,33},{2,34},{3,35},{4,36},{5,37},{6,38},{7,39},{8,40},{9,... | collective-permute-start | bytes 393224 | tf_op jit(solution)/shard_map/ppermute | solution.py:44
  50.1 0.7 shard_map.93
  51.0 0.5 collective-permute-done.9.refs_8_
  51.4 3.7 %collective-permute-start.22 = (bf16[256,512]{1,0:T(8,128)(2,1)S(1)}, bf16[256,512]{1,0:T(8,128)(2,1)S(1)}, u32[]{:S(2)}, u32[]{:S(2)}) collective-permute-start(bf16[256,512]{1,0:T(8,128)(2,1)S(1)} %get-tuple-element.70), channel_id=1, source_target_pairs={{0,96},{1,7},{2,98},{3,1},{4,100},{5,3},{6,102},{7,5},{8,104},{9,1... | collective-permute-start | bytes 786440 | tf_op jit(solution)/shard_map/ppermute | solution.py:44
  55.1 0.1 collective-permute-start.17
  55.2 0.2 collective-permute-start.18
  55.4 1.9 %shard_map.84 = (f32[4,128,256]{2,1,0:T(8,128)S(1)}, f32[4,128,256]{2,1,0:T(8,128)S(1)}, f32[256,512]{1,0:T(8,128)S(1)}, f32[256,512]{1,0:T(8,128)S(1)}, f32[9,4,256]{2,1,0:T(4,128)S(1)}) custom-call(bf16[3,256,512]{2,1,0:T(8,128)(2,1)S(1)} %fusion.16.proj, bf16[256,512]{1,0:T(8,128)(2,1)S(1)} %copy-done, f32[15,4,256]{2,1,0:T(4,128)S(1)} %copy-done.2), custom_call_target="tpu_custom_call" | custom-call | tf_op jit(solution)/shard_map/pallas_call | solution.py:286
  57.3 1.4 %shard_map.88 = (bf16[1,256,512]{2,1,0:T(8,128)(2,1)S(1)}, bf16[6,512,128]{2,1,0:T(8,128)(2,1)S(1)}) custom-call(s32[4]{0:T(128)S(1)} %pad_add_fusion.pos, bf16[256,512]{1,0:T(8,128)(2,1)S(1)} %copy-done, f32[15,4,256]{2,1,0:T(4,128)S(1)} %copy-done.2, f32[4,128,256]{2,1,0:T(8,128)S(1)} %get-tuple-element.46.query_t, ...), custom_call_target="tpu_custom_call" | custom-call | tf_op jit(solution)/shard_map/pallas_call | solution.py:286
  58.7 2.9 %collective-permute-done.17.ry2 = bf16[512,128]{1,0:T(8,128)(2,1)S(1)} collective-permute-done((bf16[512,128]{1,0:T(8,128)(2,1)S(1)}, bf16[512,128]{1,0:T(8,128)(2,1)S(1)}, u32[]{:S(2)}, u32[]{:S(2)}) %collective-permute-start.17) | collective-permute-done | bytes 131104 | tf_op jit(solution)/shard_map/ppermute | solution.py:44
  61.7 0.2 collective-permute-done.18.ry3
  61.9 2.8 %collective-permute-start.24 = (bf16[1,256,512]{2,1,0:T(8,128)(2,1)S(1)}, bf16[1,256,512]{2,1,0:T(8,128)(2,1)S(1)}, u32[]{:S(2)}, u32[]{:S(2)}) collective-permute-start(bf16[1,256,512]{2,1,0:T(8,128)(2,1)S(1)} %get-tuple-element.50.g0), channel_id=1, source_target_pairs={{0,64},{1,5},{2,66},{3,7},{4,68},{5,1},{6,70},{7,3},{8,72},{9,13},... | collective-permute-start | bytes 786440 | tf_op jit(solution)/shard_map/ppermute | solution.py:44
  64.7 0.3 shard_map.92.g0
  65.0 1.6 %collective-permute-start.28 = (bf16[2,256,512]{2,1,0:T(8,128)(2,1)S(1)}, bf16[2,256,512]{2,1,0:T(8,128)(2,1)S(1)}, u32[]{:S(2)}, u32[]{:S(2)}) collective-permute-start(bf16[2,256,512]{2,1,0:T(8,128)(2,1)S(1)} %shard_map.92.g0), channel_id=1, source_target_pairs={{0,96},{1,7},{2,98},{3,1},{4,100},{5,3},{6,102},{7,5},{8,104},{9,1... | collective-permute-start | bytes 1572872 | tf_op jit(solution)/shard_map/ppermute | solution.py:44
  66.7 0.8 collective-permute-start.27
  67.5 0.2 collective-permute-start.26
  67.6 1.0 fusion.13
  68.7 5.1 %collective-permute-start.19 = (f32[256,1024]{1,0:T(8,128)S(1)}, f32[256,1024]{1,0:T(8,128)S(1)}, u32[]{:S(2)}, u32[]{:S(2)}) collective-permute-start(f32[256,1024]{1,0:T(8,128)S(1)} %fusion.13), channel_id=1, source_target_pairs={{0,1},{1,0},{2,3},{3,2},{4,5},{5,4},{6,7},{7,6},{8,9},{9,8},{10,11... | collective-permute-start | bytes 3145736 | tf_op jit(solution)/shard_map/ppermute | solution.py:48
  73.8 0.3 collective-permute-start.23
  74.1 0.4 shard_map.94.columns
  74.5 11.3 %collective-permute-done.23.g1 = bf16[1,256,512]{2,1,0:T(8,128)(2,1)S(1)} collective-permute-done((bf16[1,256,512]{2,1,0:T(8,128)(2,1)S(1)}, bf16[1,256,512]{2,1,0:T(8,128)(2,1)S(1)}, u32[]{:S(2)}, u32[]{:S(2)}) %collective-permute-start.23) | collective-permute-done | bytes 262176 | tf_op jit(solution)/shard_map/ppermute | solution.py:44
  85.8 1.3 %shard_map.95 = (f32[1,128,512]{2,1,0:T(8,128)S(1)}, bf16[1,128,512]{2,1,0:T(8,128)(2,1)S(1)}, bf16[1,128,512]{2,1,0:T(8,128)(2,1)S(1)}, bf16[1,128,512]{2,1,0:T(8,128)(2,1)S(1)}) custom-call(s32[4]{0:T(128)S(1)} %pad_add_fusion.pos, bf16[512,1024]{1,0:T(8,128)(2,1)S(1)} %shard_map.94.columns, bf16[1,256,512]{2,1,0:T(8,128)(2,1)S(1)} %get-tuple-element.50.g0, ...), custom_call_target="tpu_custom_call" | custom-call | tf_op jit(solution)/shard_map/pallas_call | solution.py:286
  87.1 0.2 collective-permute-start.29
  87.3 3.0 %collective-permute-start.30 = (bf16[1,128,512]{2,1,0:T(8,128)(2,1)S(1)}, bf16[1,128,512]{2,1,0:T(8,128)(2,1)S(1)}, u32[]{:S(2)}, u32[]{:S(2)}) collective-permute-start(bf16[1,128,512]{2,1,0:T(8,128)(2,1)S(1)} %get-tuple-element.74), channel_id=1, source_target_pairs={{0,16},{1,65},{2,18},{3,67},{4,20},{5,69},{6,22},{7,71},{8,24},{9,... | collective-permute-start | bytes 393224 | tf_op jit(solution)/shard_map/ppermute | solution.py:44
  90.3 1.9 %shard_map.96 = (f32[2,128,512]{2,1,0:T(8,128)S(1)}, bf16[2,128,512]{2,1,0:T(8,128)(2,1)S(1)}, bf16[2,128,512]{2,1,0:T(8,128)(2,1)S(1)}, bf16[2,128,512]{2,1,0:T(8,128)(2,1)S(1)}) custom-call(s32[4]{0:T(128)S(1)} %pad_add_fusion.pos, bf16[512,1024]{1,0:T(8,128)(2,1)S(1)} %shard_map.94.columns, bf16[2,256,512]{2,1,0:T(8,128)(2,1)S(1)} %shard_map.92.g0, ...), custom_call_target="tpu_custom_call" | custom-call | tf_op jit(solution)/shard_map/pallas_call | solution.py:286
  92.2 1.1 collective-permute-start.32
  93.3 0.6 collective-permute-start.33
  94.0 0.8 collective-permute-done.29.a1
  94.8 1.3 %collective-permute-start.34 = (bf16[2,128,512]{2,1,0:T(8,128)(2,1)S(1)}, bf16[2,128,512]{2,1,0:T(8,128)(2,1)S(1)}, u32[]{:S(2)}, u32[]{:S(2)}) collective-permute-start(bf16[2,128,512]{2,1,0:T(8,128)(2,1)S(1)} %get-tuple-element.78), channel_id=1, source_target_pairs={{0,24},{1,97},{2,26},{3,99},{4,28},{5,101},{6,30},{7,103},{8,0},{9... | collective-permute-start | bytes 786440 | tf_op jit(solution)/shard_map/ppermute | solution.py:44
  96.1 1.3 %collective-permute-start.31 = (bf16[1,128,512]{2,1,0:T(8,128)(2,1)S(1)}, bf16[1,128,512]{2,1,0:T(8,128)(2,1)S(1)}, u32[]{:S(2)}, u32[]{:S(2)}) collective-permute-start(bf16[1,128,512]{2,1,0:T(8,128)(2,1)S(1)} %get-tuple-element.75), channel_id=1, source_target_pairs={{0,24},{1,97},{2,26},{3,99},{4,28},{5,101},{6,30},{7,103},{8,0},{9... | collective-permute-start | bytes 393224 | tf_op jit(solution)/shard_map/ppermute | solution.py:44
  97.4 7.6 %collective-permute-done.31.a3 = bf16[1,128,512]{2,1,0:T(8,128)(2,1)S(1)} collective-permute-done((bf16[1,128,512]{2,1,0:T(8,128)(2,1)S(1)}, bf16[1,128,512]{2,1,0:T(8,128)(2,1)S(1)}, u32[]{:S(2)}, u32[]{:S(2)}) %collective-permute-start.31) | collective-permute-done | bytes 131104 | tf_op jit(solution)/shard_map/ppermute | solution.py:44
  105.0 0.8 shard_map.97
  105.9 1.5 %collective-permute-start.35 = (bf16[3,32,512]{2,1,0:T(8,128)(2,1)S(1)}, bf16[3,32,512]{2,1,0:T(8,128)(2,1)S(1)}, u32[]{:S(2)}, u32[]{:S(2)}) collective-permute-start(bf16[3,32,512]{2,1,0:T(8,128)(2,1)S(1)} %get-tuple-element.80), channel_id=1, source_target_pairs={{0,2},{1,9},{2,4},{3,11},{4,6},{5,13},{6,0},{7,15},{8,10},{9,17},{... | collective-permute-start | bytes 294920 | tf_op jit(solution)/shard_map/ppermute | solution.py:44
  107.4 2.4 %collective-permute-start.36 = (bf16[3,32,512]{2,1,0:T(8,128)(2,1)S(1)}, bf16[3,32,512]{2,1,0:T(8,128)(2,1)S(1)}, u32[]{:S(2)}, u32[]{:S(2)}) collective-permute-start(bf16[3,32,512]{2,1,0:T(8,128)(2,1)S(1)} %get-tuple-element.81), channel_id=1, source_target_pairs={{0,4},{1,17},{2,6},{3,19},{4,0},{5,21},{6,2},{7,23},{8,12},{9,25},... | collective-permute-start | bytes 294920 | tf_op jit(solution)/shard_map/ppermute | solution.py:44
  109.7 0.5 collective-permute-start.37
  110.2 1.0 fusion.10
  111.3 1.7 %shard_map.89 = (bf16[256,512]{1,0:T(8,128)(2,1)}, f32[15,4,256]{2,1,0:T(4,128)}) custom-call(bf16[3,256,512]{2,1,0:T(8,128)(2,1)S(1)} %fusion.16.proj, bf16[256,512]{1,0:T(8,128)(2,1)S(1)} %copy-done, f32[15,4,256]{2,1,0:T(4,128)S(1)} %copy-done.2, f32[4,128,256]{2,1,0:T(8,128)S(1)} %get-tuple-element.44.out_t, ...), custom_call_target="tpu_custom_call" | custom-call | tf_op jit(solution)/shard_map/pallas_call | solution.py:286
  113.0 0.6 collective-permute-done.36
  113.5 0.8 collective-permute-done.37
  114.4 0.7 multiply_bitcast_fusion
  115.1 0.9 add_convert_fusion
  (46 shorter events, 0.7 us)
Async XLA Ops:
  0.6 3.3 %copy-start.3 = (f32[3]{0:T(128)S(1)}, f32[3]{0:T(128)}, u32[]{:S(2)}) copy-start(f32[3]{0:T(128)} %constant.27.clone) | copy-start | bytes 40
  0.6 3.3 %collective-permute-start = (bf16[256,1024]{1,0:T(8,128)(2,1)}, bf16[256,1024]{1,0:T(8,128)(2,1)S(1)}, u32[]{:S(2)}, u32[]{:S(2)}) collective-permute-start(bf16[256,1024]{1,0:T(8,128)(2,1)} %hidden.1), channel_id=1, source_target_pairs={{0,1},{1,0},{2,3},{3,2},{4,5},{5,4},{6,7},{7,6},{8,9},{9,8},{10,11... | collective-permute-start | bytes 1572872 | tf_op jit(solution)/shard_map/ppermute | solution.py:48
  3.9 3.1 %copy-start = (bf16[256,512]{1,0:T(8,128)(2,1)S(1)}, bf16[256,512]{1,0:T(8,128)(2,1)}, u32[]{:S(2)}) copy-start(bf16[256,512]{1,0:T(8,128)(2,1)} %out_grad.3) | copy-start | bytes 786436
  3.9 3.1 %copy-start.2 = (f32[15,4,256]{2,1,0:T(4,128)S(1)}, f32[15,4,256]{2,1,0:T(4,128)}, u32[]{:S(2)}) copy-start(f32[15,4,256]{2,1,0:T(4,128)} %mix.7) | copy-start | bytes 184324
  3.9 63.7 %slice-start = ((s8[6291456]{0:T(1024)(128)(4,1)}), s8[4194304]{0:T(1024)(128)(4,1)S(1)}, s32[]{:S(2)}) async-start(s8[6291456]{0:T(1024)(128)(4,1)} %bitcast.18), calls=%async_computation | async-start | bytes 8388608
  7.0 43.1 %copy-start.1 = (bf16[256,1024]{1,0:T(8,128)(2,1)S(1)}, bf16[256,1024]{1,0:T(8,128)(2,1)}, u32[]{:S(2)}) copy-start(bf16[256,1024]{1,0:T(8,128)(2,1)} %hidden.1) | copy-start | bytes 1572868
  8.3 7.8 %collective-permute-start.12 = (bf16[512,128]{1,0:T(8,128)(2,1)S(1)}, bf16[512,128]{1,0:T(8,128)(2,1)S(1)}, u32[]{:S(2)}, u32[]{:S(2)}) collective-permute-start(bf16[512,128]{1,0:T(8,128)(2,1)S(1)} %get-tuple-element.54), channel_id=1, source_target_pairs={{32,0},{33,1},{34,2},{35,3},{36,4},{37,5},{38,6},{39,7},{40,8},{41... | collective-permute-start | bytes 393224 | tf_op jit(solution)/shard_map/ppermute | solution.py:44
  9.6 9.4 %collective-permute-start.11 = (bf16[512,128]{1,0:T(8,128)(2,1)S(1)}, bf16[512,128]{1,0:T(8,128)(2,1)S(1)}, u32[]{:S(2)}, u32[]{:S(2)}) collective-permute-start(bf16[512,128]{1,0:T(8,128)(2,1)S(1)} %get-tuple-element.53), channel_id=1, source_target_pairs={{64,0},{65,1},{66,2},{67,3},{68,4},{69,5},{70,6},{71,7},{72,8},{73... | collective-permute-start | bytes 393224 | tf_op jit(solution)/shard_map/ppermute | solution.py:44
  10.9 10.9 %collective-permute-start.10 = (bf16[512,128]{1,0:T(8,128)(2,1)S(1)}, bf16[512,128]{1,0:T(8,128)(2,1)S(1)}, u32[]{:S(2)}, u32[]{:S(2)}) collective-permute-start(bf16[512,128]{1,0:T(8,128)(2,1)S(1)} %get-tuple-element.53), channel_id=1, source_target_pairs={{96,0},{97,1},{98,2},{99,3},{100,4},{101,5},{102,6},{103,7},{104,8... | collective-permute-start | bytes 393224 | tf_op jit(solution)/shard_map/ppermute | solution.py:44
  12.2 15.9 %collective-permute-start.3 = (bf16[512,128]{1,0:T(8,128)(2,1)S(1)}, bf16[512,128]{1,0:T(8,128)(2,1)S(1)}, u32[]{:S(2)}, u32[]{:S(2)}) collective-permute-start(bf16[512,128]{1,0:T(8,128)(2,1)S(1)} %get-tuple-element.47.mine), channel_id=1, source_target_pairs={{0,6},{1,7},{2,0},{3,1},{4,2},{5,3},{6,4},{7,5},{8,14},{9,15},{10,... | collective-permute-start | bytes 393224 | tf_op jit(solution)/shard_map/ppermute | solution.py:44
  15.3 13.7 %collective-permute-start.2 = (bf16[512,128]{1,0:T(8,128)(2,1)S(1)}, bf16[512,128]{1,0:T(8,128)(2,1)S(1)}, u32[]{:S(2)}, u32[]{:S(2)}) collective-permute-start(bf16[512,128]{1,0:T(8,128)(2,1)S(1)} %get-tuple-element.47.mine), channel_id=1, source_target_pairs={{0,4},{1,5},{2,6},{3,7},{4,0},{5,1},{6,2},{7,3},{8,12},{9,13},{10,... | collective-permute-start | bytes 393224 | tf_op jit(solution)/shard_map/ppermute | solution.py:44
  16.0 13.0 %collective-permute-start.1 = (bf16[512,128]{1,0:T(8,128)(2,1)S(1)}, bf16[512,128]{1,0:T(8,128)(2,1)S(1)}, u32[]{:S(2)}, u32[]{:S(2)}) collective-permute-start(bf16[512,128]{1,0:T(8,128)(2,1)S(1)} %get-tuple-element.47.mine), channel_id=1, source_target_pairs={{0,2},{1,3},{2,4},{3,5},{4,6},{5,7},{6,0},{7,1},{8,10},{9,11},{10,... | collective-permute-start | bytes 393224 | tf_op jit(solution)/shard_map/ppermute | solution.py:44
  22.5 9.8 %collective-permute-start.13 = (bf16[512,128]{1,0:T(8,128)(2,1)S(1)}, bf16[512,128]{1,0:T(8,128)(2,1)S(1)}, u32[]{:S(2)}, u32[]{:S(2)}) collective-permute-start(bf16[512,128]{1,0:T(8,128)(2,1)S(1)} %get-tuple-element.57), channel_id=1, source_target_pairs={{0,8},{1,9},{2,10},{3,11},{4,12},{5,13},{6,14},{7,15},{8,16},{9,17... | collective-permute-start | bytes 393224 | tf_op jit(solution)/shard_map/ppermute | solution.py:44
  24.5 9.5 %collective-permute-start.14 = (bf16[512,128]{1,0:T(8,128)(2,1)S(1)}, bf16[512,128]{1,0:T(8,128)(2,1)S(1)}, u32[]{:S(2)}, u32[]{:S(2)}) collective-permute-start(bf16[512,128]{1,0:T(8,128)(2,1)S(1)} %get-tuple-element.58), channel_id=1, source_target_pairs={{0,16},{1,17},{2,18},{3,19},{4,20},{5,21},{6,22},{7,23},{8,24},{9,... | collective-permute-start | bytes 393224 | tf_op jit(solution)/shard_map/ppermute | solution.py:44
  28.1 6.4 %collective-permute-start.15 = (bf16[512,128]{1,0:T(8,128)(2,1)S(1)}, bf16[512,128]{1,0:T(8,128)(2,1)S(1)}, u32[]{:S(2)}, u32[]{:S(2)}) collective-permute-start(bf16[512,128]{1,0:T(8,128)(2,1)S(1)} %get-tuple-element.59), channel_id=1, source_target_pairs={{0,24},{1,25},{2,26},{3,27},{4,28},{5,29},{6,30},{7,31},{8,0},{9,1... | collective-permute-start | bytes 393224 | tf_op jit(solution)/shard_map/ppermute | solution.py:44
  29.1 8.4 %collective-permute-start.6 = (bf16[512,128]{1,0:T(8,128)(2,1)S(1)}, bf16[512,128]{1,0:T(8,128)(2,1)S(1)}, u32[]{:S(2)}, u32[]{:S(2)}) collective-permute-start(bf16[512,128]{1,0:T(8,128)(2,1)S(1)} %shard_map.86.mine), channel_id=1, source_target_pairs={{0,24},{1,25},{2,26},{3,27},{4,28},{5,29},{6,30},{7,31},{8,0},{9,1... | collective-permute-start | bytes 393224 | tf_op jit(solution)/shard_map/ppermute | solution.py:44
  29.4 8.1 %collective-permute-start.5 = (bf16[512,128]{1,0:T(8,128)(2,1)S(1)}, bf16[512,128]{1,0:T(8,128)(2,1)S(1)}, u32[]{:S(2)}, u32[]{:S(2)}) collective-permute-start(bf16[512,128]{1,0:T(8,128)(2,1)S(1)} %shard_map.86.mine), channel_id=1, source_target_pairs={{0,16},{1,17},{2,18},{3,19},{4,20},{5,21},{6,22},{7,23},{8,24},{9,... | collective-permute-start | bytes 393224 | tf_op jit(solution)/shard_map/ppermute | solution.py:44
  32.3 6.9 %collective-permute-start.4 = (bf16[512,128]{1,0:T(8,128)(2,1)S(1)}, bf16[512,128]{1,0:T(8,128)(2,1)S(1)}, u32[]{:S(2)}, u32[]{:S(2)}) collective-permute-start(bf16[512,128]{1,0:T(8,128)(2,1)S(1)} %shard_map.86.mine), channel_id=1, source_target_pairs={{0,8},{1,9},{2,10},{3,11},{4,12},{5,13},{6,14},{7,15},{8,16},{9,17... | collective-permute-start | bytes 393224 | tf_op jit(solution)/shard_map/ppermute | solution.py:44
  34.4 33.2 %slice-start.1 = ((s8[6291456]{0:T(1024)(128)(4,1)}), s8[2097152]{0:T(1024)(128)(4,1)S(1)}, s32[]{:S(2)}) async-start(s8[6291456]{0:T(1024)(128)(4,1)} %bitcast.18), calls=%async_computation.1 | async-start | bytes 4194304
  35.1 15.7 %collective-permute-start.16 = (bf16[512,128]{1,0:T(8,128)(2,1)S(1)}, bf16[512,128]{1,0:T(8,128)(2,1)S(1)}, u32[]{:S(2)}, u32[]{:S(2)}) collective-permute-start(bf16[512,128]{1,0:T(8,128)(2,1)S(1)} %get-tuple-element.64), channel_id=1, source_target_pairs={{0,2},{1,3},{2,4},{3,5},{4,6},{5,7},{6,0},{7,1},{8,10},{9,11},{10,... | collective-permute-start | bytes 393224 | tf_op jit(solution)/shard_map/ppermute | solution.py:44
  39.3 12.1 %collective-permute-start.9 = (bf16[512,128]{1,0:T(8,128)(2,1)S(1)}, bf16[512,128]{1,0:T(8,128)(2,1)S(1)}, u32[]{:S(2)}, u32[]{:S(2)}) collective-permute-start(bf16[512,128]{1,0:T(8,128)(2,1)S(1)} %shard_map.87), channel_id=1, source_target_pairs={{0,96},{1,97},{2,98},{3,99},{4,100},{5,101},{6,102},{7,103},{8,104... | collective-permute-start | bytes 393224 | tf_op jit(solution)/shard_map/ppermute | solution.py:44
  46.0 9.1 %collective-permute-start.8 = (bf16[512,128]{1,0:T(8,128)(2,1)S(1)}, bf16[512,128]{1,0:T(8,128)(2,1)S(1)}, u32[]{:S(2)}, u32[]{:S(2)}) collective-permute-start(bf16[512,128]{1,0:T(8,128)(2,1)S(1)} %shard_map.87), channel_id=1, source_target_pairs={{0,64},{1,65},{2,66},{3,67},{4,68},{5,69},{6,70},{7,71},{8,72},{9,... | collective-permute-start | bytes 393224 | tf_op jit(solution)/shard_map/ppermute | solution.py:44
  47.3 7.9 %collective-permute-start.7 = (bf16[512,128]{1,0:T(8,128)(2,1)S(1)}, bf16[512,128]{1,0:T(8,128)(2,1)S(1)}, u32[]{:S(2)}, u32[]{:S(2)}) collective-permute-start(bf16[512,128]{1,0:T(8,128)(2,1)S(1)} %shard_map.87), channel_id=1, source_target_pairs={{0,32},{1,33},{2,34},{3,35},{4,36},{5,37},{6,38},{7,39},{8,40},{9,... | collective-permute-start | bytes 393224 | tf_op jit(solution)/shard_map/ppermute | solution.py:44
  50.8 14.3 %collective-permute-start.20 = (bf16[256,512]{1,0:T(8,128)(2,1)S(1)}, bf16[256,512]{1,0:T(8,128)(2,1)S(1)}, u32[]{:S(2)}, u32[]{:S(2)}) collective-permute-start(bf16[256,512]{1,0:T(8,128)(2,1)S(1)} %get-tuple-element.68), channel_id=1, source_target_pairs={{0,32},{1,3},{2,34},{3,5},{4,36},{5,7},{6,38},{7,1},{8,40},{9,11},... | collective-permute-start | bytes 786440 | tf_op jit(solution)/shard_map/ppermute | solution.py:44
  50.9 15.8 %collective-permute-start.21 = (bf16[256,512]{1,0:T(8,128)(2,1)S(1)}, bf16[256,512]{1,0:T(8,128)(2,1)S(1)}, u32[]{:S(2)}, u32[]{:S(2)}) collective-permute-start(bf16[256,512]{1,0:T(8,128)(2,1)S(1)} %get-tuple-element.69), channel_id=1, source_target_pairs={{0,64},{1,5},{2,66},{3,7},{4,68},{5,1},{6,70},{7,3},{8,72},{9,13},... | collective-permute-start | bytes 786440 | tf_op jit(solution)/shard_map/ppermute | solution.py:44
  51.4 16.0 %collective-permute-start.22 = (bf16[256,512]{1,0:T(8,128)(2,1)S(1)}, bf16[256,512]{1,0:T(8,128)(2,1)S(1)}, u32[]{:S(2)}, u32[]{:S(2)}) collective-permute-start(bf16[256,512]{1,0:T(8,128)(2,1)S(1)} %get-tuple-element.70), channel_id=1, source_target_pairs={{0,96},{1,7},{2,98},{3,1},{4,100},{5,3},{6,102},{7,5},{8,104},{9,1... | collective-permute-start | bytes 786440 | tf_op jit(solution)/shard_map/ppermute | solution.py:44
  55.1 6.5 %collective-permute-start.17 = (bf16[512,128]{1,0:T(8,128)(2,1)S(1)}, bf16[512,128]{1,0:T(8,128)(2,1)S(1)}, u32[]{:S(2)}, u32[]{:S(2)}) collective-permute-start(bf16[512,128]{1,0:T(8,128)(2,1)S(1)} %get-tuple-element.65), channel_id=1, source_target_pairs={{0,4},{1,5},{2,6},{3,7},{4,0},{5,1},{6,2},{7,3},{8,12},{9,13},{10,... | collective-permute-start | bytes 393224 | tf_op jit(solution)/shard_map/ppermute | solution.py:44
  55.2 6.7 %collective-permute-start.18 = (bf16[512,128]{1,0:T(8,128)(2,1)S(1)}, bf16[512,128]{1,0:T(8,128)(2,1)S(1)}, u32[]{:S(2)}, u32[]{:S(2)}) collective-permute-start(bf16[512,128]{1,0:T(8,128)(2,1)S(1)} %get-tuple-element.66), channel_id=1, source_target_pairs={{0,6},{1,7},{2,0},{3,1},{4,2},{5,3},{6,4},{7,5},{8,14},{9,15},{10,... | collective-permute-start | bytes 393224 | tf_op jit(solution)/shard_map/ppermute | solution.py:44
  61.6 7.1 %collective-permute-start.25 = (bf16[1,256,512]{2,1,0:T(8,128)(2,1)S(1)}, bf16[1,256,512]{2,1,0:T(8,128)(2,1)S(1)}, u32[]{:S(2)}, u32[]{:S(2)}) collective-permute-start(bf16[1,256,512]{2,1,0:T(8,128)(2,1)S(1)} %get-tuple-element.50.g0), channel_id=1, source_target_pairs={{0,96},{1,7},{2,98},{3,1},{4,100},{5,3},{6,102},{7,5},{8,104},{9,1... | collective-permute-start | bytes 786440 | tf_op jit(solution)/shard_map/ppermute | solution.py:44
  61.9 11.9 %collective-permute-start.24 = (bf16[1,256,512]{2,1,0:T(8,128)(2,1)S(1)}, bf16[1,256,512]{2,1,0:T(8,128)(2,1)S(1)}, u32[]{:S(2)}, u32[]{:S(2)}) collective-permute-start(bf16[1,256,512]{2,1,0:T(8,128)(2,1)S(1)} %get-tuple-element.50.g0), channel_id=1, source_target_pairs={{0,64},{1,5},{2,66},{3,7},{4,68},{5,1},{6,70},{7,3},{8,72},{9,13},... | collective-permute-start | bytes 786440 | tf_op jit(solution)/shard_map/ppermute | solution.py:44
  65.0 22.3 %collective-permute-start.28 = (bf16[2,256,512]{2,1,0:T(8,128)(2,1)S(1)}, bf16[2,256,512]{2,1,0:T(8,128)(2,1)S(1)}, u32[]{:S(2)}, u32[]{:S(2)}) collective-permute-start(bf16[2,256,512]{2,1,0:T(8,128)(2,1)S(1)} %shard_map.92.g0), channel_id=1, source_target_pairs={{0,96},{1,7},{2,98},{3,1},{4,100},{5,3},{6,102},{7,5},{8,104},{9,1... | collective-permute-start | bytes 1572872 | tf_op jit(solution)/shard_map/ppermute | solution.py:44
  66.7 23.6 %collective-permute-start.27 = (bf16[2,256,512]{2,1,0:T(8,128)(2,1)S(1)}, bf16[2,256,512]{2,1,0:T(8,128)(2,1)S(1)}, u32[]{:S(2)}, u32[]{:S(2)}) collective-permute-start(bf16[2,256,512]{2,1,0:T(8,128)(2,1)S(1)} %shard_map.92.g0), channel_id=1, source_target_pairs={{0,64},{1,5},{2,66},{3,7},{4,68},{5,1},{6,70},{7,3},{8,72},{9,13},... | collective-permute-start | bytes 1572872 | tf_op jit(solution)/shard_map/ppermute | solution.py:44
  67.5 22.8 %collective-permute-start.26 = (bf16[2,256,512]{2,1,0:T(8,128)(2,1)S(1)}, bf16[2,256,512]{2,1,0:T(8,128)(2,1)S(1)}, u32[]{:S(2)}, u32[]{:S(2)}) collective-permute-start(bf16[2,256,512]{2,1,0:T(8,128)(2,1)S(1)} %shard_map.92.g0), channel_id=1, source_target_pairs={{0,32},{1,3},{2,34},{3,5},{4,36},{5,7},{6,38},{7,1},{8,40},{9,11},... | collective-permute-start | bytes 1572872 | tf_op jit(solution)/shard_map/ppermute | solution.py:44
  68.7 46.4 %collective-permute-start.19 = (f32[256,1024]{1,0:T(8,128)S(1)}, f32[256,1024]{1,0:T(8,128)S(1)}, u32[]{:S(2)}, u32[]{:S(2)}) collective-permute-start(f32[256,1024]{1,0:T(8,128)S(1)} %fusion.13), channel_id=1, source_target_pairs={{0,1},{1,0},{2,3},{3,2},{4,5},{5,4},{6,7},{7,6},{8,9},{9,8},{10,11... | collective-permute-start | bytes 3145736 | tf_op jit(solution)/shard_map/ppermute | solution.py:48
  73.8 12.0 %collective-permute-start.23 = (bf16[1,256,512]{2,1,0:T(8,128)(2,1)S(1)}, bf16[1,256,512]{2,1,0:T(8,128)(2,1)S(1)}, u32[]{:S(2)}, u32[]{:S(2)}) collective-permute-start(bf16[1,256,512]{2,1,0:T(8,128)(2,1)S(1)} %get-tuple-element.50.g0), channel_id=1, source_target_pairs={{0,32},{1,3},{2,34},{3,5},{4,36},{5,7},{6,38},{7,1},{8,40},{9,11},... | collective-permute-start | bytes 786440 | tf_op jit(solution)/shard_map/ppermute | solution.py:44
  87.1 7.7 %collective-permute-start.29 = (bf16[1,128,512]{2,1,0:T(8,128)(2,1)S(1)}, bf16[1,128,512]{2,1,0:T(8,128)(2,1)S(1)}, u32[]{:S(2)}, u32[]{:S(2)}) collective-permute-start(bf16[1,128,512]{2,1,0:T(8,128)(2,1)S(1)} %get-tuple-element.73), channel_id=1, source_target_pairs={{0,8},{1,33},{2,10},{3,35},{4,12},{5,37},{6,14},{7,39},{8,16},{9,4... | collective-permute-start | bytes 393224 | tf_op jit(solution)/shard_map/ppermute | solution.py:44
  87.3 8.8 %collective-permute-start.30 = (bf16[1,128,512]{2,1,0:T(8,128)(2,1)S(1)}, bf16[1,128,512]{2,1,0:T(8,128)(2,1)S(1)}, u32[]{:S(2)}, u32[]{:S(2)}) collective-permute-start(bf16[1,128,512]{2,1,0:T(8,128)(2,1)S(1)} %get-tuple-element.74), channel_id=1, source_target_pairs={{0,16},{1,65},{2,18},{3,67},{4,20},{5,69},{6,22},{7,71},{8,24},{9,... | collective-permute-start | bytes 393224 | tf_op jit(solution)/shard_map/ppermute | solution.py:44
  92.2 12.8 %collective-permute-start.32 = (bf16[2,128,512]{2,1,0:T(8,128)(2,1)S(1)}, bf16[2,128,512]{2,1,0:T(8,128)(2,1)S(1)}, u32[]{:S(2)}, u32[]{:S(2)}) collective-permute-start(bf16[2,128,512]{2,1,0:T(8,128)(2,1)S(1)} %get-tuple-element.76), channel_id=1, source_target_pairs={{0,8},{1,33},{2,10},{3,35},{4,12},{5,37},{6,14},{7,39},{8,16},{9,4... | collective-permute-start | bytes 786440 | tf_op jit(solution)/shard_map/ppermute | solution.py:44
  93.3 11.7 %collective-permute-start.33 = (bf16[2,128,512]{2,1,0:T(8,128)(2,1)S(1)}, bf16[2,128,512]{2,1,0:T(8,128)(2,1)S(1)}, u32[]{:S(2)}, u32[]{:S(2)}) collective-permute-start(bf16[2,128,512]{2,1,0:T(8,128)(2,1)S(1)} %get-tuple-element.77), channel_id=1, source_target_pairs={{0,16},{1,65},{2,18},{3,67},{4,20},{5,69},{6,22},{7,71},{8,24},{9,... | collective-permute-start | bytes 786440 | tf_op jit(solution)/shard_map/ppermute | solution.py:44
  94.8 10.2 %collective-permute-start.34 = (bf16[2,128,512]{2,1,0:T(8,128)(2,1)S(1)}, bf16[2,128,512]{2,1,0:T(8,128)(2,1)S(1)}, u32[]{:S(2)}, u32[]{:S(2)}) collective-permute-start(bf16[2,128,512]{2,1,0:T(8,128)(2,1)S(1)} %get-tuple-element.78), channel_id=1, source_target_pairs={{0,24},{1,97},{2,26},{3,99},{4,28},{5,101},{6,30},{7,103},{8,0},{9... | collective-permute-start | bytes 786440 | tf_op jit(solution)/shard_map/ppermute | solution.py:44
  96.1 8.9 %collective-permute-start.31 = (bf16[1,128,512]{2,1,0:T(8,128)(2,1)S(1)}, bf16[1,128,512]{2,1,0:T(8,128)(2,1)S(1)}, u32[]{:S(2)}, u32[]{:S(2)}) collective-permute-start(bf16[1,128,512]{2,1,0:T(8,128)(2,1)S(1)} %get-tuple-element.75), channel_id=1, source_target_pairs={{0,24},{1,97},{2,26},{3,99},{4,28},{5,101},{6,30},{7,103},{8,0},{9... | collective-permute-start | bytes 393224 | tf_op jit(solution)/shard_map/ppermute | solution.py:44
  105.9 7.1 %collective-permute-start.35 = (bf16[3,32,512]{2,1,0:T(8,128)(2,1)S(1)}, bf16[3,32,512]{2,1,0:T(8,128)(2,1)S(1)}, u32[]{:S(2)}, u32[]{:S(2)}) collective-permute-start(bf16[3,32,512]{2,1,0:T(8,128)(2,1)S(1)} %get-tuple-element.80), channel_id=1, source_target_pairs={{0,2},{1,9},{2,4},{3,11},{4,6},{5,13},{6,0},{7,15},{8,10},{9,17},{... | collective-permute-start | bytes 294920 | tf_op jit(solution)/shard_map/ppermute | solution.py:44
  107.4 6.1 %collective-permute-start.36 = (bf16[3,32,512]{2,1,0:T(8,128)(2,1)S(1)}, bf16[3,32,512]{2,1,0:T(8,128)(2,1)S(1)}, u32[]{:S(2)}, u32[]{:S(2)}) collective-permute-start(bf16[3,32,512]{2,1,0:T(8,128)(2,1)S(1)} %get-tuple-element.81), channel_id=1, source_target_pairs={{0,4},{1,17},{2,6},{3,19},{4,0},{5,21},{6,2},{7,23},{8,12},{9,25},... | collective-permute-start | bytes 294920 | tf_op jit(solution)/shard_map/ppermute | solution.py:44
  109.7 4.6 %collective-permute-start.37 = (bf16[3,32,512]{2,1,0:T(8,128)(2,1)S(1)}, bf16[3,32,512]{2,1,0:T(8,128)(2,1)S(1)}, u32[]{:S(2)}, u32[]{:S(2)}) collective-permute-start(bf16[3,32,512]{2,1,0:T(8,128)(2,1)S(1)} %get-tuple-element.82), channel_id=1, source_target_pairs={{0,6},{1,25},{2,0},{3,27},{4,2},{5,29},{6,4},{7,31},{8,14},{9,1},{... | collective-permute-start | bytes 294920 | tf_op jit(solution)/shard_map/ppermute | solution.py:44
